TPU v7x, 256 devices: a whole 4x4x8 slice. The times are simulated.
256 devices in a mesh: rows: 64 (over x, z, core), cols: 4 (over y).
Axes of the slice: x: 4, y: 4, z: 8, core: 2. Of those that a mesh axis runs over, the one named last changes fastest.
Arguments:
- block_list: int32 [512, 24], P('rows', 'cols'), may hold values from -1 to 511, as said below
- points: bfloat16 [16, 131072], P(None, 'rows'), may hold values from -4 to 4
- targets: float32 [32, 131072], P(None, 'rows'), may hold values from -6 to 6
Outputs:
- solution: float32 [32, 131072], P(None, 'rows')
- residual: float32 [32, 131072], P(None, 'rows')
Inputs may be any that keep to these rules, and one draw needn't show every extreme that they name: `block_list`: A non-empty entry j of block row i satisfies j <= i. Within the 6 slots of a block row held by one index of cols, the entries lie in different groups of 8 consecutive blocks. Of all slots held by one device (8 block rows of 6 slots), at most 1 name blocks of any one group of 8 consecutive blocks, and in every draw some device reaches 1.
All inputs are finite; a program needn't handle non-finite values.
Results may differ from a plain program's by a relative error of at most 0.0057.
Values may be sent and summed in bfloat16 or wider, within the bound.
A program may use at most 64 MiB of HBM per device.

v0:
```python
import jax
import jax.numpy as jnp
from jax import lax
from jax.sharding import PartitionSpec as P

ITERS = 2


REG = 1.5
RADIUS = 0.25


def wendland(left_x, right_x):
    left_f = left_x.astype(jnp.float32)
    right_f = right_x.astype(jnp.float32)
    left_sq = jnp.sum(left_f * left_f, axis=1)
    right_sq = jnp.sum(right_f * right_f, axis=1)
    inner_prod = jnp.einsum("nda,ndb->nab", left_f, right_f, precision=lax.Precision.HIGHEST)
    dist_sq = left_sq[:, :, None] + right_sq[:, None, :] - 2.0 * inner_prod
    scaled = jnp.sqrt(jnp.maximum(dist_sq, 0.0)) / RADIUS
    remain = jnp.maximum(1.0 - scaled, 0.0)
    square = remain * remain
    return square * square * (4.0 * scaled + 1.0)


def local(block_list, points, targets):
    row_count = lax.axis_size("rows")
    row_index = lax.axis_index("rows")
    block_rows, slot_width = block_list.shape
    coord_dim, npoints = points.shape
    outputs = targets.shape[0]
    block_len = npoints // block_rows
    slot_count = block_rows * slot_width
    capacity = (slot_count + row_count - 1) // row_count
    buffer_len = row_count * capacity
    turn_rows = 4
    turn_count = block_rows // turn_rows
    entries = block_list.reshape(slot_count)
    is_live = entries >= 0
    owners = jnp.where(is_live, entries // block_rows, 0)
    local_idx = jnp.where(is_live, entries - owners * block_rows, 0)
    first_row = row_index * block_rows
    row_global = first_row + jnp.arange(slot_count, dtype=jnp.int32) // slot_width
    off_diag = is_live & (entries != row_global)
    owner_hits = (
        (owners[:, None] == jnp.arange(row_count, dtype=jnp.int32)[None, :]) & is_live[:, None]
    ).astype(jnp.int32)
    slot_rank = jnp.sum((jnp.cumsum(owner_hits, axis=0) - owner_hits) * owner_hits, axis=1)
    place_at = jnp.where(is_live, owners * capacity + slot_rank, buffer_len)
    pick_at = jnp.minimum(place_at, buffer_len - 1)
    wanted = jnp.full((buffer_len,), -1, jnp.int32).at[place_at].set(local_idx, mode="drop")
    askers = jnp.full((buffer_len,), -1, jnp.int32).at[place_at].set(row_global, mode="drop")
    request = jnp.stack([wanted, askers], axis=1).reshape(row_count, capacity, 2)
    incoming = lax.all_to_all(request, "rows", split_axis=0, concat_axis=0, tiled=True).reshape(
        buffer_len, 2
    )
    in_live = incoming[:, 0] >= 0
    in_idx = jnp.maximum(incoming[:, 0], 0)
    collect_map = (
        (in_idx[None, :] == jnp.arange(block_rows, dtype=jnp.int32)[:, None]) & in_live[None, :]
    ).astype(jnp.float32)

    def serve(blocks):
        chosen = jnp.where(in_live[:, None, None], blocks[in_idx], jnp.zeros((), blocks.dtype))
        arrived = lax.all_to_all(
            chosen.reshape(row_count, capacity, blocks.shape[1], block_len),
            "rows",
            split_axis=0,
            concat_axis=0,
            tiled=True,
        )
        gotten = arrived.reshape(buffer_len, blocks.shape[1], block_len)[pick_at]
        return jnp.where(is_live[:, None, None], gotten, jnp.zeros((), gotten.dtype))

    def collect(terms):
        flat = terms.reshape(buffer_len, -1)
        summed = jnp.dot(
            collect_map, flat, precision=lax.Precision.HIGHEST, preferred_element_type=jnp.float32
        )
        return summed.reshape(block_rows, terms.shape[1], block_len)

    def give_back(mirror):
        placed = (
            jnp.zeros((buffer_len,) + mirror.shape[1:], jnp.float32)
            .at[place_at]
            .set(mirror, mode="drop")
        )
        arrived = lax.all_to_all(
            placed.reshape(row_count, capacity, mirror.shape[1], block_len),
            "rows",
            split_axis=0,
            concat_axis=0,
            tiled=True,
        )
        return collect(arrived.reshape(buffer_len, mirror.shape[1], block_len))

    def column_total(partial_value):
        return lax.psum(partial_value, "cols")

    def global_sum(values):
        return lax.psum(values, "rows")

    own_x = points.reshape(coord_dim, block_rows, block_len).transpose(1, 0, 2)
    far_x = serve(own_x)
    grouped_x = own_x.reshape(turn_count, turn_rows, coord_dim, block_len)
    grouped_far = far_x.reshape(turn_count, turn_rows * slot_width, coord_dim, block_len)
    grouped_live = is_live.reshape(turn_count, turn_rows * slot_width)
    grouped_off = off_diag.reshape(turn_count, turn_rows * slot_width)

    def row_pass(own_w, far_w):

        def row_step(pieces):
            near_x, remote_x, live_now, off_now = (pieces[0], pieces[1], pieces[2], pieces[3])
            values = jnp.where(
                live_now[:, None, None],
                wendland(jnp.repeat(near_x, slot_width, axis=0), remote_x),
                0.0,
            )
            if own_w is None:
                direct = jnp.sum(
                    jnp.sum(values, axis=2).reshape(turn_rows, slot_width, block_len), axis=1
                )[:, None, :]
                mirror = jnp.where(off_now[:, None], jnp.sum(values, axis=1), 0.0)[:, None, :]
                return (direct, mirror)
            kernel_bf = values.astype(jnp.bfloat16)
            direct = jnp.einsum(
                "nab,nob->noa", kernel_bf, pieces[5], preferred_element_type=jnp.float32
            )
            direct = jnp.sum(direct.reshape(turn_rows, slot_width, outputs, block_len), axis=1)
            mirror = jnp.einsum(
                "nab,noa->nob",
                kernel_bf,
                jnp.repeat(pieces[4], slot_width, axis=0),
                preferred_element_type=jnp.float32,
            )
            return (direct, jnp.where(off_now[:, None, None], mirror, 0.0))

        pieces = (grouped_x, grouped_far, grouped_live, grouped_off)
        if own_w is not None:
            pieces = pieces + (
                own_w.reshape(turn_count, turn_rows, outputs, block_len),
                far_w.reshape(turn_count, turn_rows * slot_width, outputs, block_len),
            )
        results = lax.map(row_step, pieces)
        channels = results[0].shape[2]
        direct = results[0].reshape(block_rows, channels, block_len)
        return (direct, results[1].reshape(slot_count, channels, block_len))

    direct, mirror = row_pass(None, None)
    degree_part = direct + give_back(mirror)
    inv_root = 1.0 / jnp.sqrt(1.0 + column_total(degree_part))
    resid = targets.reshape(outputs, block_rows, block_len).transpose(1, 0, 2)
    direction = resid
    solution = jnp.zeros_like(resid)
    norm_now = global_sum(jnp.sum(resid * resid, axis=(0, 2)))
    for iteration in range(ITERS):
        weights = (direction * inv_root).astype(jnp.bfloat16)
        apply_far_w = serve(weights)
        apply_direct, apply_mirror = row_pass(weights, apply_far_w)
        apply_partial_value = apply_direct + give_back(apply_mirror)
        applied = REG * direction + inv_root * column_total(apply_partial_value)
        step_size = norm_now / global_sum(jnp.sum(direction * applied, axis=(0, 2)))
        solution = solution + step_size[None, :, None] * direction
        resid = resid - step_size[None, :, None] * applied
        if iteration + 1 < ITERS:
            norm_next = global_sum(jnp.sum(resid * resid, axis=(0, 2)))
            direction = resid + (norm_next / norm_now)[None, :, None] * direction
            norm_now = norm_next
    return (
        solution.transpose(1, 0, 2).reshape(outputs, npoints),
        resid.transpose(1, 0, 2).reshape(outputs, npoints),
    )


def solution(mesh):
    placed = (P("rows", "cols"), P(None, "rows"), P(None, "rows"))
    return jax.shard_map(
        local,
        mesh=mesh,
        in_specs=placed,
        out_specs=(P(None, "rows"), P(None, "rows")),
        check_vma=False,
    )
```

profile of v0, /device:TPU:1, one launch (start us, length us, event | category | flops | bytes accessed | tf_op | source)
XLA Modules:
  0.0 809.5 jit_solution(6442422851500337374)
XLA Ops:
  11.4 13.0 %all-to-all-start = ((s32[64,1,2]{2,1,0:T(1,128)}), s32[64,1,2]{2,1,0:T(1,128)S(1)}, u32[]{:S(2)}, u32[]{:S(2)}) async-start(s32[64,1,2]{2,1,0:T(1,128)} %copy.22), calls=%async_computation | async-start | bytes 65536 | tf_op jit(solution)/shard_map/all_to_all | solution.py:54
  25.2 8.4 %all-to-all-done = s32[64,1,2]{2,1,0:T(1,128)S(1)} async-done(((s32[64,1,2]{2,1,0:T(1,128)}), s32[64,1,2]{2,1,0:T(1,128)S(1)}, u32[]{:S(2)}, u32[]{:S(2)}) %all-to-all-start) | async-done | bytes 544 | tf_op jit(solution)/shard_map/all_to_all | solution.py:54
  40.1 17.2 %all-to-all-done.1 = bf16[64,1,16,256]{3,2,1,0:T(8,128)(2,1)S(1)} async-done(((bf16[64,1,16,256]{3,2,1,0:T(8,128)(2,1)}), bf16[64,1,16,256]{3,2,1,0:T(8,128)(2,1)S(1)}, u32[]{:S(2)}, u32[]{:S(2)}) %all-to-all-start.1) | async-done | bytes 524320 | tf_op jit(solution)/shard_map/all_to_all | solution.py:65
  58.1 12.5 %while.42 = (s32[]{:T(128)}, f32[2,4,1,256]{3,2,1,0:T(1,128)S(1)}, f32[2,24,1,256]{3,1,2,0:T(8,128)S(1)}, pred[2,24]{1,0:T(4,128)(4,1)S(1)}, bf16[2,4,16,256]{3,...) while((s32[]{:T(128)}, f32[2,4,1,256]{3,2,1,0:T(1,128)S(1)}, ...), condition=%wide.region_12.13_spmd, body=%wide.region_6.12_spmd.sunk | while | flops 74260480 | bytes 1274609 | solution.py:144
  58.3 5.9 fusion.105
  64.5 5.9 fusion.105
  72.0 6.4 all-to-all-start.2
  78.6 9.6 %all-to-all-done.2 = f32[64,1,1,256]{3,2,1,0:T(1,128)S(1)} async-done(((f32[64,1,1,256]{3,2,1,0:T(1,128)}), f32[64,1,1,256]{3,2,1,0:T(1,128)S(1)}, u32[]{:S(2)}, u32[]{:S(2)}) %all-to-all-start.2) | async-done | bytes 65568 | tf_op jit(solution)/shard_map/all_to_all | solution.py:88
  88.3 8.8 %psum.50 = f32[8,1,256]{2,0,1:T(8,128)S(1)} all-reduce(f32[8,1,256]{2,0,1:T(8,128)S(1)} %fusion.37), channel_id=1, replica_groups=mesh['rows'=64,'cols'=4] {'cols'}, use_global_device_ids=true, to_apply=%region_14.15 | all-reduce | flops 2048 | bytes 16384 | tf_op jit(solution)/shard_map/psum | solution.py:98
  99.0 6.5 all-to-all-start.3
  105.5 28.5 %all-to-all-done.3 = bf16[64,1,32,256]{3,2,1,0:T(8,128)(2,1)S(1)} async-done(((bf16[64,1,32,256]{3,2,1,0:T(8,128)(2,1)}), bf16[64,1,32,256]{3,2,1,0:T(8,128)(2,1)S(1)}, u32[]{:S(2)}, u32[]{:S(2)}) %all-to-all-start.3) | async-done | bytes 1048608 | tf_op jit(solution)/shard_map/all_to_all | solution.py:65
  136.2 16.1 %while.43 = (s32[]{:T(128)}, f32[2,4,32,256]{3,2,1,0:T(8,128)S(1)}, f32[2,24,32,256]{3,2,1,0:T(8,128)}, bf16[2,24,32,256]{3,2,1,0:T(8,128)(2,1)S(1)}, pred[2,24]...) while((s32[]{:T(128)}, f32[2,4,32,256]{3,2,1,0:T(8,128)S(1)}, ...), condition=%wide.region_19.20_spmd, body=%wide.region_15.19_spmd.sunk | while | flops 274375680 | bytes 14607621 | solution.py:144
  136.4 5.1 select_convert_fusion.4
  152.6 5.1 scatter_fusion
  157.7 57.4 %all_to_all.35 = f32[64,1,32,256]{3,2,1,0:T(8,128)S(1)} all-to-all(f32[64,1,32,256]{3,2,1,0:T(8,128)S(1)} %bitcast.324), channel_id=1, replica_groups=mesh['rows'=64,'cols'=4] {'rows'}, dimensions={0} | all-to-all | bytes 4194304 | tf_op jit(solution)/shard_map/all_to_all | solution.py:88
  217.9 39.1 %all-reduce.4.cloned.1.call-done = f32[8,32,256]{2,0,1:T(8,128)} async-done(((f32[8,32,256]{2,0,1:T(8,128)}), f32[8,32,256]{2,0,1:T(8,128)}) %all-reduce.4.cloned.1.call-update) | async-done | bytes 262160 | tf_op jit(solution)/shard_map/psum | solution.py:98
  258.3 126.7 %all-reduce = (f32[32]{0:T(128)S(1)}, f32[32]{0:T(128)S(1)}) all-reduce(f32[32]{0:T(128)S(1)} %get-tuple-element.383, f32[32]{0:T(128)S(1)} %get-tuple-element.382), channel_id=1, replica_groups=mesh['rows'=64,'cols'=4] {'rows'}, use_global_device_ids=true, to_apply=%region_1.2 | all-reduce | flops 64 | bytes 512 | tf_op jit(solution)/shard_map/psum | solution.py:101
  386.5 126.3 %psum.53 = f32[32]{0:T(128)S(1)} all-reduce(f32[32]{0:T(128)S(1)} %multiply_reduce_fusion.7), channel_id=1, replica_groups=mesh['rows'=64,'cols'=4] {'rows'}, use_global_device_ids=true, to_apply=%region_25.26 | all-reduce | flops 32 | bytes 256 | tf_op jit(solution)/shard_map/psum | solution.py:101
  514.7 32.5 %all_to_all.37 = bf16[64,1,32,256]{3,2,1,0:T(8,128)(2,1)S(1)} all-to-all(bf16[64,1,32,256]{3,2,1,0:T(8,128)(2,1)S(1)} %fusion.38), channel_id=1, replica_groups=mesh['rows'=64,'cols'=4] {'rows'}, dimensions={0} | all-to-all | bytes 2097152 | tf_op jit(solution)/shard_map/all_to_all | solution.py:65
  549.3 16.1 %while.44 = (s32[]{:T(128)}, f32[2,4,32,256]{3,2,1,0:T(8,128)S(1)}, f32[2,24,32,256]{3,2,1,0:T(8,128)}, bf16[2,24,32,256]{3,2,1,0:T(8,128)(2,1)S(1)}, pred[2,24]...) while((s32[]{:T(128)}, f32[2,4,32,256]{3,2,1,0:T(8,128)S(1)}, ...), condition=%wide.region_30.31_spmd, body=%wide.region_26.30_spmd.sunk | while | flops 274375680 | bytes 14607621 | solution.py:144
  565.7 5.1 scatter_fusion.1
  570.9 57.4 %all_to_all.36 = f32[64,1,32,256]{3,2,1,0:T(8,128)S(1)} all-to-all(f32[64,1,32,256]{3,2,1,0:T(8,128)S(1)} %bitcast.323), channel_id=1, replica_groups=mesh['rows'=64,'cols'=4] {'rows'}, dimensions={0} | all-to-all | bytes 4194304 | tf_op jit(solution)/shard_map/all_to_all | solution.py:88
  631.0 40.7 %all-reduce.6.cloned.1.call-done = f32[8,32,256]{2,0,1:T(8,128)} async-done(((f32[8,32,256]{2,0,1:T(8,128)}), f32[8,32,256]{2,0,1:T(8,128)}) %all-reduce.6.cloned.1.call-update) | async-done | bytes 262160 | tf_op jit(solution)/shard_map/psum | solution.py:98
  673.2 126.7 %psum.55 = f32[32]{0:T(128)S(1)} all-reduce(f32[32]{0:T(128)S(1)} %multiply_reduce_fusion.6), channel_id=1, replica_groups=mesh['rows'=64,'cols'=4] {'rows'}, use_global_device_ids=true, to_apply=%region_34.35 | all-reduce | flops 32 | bytes 256 | tf_op jit(solution)/shard_map/psum | solution.py:101
  (154 shorter events, 62.1 us)
Async XLA Ops:
  7.2 32.8 %copy-start.5 = (s32[8,6]{1,0:T(8,128)S(1)}, s32[8,6]{1,0:T(8,128)}, u32[]{:S(2)}) copy-start(s32[8,6]{1,0:T(8,128)} %param.9) | copy-start | bytes 580
  11.4 22.2 %all-to-all-start = ((s32[64,1,2]{2,1,0:T(1,128)}), s32[64,1,2]{2,1,0:T(1,128)S(1)}, u32[]{:S(2)}, u32[]{:S(2)}) async-start(s32[64,1,2]{2,1,0:T(1,128)} %copy.22), calls=%async_computation | async-start | bytes 65536 | tf_op jit(solution)/shard_map/all_to_all | solution.py:54
  35.2 22.1 %all-to-all-start.1 = ((bf16[64,1,16,256]{3,2,1,0:T(8,128)(2,1)}), bf16[64,1,16,256]{3,2,1,0:T(8,128)(2,1)S(1)}, u32[]{:S(2)}, u32[]{:S(2)}) async-start(bf16[64,1,16,256]{3,2,1,0:T(8,128)(2,1)} %bitcast_select_fusion.2), calls=%async_computation.1 | async-start | bytes 1048576 | tf_op jit(solution)/shard_map/all_to_all | solution.py:65
  58.0 20.4 %copy-start.4 = (f32[32,2048]{1,0:T(8,128)S(1)}, f32[32,2048]{1,0:T(8,128)}, u32[]{:S(2)}) copy-start(f32[32,2048]{1,0:T(8,128)} %param.11) | copy-start | bytes 786436
  72.0 16.2 %all-to-all-start.2 = ((f32[64,1,1,256]{3,2,1,0:T(1,128)}), f32[64,1,1,256]{3,2,1,0:T(1,128)S(1)}, u32[]{:S(2)}, u32[]{:S(2)}) async-start(f32[64,1,1,256]{3,2,1,0:T(1,128)} %reshape.420), calls=%async_computation.2 | async-start | bytes 131072 | tf_op jit(solution)/shard_map/all_to_all | solution.py:88
  78.5 20.5 %copy-start = (f32[4,8,8,256]{3,2,1,0:T(8,128)}, f32[4,8,8,256]{3,2,1,0:T(8,128)S(1)}, u32[]{:S(2)}) copy-start(f32[4,8,8,256]{3,2,1,0:T(8,128)S(1)} %copy.51) | copy-start | bytes 786436
  99.0 35.1 %all-to-all-start.3 = ((bf16[64,1,32,256]{3,2,1,0:T(8,128)(2,1)}), bf16[64,1,32,256]{3,2,1,0:T(8,128)(2,1)S(1)}, u32[]{:S(2)}, u32[]{:S(2)}) async-start(bf16[64,1,32,256]{3,2,1,0:T(8,128)(2,1)} %fusion.39), calls=%async_computation.3 | async-start | bytes 2097152 | tf_op jit(solution)/shard_map/all_to_all | solution.py:65
  105.5 151.6 %all-reduce.4.cloned.1.call-start = ((), (), s32[]{:S(2)}) async-start(), calls=%async_computation.7 | async-start | bytes 524288 | tf_op jit(solution)/shard_map/psum | solution.py:98
  157.7 99.3 %copy-start.1 = (f32[4,8,8,256]{3,2,1,0:T(8,128)S(1)}, f32[4,8,8,256]{3,2,1,0:T(8,128)}, u32[]{:S(2)}) copy-start(f32[4,8,8,256]{3,2,1,0:T(8,128)} %copy-done) | copy-start | bytes 786436
  217.9 453.9 %all-reduce.6.cloned.1.call-start = ((), (), s32[]{:S(2)}) async-start(), calls=%async_computation.8 | async-start | bytes 524288 | tf_op jit(solution)/shard_map/psum | solution.py:98
  570.8 100.9 %copy-start.2 = (f32[4,8,8,256]{3,2,1,0:T(8,128)S(1)}, f32[4,8,8,256]{3,2,1,0:T(8,128)}, u32[]{:S(2)}) copy-start(f32[4,8,8,256]{3,2,1,0:T(8,128)} %copy-done) | copy-start | bytes 786436
  570.8 100.9 %copy-start.3 = (f32[8,32,256]{2,0,1:T(8,128)S(1)}, f32[8,32,256]{2,0,1:T(8,128)}, u32[]{:S(2)}) copy-start(f32[8,32,256]{2,0,1:T(8,128)} %all-reduce.4.cloned.1.call-done) | copy-start | bytes 786436
Sparse Core Ops, SparseCore 0:
  218.0 38.9 all-reduce.3
  631.1 40.5 all-reduce.5
where the time goes:
time: 811 us; the launch traced here: 810 us
  blocking collectives  536 us (66%)
  waiting for transfers between devices  144 us (18%)
  matrix products  47.9 us (6%)
  starting transfers between devices  30.7 us (4%)
  local copies, waits for them, and re-layouts  25.6 us (3%)
  between operations  14.4 us (2%)
  other arithmetic  10.8 us (1%)
    psum x3, blocking collectives, global_sum(): return lax.psum(values, 'rows')  380 us
    all_to_all x2, blocking collectives, give_back(): lax.all_to_all(placed.reshape(row_count, capacity, mirror.shape[1], block...  115 us
    psum x2, waiting for transfers between devices, column_total(): return lax.psum(partial_value, 'cols')  79.9 us
    all_to_all x2, waiting for transfers between devices, serve(): lax.all_to_all(chosen.reshape(row_count, capacity, blocks.shape[1], block...  45.8 us
    all_to_all x1, blocking collectives, serve(): lax.all_to_all(chosen.reshape(row_count, capacity, blocks.shape[1], block...  32.5 us
    dot_general x6, matrix products, wendland(): jnp.einsum('nda,ndb->nab', left_f, right_f, precision=lax.Precision.HIGHEST)  32.3 us
  transfers between devices with their start and end apart: 6, of which 6 were waited for; matrix products, arithmetic and copies ran while one was open for 0% of the time, Pallas kernels for 0%

commit v1 on v0

--- a/solution.py
+++ b/solution.py
@@ -97,8 +97,11 @@
     def column_total(partial_value):
         return lax.psum(partial_value, "cols")
 
+    col_index = lax.axis_index("cols")
+
     def global_sum(values):
-        return lax.psum(values, "rows")
+        masked = jnp.where(col_index == 0, values, jnp.zeros_like(values))
+        return lax.psum(masked, ("rows", "cols"))
 
     own_x = points.reshape(coord_dim, block_rows, block_len).transpose(1, 0, 2)
     far_x = serve(own_x)

time: 811 us -> 662 us (0.82)
  blocking collectives: 536 us -> 389 us
    psum x3, blocking collectives: 380 us -> 230 us  [global_sum(): return lax.psum(masked, ('rows', 'cols'))]
where the time goes in v1:
time: 662 us; the launch traced here: 661 us
  blocking collectives  389 us (59%)
  waiting for transfers between devices  142 us (21%)
  matrix products  48 us (7%)
  starting transfers between devices  30.7 us (5%)
  local copies, waits for them, and re-layouts  25.6 us (4%)
  between operations  14.4 us (2%)
  other arithmetic  10.8 us (2%)
    psum x3, blocking collectives, global_sum(): return lax.psum(masked, ('rows', 'cols'))  230 us
    all_to_all x2, blocking collectives, give_back(): lax.all_to_all(placed.reshape(row_count, capacity, mirror.shape[1], block...  115 us
    psum x2, waiting for transfers between devices, column_total(): return lax.psum(partial_value, 'cols')  78.2 us
    all_to_all x2, waiting for transfers between devices, serve(): lax.all_to_all(chosen.reshape(row_count, capacity, blocks.shape[1], block...  45.8 us
    all_to_all x1, blocking collectives, serve(): lax.all_to_all(chosen.reshape(row_count, capacity, blocks.shape[1], block...  35.9 us
    dot_general x6, matrix products, wendland(): jnp.einsum('nda,ndb->nab', left_f, right_f, precision=lax.Precision.HIGHEST)  32.3 us
  transfers between devices with their start and end apart: 6, of which 6 were waited for; matrix products, arithmetic and copies ran while one was open for 0% of the time, Pallas kernels for 0%

profile of v1, /device:TPU:1, one launch (start us, length us, event | category | flops | bytes accessed | tf_op | source)
XLA Modules:
  0.0 661.1 jit_solution(2877136188810748866)
XLA Ops:
  11.4 13.0 %all-to-all-start = ((s32[64,1,2]{2,1,0:T(1,128)}), s32[64,1,2]{2,1,0:T(1,128)S(1)}, u32[]{:S(2)}, u32[]{:S(2)}) async-start(s32[64,1,2]{2,1,0:T(1,128)} %copy.22), calls=%async_computation | async-start | bytes 65536 | tf_op jit(solution)/shard_map/all_to_all | solution.py:54
  25.2 8.4 %all-to-all-done = s32[64,1,2]{2,1,0:T(1,128)S(1)} async-done(((s32[64,1,2]{2,1,0:T(1,128)}), s32[64,1,2]{2,1,0:T(1,128)S(1)}, u32[]{:S(2)}, u32[]{:S(2)}) %all-to-all-start) | async-done | bytes 544 | tf_op jit(solution)/shard_map/all_to_all | solution.py:54
  40.1 17.2 %all-to-all-done.1 = bf16[64,1,16,256]{3,2,1,0:T(8,128)(2,1)S(1)} async-done(((bf16[64,1,16,256]{3,2,1,0:T(8,128)(2,1)}), bf16[64,1,16,256]{3,2,1,0:T(8,128)(2,1)S(1)}, u32[]{:S(2)}, u32[]{:S(2)}) %all-to-all-start.1) | async-done | bytes 524320 | tf_op jit(solution)/shard_map/all_to_all | solution.py:65
  58.1 12.5 %while.42 = (s32[]{:T(128)}, f32[2,4,1,256]{3,2,1,0:T(1,128)S(1)}, f32[2,24,1,256]{3,1,2,0:T(8,128)S(1)}, pred[2,24]{1,0:T(4,128)(4,1)S(1)}, bf16[2,4,16,256]{3,...) while((s32[]{:T(128)}, f32[2,4,1,256]{3,2,1,0:T(1,128)S(1)}, ...), condition=%wide.region_12.13_spmd, body=%wide.region_6.12_spmd.sunk | while | flops 74260480 | bytes 1274609 | solution.py:147
  58.3 5.9 fusion.105
  64.5 5.9 fusion.105
  72.0 6.4 all-to-all-start.2
  78.6 9.6 %all-to-all-done.2 = f32[64,1,1,256]{3,2,1,0:T(1,128)S(1)} async-done(((f32[64,1,1,256]{3,2,1,0:T(1,128)}), f32[64,1,1,256]{3,2,1,0:T(1,128)S(1)}, u32[]{:S(2)}, u32[]{:S(2)}) %all-to-all-start.2) | async-done | bytes 65568 | tf_op jit(solution)/shard_map/all_to_all | solution.py:88
  88.3 8.8 %psum.50 = f32[8,1,256]{2,0,1:T(8,128)S(1)} all-reduce(f32[8,1,256]{2,0,1:T(8,128)S(1)} %fusion.37), channel_id=1, replica_groups=mesh['rows'=64,'cols'=4] {'cols'}, use_global_device_ids=true, to_apply=%region_14.15 | all-reduce | flops 2048 | bytes 16384 | tf_op jit(solution)/shard_map/psum | solution.py:98
  99.0 6.5 all-to-all-start.3
  105.5 28.5 %all-to-all-done.3 = bf16[64,1,32,256]{3,2,1,0:T(8,128)(2,1)S(1)} async-done(((bf16[64,1,32,256]{3,2,1,0:T(8,128)(2,1)}), bf16[64,1,32,256]{3,2,1,0:T(8,128)(2,1)S(1)}, u32[]{:S(2)}, u32[]{:S(2)}) %all-to-all-start.3) | async-done | bytes 1048608 | tf_op jit(solution)/shard_map/all_to_all | solution.py:65
  136.2 16.1 %while.43 = (s32[]{:T(128)}, f32[2,4,32,256]{3,2,1,0:T(8,128)S(1)}, f32[2,24,32,256]{3,2,1,0:T(8,128)}, bf16[2,24,32,256]{3,2,1,0:T(8,128)(2,1)S(1)}, pred[2,24]...) while((s32[]{:T(128)}, f32[2,4,32,256]{3,2,1,0:T(8,128)S(1)}, ...), condition=%wide.region_19.20_spmd, body=%wide.region_15.19_spmd.sunk | while | flops 274375680 | bytes 14607621 | solution.py:147
  136.4 5.1 select_convert_fusion.4
  152.6 5.1 scatter_fusion
  157.7 57.4 %all_to_all.35 = f32[64,1,32,256]{3,2,1,0:T(8,128)S(1)} all-to-all(f32[64,1,32,256]{3,2,1,0:T(8,128)S(1)} %bitcast.324), channel_id=1, replica_groups=mesh['rows'=64,'cols'=4] {'rows'}, dimensions={0} | all-to-all | bytes 4194304 | tf_op jit(solution)/shard_map/all_to_all | solution.py:88
  217.9 39.1 %all-reduce.4.cloned.1.call-done = f32[8,32,256]{2,0,1:T(8,128)} async-done(((f32[8,32,256]{2,0,1:T(8,128)}), f32[8,32,256]{2,0,1:T(8,128)}) %all-reduce.4.cloned.1.call-update) | async-done | bytes 262160 | tf_op jit(solution)/shard_map/psum | solution.py:98
  258.3 78.0 %all-reduce = (f32[32]{0:T(128)S(1)}, f32[32]{0:T(128)S(1)}) all-reduce(f32[32]{0:T(128)S(1)} %get-tuple-element.459, f32[32]{0:T(128)S(1)} %get-tuple-element.458), channel_id=1, replica_groups=mesh['rows'=64,'cols'=4] {'rows','cols'}, use_global_device_ids=true, to_apply=%region_1.2 | all-reduce | flops 64 | bytes 512 | tf_op jit(solution)/shard_map/psum | solution.py:104
  337.8 73.5 %psum.53 = f32[32]{0:T(128)S(1)} all-reduce(f32[32]{0:T(128)S(1)} %broadcast_select_fusion.5), channel_id=1, replica_groups=mesh['rows'=64,'cols'=4] {'rows','cols'}, use_global_device_ids=true, to_apply=%region_25.26 | all-reduce | flops 32 | bytes 256 | tf_op jit(solution)/shard_map/psum | solution.py:104
  413.2 35.9 %all_to_all.37 = bf16[64,1,32,256]{3,2,1,0:T(8,128)(2,1)S(1)} all-to-all(bf16[64,1,32,256]{3,2,1,0:T(8,128)(2,1)S(1)} %fusion.38), channel_id=1, replica_groups=mesh['rows'=64,'cols'=4] {'rows'}, dimensions={0} | all-to-all | bytes 2097152 | tf_op jit(solution)/shard_map/all_to_all | solution.py:65
  451.2 16.1 %while.44 = (s32[]{:T(128)}, f32[2,4,32,256]{3,2,1,0:T(8,128)S(1)}, f32[2,24,32,256]{3,2,1,0:T(8,128)}, bf16[2,24,32,256]{3,2,1,0:T(8,128)(2,1)S(1)}, pred[2,24]...) while((s32[]{:T(128)}, f32[2,4,32,256]{3,2,1,0:T(8,128)S(1)}, ...), condition=%wide.region_30.31_spmd, body=%wide.region_26.30_spmd.sunk | while | flops 274375680 | bytes 14607621 | solution.py:147
  467.6 5.1 scatter_fusion.1
  472.8 57.3 %all_to_all.36 = f32[64,1,32,256]{3,2,1,0:T(8,128)S(1)} all-to-all(f32[64,1,32,256]{3,2,1,0:T(8,128)S(1)} %bitcast.323), channel_id=1, replica_groups=mesh['rows'=64,'cols'=4] {'rows'}, dimensions={0} | all-to-all | bytes 4194304 | tf_op jit(solution)/shard_map/all_to_all | solution.py:88
  532.8 39.1 %all-reduce.6.cloned.1.call-done = f32[8,32,256]{2,0,1:T(8,128)} async-done(((f32[8,32,256]{2,0,1:T(8,128)}), f32[8,32,256]{2,0,1:T(8,128)}) %all-reduce.6.cloned.1.call-update) | async-done | bytes 262160 | tf_op jit(solution)/shard_map/psum | solution.py:98
  573.5 78.0 %psum.55 = f32[32]{0:T(128)S(1)} all-reduce(f32[32]{0:T(128)S(1)} %broadcast_select_fusion.4), channel_id=1, replica_groups=mesh['rows'=64,'cols'=4] {'rows','cols'}, use_global_device_ids=true, to_apply=%region_34.35 | all-reduce | flops 32 | bytes 256 | tf_op jit(solution)/shard_map/psum | solution.py:104
  (157 shorter events, 62.1 us)
Async XLA Ops:
  7.2 32.8 %copy-start.5 = (s32[8,6]{1,0:T(8,128)S(1)}, s32[8,6]{1,0:T(8,128)}, u32[]{:S(2)}) copy-start(s32[8,6]{1,0:T(8,128)} %param.9) | copy-start | bytes 580
  11.4 22.2 %all-to-all-start = ((s32[64,1,2]{2,1,0:T(1,128)}), s32[64,1,2]{2,1,0:T(1,128)S(1)}, u32[]{:S(2)}, u32[]{:S(2)}) async-start(s32[64,1,2]{2,1,0:T(1,128)} %copy.22), calls=%async_computation | async-start | bytes 65536 | tf_op jit(solution)/shard_map/all_to_all | solution.py:54
  35.2 22.1 %all-to-all-start.1 = ((bf16[64,1,16,256]{3,2,1,0:T(8,128)(2,1)}), bf16[64,1,16,256]{3,2,1,0:T(8,128)(2,1)S(1)}, u32[]{:S(2)}, u32[]{:S(2)}) async-start(bf16[64,1,16,256]{3,2,1,0:T(8,128)(2,1)} %bitcast_select_fusion.2), calls=%async_computation.1 | async-start | bytes 1048576 | tf_op jit(solution)/shard_map/all_to_all | solution.py:65
  58.0 20.4 %copy-start.4 = (f32[32,2048]{1,0:T(8,128)S(1)}, f32[32,2048]{1,0:T(8,128)}, u32[]{:S(2)}) copy-start(f32[32,2048]{1,0:T(8,128)} %param.11) | copy-start | bytes 786436
  72.0 16.2 %all-to-all-start.2 = ((f32[64,1,1,256]{3,2,1,0:T(1,128)}), f32[64,1,1,256]{3,2,1,0:T(1,128)S(1)}, u32[]{:S(2)}, u32[]{:S(2)}) async-start(f32[64,1,1,256]{3,2,1,0:T(1,128)} %reshape.420), calls=%async_computation.2 | async-start | bytes 131072 | tf_op jit(solution)/shard_map/all_to_all | solution.py:88
  78.5 20.5 %copy-start = (f32[4,8,8,256]{3,2,1,0:T(8,128)}, f32[4,8,8,256]{3,2,1,0:T(8,128)S(1)}, u32[]{:S(2)}) copy-start(f32[4,8,8,256]{3,2,1,0:T(8,128)S(1)} %copy.51) | copy-start | bytes 786436
  99.0 35.1 %all-to-all-start.3 = ((bf16[64,1,32,256]{3,2,1,0:T(8,128)(2,1)}), bf16[64,1,32,256]{3,2,1,0:T(8,128)(2,1)S(1)}, u32[]{:S(2)}, u32[]{:S(2)}) async-start(bf16[64,1,32,256]{3,2,1,0:T(8,128)(2,1)} %fusion.39), calls=%async_computation.3 | async-start | bytes 2097152 | tf_op jit(solution)/shard_map/all_to_all | solution.py:65
  105.5 151.6 %all-reduce.4.cloned.1.call-start = ((), (), s32[]{:S(2)}) async-start(), calls=%async_computation.7 | async-start | bytes 524288 | tf_op jit(solution)/shard_map/psum | solution.py:98
  157.7 99.3 %copy-start.1 = (f32[4,8,8,256]{3,2,1,0:T(8,128)S(1)}, f32[4,8,8,256]{3,2,1,0:T(8,128)}, u32[]{:S(2)}) copy-start(f32[4,8,8,256]{3,2,1,0:T(8,128)} %copy-done) | copy-start | bytes 786436
  217.9 354.1 %all-reduce.6.cloned.1.call-start = ((), (), s32[]{:S(2)}) async-start(), calls=%async_computation.8 | async-start | bytes 524288 | tf_op jit(solution)/shard_map/psum | solution.py:98
  472.8 99.2 %copy-start.2 = (f32[4,8,8,256]{3,2,1,0:T(8,128)S(1)}, f32[4,8,8,256]{3,2,1,0:T(8,128)}, u32[]{:S(2)}) copy-start(f32[4,8,8,256]{3,2,1,0:T(8,128)} %copy-done) | copy-start | bytes 786436
  472.8 99.2 %copy-start.3 = (f32[8,32,256]{2,0,1:T(8,128)S(1)}, f32[8,32,256]{2,0,1:T(8,128)}, u32[]{:S(2)}) copy-start(f32[8,32,256]{2,0,1:T(8,128)} %all-reduce.4.cloned.1.call-done) | copy-start | bytes 786436
Sparse Core Ops, SparseCore 0:
  218.0 38.9 all-reduce.3
  533.0 38.9 all-reduce.5

commit v2 on v0

--- a/solution.py
+++ b/solution.py
@@ -1,7 +1,13 @@
+import functools
+
 import jax
 import jax.numpy as jnp
 from jax import lax
+from jax.experimental import pallas as pl
+from jax.experimental.pallas import tpu as pltpu
 from jax.sharding import PartitionSpec as P
+
+MESH = pl.DeviceIdType.MESH
 
 ITERS = 2
 
@@ -21,6 +27,87 @@
     remain = jnp.maximum(1.0 - scaled, 0.0)
     square = remain * remain
     return square * square * (4.0 * scaled + 1.0)
+
+
+def allsum_kernel(axis, n, x_ref, o_ref, recv, send_sem, recv_sem):
+    me = lax.axis_index(axis)
+    barrier = pltpu.get_barrier_semaphore()
+
+    def greet(k, carry):
+        peer = lax.rem(me + k, n)
+        pl.semaphore_signal(barrier, inc=1, device_id={axis: peer}, device_id_type=MESH)
+        return carry
+
+    lax.fori_loop(1, n, greet, 0)
+    pl.semaphore_wait(barrier, n - 1)
+
+    def outgoing(peer):
+        return pltpu.make_async_remote_copy(
+            src_ref=x_ref,
+            dst_ref=recv.at[me],
+            send_sem=send_sem.at[peer],
+            recv_sem=recv_sem.at[me],
+            device_id={axis: peer},
+            device_id_type=MESH,
+        )
+
+    def incoming(peer):
+        return pltpu.make_async_remote_copy(
+            src_ref=x_ref,
+            dst_ref=recv.at[peer],
+            send_sem=send_sem.at[peer],
+            recv_sem=recv_sem.at[peer],
+            device_id={axis: peer},
+            device_id_type=MESH,
+        )
+
+    def start(k, carry):
+        outgoing(lax.rem(me + k, n)).start()
+        return carry
+
+    lax.fori_loop(1, n, start, 0)
+    recv[me] = x_ref[...]
+
+    def finish(k, carry):
+        peer = lax.rem(me + k, n)
+        outgoing(peer).wait_send()
+        incoming(peer).wait_recv()
+        return carry
+
+    lax.fori_loop(1, n, finish, 0)
+    o_ref[...] = recv[0]
+
+    def add(s, carry):
+        o_ref[...] += recv[s]
+        return carry
+
+    lax.fori_loop(1, n, add, 0)
+
+
+def allsum(x, axis, cid):
+    n = lax.axis_size(axis)
+    shape = x.shape
+    flat = x.reshape(-1)
+    size = flat.shape[0]
+    lanes = 128 if size % 128 == 0 else 0
+    if lanes and (size // 128) % 8 == 0:
+        tile = flat.reshape(size // 128, 128)
+    else:
+        rows_pad = -(-size // 1024) * 8
+        tile = jnp.pad(flat, (0, rows_pad * 128 - size)).reshape(rows_pad, 128)
+    out = pl.pallas_call(
+        functools.partial(allsum_kernel, axis, n),
+        out_shape=jax.ShapeDtypeStruct(tile.shape, jnp.float32),
+        in_specs=[pl.BlockSpec(memory_space=pltpu.VMEM)],
+        out_specs=pl.BlockSpec(memory_space=pltpu.VMEM),
+        scratch_shapes=[
+            pltpu.VMEM((n,) + tile.shape, jnp.float32),
+            pltpu.SemaphoreType.DMA((n,)),
+            pltpu.SemaphoreType.DMA((n,)),
+        ],
+        compiler_params=pltpu.CompilerParams(collective_id=cid, has_side_effects=True),
+    )(tile)
+    return out.reshape(-1)[:size].reshape(shape)
 
 
 def local(block_list, points, targets):
@@ -95,10 +182,10 @@
         return collect(arrived.reshape(buffer_len, mirror.shape[1], block_len))
 
     def column_total(partial_value):
-        return lax.psum(partial_value, "cols")
+        return allsum(partial_value, "cols", 1 if partial_value.shape[1] == 1 else 2)
 
     def global_sum(values):
-        return lax.psum(values, "rows")
+        return allsum(values, "rows", 0)
 
     own_x = points.reshape(coord_dim, block_rows, block_len).transpose(1, 0, 2)
     far_x = serve(own_x)

time: 811 us -> 444 us (0.55)
  blocking collectives: 536 us -> 151 us
  Pallas kernels: 0 us -> 110 us
  waiting for transfers between devices: 144 us -> 63.9 us
  between operations: 14.4 us -> 1.05 us
    psum x4 -> x0, blocking collectives: 388 us -> none  [the longest x3 380 us: global_sum(): return lax.psum(values, 'rows')]
    pallas_call x0 -> x7, Pallas kernels: none -> 110 us  [allsum(): pl.pallas_call(functools.partial(allsum_kernel, axis, n), out_shape=jax.S...]
    psum x2 -> x0, waiting for transfers between devices: 79.9 us -> none  [column_total(): return lax.psum(partial_value, 'cols')]
  transfers between devices with their start and end apart: 6 -> 4, of which waited for: 6 -> 4; matrix products, arithmetic and copies ran while one was open for 0% -> 0% of each run, Pallas kernels for 0% -> 0%
where the time goes in v2:
time: 444 us; the launch traced here: 442 us
  blocking collectives  151 us (34%)
  Pallas kernels  110 us (25%)
  waiting for transfers between devices  63.9 us (14%)
  matrix products  46.5 us (10%)
  local copies, waits for them, and re-layouts  31.4 us (7%)
  starting transfers between devices  29.7 us (7%)
  other arithmetic  8.1 us (2%)
    all_to_all x2, blocking collectives, give_back(): lax.all_to_all(placed.reshape(row_count, capacity, mirror.shape[1], block...  115 us
    pallas_call x7, Pallas kernels, allsum(): pl.pallas_call(functools.partial(allsum_kernel, axis, n), out_shape=jax.S...  110 us
    all_to_all x2, waiting for transfers between devices, serve(): lax.all_to_all(chosen.reshape(row_count, capacity, blocks.shape[1], block...  45.8 us
    all_to_all x1, blocking collectives, serve(): lax.all_to_all(chosen.reshape(row_count, capacity, blocks.shape[1], block...  36.4 us
    dot_general x6, matrix products, wendland(): jnp.einsum('nda,ndb->nab', left_f, right_f, precision=lax.Precision.HIGHEST)  32.3 us
    all_to_all x1, starting transfers between devices, local(): lax.all_to_all(request, 'rows', split_axis=0, concat_axis=0, tiled=True)  13 us
    scatter x3, local copies, waits for them, and re-layouts, give_back(): placed = jnp.zeros((buffer_len,) + mirror.shape[1:], jnp.float32).at[plac...  11.1 us
    all_to_all x2, starting transfers between devices, serve(): lax.all_to_all(chosen.reshape(row_count, capacity, blocks.shape[1], block...  10.4 us
  transfers between devices with their start and end apart: 4, of which 4 were waited for; matrix products, arithmetic and copies ran while one was open for 0% of the time, Pallas kernels for 0%

profile of v2, /device:TPU:1, one launch (start us, length us, event | category | flops | bytes accessed | tf_op | source)
XLA Modules:
  0.0 442.5 jit_solution(15733884594055658774)
XLA Ops:
  4.9 13.0 %all-to-all-start = ((s32[64,1,2]{2,1,0:T(1,128)}), s32[64,1,2]{2,1,0:T(1,128)S(1)}, u32[]{:S(2)}, u32[]{:S(2)}) async-start(s32[64,1,2]{2,1,0:T(1,128)} %copy.25), calls=%async_computation | async-start | bytes 65536 | tf_op jit(solution)/shard_map/all_to_all | solution.py:141
  18.7 8.4 %all-to-all-done = s32[64,1,2]{2,1,0:T(1,128)S(1)} async-done(((s32[64,1,2]{2,1,0:T(1,128)}), s32[64,1,2]{2,1,0:T(1,128)S(1)}, u32[]{:S(2)}, u32[]{:S(2)}) %all-to-all-start) | async-done | bytes 544 | tf_op jit(solution)/shard_map/all_to_all | solution.py:141
  33.6 17.2 %all-to-all-done.1 = bf16[64,1,16,256]{3,2,1,0:T(8,128)(2,1)S(1)} async-done(((bf16[64,1,16,256]{3,2,1,0:T(8,128)(2,1)}), bf16[64,1,16,256]{3,2,1,0:T(8,128)(2,1)S(1)}, u32[]{:S(2)}, u32[]{:S(2)}) %all-to-all-start.1) | async-done | bytes 524320 | tf_op jit(solution)/shard_map/all_to_all | solution.py:152
  51.5 12.5 %while.42 = (s32[]{:T(128)}, f32[2,4,1,256]{3,2,1,0:T(1,128)S(1)}, f32[2,24,1,256]{3,1,2,0:T(8,128)S(1)}, pred[2,24]{1,0:T(4,128)(4,1)S(1)}, bf16[2,4,16,256]{3,...) while((s32[]{:T(128)}, f32[2,4,1,256]{3,2,1,0:T(1,128)S(1)}, ...), condition=%wide.region_11.12_spmd, body=%wide.region_5.11_spmd.sunk | while | flops 74260480 | bytes 1274609 | solution.py:231
  51.7 5.9 %fusion.110 = (f32[24,256]{1,0:T(8,128)S(1)}, f32[24,256]{1,0:T(8,128)S(1)}) fusion(bf16[24,16,256]{2,1,0:T(8,128)(2,1)S(1)} %bitcast.359, bf16[2,24,16,256]{3,2,1,0:T(8,128)(2,1)S(1)} %get-tuple-element.608, s32[]{:T(128)} %get-tuple-element.594, f32[24,256]{1,0:T(8,128)S(1)} %multiply_reduce_fusion.15, f32[24,256]{1,0:T(8,128)S(1)} %add.329, ...), kind=kOutput, calls=%fused_computation.160.clone.1 | convolution fusion | flops 73912320 | bytes 492036 | tf_op jit(solution)/shard_map/while/body/eval_jaxpr/nda,ndb->nab/dot_general | solution.py:24
  58.0 5.9 %fusion.110 = (f32[24,256]{1,0:T(8,128)S(1)}, f32[24,256]{1,0:T(8,128)S(1)}) fusion(bf16[24,16,256]{2,1,0:T(8,128)(2,1)S(1)} %bitcast.359, bf16[2,24,16,256]{3,2,1,0:T(8,128)(2,1)S(1)} %get-tuple-element.608, s32[]{:T(128)} %get-tuple-element.594, f32[24,256]{1,0:T(8,128)S(1)} %multiply_reduce_fusion.15, f32[24,256]{1,0:T(8,128)S(1)} %add.329, ...), kind=kOutput, calls=%fused_computation.160.clone.1 | convolution fusion | flops 73912320 | bytes 492036 | tf_op jit(solution)/shard_map/while/body/eval_jaxpr/nda,ndb->nab/dot_general | solution.py:24
  65.5 6.3 %all-to-all-start.2 = ((f32[64,1,1,256]{3,2,1,0:T(1,128)}), f32[64,1,1,256]{3,2,1,0:T(1,128)S(1)}, u32[]{:S(2)}, u32[]{:S(2)}) async-start(f32[64,1,1,256]{3,2,1,0:T(1,128)} %reshape.460), calls=%async_computation.2 | async-start | bytes 131072 | tf_op jit(solution)/shard_map/all_to_all | solution.py:175
  71.9 9.7 %all-to-all-done.2 = f32[64,1,1,256]{3,2,1,0:T(1,128)S(1)} async-done(((f32[64,1,1,256]{3,2,1,0:T(1,128)}), f32[64,1,1,256]{3,2,1,0:T(1,128)S(1)}, u32[]{:S(2)}, u32[]{:S(2)}) %all-to-all-start.2) | async-done | bytes 65568 | tf_op jit(solution)/shard_map/all_to_all | solution.py:175
  82.4 6.4 %shard_map.51 = f32[16,128]{1,0:T(8,128)} custom-call(f32[16,128]{1,0:T(8,128)} %reshape_reshape.26.x_ref), custom_call_target="tpu_custom_call" | custom-call | tf_op jit(solution)/shard_map/pallas_call | solution.py:98
  91.3 5.6 %all-to-all-start.3 = ((bf16[64,1,32,256]{3,2,1,0:T(8,128)(2,1)}), bf16[64,1,32,256]{3,2,1,0:T(8,128)(2,1)S(1)}, u32[]{:S(2)}, u32[]{:S(2)}) async-start(bf16[64,1,32,256]{3,2,1,0:T(8,128)(2,1)} %bitcast_select_fusion.1), calls=%async_computation.3 | async-start | bytes 2097152 | tf_op jit(solution)/shard_map/all_to_all | solution.py:152
  97.0 28.6 %all-to-all-done.3 = bf16[64,1,32,256]{3,2,1,0:T(8,128)(2,1)S(1)} async-done(((bf16[64,1,32,256]{3,2,1,0:T(8,128)(2,1)}), bf16[64,1,32,256]{3,2,1,0:T(8,128)(2,1)S(1)}, u32[]{:S(2)}, u32[]{:S(2)}) %all-to-all-start.3) | async-done | bytes 1048608 | tf_op jit(solution)/shard_map/all_to_all | solution.py:152
  127.7 16.1 %while.43 = (s32[]{:T(128)}, f32[2,4,32,256]{3,2,1,0:T(8,128)S(1)}, f32[2,24,32,256]{3,2,1,0:T(8,128)}, bf16[2,24,32,256]{3,2,1,0:T(8,128)(2,1)S(1)}, pred[2,24]...) while((s32[]{:T(128)}, f32[2,4,32,256]{3,2,1,0:T(8,128)S(1)}, ...), condition=%wide.region_17.18_spmd, body=%wide.region_13.17_spmd.sunk | while | flops 274375680 | bytes 14607621 | solution.py:231
  144.0 5.1 %scatter_fusion = f32[64,32,256]{2,1,0:T(8,128)S(1)} fusion(f32[64,32,256]{2,1,0:T(8,128)S(1)} %broadcast.459.clone, s32[48]{0:T(128)S(1)} %fusion.70, f32[48,32,256]{2,1,0:T(8,128)} %bitcast.51), kind=kCustom, calls=%fused_computation.9 | custom fusion | bytes 4718784 | tf_op jit(solution)/shard_map/scatter | solution.py:173
  149.2 57.3 %all_to_all.35 = f32[64,1,32,256]{3,2,1,0:T(8,128)S(1)} all-to-all(f32[64,1,32,256]{3,2,1,0:T(8,128)S(1)} %bitcast.350), channel_id=1, replica_groups=mesh['rows'=64,'cols'=4] {'rows'}, dimensions={0} | all-to-all | bytes 4194304 | tf_op jit(solution)/shard_map/all_to_all | solution.py:175
  209.3 16.4 %shard_map.52 = f32[512,128]{1,0:T(8,128)} custom-call(f32[512,128]{1,0:T(8,128)} %reshape_reshape.28.x_ref), custom_call_target="tpu_custom_call" | custom-call | tf_op jit(solution)/shard_map/pallas_call | solution.py:98
  227.6 18.5 %shard_map.50 = f32[8,128]{1,0:T(8,128)} custom-call(f32[8,128]{1,0:T(8,128)} %get-tuple-element.403.x_ref), custom_call_target="tpu_custom_call" | custom-call | tf_op jit(solution)/shard_map/pallas_call | solution.py:98
  246.1 16.7 %shard_map.53 = f32[8,128]{1,0:T(8,128)} custom-call(f32[8,128]{1,0:T(8,128)} %get-tuple-element.402.x_ref), custom_call_target="tpu_custom_call" | custom-call | tf_op jit(solution)/shard_map/pallas_call | solution.py:98
  264.2 17.3 %shard_map.54 = f32[8,128]{1,0:T(8,128)} custom-call(f32[8,128]{1,0:T(8,128)} %pad_bitcast_fusion.1.x_ref), custom_call_target="tpu_custom_call" | custom-call | tf_op jit(solution)/shard_map/pallas_call | solution.py:98
  283.2 36.4 %all_to_all.37 = bf16[64,1,32,256]{3,2,1,0:T(8,128)(2,1)S(1)} all-to-all(bf16[64,1,32,256]{3,2,1,0:T(8,128)(2,1)S(1)} %bitcast_select_fusion), channel_id=1, replica_groups=mesh['rows'=64,'cols'=4] {'rows'}, dimensions={0} | all-to-all | bytes 2097152 | tf_op jit(solution)/shard_map/all_to_all | solution.py:152
  321.7 16.1 %while.44 = (s32[]{:T(128)}, f32[2,4,32,256]{3,2,1,0:T(8,128)S(1)}, f32[2,24,32,256]{3,2,1,0:T(8,128)}, bf16[2,24,32,256]{3,2,1,0:T(8,128)(2,1)S(1)}, pred[2,24]...) while((s32[]{:T(128)}, f32[2,4,32,256]{3,2,1,0:T(8,128)S(1)}, ...), condition=%wide.region_25.26_spmd, body=%wide.region_21.25_spmd.sunk | while | flops 274375680 | bytes 14607621 | solution.py:231
  338.1 5.1 %scatter_fusion.1 = f32[64,32,256]{2,1,0:T(8,128)S(1)} fusion(f32[64,32,256]{2,1,0:T(8,128)S(1)} %broadcast.459, s32[48]{0:T(128)S(1)} %fusion.70, f32[48,32,256]{2,1,0:T(8,128)} %bitcast.63), kind=kCustom, calls=%fused_computation.10 | custom fusion | bytes 4718784 | tf_op jit(solution)/shard_map/scatter | solution.py:173
  343.2 57.2 %all_to_all.36 = f32[64,1,32,256]{3,2,1,0:T(8,128)S(1)} all-to-all(f32[64,1,32,256]{3,2,1,0:T(8,128)S(1)} %bitcast.349), channel_id=1, replica_groups=mesh['rows'=64,'cols'=4] {'rows'}, dimensions={0} | all-to-all | bytes 4194304 | tf_op jit(solution)/shard_map/all_to_all | solution.py:175
  403.3 16.4 %shard_map.55 = f32[512,128]{1,0:T(8,128)} custom-call(f32[512,128]{1,0:T(8,128)} %reshape_reshape.31.x_ref), custom_call_target="tpu_custom_call" | custom-call | tf_op jit(solution)/shard_map/pallas_call | solution.py:98
  421.6 18.5 %shard_map.56 = f32[8,128]{1,0:T(8,128)} custom-call(f32[8,128]{1,0:T(8,128)} %pad_bitcast_fusion.x_ref), custom_call_target="tpu_custom_call" | custom-call | tf_op jit(solution)/shard_map/pallas_call | solution.py:98
  (153 shorter events, 68.8 us)
Async XLA Ops:
  0.6 32.8 %copy-start.2 = (s32[8,6]{1,0:T(8,128)S(1)}, s32[8,6]{1,0:T(8,128)}, u32[]{:S(2)}) copy-start(s32[8,6]{1,0:T(8,128)} %param.9) | copy-start | bytes 580
  4.9 22.2 %all-to-all-start = ((s32[64,1,2]{2,1,0:T(1,128)}), s32[64,1,2]{2,1,0:T(1,128)S(1)}, u32[]{:S(2)}, u32[]{:S(2)}) async-start(s32[64,1,2]{2,1,0:T(1,128)} %copy.25), calls=%async_computation | async-start | bytes 65536 | tf_op jit(solution)/shard_map/all_to_all | solution.py:141
  28.7 22.1 %all-to-all-start.1 = ((bf16[64,1,16,256]{3,2,1,0:T(8,128)(2,1)}), bf16[64,1,16,256]{3,2,1,0:T(8,128)(2,1)S(1)}, u32[]{:S(2)}, u32[]{:S(2)}) async-start(bf16[64,1,16,256]{3,2,1,0:T(8,128)(2,1)} %bitcast_select_fusion.2), calls=%async_computation.1 | async-start | bytes 1048576 | tf_op jit(solution)/shard_map/all_to_all | solution.py:152
  51.5 38.0 %copy-start = (f32[32,2048]{1,0:T(8,128)S(1)}, f32[32,2048]{1,0:T(8,128)}, u32[]{:S(2)}) copy-start(f32[32,2048]{1,0:T(8,128)} %param.11) | copy-start | bytes 786436
  65.5 16.1 %all-to-all-start.2 = ((f32[64,1,1,256]{3,2,1,0:T(1,128)}), f32[64,1,1,256]{3,2,1,0:T(1,128)S(1)}, u32[]{:S(2)}, u32[]{:S(2)}) async-start(f32[64,1,1,256]{3,2,1,0:T(1,128)} %reshape.460), calls=%async_computation.2 | async-start | bytes 131072 | tf_op jit(solution)/shard_map/all_to_all | solution.py:175
  91.3 34.2 %all-to-all-start.3 = ((bf16[64,1,32,256]{3,2,1,0:T(8,128)(2,1)}), bf16[64,1,32,256]{3,2,1,0:T(8,128)(2,1)S(1)}, u32[]{:S(2)}, u32[]{:S(2)}) async-start(bf16[64,1,32,256]{3,2,1,0:T(8,128)(2,1)} %bitcast_select_fusion.1), calls=%async_computation.3 | async-start | bytes 2097152 | tf_op jit(solution)/shard_map/all_to_all | solution.py:152
  206.5 20.3 %copy-start.1 = (f32[32,2048]{1,0:T(8,128)S(1)}, f32[32,2048]{1,0:T(8,128)}, u32[]{:S(2)}) copy-start(f32[32,2048]{1,0:T(8,128)} %param.11) | copy-start | bytes 786436

commit v3 on v2

--- a/solution.py
+++ b/solution.py
@@ -89,8 +89,9 @@
     shape = x.shape
     flat = x.reshape(-1)
     size = flat.shape[0]
-    lanes = 128 if size % 128 == 0 else 0
-    if lanes and (size // 128) % 8 == 0:
+    if size <= 128:
+        tile = jnp.pad(flat, (0, 128 - size)).reshape(1, 128)
+    elif size % 1024 == 0:
         tile = flat.reshape(size // 128, 128)
     else:
         rows_pad = -(-size // 1024) * 8
@@ -239,14 +240,20 @@
     resid = targets.reshape(outputs, block_rows, block_len).transpose(1, 0, 2)
     direction = resid
     solution = jnp.zeros_like(resid)
-    norm_now = global_sum(jnp.sum(resid * resid, axis=(0, 2)))
+    norm_now = jnp.sum(resid * resid, axis=(0, 2))
     for iteration in range(ITERS):
         weights = (direction * inv_root).astype(jnp.bfloat16)
         apply_far_w = serve(weights)
         apply_direct, apply_mirror = row_pass(weights, apply_far_w)
         apply_partial_value = apply_direct + give_back(apply_mirror)
         applied = REG * direction + inv_root * column_total(apply_partial_value)
-        step_size = norm_now / global_sum(jnp.sum(direction * applied, axis=(0, 2)))
+        curvature = jnp.sum(direction * applied, axis=(0, 2))
+        if iteration == 0:
+            both = global_sum(jnp.concatenate([norm_now, curvature]))
+            norm_now, curvature = both[:outputs], both[outputs:]
+        else:
+            curvature = global_sum(curvature)
+        step_size = norm_now / curvature
         solution = solution + step_size[None, :, None] * direction
         resid = resid - step_size[None, :, None] * applied
         if iteration + 1 < ITERS:

time: 444 us -> 412 us (0.928)
  Pallas kernels: 110 us -> 80.8 us
    pallas_call x7 -> x6, Pallas kernels: 110 us -> 80.8 us  [allsum(): pl.pallas_call(functools.partial(allsum_kernel, axis, n), out_shape=jax.S...]
where the time goes in v3:
time: 412 us; the launch traced here: 411 us
  blocking collectives  149 us (36%)
  Pallas kernels  80.8 us (20%)
  waiting for transfers between devices  63.9 us (16%)
  matrix products  46.5 us (11%)
  local copies, waits for them, and re-layouts  30.7 us (7%)
  starting transfers between devices  29.7 us (7%)
  other arithmetic  8.82 us (2%)
    all_to_all x2, blocking collectives, give_back(): lax.all_to_all(placed.reshape(row_count, capacity, mirror.shape[1], block...  115 us
    pallas_call x6, Pallas kernels, allsum(): pl.pallas_call(functools.partial(allsum_kernel, axis, n), out_shape=jax.S...  80.8 us
    all_to_all x2, waiting for transfers between devices, serve(): lax.all_to_all(chosen.reshape(row_count, capacity, blocks.shape[1], block...  45.8 us
    all_to_all x1, blocking collectives, serve(): lax.all_to_all(chosen.reshape(row_count, capacity, blocks.shape[1], block...  34.7 us
    dot_general x6, matrix products, wendland(): jnp.einsum('nda,ndb->nab', left_f, right_f, precision=lax.Precision.HIGHEST)  32.3 us
    all_to_all x1, starting transfers between devices, local(): lax.all_to_all(request, 'rows', split_axis=0, concat_axis=0, tiled=True)  13 us
    scatter x3, local copies, waits for them, and re-layouts, give_back(): placed = jnp.zeros((buffer_len,) + mirror.shape[1:], jnp.float32).at[plac...  11.1 us
    all_to_all x2, starting transfers between devices, serve(): lax.all_to_all(chosen.reshape(row_count, capacity, blocks.shape[1], block...  10.4 us
  transfers between devices with their start and end apart: 4, of which 4 were waited for; matrix products, arithmetic and copies ran while one was open for 0% of the time, Pallas kernels for 0%

profile of v3, /device:TPU:1, one launch (start us, length us, event | category | flops | bytes accessed | tf_op | source)
XLA Modules:
  0.0 411.2 jit_solution(16126703831412252010)
XLA Ops:
  4.9 13.0 %all-to-all-start = ((s32[64,1,2]{2,1,0:T(1,128)}), s32[64,1,2]{2,1,0:T(1,128)S(1)}, u32[]{:S(2)}, u32[]{:S(2)}) async-start(s32[64,1,2]{2,1,0:T(1,128)} %copy.25), calls=%async_computation | async-start | bytes 65536 | tf_op jit(solution)/shard_map/all_to_all | solution.py:142
  18.7 8.4 %all-to-all-done = s32[64,1,2]{2,1,0:T(1,128)S(1)} async-done(((s32[64,1,2]{2,1,0:T(1,128)}), s32[64,1,2]{2,1,0:T(1,128)S(1)}, u32[]{:S(2)}, u32[]{:S(2)}) %all-to-all-start) | async-done | bytes 544 | tf_op jit(solution)/shard_map/all_to_all | solution.py:142
  33.6 17.2 %all-to-all-done.1 = bf16[64,1,16,256]{3,2,1,0:T(8,128)(2,1)S(1)} async-done(((bf16[64,1,16,256]{3,2,1,0:T(8,128)(2,1)}), bf16[64,1,16,256]{3,2,1,0:T(8,128)(2,1)S(1)}, u32[]{:S(2)}, u32[]{:S(2)}) %all-to-all-start.1) | async-done | bytes 524320 | tf_op jit(solution)/shard_map/all_to_all | solution.py:153
  51.5 12.5 %while.42 = (s32[]{:T(128)}, f32[2,4,1,256]{3,2,1,0:T(1,128)S(1)}, f32[2,24,1,256]{3,1,2,0:T(8,128)S(1)}, pred[2,24]{1,0:T(4,128)(4,1)S(1)}, bf16[2,4,16,256]{3,...) while((s32[]{:T(128)}, f32[2,4,1,256]{3,2,1,0:T(1,128)S(1)}, ...), condition=%wide.region_11.12_spmd, body=%wide.region_5.11_spmd.sunk | while | flops 74260480 | bytes 1274609 | solution.py:232
  51.7 5.9 %fusion.114 = (f32[24,256]{1,0:T(8,128)S(1)}, f32[24,256]{1,0:T(8,128)S(1)}) fusion(bf16[24,16,256]{2,1,0:T(8,128)(2,1)S(1)} %bitcast.359, bf16[2,24,16,256]{3,2,1,0:T(8,128)(2,1)S(1)} %get-tuple-element.606, s32[]{:T(128)} %get-tuple-element.592, f32[24,256]{1,0:T(8,128)S(1)} %multiply_reduce_fusion.15, f32[24,256]{1,0:T(8,128)S(1)} %add.327, ...), kind=kOutput, calls=%fused_computation.164.clone.1 | convolution fusion | flops 73912320 | bytes 492036 | tf_op jit(solution)/shard_map/while/body/eval_jaxpr/nda,ndb->nab/dot_general | solution.py:24
  58.0 5.9 %fusion.114 = (f32[24,256]{1,0:T(8,128)S(1)}, f32[24,256]{1,0:T(8,128)S(1)}) fusion(bf16[24,16,256]{2,1,0:T(8,128)(2,1)S(1)} %bitcast.359, bf16[2,24,16,256]{3,2,1,0:T(8,128)(2,1)S(1)} %get-tuple-element.606, s32[]{:T(128)} %get-tuple-element.592, f32[24,256]{1,0:T(8,128)S(1)} %multiply_reduce_fusion.15, f32[24,256]{1,0:T(8,128)S(1)} %add.327, ...), kind=kOutput, calls=%fused_computation.164.clone.1 | convolution fusion | flops 73912320 | bytes 492036 | tf_op jit(solution)/shard_map/while/body/eval_jaxpr/nda,ndb->nab/dot_general | solution.py:24
  65.5 6.3 %all-to-all-start.2 = ((f32[64,1,1,256]{3,2,1,0:T(1,128)}), f32[64,1,1,256]{3,2,1,0:T(1,128)S(1)}, u32[]{:S(2)}, u32[]{:S(2)}) async-start(f32[64,1,1,256]{3,2,1,0:T(1,128)} %reshape.478), calls=%async_computation.2 | async-start | bytes 131072 | tf_op jit(solution)/shard_map/all_to_all | solution.py:176
  71.9 9.7 %all-to-all-done.2 = f32[64,1,1,256]{3,2,1,0:T(1,128)S(1)} async-done(((f32[64,1,1,256]{3,2,1,0:T(1,128)}), f32[64,1,1,256]{3,2,1,0:T(1,128)S(1)}, u32[]{:S(2)}, u32[]{:S(2)}) %all-to-all-start.2) | async-done | bytes 65568 | tf_op jit(solution)/shard_map/all_to_all | solution.py:176
  82.4 6.4 %shard_map.50 = f32[16,128]{1,0:T(8,128)} custom-call(f32[16,128]{1,0:T(8,128)} %reshape_reshape.26.x_ref), custom_call_target="tpu_custom_call" | custom-call | tf_op jit(solution)/shard_map/pallas_call | solution.py:99
  91.3 5.6 %all-to-all-start.3 = ((bf16[64,1,32,256]{3,2,1,0:T(8,128)(2,1)}), bf16[64,1,32,256]{3,2,1,0:T(8,128)(2,1)S(1)}, u32[]{:S(2)}, u32[]{:S(2)}) async-start(bf16[64,1,32,256]{3,2,1,0:T(8,128)(2,1)} %bitcast_select_fusion.1), calls=%async_computation.3 | async-start | bytes 2097152 | tf_op jit(solution)/shard_map/all_to_all | solution.py:153
  97.0 28.6 %all-to-all-done.3 = bf16[64,1,32,256]{3,2,1,0:T(8,128)(2,1)S(1)} async-done(((bf16[64,1,32,256]{3,2,1,0:T(8,128)(2,1)}), bf16[64,1,32,256]{3,2,1,0:T(8,128)(2,1)S(1)}, u32[]{:S(2)}, u32[]{:S(2)}) %all-to-all-start.3) | async-done | bytes 1048608 | tf_op jit(solution)/shard_map/all_to_all | solution.py:153
  127.7 16.1 %while.43 = (s32[]{:T(128)}, f32[2,4,32,256]{3,2,1,0:T(8,128)S(1)}, f32[2,24,32,256]{3,2,1,0:T(8,128)}, bf16[2,24,32,256]{3,2,1,0:T(8,128)(2,1)S(1)}, pred[2,24]...) while((s32[]{:T(128)}, f32[2,4,32,256]{3,2,1,0:T(8,128)S(1)}, ...), condition=%wide.region_17.18_spmd, body=%wide.region_13.17_spmd.sunk | while | flops 274375680 | bytes 14607621 | solution.py:232
  144.0 5.1 %scatter_fusion = f32[64,32,256]{2,1,0:T(8,128)S(1)} fusion(f32[64,32,256]{2,1,0:T(8,128)S(1)} %broadcast.454.clone, s32[48]{0:T(128)S(1)} %fusion.71, f32[48,32,256]{2,1,0:T(8,128)} %bitcast.49), kind=kCustom, calls=%fused_computation.9 | custom fusion | bytes 4718784 | tf_op jit(solution)/shard_map/scatter | solution.py:174
  149.2 57.3 %all_to_all.35 = f32[64,1,32,256]{3,2,1,0:T(8,128)S(1)} all-to-all(f32[64,1,32,256]{3,2,1,0:T(8,128)S(1)} %bitcast.350), channel_id=1, replica_groups=mesh['rows'=64,'cols'=4] {'rows'}, dimensions={0} | all-to-all | bytes 4194304 | tf_op jit(solution)/shard_map/all_to_all | solution.py:176
  209.3 16.4 %shard_map.51 = f32[512,128]{1,0:T(8,128)} custom-call(f32[512,128]{1,0:T(8,128)} %reshape_reshape.28.x_ref), custom_call_target="tpu_custom_call" | custom-call | tf_op jit(solution)/shard_map/pallas_call | solution.py:99
  227.5 14.0 %shard_map.52 = f32[1,128]{1,0:T(1,128)} custom-call(f32[1,128]{1,0:T(1,128)} %fusion.76.x_ref), custom_call_target="tpu_custom_call" | custom-call | tf_op jit(solution)/shard_map/pallas_call | solution.py:99
  243.1 13.5 %shard_map.53 = f32[1,128]{1,0:T(1,128)} custom-call(f32[1,128]{1,0:T(1,128)} %pad_bitcast_fusion.1.x_ref), custom_call_target="tpu_custom_call" | custom-call | tf_op jit(solution)/shard_map/pallas_call | solution.py:99
  258.2 34.7 %all_to_all.37 = bf16[64,1,32,256]{3,2,1,0:T(8,128)(2,1)S(1)} all-to-all(bf16[64,1,32,256]{3,2,1,0:T(8,128)(2,1)S(1)} %bitcast_select_fusion), channel_id=1, replica_groups=mesh['rows'=64,'cols'=4] {'rows'}, dimensions={0} | all-to-all | bytes 2097152 | tf_op jit(solution)/shard_map/all_to_all | solution.py:153
  295.1 16.1 %while.44 = (s32[]{:T(128)}, f32[2,4,32,256]{3,2,1,0:T(8,128)S(1)}, f32[2,24,32,256]{3,2,1,0:T(8,128)}, bf16[2,24,32,256]{3,2,1,0:T(8,128)(2,1)S(1)}, pred[2,24]...) while((s32[]{:T(128)}, f32[2,4,32,256]{3,2,1,0:T(8,128)S(1)}, ...), condition=%wide.region_25.26_spmd, body=%wide.region_21.25_spmd.sunk | while | flops 274375680 | bytes 14607621 | solution.py:232
  295.3 5.1 %select_convert_fusion.5 = bf16[24,256,256]{2,1,0:T(8,128)(2,1)S(1)} fusion(f32[24,256]{1,0:T(8,128)S(1)} %multiply_reduce_fusion.18, f32[24,256]{1,0:T(8,128)S(1)} %add.339, pred[24]{0:T(512)(128)(4,1)S(1)} %get-tuple-element.580, bf16[24,16,256]{2,1,0:T(8,128)(2,1)S(1)} %bitcast.361, bf16[2,24,16,256]{3,2,1,0:T(8,128)(2,1)S(1)} %get-tuple-element.671, ...), kind=kOutput, calls=%fused_computation.43.clone.1 | convolution fusion | flops 72351744 | bytes 3588612 | tf_op jit(solution)/shard_map/while/body/eval_jaxpr/nda,ndb->nab/dot_general | solution.py:24
  311.4 5.1 %scatter_fusion.1 = f32[64,32,256]{2,1,0:T(8,128)S(1)} fusion(f32[64,32,256]{2,1,0:T(8,128)S(1)} %broadcast.454, s32[48]{0:T(128)S(1)} %fusion.71, f32[48,32,256]{2,1,0:T(8,128)} %bitcast.61), kind=kCustom, calls=%fused_computation.10 | custom fusion | bytes 4718784 | tf_op jit(solution)/shard_map/scatter | solution.py:174
  316.6 57.2 %all_to_all.36 = f32[64,1,32,256]{3,2,1,0:T(8,128)S(1)} all-to-all(f32[64,1,32,256]{3,2,1,0:T(8,128)S(1)} %bitcast.349), channel_id=1, replica_groups=mesh['rows'=64,'cols'=4] {'rows'}, dimensions={0} | all-to-all | bytes 4194304 | tf_op jit(solution)/shard_map/all_to_all | solution.py:176
  376.6 16.4 %shard_map.54 = f32[512,128]{1,0:T(8,128)} custom-call(f32[512,128]{1,0:T(8,128)} %reshape_reshape.31.x_ref), custom_call_target="tpu_custom_call" | custom-call | tf_op jit(solution)/shard_map/pallas_call | solution.py:99
  394.8 14.0 %shard_map.55 = f32[1,128]{1,0:T(1,128)} custom-call(f32[1,128]{1,0:T(1,128)} %pad_bitcast_fusion.x_ref), custom_call_target="tpu_custom_call" | custom-call | tf_op jit(solution)/shard_map/pallas_call | solution.py:99
  (154 shorter events, 63.6 us)
Async XLA Ops:
  0.6 32.8 %copy-start.2 = (s32[8,6]{1,0:T(8,128)S(1)}, s32[8,6]{1,0:T(8,128)}, u32[]{:S(2)}) copy-start(s32[8,6]{1,0:T(8,128)} %param.9) | copy-start | bytes 580
  4.9 22.2 %all-to-all-start = ((s32[64,1,2]{2,1,0:T(1,128)}), s32[64,1,2]{2,1,0:T(1,128)S(1)}, u32[]{:S(2)}, u32[]{:S(2)}) async-start(s32[64,1,2]{2,1,0:T(1,128)} %copy.25), calls=%async_computation | async-start | bytes 65536 | tf_op jit(solution)/shard_map/all_to_all | solution.py:142
  28.7 22.1 %all-to-all-start.1 = ((bf16[64,1,16,256]{3,2,1,0:T(8,128)(2,1)}), bf16[64,1,16,256]{3,2,1,0:T(8,128)(2,1)S(1)}, u32[]{:S(2)}, u32[]{:S(2)}) async-start(bf16[64,1,16,256]{3,2,1,0:T(8,128)(2,1)} %bitcast_select_fusion.2), calls=%async_computation.1 | async-start | bytes 1048576 | tf_op jit(solution)/shard_map/all_to_all | solution.py:153
  51.5 38.0 %copy-start = (f32[32,2048]{1,0:T(8,128)S(1)}, f32[32,2048]{1,0:T(8,128)}, u32[]{:S(2)}) copy-start(f32[32,2048]{1,0:T(8,128)} %param.11) | copy-start | bytes 786436
  65.5 16.1 %all-to-all-start.2 = ((f32[64,1,1,256]{3,2,1,0:T(1,128)}), f32[64,1,1,256]{3,2,1,0:T(1,128)S(1)}, u32[]{:S(2)}, u32[]{:S(2)}) async-start(f32[64,1,1,256]{3,2,1,0:T(1,128)} %reshape.478), calls=%async_computation.2 | async-start | bytes 131072 | tf_op jit(solution)/shard_map/all_to_all | solution.py:176
  91.3 34.2 %all-to-all-start.3 = ((bf16[64,1,32,256]{3,2,1,0:T(8,128)(2,1)}), bf16[64,1,32,256]{3,2,1,0:T(8,128)(2,1)S(1)}, u32[]{:S(2)}, u32[]{:S(2)}) async-start(bf16[64,1,32,256]{3,2,1,0:T(8,128)(2,1)} %bitcast_select_fusion.1), calls=%async_computation.3 | async-start | bytes 2097152 | tf_op jit(solution)/shard_map/all_to_all | solution.py:153
  206.5 20.3 %copy-start.1 = (f32[32,2048]{1,0:T(8,128)S(1)}, f32[32,2048]{1,0:T(8,128)}, u32[]{:S(2)}) copy-start(f32[32,2048]{1,0:T(8,128)} %param.11) | copy-start | bytes 786436
  373.8 35.0 %copy-start.3 = (f32[1,128]{1,0:T(1,128)S(1)}, f32[1,128]{1,0:T(1,128)}, u32[]{:S(2)}) copy-start(f32[1,128]{1,0:T(1,128)} %shard_map.53) | copy-start | bytes 1540

commit v4 on v3

v4 whole, which is shorter than its diff:
```python
import functools

import jax
import jax.numpy as jnp
from jax import lax
from jax.experimental import pallas as pl
from jax.experimental.pallas import tpu as pltpu
from jax.sharding import PartitionSpec as P

MESH = pl.DeviceIdType.MESH

ITERS = 2


REG = 1.5
RADIUS = 0.25


def wendland(left_x, right_x):
    left_f = left_x.astype(jnp.float32)
    right_f = right_x.astype(jnp.float32)
    left_sq = jnp.sum(left_f * left_f, axis=1)
    right_sq = jnp.sum(right_f * right_f, axis=1)
    inner_prod = jnp.einsum("nda,ndb->nab", left_f, right_f, precision=lax.Precision.HIGHEST)
    dist_sq = left_sq[:, :, None] + right_sq[:, None, :] - 2.0 * inner_prod
    scaled = jnp.sqrt(jnp.maximum(dist_sq, 0.0)) / RADIUS
    remain = jnp.maximum(1.0 - scaled, 0.0)
    square = remain * remain
    return square * square * (4.0 * scaled + 1.0)


def allsum_kernel(axis, n, x_ref, o_ref, recv, send_sem, recv_sem):
    me = lax.axis_index(axis)
    barrier = pltpu.get_barrier_semaphore()

    def greet(k, carry):
        peer = lax.rem(me + k, n)
        pl.semaphore_signal(barrier, inc=1, device_id={axis: peer}, device_id_type=MESH)
        return carry

    lax.fori_loop(1, n, greet, 0)
    pl.semaphore_wait(barrier, n - 1)

    def outgoing(peer):
        return pltpu.make_async_remote_copy(
            src_ref=x_ref,
            dst_ref=recv.at[me],
            send_sem=send_sem.at[peer],
            recv_sem=recv_sem.at[me],
            device_id={axis: peer},
            device_id_type=MESH,
        )

    def incoming(peer):
        return pltpu.make_async_remote_copy(
            src_ref=x_ref,
            dst_ref=recv.at[peer],
            send_sem=send_sem.at[peer],
            recv_sem=recv_sem.at[peer],
            device_id={axis: peer},
            device_id_type=MESH,
        )

    def start(k, carry):
        outgoing(lax.rem(me + k, n)).start()
        return carry

    lax.fori_loop(1, n, start, 0)
    recv[me] = x_ref[...]

    def finish(k, carry):
        peer = lax.rem(me + k, n)
        outgoing(peer).wait_send()
        incoming(peer).wait_recv()
        return carry

    lax.fori_loop(1, n, finish, 0)
    o_ref[...] = recv[0]

    def add(s, carry):
        o_ref[...] += recv[s]
        return carry

    lax.fori_loop(1, n, add, 0)


def allsum(x, axis, cid):
    n = lax.axis_size(axis)
    shape = x.shape
    flat = x.reshape(-1)
    size = flat.shape[0]
    if size <= 128:
        tile = jnp.pad(flat, (0, 128 - size)).reshape(1, 128)
    elif size % 1024 == 0:
        tile = flat.reshape(size // 128, 128)
    else:
        rows_pad = -(-size // 1024) * 8
        tile = jnp.pad(flat, (0, rows_pad * 128 - size)).reshape(rows_pad, 128)
    out = pl.pallas_call(
        functools.partial(allsum_kernel, axis, n),
        out_shape=jax.ShapeDtypeStruct(tile.shape, jnp.float32),
        in_specs=[pl.BlockSpec(memory_space=pltpu.VMEM)],
        out_specs=pl.BlockSpec(memory_space=pltpu.VMEM),
        scratch_shapes=[
            pltpu.VMEM((n,) + tile.shape, jnp.float32),
            pltpu.SemaphoreType.DMA((n,)),
            pltpu.SemaphoreType.DMA((n,)),
        ],
        compiler_params=pltpu.CompilerParams(collective_id=cid, has_side_effects=True),
    )(tile)
    return out.reshape(-1)[:size].reshape(shape)


def local(block_list, points, targets):
    row_count = lax.axis_size("rows")
    row_index = lax.axis_index("rows")
    block_rows, slot_width = block_list.shape
    coord_dim, npoints = points.shape
    outputs = targets.shape[0]
    block_len = npoints // block_rows
    slot_count = block_rows * slot_width
    entries = block_list.reshape(slot_count)
    is_live = entries >= 0
    owners = jnp.where(is_live, entries // block_rows, 0)
    local_idx = jnp.where(is_live, entries - owners * block_rows, 0)
    slot_row = jnp.arange(slot_count, dtype=jnp.int32) // slot_width
    first_row = row_index * block_rows
    place_at = jnp.where(is_live, owners, row_count)
    pick_at = jnp.minimum(place_at, row_count - 1)
    wanted = jnp.full((row_count,), -1, jnp.int32).at[place_at].set(local_idx, mode="drop")
    asking_row = jnp.full((row_count,), -1, jnp.int32).at[place_at].set(slot_row, mode="drop")
    ask_live = asking_row >= 0
    ask_row = jnp.maximum(asking_row, 0)
    request = jnp.stack([wanted, asking_row], axis=1).reshape(row_count, 1, 2)
    incoming = lax.all_to_all(request, "rows", split_axis=0, concat_axis=0, tiled=True).reshape(
        row_count, 2
    )
    in_live = incoming[:, 0] >= 0
    in_idx = jnp.maximum(incoming[:, 0], 0)
    their_row = jnp.arange(row_count, dtype=jnp.int32) * block_rows + jnp.maximum(incoming[:, 1], 0)
    in_off = in_live & (their_row != first_row + in_idx)
    collect_map = (
        (in_idx[None, :] == jnp.arange(block_rows, dtype=jnp.int32)[:, None]) & in_off[None, :]
    ).astype(jnp.float32)

    def swap(parts):
        return lax.all_to_all(parts, "rows", split_axis=0, concat_axis=0, tiled=True)

    def asked_part(blocks):
        return jnp.where(ask_live[:, None, None], blocks[ask_row], jnp.zeros((), blocks.dtype))

    def served_part(blocks):
        return jnp.where(in_live[:, None, None], blocks[in_idx], jnp.zeros((), blocks.dtype))

    def per_slot(got):
        chosen = got[pick_at]
        return jnp.where(is_live[:, None, None], chosen, jnp.zeros((), chosen.dtype))

    def collect(terms):
        flat = terms.reshape(row_count, -1)
        summed = jnp.dot(
            collect_map, flat, precision=lax.Precision.HIGHEST, preferred_element_type=jnp.float32
        )
        return summed.reshape((block_rows,) + terms.shape[1:])

    def column_total(partial_value):
        return allsum(partial_value, "cols", 1 if partial_value.shape[1] == 1 else 2)

    def global_sum(values):
        return allsum(values, "rows", 0)

    own_x = points.reshape(coord_dim, block_rows, block_len).transpose(1, 0, 2)
    their_x = swap(asked_part(own_x))
    far_x = per_slot(swap(served_part(own_x)))
    left_x = jnp.concatenate([own_x[slot_row], their_x], axis=0)
    right_x = jnp.concatenate([far_x, own_x[in_idx]], axis=0)
    pair_live = jnp.concatenate([is_live, in_off], axis=0)
    pair_count = slot_count + row_count
    chunk = 16
    pad = (-pair_count) % chunk
    left_x = jnp.pad(left_x, ((0, pad), (0, 0), (0, 0)))
    right_x = jnp.pad(right_x, ((0, pad), (0, 0), (0, 0)))
    pair_live = jnp.pad(pair_live, (0, pad))

    def pair_step(pieces):
        lx, rx, live = pieces
        values = jnp.where(live[:, None, None], wendland(lx, rx), 0.0)
        return (values.astype(jnp.bfloat16), jnp.sum(values, axis=2), jnp.sum(values, axis=1))

    kernel_bf, row_sums, col_sums = lax.map(
        pair_step,
        (
            left_x.reshape(-1, chunk, coord_dim, block_len),
            right_x.reshape(-1, chunk, coord_dim, block_len),
            pair_live.reshape(-1, chunk),
        ),
    )
    kernel_bf = kernel_bf.reshape(-1, block_len, block_len)
    row_sums = row_sums.reshape(-1, block_len)
    col_sums = col_sums.reshape(-1, block_len)
    own_k = kernel_bf[:slot_count]
    in_k = kernel_bf[slot_count:pair_count]
    degree_direct = jnp.sum(row_sums[:slot_count].reshape(block_rows, slot_width, block_len), axis=1)
    degree_mirror = collect(col_sums[slot_count:pair_count])
    degree_part = (degree_direct + degree_mirror)[:, None, :]
    inv_root = 1.0 / jnp.sqrt(1.0 + column_total(degree_part))

    def apply_partial(weights):
        got = swap(jnp.stack([asked_part(weights), served_part(weights)], axis=1))
        their_w = got[:, 0]
        far_w = per_slot(got[:, 1])
        direct = jnp.einsum("sab,sob->soa", own_k, far_w, preferred_element_type=jnp.float32)
        direct = jnp.sum(direct.reshape(block_rows, slot_width, outputs, block_len), axis=1)
        mirror = jnp.einsum("eab,eoa->eob", in_k, their_w, preferred_element_type=jnp.float32)
        return direct + collect(mirror)

    resid = targets.reshape(outputs, block_rows, block_len).transpose(1, 0, 2)
    direction = resid
    solution = jnp.zeros_like(resid)
    norm_now = jnp.sum(resid * resid, axis=(0, 2))
    for iteration in range(ITERS):
        weights = (direction * inv_root).astype(jnp.bfloat16)
        applied = REG * direction + inv_root * column_total(apply_partial(weights))
        curvature = jnp.sum(direction * applied, axis=(0, 2))
        if iteration == 0:
            both = global_sum(jnp.concatenate([norm_now, curvature]))
            norm_now, curvature = both[:outputs], both[outputs:]
        else:
            curvature = global_sum(curvature)
        step_size = norm_now / curvature
        solution = solution + step_size[None, :, None] * direction
        resid = resid - step_size[None, :, None] * applied
        if iteration + 1 < ITERS:
            norm_next = global_sum(jnp.sum(resid * resid, axis=(0, 2)))
            direction = resid + (norm_next / norm_now)[None, :, None] * direction
            norm_now = norm_next
    return (
        solution.transpose(1, 0, 2).reshape(outputs, npoints),
        resid.transpose(1, 0, 2).reshape(outputs, npoints),
    )


def solution(mesh):
    placed = (P("rows", "cols"), P(None, "rows"), P(None, "rows"))
    return jax.shard_map(
        local,
        mesh=mesh,
        in_specs=placed,
        out_specs=(P(None, "rows"), P(None, "rows")),
        check_vma=False,
    )
```

time: 412 us -> 357 us (0.87)
  blocking collectives: 149 us -> 57.4 us
  waiting for transfers between devices: 63.9 us -> 76.3 us
  matrix products: 46.5 us -> 56.4 us
  other arithmetic: 8.82 us -> 17.6 us
  local copies, waits for them, and re-layouts: 30.7 us -> 34.9 us
    all_to_all x3 -> x1, blocking collectives: 149 us -> 57.4 us  [swap(): lax.all_to_all(parts, 'rows', split_axis=0, concat_axis=0, tiled=True)]
    all_to_all x3, waiting for transfers between devices: 55.6 us -> 69.5 us  [swap(): lax.all_to_all(parts, 'rows', split_axis=0, concat_axis=0, tiled=True)]
    slice x0 -> x4, local copies, waits for them, and re-layouts: none -> 13.8 us  [the longest x1 7.66 us: local(): in_k = kernel_bf[slot_count:pair_count]]
    dot_general x8 -> x4, matrix products: 10.2 us -> 21.9 us  [the longest x2 12 us: apply_partial(): jnp.einsum('sab,sob->soa', own_k, far_w, preferred_element_type=jnp.float32)]
    scatter x5 -> x2, local copies, waits for them, and re-layouts: 12.5 us -> 1.45 us  [local(): jnp.full((row_count,), -1, jnp.int32).at[place_at]]
    reduce_sum x13 -> x10, other arithmetic: 0.68 us -> 7.65 us  [the longest x7 4.55 us: pair_step(): jnp.sum(values, axis=1)]
    gather x6 -> x10, local copies, waits for them, and re-layouts: 3.64 us -> 8.19 us  [the longest x3 3.95 us: per_slot(): chosen = got[pick_at]]
    dot_general x6 -> x7, matrix products: 32.3 us -> 30.4 us  [wendland(): jnp.einsum('nda,ndb->nab', left_f, right_f, precision=lax.Precision.HIGHEST)]
  transfers between devices with their start and end apart: 4 -> 4, of which waited for: 4 -> 4; matrix products, arithmetic and copies ran while one was open for 0% -> 5% of each run, Pallas kernels for 0% -> 0%
where the time goes in v4:
time: 357 us; the launch traced here: 356 us
  Pallas kernels  80.8 us (23%)
  waiting for transfers between devices  76.3 us (21%)
  blocking collectives  57.4 us (16%)
  matrix products  56.4 us (16%)
  local copies, waits for them, and re-layouts  34.9 us (10%)
  starting transfers between devices  31.5 us (9%)
  other arithmetic  17.6 us (5%)
    pallas_call x6, Pallas kernels, allsum(): pl.pallas_call(functools.partial(allsum_kernel, axis, n), out_shape=jax.S...  80.8 us
    all_to_all x3, waiting for transfers between devices, swap(): lax.all_to_all(parts, 'rows', split_axis=0, concat_axis=0, tiled=True)  69.5 us
    all_to_all x1, blocking collectives, swap(): lax.all_to_all(parts, 'rows', split_axis=0, concat_axis=0, tiled=True)  57.4 us
    dot_general x7, matrix products, wendland(): jnp.einsum('nda,ndb->nab', left_f, right_f, precision=lax.Precision.HIGHEST)  30.4 us
    all_to_all x3, starting transfers between devices, swap(): lax.all_to_all(parts, 'rows', split_axis=0, concat_axis=0, tiled=True)  18.5 us
    all_to_all x1, starting transfers between devices, local(): lax.all_to_all(request, 'rows', split_axis=0, concat_axis=0, tiled=True)  13 us
    dot_general x2, matrix products, apply_partial(): jnp.einsum('sab,sob->soa', own_k, far_w, preferred_element_type=jnp.float32)  12 us
    dot_general x2, matrix products, apply_partial(): jnp.einsum('eab,eoa->eob', in_k, their_w, preferred_element_type=jnp.floa...  9.84 us
  transfers between devices with their start and end apart: 4, of which 4 were waited for; matrix products, arithmetic and copies ran while one was open for 5% of the time, Pallas kernels for 0%

profile of v4, /device:TPU:1, one launch (start us, length us, event | category | flops | bytes accessed | tf_op | source)
XLA Modules:
  0.0 356.3 jit_solution(3295848996870444303)
XLA Ops:
  4.4 13.0 %all-to-all-start = ((s32[64,1,2]{2,1,0:T(1,128)}), s32[64,1,2]{2,1,0:T(1,128)S(1)}, u32[]{:S(2)}, u32[]{:S(2)}) async-start(s32[64,1,2]{2,1,0:T(1,128)} %copy.26), calls=%async_computation | async-start | bytes 65536 | tf_op jit(solution)/shard_map/all_to_all | solution.py:135
  19.8 6.8 %all-to-all-done = s32[64,1,2]{2,1,0:T(1,128)S(1)} async-done(((s32[64,1,2]{2,1,0:T(1,128)}), s32[64,1,2]{2,1,0:T(1,128)S(1)}, u32[]{:S(2)}, u32[]{:S(2)}) %all-to-all-start) | async-done | bytes 544 | tf_op jit(solution)/shard_map/all_to_all | solution.py:135
  26.6 4.7 %all-to-all-start.1 = ((bf16[64,16,256]{2,1,0:T(8,128)(2,1)}), bf16[64,16,256]{2,1,0:T(8,128)(2,1)S(1)}, u32[]{:S(2)}, u32[]{:S(2)}) async-start(bf16[64,16,256]{2,1,0:T(8,128)(2,1)} %broadcast_select_fusion.1), calls=%async_computation.1 | async-start | bytes 1048576 | tf_op jit(solution)/shard_map/all_to_all | solution.py:147
  33.1 15.7 %all-to-all-done.1 = bf16[64,16,256]{2,1,0:T(8,128)(2,1)S(1)} async-done(((bf16[64,16,256]{2,1,0:T(8,128)(2,1)}), bf16[64,16,256]{2,1,0:T(8,128)(2,1)S(1)}, u32[]{:S(2)}, u32[]{:S(2)}) %all-to-all-start.1) | async-done | bytes 524320 | tf_op jit(solution)/shard_map/all_to_all | solution.py:147
  48.7 6.4 %all-to-all-start.2 = ((bf16[64,16,256]{2,1,0:T(8,128)(2,1)}), bf16[64,16,256]{2,1,0:T(8,128)(2,1)S(1)}, u32[]{:S(2)}, u32[]{:S(2)}) async-start(bf16[64,16,256]{2,1,0:T(8,128)(2,1)} %broadcast_select_fusion), calls=%async_computation.2 | async-start | bytes 1048576 | tf_op jit(solution)/shard_map/all_to_all | solution.py:147
  56.0 16.4 %all-to-all-done.2 = bf16[64,16,256]{2,1,0:T(8,128)(2,1)S(1)} async-done(((bf16[64,16,256]{2,1,0:T(8,128)(2,1)}), bf16[64,16,256]{2,1,0:T(8,128)(2,1)S(1)}, u32[]{:S(2)}, u32[]{:S(2)}) %all-to-all-start.2) | async-done | bytes 524320 | tf_op jit(solution)/shard_map/all_to_all | solution.py:147
  73.2 36.3 %while.16 = (s32[]{:T(128)}, bf16[7,16,256,256]{3,2,1,0:T(8,128)(2,1)}, f32[7,16,256]{2,1,0:T(8,128)S(1)}, f32[7,16,256]{2,1,0:T(8,128)S(1)}, pred[7,16]{1,0:T(8...) while((s32[]{:T(128)}, ...), condition=%wide.region_8.9_spmd, body=%wide.region_3.8_spmd.sunk | while | flops 50708480 | bytes 11176069 | solution.py:190
  73.4 4.4 %bitcast_dynamic-update-slice_fusion.6 = (bf16[7,16,256,256]{3,2,1,0:T(8,128)(2,1)}, f32[16,256,256]{2,1,0:T(8,128)S(1)}) fusion(bf16[7,16,256,256]{3,2,1,0:T(8,128)(2,1)} %get-tuple-element.188, s32[]{:T(128)} %get-tuple-element.187, bf16[7,16,16,256]{3,2,1,0:T(8,128)(2,1)S(1)} %get-tuple-element.201, ...), kind=kOutput, calls=%fused_computation.13.clone.1 | convolution fusion | flops 48234496 | bytes 6588416 | tf_op jit(solution)/shard_map/while/body/eval_jaxpr/nda,ndb->nab/dot_general | solution.py:24
  83.8 4.4 %bitcast_dynamic-update-slice_fusion.6 = (bf16[7,16,256,256]{3,2,1,0:T(8,128)(2,1)}, f32[16,256,256]{2,1,0:T(8,128)S(1)}) fusion(bf16[7,16,256,256]{3,2,1,0:T(8,128)(2,1)} %get-tuple-element.188, s32[]{:T(128)} %get-tuple-element.187, bf16[7,16,16,256]{3,2,1,0:T(8,128)(2,1)S(1)} %get-tuple-element.201, ...), kind=kOutput, calls=%fused_computation.13.clone.1 | convolution fusion | flops 48234496 | bytes 6588416 | tf_op jit(solution)/shard_map/while/body/eval_jaxpr/nda,ndb->nab/dot_general | solution.py:24
  110.4 6.4 %shard_map.50 = f32[16,128]{1,0:T(8,128)} custom-call(f32[16,128]{1,0:T(8,128)} %reshape_reshape_broadcast_in_dim.3.x_ref), custom_call_target="tpu_custom_call" | custom-call | tf_op jit(solution)/shard_map/pallas_call | solution.py:99
  120.6 7.4 %all-to-all-start.3 = ((bf16[64,2,32,256]{3,2,1,0:T(8,128)(2,1)}), bf16[64,2,32,256]{3,2,1,0:T(8,128)(2,1)S(1)}, u32[]{:S(2)}, u32[]{:S(2)}) async-start(bf16[64,2,32,256]{3,2,1,0:T(8,128)(2,1)} %pad_maximum_fusion), calls=%async_computation.3 | async-start | bytes 4194304 | tf_op jit(solution)/shard_map/all_to_all | solution.py:147
  128.0 7.7 %slice.70 = bf16[4,16,256,256]{3,2,1,0:T(8,128)(2,1)} slice(bf16[7,16,256,256]{3,2,1,0:T(8,128)(2,1)} %get-tuple-element.95), slice={[3:7], [0:16], [0:256], [0:256]} | slice | bytes 16777216 | tf_op jit(solution)/shard_map/slice | solution.py:202
  135.7 6.1 %slice.67 = bf16[3,16,256,256]{3,2,1,0:T(8,128)(2,1)} slice(bf16[7,16,256,256]{3,2,1,0:T(8,128)(2,1)} %get-tuple-element.95), slice={[0:3], [0:16], [0:256], [0:256]} | slice | bytes 12582912 | tf_op jit(solution)/shard_map/slice | solution.py:201
  141.8 37.4 %all-to-all-done.3 = bf16[64,2,32,256]{3,2,1,0:T(8,128)(2,1)S(1)} async-done(((bf16[64,2,32,256]{3,2,1,0:T(8,128)(2,1)}), bf16[64,2,32,256]{3,2,1,0:T(8,128)(2,1)S(1)}, u32[]{:S(2)}, u32[]{:S(2)}) %all-to-all-start.3) | async-done | bytes 2097184 | tf_op jit(solution)/shard_map/all_to_all | solution.py:147
  180.9 6.1 %fusion.21 = f32[48,32,256]{2,1,0:T(8,128)} fusion(bf16[48,256,256]{2,1,0:T(8,128)(2,1)} %bitcast.247, bf16[48,32,256]{2,1,0:T(8,128)(2,1)} %gather_fusion.6, pred[48]{0:T(512)(128)(4,1)S(1)} %broadcast_compare_fusion.1), kind=kOutput, calls=%fused_computation.49 | convolution fusion | flops 201719808 | bytes 8650800 | tf_op jit(solution)/shard_map/sab,sob->soa/dot_general | solution.py:212
  188.6 4.9 %fusion.18 = f32[64,32,256]{2,1,0:T(8,128)S(1)} fusion(bf16[64,256,256]{2,1,0:T(8,128)(2,1)} %bitcast.245, bf16[64,2,32,256]{3,2,1,0:T(8,128)(2,1)S(1)} %all-to-all-done.3), kind=kOutput, calls=%fused_computation.39 | convolution fusion | flops 268435456 | bytes 11534336 | tf_op jit(solution)/shard_map/eab,eoa->eob/dot_general | solution.py:214
  196.3 16.4 %shard_map.51 = f32[512,128]{1,0:T(8,128)} custom-call(f32[512,128]{1,0:T(8,128)} %reshape_reshape.13.x_ref), custom_call_target="tpu_custom_call" | custom-call | tf_op jit(solution)/shard_map/pallas_call | solution.py:99
  214.6 14.0 %shard_map.52 = f32[1,128]{1,0:T(1,128)} custom-call(f32[1,128]{1,0:T(1,128)} %fusion.58.x_ref), custom_call_target="tpu_custom_call" | custom-call | tf_op jit(solution)/shard_map/pallas_call | solution.py:99
  230.1 13.5 %shard_map.53 = f32[1,128]{1,0:T(1,128)} custom-call(f32[1,128]{1,0:T(1,128)} %pad_bitcast_fusion.1.x_ref), custom_call_target="tpu_custom_call" | custom-call | tf_op jit(solution)/shard_map/pallas_call | solution.py:99
  246.2 57.4 %all_to_all.25 = bf16[64,2,32,256]{3,2,1,0:T(8,128)(2,1)S(1)} all-to-all(bf16[64,2,32,256]{3,2,1,0:T(8,128)(2,1)S(1)} %pad_maximum_fusion.1), channel_id=1, replica_groups=mesh['rows'=64,'cols'=4] {'rows'}, dimensions={0} | all-to-all | bytes 4194304 | tf_op jit(solution)/shard_map/all_to_all | solution.py:147
  306.5 5.9 %fusion.19 = f32[48,32,256]{2,1,0:T(8,128)} fusion(bf16[48,256,256]{2,1,0:T(8,128)(2,1)} %bitcast.248, bf16[48,32,256]{2,1,0:T(8,128)(2,1)S(1)} %gather_fusion.9, pred[48]{0:T(512)(128)(4,1)S(1)} %broadcast_compare_fusion.1), kind=kOutput, calls=%fused_computation.47 | convolution fusion | flops 201719808 | bytes 8650800 | tf_op jit(solution)/shard_map/sab,sob->soa/dot_general | solution.py:212
  313.9 4.9 %fusion.17 = f32[64,32,256]{2,1,0:T(8,128)S(1)} fusion(bf16[64,256,256]{2,1,0:T(8,128)(2,1)} %bitcast.246, bf16[64,2,32,256]{3,2,1,0:T(8,128)(2,1)S(1)} %all_to_all.25), kind=kOutput, calls=%fused_computation.36 | convolution fusion | flops 268435456 | bytes 11534336 | tf_op jit(solution)/shard_map/eab,eoa->eob/dot_general | solution.py:214
  321.7 16.4 %shard_map.54 = f32[512,128]{1,0:T(8,128)} custom-call(f32[512,128]{1,0:T(8,128)} %reshape_reshape.15.x_ref), custom_call_target="tpu_custom_call" | custom-call | tf_op jit(solution)/shard_map/pallas_call | solution.py:99
  339.9 14.0 %shard_map.55 = f32[1,128]{1,0:T(1,128)} custom-call(f32[1,128]{1,0:T(1,128)} %pad_bitcast_fusion.x_ref), custom_call_target="tpu_custom_call" | custom-call | tf_op jit(solution)/shard_map/pallas_call | solution.py:99
  (126 shorter events, 64.5 us)
Async XLA Ops:
  4.4 22.2 %all-to-all-start = ((s32[64,1,2]{2,1,0:T(1,128)}), s32[64,1,2]{2,1,0:T(1,128)S(1)}, u32[]{:S(2)}, u32[]{:S(2)}) async-start(s32[64,1,2]{2,1,0:T(1,128)} %copy.26), calls=%async_computation | async-start | bytes 65536 | tf_op jit(solution)/shard_map/all_to_all | solution.py:135
  26.6 22.1 %all-to-all-start.1 = ((bf16[64,16,256]{2,1,0:T(8,128)(2,1)}), bf16[64,16,256]{2,1,0:T(8,128)(2,1)S(1)}, u32[]{:S(2)}, u32[]{:S(2)}) async-start(bf16[64,16,256]{2,1,0:T(8,128)(2,1)} %broadcast_select_fusion.1), calls=%async_computation.1 | async-start | bytes 1048576 | tf_op jit(solution)/shard_map/all_to_all | solution.py:147
  48.7 23.7 %all-to-all-start.2 = ((bf16[64,16,256]{2,1,0:T(8,128)(2,1)}), bf16[64,16,256]{2,1,0:T(8,128)(2,1)S(1)}, u32[]{:S(2)}, u32[]{:S(2)}) async-start(bf16[64,16,256]{2,1,0:T(8,128)(2,1)} %broadcast_select_fusion), calls=%async_computation.2 | async-start | bytes 1048576 | tf_op jit(solution)/shard_map/all_to_all | solution.py:147
  73.2 44.3 %copy-start = (f32[32,2048]{1,0:T(8,128)S(1)}, f32[32,2048]{1,0:T(8,128)}, u32[]{:S(2)}) copy-start(f32[32,2048]{1,0:T(8,128)} %param.7) | copy-start | bytes 786436
  120.6 58.7 %all-to-all-start.3 = ((bf16[64,2,32,256]{3,2,1,0:T(8,128)(2,1)}), bf16[64,2,32,256]{3,2,1,0:T(8,128)(2,1)S(1)}, u32[]{:S(2)}, u32[]{:S(2)}) async-start(bf16[64,2,32,256]{3,2,1,0:T(8,128)(2,1)} %pad_maximum_fusion), calls=%async_computation.3 | async-start | bytes 4194304 | tf_op jit(solution)/shard_map/all_to_all | solution.py:147
  318.9 35.0 %copy-start.1 = (f32[1,128]{1,0:T(1,128)S(1)}, f32[1,128]{1,0:T(1,128)}, u32[]{:S(2)}) copy-start(f32[1,128]{1,0:T(1,128)} %shard_map.53) | copy-start | bytes 1540

commit v5 on v4

--- a/solution.py
+++ b/solution.py
@@ -111,6 +111,78 @@
     return out.reshape(-1)[:size].reshape(shape)
 
 
+def swap_kernel(axis, n, count, *refs):
+    ins, outs = refs[:count], refs[count:2 * count]
+    landed = refs[2 * count:3 * count]
+    send_sem, recv_sem = refs[3 * count:]
+    me = lax.axis_index(axis)
+    barrier = pltpu.get_barrier_semaphore()
+
+    def greet(k, carry):
+        peer = lax.rem(me + k, n)
+        pl.semaphore_signal(barrier, inc=1, device_id={axis: peer}, device_id_type=MESH)
+        return carry
+
+    lax.fori_loop(1, n, greet, 0)
+    pl.semaphore_wait(barrier, n - 1)
+
+    def outgoing(a, peer):
+        return pltpu.make_async_remote_copy(
+            src_ref=ins[a].at[peer],
+            dst_ref=landed[a].at[me],
+            send_sem=send_sem.at[a, peer],
+            recv_sem=recv_sem.at[a, me],
+            device_id={axis: peer},
+            device_id_type=MESH,
+        )
+
+    def incoming(a, peer):
+        return pltpu.make_async_remote_copy(
+            src_ref=ins[a].at[peer],
+            dst_ref=landed[a].at[peer],
+            send_sem=send_sem.at[a, peer],
+            recv_sem=recv_sem.at[a, peer],
+            device_id={axis: peer},
+            device_id_type=MESH,
+        )
+
+    def start(k, carry):
+        peer = lax.rem(me + k, n)
+        for a in range(count):
+            outgoing(a, peer).start()
+        return carry
+
+    lax.fori_loop(1, n, start, 0)
+    for a in range(count):
+        landed[a][me] = ins[a][me]
+
+    def finish(k, carry):
+        peer = lax.rem(me + k, n)
+        for a in range(count):
+            outgoing(a, peer).wait_send()
+            incoming(a, peer).wait_recv()
+        return carry
+
+    lax.fori_loop(1, n, finish, 0)
+    for a in range(count):
+        outs[a][...] = landed[a][...]
+
+
+def swap_all(arrays, axis, cid):
+    n = lax.axis_size(axis)
+    count = len(arrays)
+    vmem = pl.BlockSpec(memory_space=pltpu.VMEM)
+    return pl.pallas_call(
+        functools.partial(swap_kernel, axis, n, count),
+        out_shape=[jax.ShapeDtypeStruct(a.shape, a.dtype) for a in arrays],
+        in_specs=[vmem] * count,
+        out_specs=[vmem] * count,
+        scratch_shapes=[pltpu.VMEM(a.shape, a.dtype) for a in arrays]
+        + [pltpu.SemaphoreType.DMA((count, n)), pltpu.SemaphoreType.DMA((count, n))],
+        compiler_params=pltpu.CompilerParams(collective_id=cid, has_side_effects=True),
+    )(*arrays)
+
+
 def local(block_list, points, targets):
     row_count = lax.axis_size("rows")
     row_index = lax.axis_index("rows")
@@ -131,10 +203,12 @@
     asking_row = jnp.full((row_count,), -1, jnp.int32).at[place_at].set(slot_row, mode="drop")
     ask_live = asking_row >= 0
     ask_row = jnp.maximum(asking_row, 0)
-    request = jnp.stack([wanted, asking_row], axis=1).reshape(row_count, 1, 2)
-    incoming = lax.all_to_all(request, "rows", split_axis=0, concat_axis=0, tiled=True).reshape(
-        row_count, 2
-    )
+    request = jnp.zeros((row_count, 8, 128), jnp.int32)
+    request = request.at[:, 0, 0].set(wanted).at[:, 0, 1].set(asking_row)
+    own_x = points.reshape(coord_dim, block_rows, block_len).transpose(1, 0, 2)
+    asked_x = jnp.where(ask_live[:, None, None], own_x[ask_row], jnp.zeros((), own_x.dtype))
+    got_request, their_x = swap_all([request, asked_x], "rows", 3)
+    incoming = got_request[:, 0, :2]
     in_live = incoming[:, 0] >= 0
     in_idx = jnp.maximum(incoming[:, 0], 0)
     their_row = jnp.arange(row_count, dtype=jnp.int32) * block_rows + jnp.maximum(incoming[:, 1], 0)
@@ -143,8 +217,10 @@
         (in_idx[None, :] == jnp.arange(block_rows, dtype=jnp.int32)[:, None]) & in_off[None, :]
     ).astype(jnp.float32)
 
-    def swap(parts):
-        return lax.all_to_all(parts, "rows", split_axis=0, concat_axis=0, tiled=True)
+    def swap(parts, cid):
+        shape = parts.shape
+        flat = parts.reshape(shape[0], -1, shape[-1])
+        return swap_all([flat], "rows", cid)[0].reshape(shape)
 
     def asked_part(blocks):
         return jnp.where(ask_live[:, None, None], blocks[ask_row], jnp.zeros((), blocks.dtype))
@@ -169,9 +245,7 @@
     def global_sum(values):
         return allsum(values, "rows", 0)
 
-    own_x = points.reshape(coord_dim, block_rows, block_len).transpose(1, 0, 2)
-    their_x = swap(asked_part(own_x))
-    far_x = per_slot(swap(served_part(own_x)))
+    far_x = per_slot(swap(served_part(own_x), 4))
     left_x = jnp.concatenate([own_x[slot_row], their_x], axis=0)
     right_x = jnp.concatenate([far_x, own_x[in_idx]], axis=0)
     pair_live = jnp.concatenate([is_live, in_off], axis=0)
@@ -206,7 +280,7 @@
     inv_root = 1.0 / jnp.sqrt(1.0 + column_total(degree_part))
 
     def apply_partial(weights):
-        got = swap(jnp.stack([asked_part(weights), served_part(weights)], axis=1))
+        got = swap(jnp.stack([asked_part(weights), served_part(weights)], axis=1), 5)
         their_w = got[:, 0]
         far_w = per_slot(got[:, 1])
         direct = jnp.einsum("sab,sob->soa", own_k, far_w, preferred_element_type=jnp.float32)

time: 357 us -> 378 us (1.059)
  Pallas kernels: 80.8 us -> 259 us
  waiting for transfers between devices: 76.3 us -> 0 us
  blocking collectives: 57.4 us -> 0 us
  starting transfers between devices: 31.5 us -> 0 us
  local copies, waits for them, and re-layouts: 34.9 us -> 44.2 us
    pallas_call x0 -> x4, Pallas kernels: none -> 178 us  [swap_all(): pl.pallas_call(functools.partial(swap_kernel, axis, n, count), out_shape=...]
    all_to_all x4 -> x0, waiting for transfers between devices: 76.3 us -> none  [the longest x3 69.5 us: swap(): lax.all_to_all(parts, 'rows', split_axis=0, concat_axis=0, tiled=True)]
    all_to_all x1 -> x0, blocking collectives: 57.4 us -> none  [swap(): lax.all_to_all(parts, 'rows', split_axis=0, concat_axis=0, tiled=True)]
    all_to_all x4 -> x0, starting transfers between devices: 31.5 us -> none  [the longest x3 18.5 us: swap(): lax.all_to_all(parts, 'rows', split_axis=0, concat_axis=0, tiled=True)]
    scatter x0 -> x2, local copies, waits for them, and re-layouts: none -> 6.16 us  [local(): request = request.at[:, 0, 0].set(wanted).at[:, 0, 1].set(asking_row)]
    another operation x0 -> x6, local copies, waits for them, and re-layouts: none -> 3.86 us  [the longest x2 3.07 us: apply_partial(): jnp.stack([asked_part(weights), served_part(weights)], axis=1)]
  transfers between devices with their start and end apart: 4 -> 0, of which waited for: 4 -> 0; matrix products, arithmetic and copies ran while one was open for 5% -> 0% of each run, Pallas kernels for 0% -> 0%
where the time goes in v5:
time: 378 us; the launch traced here: 377 us
  Pallas kernels  259 us (69%)
  matrix products  53.8 us (14%)
  local copies, waits for them, and re-layouts  44.2 us (12%)
  other arithmetic  18.4 us (5%)
    pallas_call x4, Pallas kernels, swap_all(): pl.pallas_call(functools.partial(swap_kernel, axis, n, count), out_shape=...  178 us
    pallas_call x6, Pallas kernels, allsum(): pl.pallas_call(functools.partial(allsum_kernel, axis, n), out_shape=jax.S...  80.9 us
    dot_general x7, matrix products, wendland(): jnp.einsum('nda,ndb->nab', left_f, right_f, precision=lax.Precision.HIGHEST)  30.4 us
    dot_general x2, matrix products, apply_partial(): jnp.einsum('eab,eoa->eob', in_k, their_w, preferred_element_type=jnp.floa...  10.3 us
    dot_general x2, matrix products, apply_partial(): jnp.einsum('sab,sob->soa', own_k, far_w, preferred_element_type=jnp.float32)  8.96 us
    slice x1, local copies, waits for them, and re-layouts, local(): in_k = kernel_bf[slot_count:pair_count]  7.81 us

profile of v5, /device:TPU:1, one launch (start us, length us, event | category | flops | bytes accessed | tf_op | source)
XLA Modules:
  0.0 377.3 jit_solution(10033102184050050666)
XLA Ops:
  6.9 6.1 %scatter.27.refs_0_ = s32[64,8,128]{2,1,0:T(8,128)S(1)} dynamic-update-slice(s32[64,8,128]{2,1,0:T(8,128)S(1)} %scatter.25, s32[64,1,1]{2,1,0:T(1,128)S(1)} %copy.48, s32[]{:T(128)} %copy.132, s32[]{:T(128)} %bitcast.10, s32[]{:T(128)} %bitcast.11) | dynamic-update-slice | bytes 516 | tf_op jit(solution)/shard_map/scatter | solution.py:207
  13.8 34.7 %shard_map.50 = (s32[64,8,128]{2,1,0:T(8,128)}, bf16[64,16,256]{2,1,0:T(8,128)(2,1)}) custom-call(s32[64,8,128]{2,1,0:T(8,128)} %copy-done.5, bf16[64,16,256]{2,1,0:T(8,128)(2,1)} %broadcast_select_fusion.1.refs_1_), custom_call_target="tpu_custom_call" | custom-call | tf_op jit(solution)/shard_map/pallas_call | solution.py:175
  51.2 23.3 %shard_map.51 = bf16[64,16,256]{2,1,0:T(8,128)(2,1)} custom-call(bf16[64,16,256]{2,1,0:T(8,128)(2,1)} %broadcast_select_fusion.refs_0_), custom_call_target="tpu_custom_call" | custom-call | tf_op jit(solution)/shard_map/pallas_call | solution.py:175
  77.3 36.4 %while.18 = (s32[]{:T(128)}, bf16[7,16,256,256]{3,2,1,0:T(8,128)(2,1)}, f32[7,16,256]{2,1,0:T(8,128)S(1)}, f32[7,16,256]{2,1,0:T(8,128)S(1)}, pred[7,16]{1,0:T(8...) while((s32[]{:T(128)}, ...), condition=%wide.region_8.9_spmd, body=%wide.region_3.8_spmd.sunk | while | flops 50708480 | bytes 11176069 | solution.py:264
  77.4 4.4 %bitcast_dynamic-update-slice_fusion.6 = (bf16[7,16,256,256]{3,2,1,0:T(8,128)(2,1)}, f32[16,256,256]{2,1,0:T(8,128)S(1)}) fusion(bf16[7,16,256,256]{3,2,1,0:T(8,128)(2,1)} %get-tuple-element.218, s32[]{:T(128)} %get-tuple-element.217, bf16[7,16,16,256]{3,2,1,0:T(8,128)(2,1)S(1)} %get-tuple-element.231, ...), kind=kOutput, calls=%fused_computation.13.clone.1 | convolution fusion | flops 48234496 | bytes 6588416 | tf_op jit(solution)/shard_map/while/body/eval_jaxpr/nda,ndb->nab/dot_general | solution.py:24
  82.7 4.3 %bitcast_dynamic-update-slice_fusion.6 = (bf16[7,16,256,256]{3,2,1,0:T(8,128)(2,1)}, f32[16,256,256]{2,1,0:T(8,128)S(1)}) fusion(bf16[7,16,256,256]{3,2,1,0:T(8,128)(2,1)} %get-tuple-element.218, s32[]{:T(128)} %get-tuple-element.217, bf16[7,16,16,256]{3,2,1,0:T(8,128)(2,1)S(1)} %get-tuple-element.231, ...), kind=kOutput, calls=%fused_computation.13.clone.1 | convolution fusion | flops 48234496 | bytes 6588416 | tf_op jit(solution)/shard_map/while/body/eval_jaxpr/nda,ndb->nab/dot_general | solution.py:24
  87.8 4.4 %bitcast_dynamic-update-slice_fusion.6 = (bf16[7,16,256,256]{3,2,1,0:T(8,128)(2,1)}, f32[16,256,256]{2,1,0:T(8,128)S(1)}) fusion(bf16[7,16,256,256]{3,2,1,0:T(8,128)(2,1)} %get-tuple-element.218, s32[]{:T(128)} %get-tuple-element.217, bf16[7,16,16,256]{3,2,1,0:T(8,128)(2,1)S(1)} %get-tuple-element.231, ...), kind=kOutput, calls=%fused_computation.13.clone.1 | convolution fusion | flops 48234496 | bytes 6588416 | tf_op jit(solution)/shard_map/while/body/eval_jaxpr/nda,ndb->nab/dot_general | solution.py:24
  93.1 4.3 %bitcast_dynamic-update-slice_fusion.6 = (bf16[7,16,256,256]{3,2,1,0:T(8,128)(2,1)}, f32[16,256,256]{2,1,0:T(8,128)S(1)}) fusion(bf16[7,16,256,256]{3,2,1,0:T(8,128)(2,1)} %get-tuple-element.218, s32[]{:T(128)} %get-tuple-element.217, bf16[7,16,16,256]{3,2,1,0:T(8,128)(2,1)S(1)} %get-tuple-element.231, ...), kind=kOutput, calls=%fused_computation.13.clone.1 | convolution fusion | flops 48234496 | bytes 6588416 | tf_op jit(solution)/shard_map/while/body/eval_jaxpr/nda,ndb->nab/dot_general | solution.py:24
  98.2 4.3 %bitcast_dynamic-update-slice_fusion.6 = (bf16[7,16,256,256]{3,2,1,0:T(8,128)(2,1)}, f32[16,256,256]{2,1,0:T(8,128)S(1)}) fusion(bf16[7,16,256,256]{3,2,1,0:T(8,128)(2,1)} %get-tuple-element.218, s32[]{:T(128)} %get-tuple-element.217, bf16[7,16,16,256]{3,2,1,0:T(8,128)(2,1)S(1)} %get-tuple-element.231, ...), kind=kOutput, calls=%fused_computation.13.clone.1 | convolution fusion | flops 48234496 | bytes 6588416 | tf_op jit(solution)/shard_map/while/body/eval_jaxpr/nda,ndb->nab/dot_general | solution.py:24
  103.4 4.3 %bitcast_dynamic-update-slice_fusion.6 = (bf16[7,16,256,256]{3,2,1,0:T(8,128)(2,1)}, f32[16,256,256]{2,1,0:T(8,128)S(1)}) fusion(bf16[7,16,256,256]{3,2,1,0:T(8,128)(2,1)} %get-tuple-element.218, s32[]{:T(128)} %get-tuple-element.217, bf16[7,16,16,256]{3,2,1,0:T(8,128)(2,1)S(1)} %get-tuple-element.231, ...), kind=kOutput, calls=%fused_computation.13.clone.1 | convolution fusion | flops 48234496 | bytes 6588416 | tf_op jit(solution)/shard_map/while/body/eval_jaxpr/nda,ndb->nab/dot_general | solution.py:24
  108.6 4.3 %bitcast_dynamic-update-slice_fusion.6 = (bf16[7,16,256,256]{3,2,1,0:T(8,128)(2,1)}, f32[16,256,256]{2,1,0:T(8,128)S(1)}) fusion(bf16[7,16,256,256]{3,2,1,0:T(8,128)(2,1)} %get-tuple-element.218, s32[]{:T(128)} %get-tuple-element.217, bf16[7,16,16,256]{3,2,1,0:T(8,128)(2,1)S(1)} %get-tuple-element.231, ...), kind=kOutput, calls=%fused_computation.13.clone.1 | convolution fusion | flops 48234496 | bytes 6588416 | tf_op jit(solution)/shard_map/while/body/eval_jaxpr/nda,ndb->nab/dot_general | solution.py:24
  114.4 6.4 %shard_map.52 = f32[16,128]{1,0:T(8,128)} custom-call(f32[16,128]{1,0:T(8,128)} %reshape_reshape_broadcast_in_dim.3.x_ref), custom_call_target="tpu_custom_call" | custom-call | tf_op jit(solution)/shard_map/pallas_call | solution.py:99
  124.8 60.2 %shard_map.53 = bf16[64,64,256]{2,1,0:T(8,128)(2,1)} custom-call(bf16[64,64,256]{2,1,0:T(8,128)(2,1)} %bitcast.268), custom_call_target="tpu_custom_call" | custom-call | tf_op jit(solution)/shard_map/pallas_call | solution.py:175
  185.0 7.8 %slice.121 = bf16[4,16,256,256]{3,2,1,0:T(8,128)(2,1)} slice(bf16[7,16,256,256]{3,2,1,0:T(8,128)(2,1)} %get-tuple-element.123), slice={[3:7], [0:16], [0:256], [0:256]} | slice | bytes 16777216 | tf_op jit(solution)/shard_map/slice | solution.py:276
  192.8 4.9 %fusion.18 = f32[64,32,256]{2,1,0:T(8,128)S(1)} fusion(bf16[64,256,256]{2,1,0:T(8,128)(2,1)} %bitcast.249, bf16[64,2,32,256]{3,2,1,0:T(8,128)(2,1)S(1)} %bitcast.258), kind=kOutput, calls=%fused_computation.39 | convolution fusion | flops 268435456 | bytes 11534336 | tf_op jit(solution)/shard_map/eab,eoa->eob/dot_general | solution.py:288
  199.4 3.3 slice.118
  210.1 16.7 %shard_map.54 = f32[512,128]{1,0:T(8,128)} custom-call(f32[512,128]{1,0:T(8,128)} %reshape_reshape.13.x_ref), custom_call_target="tpu_custom_call" | custom-call | tf_op jit(solution)/shard_map/pallas_call | solution.py:99
  228.6 13.8 %shard_map.55 = f32[1,128]{1,0:T(1,128)} custom-call(f32[1,128]{1,0:T(1,128)} %fusion.58.x_ref), custom_call_target="tpu_custom_call" | custom-call | tf_op jit(solution)/shard_map/pallas_call | solution.py:99
  243.9 13.7 %shard_map.56 = f32[1,128]{1,0:T(1,128)} custom-call(f32[1,128]{1,0:T(1,128)} %pad_bitcast_fusion.1.x_ref), custom_call_target="tpu_custom_call" | custom-call | tf_op jit(solution)/shard_map/pallas_call | solution.py:99
  263.9 60.3 %shard_map.57 = bf16[64,64,256]{2,1,0:T(8,128)(2,1)} custom-call(bf16[64,64,256]{2,1,0:T(8,128)(2,1)} %bitcast.269), custom_call_target="tpu_custom_call" | custom-call | tf_op jit(solution)/shard_map/pallas_call | solution.py:175
  324.2 5.4 %fusion.17 = f32[64,32,256]{2,1,0:T(8,128)S(1)} fusion(bf16[64,256,256]{2,1,0:T(8,128)(2,1)} %bitcast.250, bf16[64,2,32,256]{3,2,1,0:T(8,128)(2,1)} %bitcast.260), kind=kOutput, calls=%fused_computation.36 | convolution fusion | flops 268435456 | bytes 11534336 | tf_op jit(solution)/shard_map/eab,eoa->eob/dot_general | solution.py:288
  332.5 5.9 %fusion.19 = f32[48,32,256]{2,1,0:T(8,128)} fusion(bf16[48,256,256]{2,1,0:T(8,128)(2,1)} %bitcast.252, bf16[48,32,256]{2,1,0:T(8,128)(2,1)S(1)} %gather_fusion.9, pred[48]{0:T(512)(128)(4,1)S(1)} %broadcast_compare_fusion.1), kind=kOutput, calls=%fused_computation.47 | convolution fusion | flops 201719808 | bytes 8650800 | tf_op jit(solution)/shard_map/sab,sob->soa/dot_general | solution.py:286
  342.8 16.5 %shard_map.58 = f32[512,128]{1,0:T(8,128)} custom-call(f32[512,128]{1,0:T(8,128)} %reshape_reshape.15.x_ref), custom_call_target="tpu_custom_call" | custom-call | tf_op jit(solution)/shard_map/pallas_call | solution.py:99
  361.1 13.8 %shard_map.59 = f32[1,128]{1,0:T(1,128)} custom-call(f32[1,128]{1,0:T(1,128)} %pad_bitcast_fusion.x_ref), custom_call_target="tpu_custom_call" | custom-call | tf_op jit(solution)/shard_map/pallas_call | solution.py:99
  (140 shorter events, 52.6 us)
Async XLA Ops:
  13.1 0.7 copy-start.5
  48.5 28.7 %copy-start.6 = (bf16[64,16,256]{2,1,0:T(8,128)(2,1)S(1)}, bf16[64,16,256]{2,1,0:T(8,128)(2,1)}, u32[]{:S(2)}) copy-start(bf16[64,16,256]{2,1,0:T(8,128)(2,1)} %get-tuple-element.120) | copy-start | bytes 1572868
  77.2 44.3 %copy-start.3 = (f32[32,2048]{1,0:T(8,128)S(1)}, f32[32,2048]{1,0:T(8,128)}, u32[]{:S(2)}) copy-start(f32[32,2048]{1,0:T(8,128)} %param.11) | copy-start | bytes 786436
  185.0 7.8 %copy-start.1 = (bf16[64,64,256]{2,1,0:T(8,128)(2,1)S(1)}, bf16[64,64,256]{2,1,0:T(8,128)(2,1)}, u32[]{:S(2)}) copy-start(bf16[64,64,256]{2,1,0:T(8,128)(2,1)} %shard_map.53) | copy-start | bytes 6291460
  199.3 3.3 copy-start.4
  202.6 3.1 copy-start
  324.2 5.4 %copy-start.2 = (bf16[64,64,256]{2,1,0:T(8,128)(2,1)S(1)}, bf16[64,64,256]{2,1,0:T(8,128)(2,1)}, u32[]{:S(2)}) copy-start(bf16[64,64,256]{2,1,0:T(8,128)(2,1)} %shard_map.57) | copy-start | bytes 6291460
  338.4 36.5 %copy-start.7 = (f32[1,128]{1,0:T(1,128)S(1)}, f32[1,128]{1,0:T(1,128)}, u32[]{:S(2)}) copy-start(f32[1,128]{1,0:T(1,128)} %shard_map.56) | copy-start | bytes 1540

commit v6 on v4

--- a/solution.py
+++ b/solution.py
@@ -146,6 +146,17 @@
     def swap(parts):
         return lax.all_to_all(parts, "rows", split_axis=0, concat_axis=0, tiled=True)
 
+    peer_ids = jnp.arange(row_count, dtype=jnp.int32)
+    to_lower = (peer_ids <= row_index)[:, None, None]
+    from_self = (peer_ids == row_index)[:, None, None]
+
+    def both_ways(blocks):
+        got = swap(jnp.where(to_lower, asked_part(blocks), served_part(blocks)))
+        their = jnp.where(peer_ids[:, None, None] >= row_index, got, jnp.zeros((), got.dtype))
+        served_self = blocks[in_idx[row_index]]
+        far = jnp.where(from_self, served_self[None], got)
+        return their, per_slot(far)
+
     def asked_part(blocks):
         return jnp.where(ask_live[:, None, None], blocks[ask_row], jnp.zeros((), blocks.dtype))
 
@@ -170,8 +181,7 @@
         return allsum(values, "rows", 0)
 
     own_x = points.reshape(coord_dim, block_rows, block_len).transpose(1, 0, 2)
-    their_x = swap(asked_part(own_x))
-    far_x = per_slot(swap(served_part(own_x)))
+    their_x, far_x = both_ways(own_x)
     left_x = jnp.concatenate([own_x[slot_row], their_x], axis=0)
     right_x = jnp.concatenate([far_x, own_x[in_idx]], axis=0)
     pair_live = jnp.concatenate([is_live, in_off], axis=0)
@@ -206,9 +216,7 @@
     inv_root = 1.0 / jnp.sqrt(1.0 + column_total(degree_part))
 
     def apply_partial(weights):
-        got = swap(jnp.stack([asked_part(weights), served_part(weights)], axis=1))
-        their_w = got[:, 0]
-        far_w = per_slot(got[:, 1])
+        their_w, far_w = both_ways(weights)
         direct = jnp.einsum("sab,sob->soa", own_k, far_w, preferred_element_type=jnp.float32)
         direct = jnp.sum(direct.reshape(block_rows, slot_width, outputs, block_len), axis=1)
         mirror = jnp.einsum("eab,eoa->eob", in_k, their_w, preferred_element_type=jnp.float32)

time: 357 us -> 286 us (0.80)
  blocking collectives: 57.4 us -> 0 us
  waiting for transfers between devices: 76.3 us -> 64.3 us
    all_to_all x1 -> x0, blocking collectives: 57.4 us -> none  [swap(): lax.all_to_all(parts, 'rows', split_axis=0, concat_axis=0, tiled=True)]
    all_to_all x3, waiting for transfers between devices: 69.5 us -> 56.6 us  [swap(): lax.all_to_all(parts, 'rows', split_axis=0, concat_axis=0, tiled=True)]
  transfers between devices with their start and end apart: 4 -> 4, of which waited for: 4 -> 4; matrix products, arithmetic and copies ran while one was open for 5% -> 6% of each run, Pallas kernels for 0% -> 0%
where the time goes in v6:
time: 286 us; the launch traced here: 285 us
  Pallas kernels  81.2 us (28%)
  waiting for transfers between devices  64.3 us (22%)
  matrix products  54.4 us (19%)
  local copies, waits for them, and re-layouts  34.6 us (12%)
  starting transfers between devices  31.8 us (11%)
  other arithmetic  14.8 us (5%)
  between operations  3.21 us (1%)
    pallas_call x6, Pallas kernels, allsum(): pl.pallas_call(functools.partial(allsum_kernel, axis, n), out_shape=jax.S...  81.2 us
    all_to_all x3, waiting for transfers between devices, swap(): lax.all_to_all(parts, 'rows', split_axis=0, concat_axis=0, tiled=True)  56.6 us
    dot_general x7, matrix products, wendland(): jnp.einsum('nda,ndb->nab', left_f, right_f, precision=lax.Precision.HIGHEST)  30.4 us
    all_to_all x3, starting transfers between devices, swap(): lax.all_to_all(parts, 'rows', split_axis=0, concat_axis=0, tiled=True)  18.8 us
    all_to_all x1, starting transfers between devices, local(): lax.all_to_all(request, 'rows', split_axis=0, concat_axis=0, tiled=True)  13 us
    dot_general x2, matrix products, apply_partial(): jnp.einsum('sab,sob->soa', own_k, far_w, preferred_element_type=jnp.float32)  9.97 us
    dot_general x2, matrix products, apply_partial(): jnp.einsum('eab,eoa->eob', in_k, their_w, preferred_element_type=jnp.floa...  9.88 us
    all_to_all x1, waiting for transfers between devices, local(): lax.all_to_all(request, 'rows', split_axis=0, concat_axis=0, tiled=True)  7.7 us
  transfers between devices with their start and end apart: 4, of which 4 were waited for; matrix products, arithmetic and copies ran while one was open for 6% of the time, Pallas kernels for 0%

profile of v6, /device:TPU:1, one launch (start us, length us, event | category | flops | bytes accessed | tf_op | source)
XLA Modules:
  0.0 284.7 jit_solution(6257147290880059952)
XLA Ops:
  4.5 13.0 %all-to-all-start = ((s32[64,1,2]{2,1,0:T(1,128)}), s32[64,1,2]{2,1,0:T(1,128)S(1)}, u32[]{:S(2)}, u32[]{:S(2)}) async-start(s32[64,1,2]{2,1,0:T(1,128)} %copy.26), calls=%async_computation | async-start | bytes 65536 | tf_op jit(solution)/shard_map/all_to_all | solution.py:135
  18.9 7.7 %all-to-all-done = s32[64,1,2]{2,1,0:T(1,128)S(1)} async-done(((s32[64,1,2]{2,1,0:T(1,128)}), s32[64,1,2]{2,1,0:T(1,128)S(1)}, u32[]{:S(2)}, u32[]{:S(2)}) %all-to-all-start) | async-done | bytes 544 | tf_op jit(solution)/shard_map/all_to_all | solution.py:135
  28.5 4.7 %all-to-all-start.1 = ((bf16[64,16,256]{2,1,0:T(8,128)(2,1)}), bf16[64,16,256]{2,1,0:T(8,128)(2,1)S(1)}, u32[]{:S(2)}, u32[]{:S(2)}) async-start(bf16[64,16,256]{2,1,0:T(8,128)(2,1)} %select_select_fusion.2), calls=%async_computation.1 | async-start | bytes 1048576 | tf_op jit(solution)/shard_map/all_to_all | solution.py:147
  37.3 13.3 %all-to-all-done.1 = bf16[64,16,256]{2,1,0:T(8,128)(2,1)S(1)} async-done(((bf16[64,16,256]{2,1,0:T(8,128)(2,1)}), bf16[64,16,256]{2,1,0:T(8,128)(2,1)S(1)}, u32[]{:S(2)}, u32[]{:S(2)}) %all-to-all-start.1) | async-done | bytes 524320 | tf_op jit(solution)/shard_map/all_to_all | solution.py:147
  51.7 36.3 %while.16 = (s32[]{:T(128)}, bf16[7,16,256,256]{3,2,1,0:T(8,128)(2,1)}, f32[7,16,256]{2,1,0:T(8,128)S(1)}, f32[7,16,256]{2,1,0:T(8,128)S(1)}, pred[7,16]{1,0:T(8...) while((s32[]{:T(128)}, ...), condition=%wide.region_8.9_spmd, body=%wide.region_3.8_spmd.sunk | while | flops 50708480 | bytes 11176069 | solution.py:200
  51.9 4.4 %bitcast_dynamic-update-slice_fusion.6 = (bf16[7,16,256,256]{3,2,1,0:T(8,128)(2,1)}, f32[16,256,256]{2,1,0:T(8,128)S(1)}) fusion(bf16[7,16,256,256]{3,2,1,0:T(8,128)(2,1)} %get-tuple-element.196, s32[]{:T(128)} %get-tuple-element.195, bf16[7,16,16,256]{3,2,1,0:T(8,128)(2,1)S(1)} %get-tuple-element.209, ...), kind=kOutput, calls=%fused_computation.13.clone.1 | convolution fusion | flops 48234496 | bytes 6588416 | tf_op jit(solution)/shard_map/while/body/eval_jaxpr/nda,ndb->nab/dot_general | solution.py:24
  57.1 4.3 %bitcast_dynamic-update-slice_fusion.6 = (bf16[7,16,256,256]{3,2,1,0:T(8,128)(2,1)}, f32[16,256,256]{2,1,0:T(8,128)S(1)}) fusion(bf16[7,16,256,256]{3,2,1,0:T(8,128)(2,1)} %get-tuple-element.196, s32[]{:T(128)} %get-tuple-element.195, bf16[7,16,16,256]{3,2,1,0:T(8,128)(2,1)S(1)} %get-tuple-element.209, ...), kind=kOutput, calls=%fused_computation.13.clone.1 | convolution fusion | flops 48234496 | bytes 6588416 | tf_op jit(solution)/shard_map/while/body/eval_jaxpr/nda,ndb->nab/dot_general | solution.py:24
  62.3 4.4 %bitcast_dynamic-update-slice_fusion.6 = (bf16[7,16,256,256]{3,2,1,0:T(8,128)(2,1)}, f32[16,256,256]{2,1,0:T(8,128)S(1)}) fusion(bf16[7,16,256,256]{3,2,1,0:T(8,128)(2,1)} %get-tuple-element.196, s32[]{:T(128)} %get-tuple-element.195, bf16[7,16,16,256]{3,2,1,0:T(8,128)(2,1)S(1)} %get-tuple-element.209, ...), kind=kOutput, calls=%fused_computation.13.clone.1 | convolution fusion | flops 48234496 | bytes 6588416 | tf_op jit(solution)/shard_map/while/body/eval_jaxpr/nda,ndb->nab/dot_general | solution.py:24
  88.9 6.4 %shard_map.50 = f32[16,128]{1,0:T(8,128)} custom-call(f32[16,128]{1,0:T(8,128)} %reshape_reshape_broadcast_in_dim.3.x_ref), custom_call_target="tpu_custom_call" | custom-call | tf_op jit(solution)/shard_map/pallas_call | solution.py:99
  98.7 7.5 %all-to-all-start.2 = ((bf16[64,32,256]{2,1,0:T(8,128)(2,1)}), bf16[64,32,256]{2,1,0:T(8,128)(2,1)S(1)}, u32[]{:S(2)}, u32[]{:S(2)}) async-start(bf16[64,32,256]{2,1,0:T(8,128)(2,1)} %select_select_fusion.1), calls=%async_computation.2 | async-start | bytes 2097152 | tf_op jit(solution)/shard_map/all_to_all | solution.py:147
  106.2 7.7 %slice.56 = bf16[4,16,256,256]{3,2,1,0:T(8,128)(2,1)} slice(bf16[7,16,256,256]{3,2,1,0:T(8,128)(2,1)} %get-tuple-element.95), slice={[3:7], [0:16], [0:256], [0:256]} | slice | bytes 16777216 | tf_op jit(solution)/shard_map/slice | solution.py:212
  113.9 6.1 %slice.54 = bf16[3,16,256,256]{3,2,1,0:T(8,128)(2,1)} slice(bf16[7,16,256,256]{3,2,1,0:T(8,128)(2,1)} %get-tuple-element.95), slice={[0:3], [0:16], [0:256], [0:256]} | slice | bytes 12582912 | tf_op jit(solution)/shard_map/slice | solution.py:211
  120.0 14.7 %all-to-all-done.2 = bf16[64,32,256]{2,1,0:T(8,128)(2,1)S(1)} async-done(((bf16[64,32,256]{2,1,0:T(8,128)(2,1)}), bf16[64,32,256]{2,1,0:T(8,128)(2,1)S(1)}, u32[]{:S(2)}, u32[]{:S(2)}) %all-to-all-start.2) | async-done | bytes 1048608 | tf_op jit(solution)/shard_map/all_to_all | solution.py:147
  136.4 5.0 %fusion.25 = f32[48,32,256]{2,1,0:T(8,128)S(1)} fusion(bf16[48,256,256]{2,1,0:T(8,128)(2,1)} %bitcast.234, bf16[48,32,256]{2,1,0:T(8,128)(2,1)} %gather_fusion.6, pred[48]{0:T(512)(128)(4,1)S(1)} %copy-done.7), kind=kOutput, calls=%fused_computation.47 | convolution fusion | flops 201719808 | bytes 8650800 | tf_op jit(solution)/shard_map/sab,sob->soa/dot_general | solution.py:220
  141.5 4.9 %fusion.19 = f32[64,32,256]{2,1,0:T(8,128)S(1)} fusion(bf16[64,256,256]{2,1,0:T(8,128)(2,1)} %bitcast.232, bf16[64,32,256]{2,1,0:T(8,128)(2,1)S(1)} %all-to-all-done.2, pred[64]{0:T(512)(128)(4,1)S(1)} %get-tuple-element.131), kind=kOutput, calls=%fused_computation.36 | convolution fusion | flops 268959744 | bytes 11534400 | tf_op jit(solution)/shard_map/eab,eoa->eob/dot_general | solution.py:222
  149.3 16.8 %shard_map.51 = f32[512,128]{1,0:T(8,128)} custom-call(f32[512,128]{1,0:T(8,128)} %reshape_reshape.13.x_ref), custom_call_target="tpu_custom_call" | custom-call | tf_op jit(solution)/shard_map/pallas_call | solution.py:99
  167.9 13.8 %shard_map.52 = f32[1,128]{1,0:T(1,128)} custom-call(f32[1,128]{1,0:T(1,128)} %fusion.64.x_ref), custom_call_target="tpu_custom_call" | custom-call | tf_op jit(solution)/shard_map/pallas_call | solution.py:99
  183.3 13.6 %shard_map.53 = f32[1,128]{1,0:T(1,128)} custom-call(f32[1,128]{1,0:T(1,128)} %pad_bitcast_fusion.1.x_ref), custom_call_target="tpu_custom_call" | custom-call | tf_op jit(solution)/shard_map/pallas_call | solution.py:99
  200.2 6.6 %all-to-all-start.3 = ((bf16[64,32,256]{2,1,0:T(8,128)(2,1)}), bf16[64,32,256]{2,1,0:T(8,128)(2,1)S(1)}, u32[]{:S(2)}, u32[]{:S(2)}) async-start(bf16[64,32,256]{2,1,0:T(8,128)(2,1)} %select_select_fusion), calls=%async_computation.3 | async-start | bytes 2097152 | tf_op jit(solution)/shard_map/all_to_all | solution.py:147
  206.8 28.5 %all-to-all-done.3 = bf16[64,32,256]{2,1,0:T(8,128)(2,1)S(1)} async-done(((bf16[64,32,256]{2,1,0:T(8,128)(2,1)}), bf16[64,32,256]{2,1,0:T(8,128)(2,1)S(1)}, u32[]{:S(2)}, u32[]{:S(2)}) %all-to-all-start.3) | async-done | bytes 1048608 | tf_op jit(solution)/shard_map/all_to_all | solution.py:147
  237.0 5.0 %fusion.23 = f32[48,32,256]{2,1,0:T(8,128)S(1)} fusion(bf16[48,256,256]{2,1,0:T(8,128)(2,1)} %bitcast.235, bf16[48,32,256]{2,1,0:T(8,128)(2,1)} %gather_fusion.9, pred[48]{0:T(512)(128)(4,1)S(1)} %copy-done.7), kind=kOutput, calls=%fused_computation.45 | convolution fusion | flops 201719808 | bytes 8650800 | tf_op jit(solution)/shard_map/sab,sob->soa/dot_general | solution.py:220
  242.1 4.9 %fusion.17 = f32[64,32,256]{2,1,0:T(8,128)S(1)} fusion(bf16[64,256,256]{2,1,0:T(8,128)(2,1)} %bitcast.233, bf16[64,32,256]{2,1,0:T(8,128)(2,1)S(1)} %all-to-all-done.3, pred[64]{0:T(512)(128)(4,1)S(1)} %get-tuple-element.131), kind=kOutput, calls=%fused_computation.33 | convolution fusion | flops 268959744 | bytes 11534400 | tf_op jit(solution)/shard_map/eab,eoa->eob/dot_general | solution.py:222
  249.9 16.8 %shard_map.54 = f32[512,128]{1,0:T(8,128)} custom-call(f32[512,128]{1,0:T(8,128)} %reshape_reshape.15.x_ref), custom_call_target="tpu_custom_call" | custom-call | tf_op jit(solution)/shard_map/pallas_call | solution.py:99
  268.5 13.8 %shard_map.55 = f32[1,128]{1,0:T(1,128)} custom-call(f32[1,128]{1,0:T(1,128)} %pad_bitcast_fusion.x_ref), custom_call_target="tpu_custom_call" | custom-call | tf_op jit(solution)/shard_map/pallas_call | solution.py:99
  (144 shorter events, 57.1 us)
Async XLA Ops:
  0.6 32.6 %copy-start.1 = (bf16[16,2048]{1,0:T(8,128)(2,1)S(1)}, bf16[16,2048]{1,0:T(8,128)(2,1)}, u32[]{:S(2)}) copy-start(bf16[16,2048]{1,0:T(8,128)(2,1)} %param.6) | copy-start | bytes 196612
  4.5 22.2 %all-to-all-start = ((s32[64,1,2]{2,1,0:T(1,128)}), s32[64,1,2]{2,1,0:T(1,128)S(1)}, u32[]{:S(2)}, u32[]{:S(2)}) async-start(s32[64,1,2]{2,1,0:T(1,128)} %copy.26), calls=%async_computation | async-start | bytes 65536 | tf_op jit(solution)/shard_map/all_to_all | solution.py:135
  26.7 9.7 %copy-start.2 = (pred[64]{0:T(512)(128)(4,1)}, pred[64]{0:T(512)(128)(4,1)S(1)}, u32[]{:S(2)}) copy-start(pred[64]{0:T(512)(128)(4,1)S(1)} %compare_bitcast_fusion) | copy-start | bytes 196
  28.5 22.1 %all-to-all-start.1 = ((bf16[64,16,256]{2,1,0:T(8,128)(2,1)}), bf16[64,16,256]{2,1,0:T(8,128)(2,1)S(1)}, u32[]{:S(2)}, u32[]{:S(2)}) async-start(bf16[64,16,256]{2,1,0:T(8,128)(2,1)} %select_select_fusion.2), calls=%async_computation.1 | async-start | bytes 1048576 | tf_op jit(solution)/shard_map/all_to_all | solution.py:147
  33.9 17.8 %copy-start.4 = (pred[64]{0:T(512)(128)(4,1)}, pred[64]{0:T(512)(128)(4,1)S(1)}, u32[]{:S(2)}) copy-start(pred[64]{0:T(512)(128)(4,1)S(1)} %get-tuple-element.130) | copy-start | bytes 196
  33.9 17.8 %copy-start.6 = (pred[48]{0:T(512)(128)(4,1)}, pred[48]{0:T(512)(128)(4,1)S(1)}, u32[]{:S(2)}) copy-start(pred[48]{0:T(512)(128)(4,1)S(1)} %broadcast_compare_fusion.1) | copy-start | bytes 148
  50.8 0.9 copy-start.8
  51.7 44.4 %copy-start = (f32[32,2048]{1,0:T(8,128)S(1)}, f32[32,2048]{1,0:T(8,128)}, u32[]{:S(2)}) copy-start(f32[32,2048]{1,0:T(8,128)} %param.7) | copy-start | bytes 786436
  88.1 9.3 %copy-start.3 = (pred[64]{0:T(512)(128)(4,1)S(1)}, pred[64]{0:T(512)(128)(4,1)}, u32[]{:S(2)}) copy-start(pred[64]{0:T(512)(128)(4,1)} %copy-done.2) | copy-start | bytes 196
  98.7 36.1 %all-to-all-start.2 = ((bf16[64,32,256]{2,1,0:T(8,128)(2,1)}), bf16[64,32,256]{2,1,0:T(8,128)(2,1)S(1)}, u32[]{:S(2)}, u32[]{:S(2)}) async-start(bf16[64,32,256]{2,1,0:T(8,128)(2,1)} %select_select_fusion.1), calls=%async_computation.2 | async-start | bytes 2097152 | tf_op jit(solution)/shard_map/all_to_all | solution.py:147
  113.9 20.9 %copy-start.5 = (pred[64]{0:T(512)(128)(4,1)S(1)}, pred[64]{0:T(512)(128)(4,1)}, u32[]{:S(2)}) copy-start(pred[64]{0:T(512)(128)(4,1)} %copy-done.4) | copy-start | bytes 196
  113.9 22.6 %copy-start.7 = (pred[48]{0:T(512)(128)(4,1)S(1)}, pred[48]{0:T(512)(128)(4,1)}, u32[]{:S(2)}) copy-start(pred[48]{0:T(512)(128)(4,1)} %copy-done.6) | copy-start | bytes 148
  200.2 35.1 %all-to-all-start.3 = ((bf16[64,32,256]{2,1,0:T(8,128)(2,1)}), bf16[64,32,256]{2,1,0:T(8,128)(2,1)S(1)}, u32[]{:S(2)}, u32[]{:S(2)}) async-start(bf16[64,32,256]{2,1,0:T(8,128)(2,1)} %select_select_fusion), calls=%async_computation.3 | async-start | bytes 2097152 | tf_op jit(solution)/shard_map/all_to_all | solution.py:147
  247.1 35.2 %copy-start.9 = (f32[1,128]{1,0:T(1,128)S(1)}, f32[1,128]{1,0:T(1,128)}, u32[]{:S(2)}) copy-start(f32[1,128]{1,0:T(1,128)} %shard_map.53) | copy-start | bytes 1540

commit v7 on v6

--- a/solution.py
+++ b/solution.py
@@ -109,6 +109,112 @@
         compiler_params=pltpu.CompilerParams(collective_id=cid, has_side_effects=True),
     )(tile)
     return out.reshape(-1)[:size].reshape(shape)
+
+
+def fused_kernel(n_rows, n_cols, z_ref, g_ref, zo_ref, go_ref, recv_z, recv_g, sems):
+    row = lax.axis_index("rows")
+    col = lax.axis_index("cols")
+    total = n_rows * n_cols
+    me = row * n_cols + col
+    barrier = pltpu.get_barrier_semaphore()
+
+    def peer_of(k):
+        peer = lax.rem(me + k, total)
+        return peer, (peer // n_cols, lax.rem(peer, n_cols))
+
+    def greet(k, carry):
+        _, device = peer_of(k)
+        pl.semaphore_signal(barrier, inc=1, device_id=device, device_id_type=MESH)
+        return carry
+
+    lax.fori_loop(1, total, greet, 0)
+    pl.semaphore_wait(barrier, total - 1)
+    z_send, z_recv, g_send, g_recv = sems
+
+    def z_copy(peer, slot):
+        return pltpu.make_async_remote_copy(
+            src_ref=z_ref,
+            dst_ref=recv_z.at[slot],
+            send_sem=z_send.at[peer],
+            recv_sem=z_recv.at[slot],
+            device_id={"cols": peer},
+            device_id_type=MESH,
+        )
+
+    def g_copy(peer, slot):
+        return pltpu.make_async_remote_copy(
+            src_ref=g_ref,
+            dst_ref=recv_g.at[slot],
+            send_sem=g_send.at[peer],
+            recv_sem=g_recv.at[slot],
+            device_id=(peer // n_cols, lax.rem(peer, n_cols)),
+            device_id_type=MESH,
+        )
+
+    for k in range(1, n_cols):
+        z_copy(lax.rem(col + k, n_cols), col).start()
+
+    def start(k, carry):
+        peer, _ = peer_of(k)
+        g_copy(peer, me).start()
+        return carry
+
+    lax.fori_loop(1, total, start, 0)
+    recv_z[col] = z_ref[...]
+    recv_g[me] = g_ref[...]
+    for k in range(1, n_cols):
+        peer = lax.rem(col + k, n_cols)
+        z_copy(peer, col).wait_send()
+        z_copy(peer, peer).wait_recv()
+    zo_ref[...] = recv_z[0]
+    for k in range(1, n_cols):
+        zo_ref[...] += recv_z[k]
+
+    def finish(k, carry):
+        peer, _ = peer_of(k)
+        g_copy(peer, me).wait_send()
+        g_copy(peer, peer).wait_recv()
+        return carry
+
+    lax.fori_loop(1, total, finish, 0)
+    go_ref[...] = recv_g[0]
+
+    def add(s, carry):
+        go_ref[...] += recv_g[s]
+        return carry
+
+    lax.fori_loop(1, total, add, 0)
+
+
+def fused_sum(z, g, cid):
+    n_rows = lax.axis_size("rows")
+    n_cols = lax.axis_size("cols")
+    total = n_rows * n_cols
+    z_tile = z.reshape(-1, z.shape[-1])
+    size = g.shape[0]
+    g_tile = jnp.pad(g, (0, 128 - size)).reshape(1, 128)
+    vmem = pl.BlockSpec(memory_space=pltpu.VMEM)
+    z_out, g_out = pl.pallas_call(
+        functools.partial(fused_kernel, n_rows, n_cols),
+        out_shape=[
+            jax.ShapeDtypeStruct(z_tile.shape, jnp.float32),
+            jax.ShapeDtypeStruct(g_tile.shape, jnp.float32),
+        ],
+        in_specs=[vmem, vmem],
+        out_specs=[vmem, vmem],
+        scratch_shapes=[
+            pltpu.VMEM((n_cols,) + z_tile.shape, jnp.float32),
+            pltpu.VMEM((total,) + g_tile.shape, jnp.float32),
+            [
+                pltpu.SemaphoreType.DMA((n_cols,)),
+                pltpu.SemaphoreType.DMA((n_cols,)),
+                pltpu.SemaphoreType.DMA((total,)),
+                pltpu.SemaphoreType.DMA((total,)),
+            ],
+        ],
+        compiler_params=pltpu.CompilerParams(collective_id=cid, has_side_effects=True),
+    )(z_tile, g_tile)
+    return z_out.reshape(z.shape), g_out.reshape(-1)[:size]
 
 
 def local(block_list, points, targets):
@@ -226,15 +332,19 @@
     direction = resid
     solution = jnp.zeros_like(resid)
     norm_now = jnp.sum(resid * resid, axis=(0, 2))
+    first_col = lax.axis_index("cols") == 0
     for iteration in range(ITERS):
         weights = (direction * inv_root).astype(jnp.bfloat16)
-        applied = REG * direction + inv_root * column_total(apply_partial(weights))
-        curvature = jnp.sum(direction * applied, axis=(0, 2))
+        z_part = apply_partial(weights)
+        own_term = jnp.where(first_col, REG * jnp.sum(direction * direction, axis=(0, 2)), 0.0)
+        curv_part = own_term + jnp.sum(direction * (inv_root * z_part), axis=(0, 2))
         if iteration == 0:
-            both = global_sum(jnp.concatenate([norm_now, curvature]))
+            norm_part = jnp.where(first_col, norm_now, 0.0)
+            z_total, both = fused_sum(z_part, jnp.concatenate([norm_part, curv_part]), 6)
             norm_now, curvature = both[:outputs], both[outputs:]
         else:
-            curvature = global_sum(curvature)
+            z_total, curvature = fused_sum(z_part, curv_part, 7)
+        applied = REG * direction + inv_root * z_total
         step_size = norm_now / curvature
         solution = solution + step_size[None, :, None] * direction
         resid = resid - step_size[None, :, None] * applied

time: 286 us -> 312 us (1.091)
  local copies, waits for them, and re-layouts: 34.6 us -> 47.9 us
  Pallas kernels: 81.2 us -> 89.8 us
    pallas_call x0 -> x2, Pallas kernels: none -> 69.9 us  [fused_sum(): pl.pallas_call(functools.partial(fused_kernel, n_rows, n_cols), out_shape...]
    pallas_call x6 -> x2, Pallas kernels: 81.2 us -> 19.9 us  [allsum(): pl.pallas_call(functools.partial(allsum_kernel, axis, n), out_shape=jax.S...]
    dynamic_update_slice x14, local copies, waits for them, and re-layouts: 0.12 us -> 8.53 us  [local(): lax.map(pair_step, (left_x.reshape(-1, chunk, coord_dim, block_len), righ...]
    broadcast_in_dim x7, local copies, waits for them, and re-layouts: 0.08 us -> 4.47 us  [pair_step(): values = jnp.where(live[:, None, None], wendland(lx, rx), 0.0)]
where the time goes in v7:
time: 312 us; the launch traced here: 311 us
  Pallas kernels  89.8 us (29%)
  waiting for transfers between devices  64 us (21%)
  matrix products  54.7 us (18%)
  local copies, waits for them, and re-layouts  47.9 us (15%)
  starting transfers between devices  33.8 us (11%)
  other arithmetic  17.5 us (6%)
  between operations  3.2 us (1%)
    pallas_call x2, Pallas kernels, fused_sum(): pl.pallas_call(functools.partial(fused_kernel, n_rows, n_cols), out_shape...  69.9 us
    all_to_all x3, waiting for transfers between devices, swap(): lax.all_to_all(parts, 'rows', split_axis=0, concat_axis=0, tiled=True)  56.4 us
    dot_general x7, matrix products, wendland(): jnp.einsum('nda,ndb->nab', left_f, right_f, precision=lax.Precision.HIGHEST)  30.2 us
    all_to_all x3, starting transfers between devices, swap(): lax.all_to_all(parts, 'rows', split_axis=0, concat_axis=0, tiled=True)  20.8 us
    pallas_call x2, Pallas kernels, allsum(): pl.pallas_call(functools.partial(allsum_kernel, axis, n), out_shape=jax.S...  19.9 us
    all_to_all x1, starting transfers between devices, local(): lax.all_to_all(request, 'rows', split_axis=0, concat_axis=0, tiled=True)  13 us
    dot_general x2, matrix products, apply_partial(): jnp.einsum('sab,sob->soa', own_k, far_w, preferred_element_type=jnp.float32)  9.96 us
    dot_general x2, matrix products, apply_partial(): jnp.einsum('eab,eoa->eob', in_k, their_w, preferred_element_type=jnp.floa...  9.92 us
  transfers between devices with their start and end apart: 4, of which 4 were waited for; matrix products, arithmetic and copies ran while one was open for 6% of the time, Pallas kernels for 0%

profile of v7, /device:TPU:1, one launch (start us, length us, event | category | flops | bytes accessed | tf_op | source)
XLA Modules:
  0.0 311.0 jit_solution(7839745303427143329)
XLA Ops:
  4.5 13.0 %all-to-all-start = ((s32[64,1,2]{2,1,0:T(1,128)}), s32[64,1,2]{2,1,0:T(1,128)S(1)}, u32[]{:S(2)}, u32[]{:S(2)}) async-start(s32[64,1,2]{2,1,0:T(1,128)} %copy.34), calls=%async_computation | async-start | bytes 65536 | tf_op jit(solution)/shard_map/all_to_all | solution.py:241
  19.0 7.7 %all-to-all-done = s32[64,1,2]{2,1,0:T(1,128)S(1)} async-done(((s32[64,1,2]{2,1,0:T(1,128)}), s32[64,1,2]{2,1,0:T(1,128)S(1)}, u32[]{:S(2)}, u32[]{:S(2)}) %all-to-all-start) | async-done | bytes 544 | tf_op jit(solution)/shard_map/all_to_all | solution.py:241
  28.5 4.7 %all-to-all-start.1 = ((bf16[64,16,256]{2,1,0:T(8,128)(2,1)}), bf16[64,16,256]{2,1,0:T(8,128)(2,1)S(1)}, u32[]{:S(2)}, u32[]{:S(2)}) async-start(bf16[64,16,256]{2,1,0:T(8,128)(2,1)} %select_select_fusion.2), calls=%async_computation.1 | async-start | bytes 1048576 | tf_op jit(solution)/shard_map/all_to_all | solution.py:253
  37.4 13.2 %all-to-all-done.1 = bf16[64,16,256]{2,1,0:T(8,128)(2,1)S(1)} async-done(((bf16[64,16,256]{2,1,0:T(8,128)(2,1)}), bf16[64,16,256]{2,1,0:T(8,128)(2,1)S(1)}, u32[]{:S(2)}, u32[]{:S(2)}) %all-to-all-start.1) | async-done | bytes 524320 | tf_op jit(solution)/shard_map/all_to_all | solution.py:253
  51.7 48.6 %while.16 = (s32[]{:T(128)}, bf16[7,16,256,256]{3,2,1,0:T(8,128)(2,1)}, f32[7,16,256]{2,1,0:T(8,128)}, f32[7,16,256]{2,1,0:T(8,128)}, pred[7,16]{1,0:T(8,128)(4,...) while((s32[]{:T(128)}, ...), condition=%wide.region_7.8_spmd, body=%wide.region_2.7_spmd.sunk | while | flops 50708480 | bytes 11177085 | solution.py:306
  52.5 4.4 %bitcast_dynamic-update-slice_fusion.6 = (bf16[7,16,256,256]{3,2,1,0:T(8,128)(2,1)}, f32[16,256,256]{2,1,0:T(8,128)S(1)}) fusion(bf16[7,16,256,256]{3,2,1,0:T(8,128)(2,1)} %get-tuple-element.212, s32[]{:T(128)} %get-tuple-element.211, bf16[7,16,16,256]{3,2,1,0:T(8,128)(2,1)S(1)} %get-tuple-element.225, ...), kind=kOutput, calls=%fused_computation.13.clone.1 | convolution fusion | flops 48234496 | bytes 6588416 | tf_op jit(solution)/shard_map/while/body/eval_jaxpr/nda,ndb->nab/dot_general | solution.py:24
  59.5 4.3 %bitcast_dynamic-update-slice_fusion.6 = (bf16[7,16,256,256]{3,2,1,0:T(8,128)(2,1)}, f32[16,256,256]{2,1,0:T(8,128)S(1)}) fusion(bf16[7,16,256,256]{3,2,1,0:T(8,128)(2,1)} %get-tuple-element.212, s32[]{:T(128)} %get-tuple-element.211, bf16[7,16,16,256]{3,2,1,0:T(8,128)(2,1)S(1)} %get-tuple-element.225, ...), kind=kOutput, calls=%fused_computation.13.clone.1 | convolution fusion | flops 48234496 | bytes 6588416 | tf_op jit(solution)/shard_map/while/body/eval_jaxpr/nda,ndb->nab/dot_general | solution.py:24
  66.4 4.3 %bitcast_dynamic-update-slice_fusion.6 = (bf16[7,16,256,256]{3,2,1,0:T(8,128)(2,1)}, f32[16,256,256]{2,1,0:T(8,128)S(1)}) fusion(bf16[7,16,256,256]{3,2,1,0:T(8,128)(2,1)} %get-tuple-element.212, s32[]{:T(128)} %get-tuple-element.211, bf16[7,16,16,256]{3,2,1,0:T(8,128)(2,1)S(1)} %get-tuple-element.225, ...), kind=kOutput, calls=%fused_computation.13.clone.1 | convolution fusion | flops 48234496 | bytes 6588416 | tf_op jit(solution)/shard_map/while/body/eval_jaxpr/nda,ndb->nab/dot_general | solution.py:24
  73.4 4.3 %bitcast_dynamic-update-slice_fusion.6 = (bf16[7,16,256,256]{3,2,1,0:T(8,128)(2,1)}, f32[16,256,256]{2,1,0:T(8,128)S(1)}) fusion(bf16[7,16,256,256]{3,2,1,0:T(8,128)(2,1)} %get-tuple-element.212, s32[]{:T(128)} %get-tuple-element.211, bf16[7,16,16,256]{3,2,1,0:T(8,128)(2,1)S(1)} %get-tuple-element.225, ...), kind=kOutput, calls=%fused_computation.13.clone.1 | convolution fusion | flops 48234496 | bytes 6588416 | tf_op jit(solution)/shard_map/while/body/eval_jaxpr/nda,ndb->nab/dot_general | solution.py:24
  87.3 4.3 %bitcast_dynamic-update-slice_fusion.6 = (bf16[7,16,256,256]{3,2,1,0:T(8,128)(2,1)}, f32[16,256,256]{2,1,0:T(8,128)S(1)}) fusion(bf16[7,16,256,256]{3,2,1,0:T(8,128)(2,1)} %get-tuple-element.212, s32[]{:T(128)} %get-tuple-element.211, bf16[7,16,16,256]{3,2,1,0:T(8,128)(2,1)S(1)} %get-tuple-element.225, ...), kind=kOutput, calls=%fused_computation.13.clone.1 | convolution fusion | flops 48234496 | bytes 6588416 | tf_op jit(solution)/shard_map/while/body/eval_jaxpr/nda,ndb->nab/dot_general | solution.py:24
  102.8 6.4 %shard_map.50 = f32[16,128]{1,0:T(8,128)} custom-call(f32[16,128]{1,0:T(8,128)} %reshape_reshape_broadcast_in_dim.3.x_ref), custom_call_target="tpu_custom_call" | custom-call | tf_op jit(solution)/shard_map/pallas_call | solution.py:99
  112.7 7.5 %all-to-all-start.2 = ((bf16[64,32,256]{2,1,0:T(8,128)(2,1)}), bf16[64,32,256]{2,1,0:T(8,128)(2,1)S(1)}, u32[]{:S(2)}, u32[]{:S(2)}) async-start(bf16[64,32,256]{2,1,0:T(8,128)(2,1)} %select_select_fusion.1), calls=%async_computation.2 | async-start | bytes 2097152 | tf_op jit(solution)/shard_map/all_to_all | solution.py:253
  120.3 7.7 %slice.56 = bf16[4,16,256,256]{3,2,1,0:T(8,128)(2,1)} slice(bf16[7,16,256,256]{3,2,1,0:T(8,128)(2,1)} %get-tuple-element.99), slice={[3:7], [0:16], [0:256], [0:256]} | slice | bytes 16777216 | tf_op jit(solution)/shard_map/slice | solution.py:318
  127.9 6.2 %slice.54 = bf16[3,16,256,256]{3,2,1,0:T(8,128)(2,1)} slice(bf16[7,16,256,256]{3,2,1,0:T(8,128)(2,1)} %get-tuple-element.99), slice={[0:3], [0:16], [0:256], [0:256]} | slice | bytes 12582912 | tf_op jit(solution)/shard_map/slice | solution.py:317
  134.1 14.7 %all-to-all-done.2 = bf16[64,32,256]{2,1,0:T(8,128)(2,1)S(1)} async-done(((bf16[64,32,256]{2,1,0:T(8,128)(2,1)}), bf16[64,32,256]{2,1,0:T(8,128)(2,1)S(1)}, u32[]{:S(2)}, u32[]{:S(2)}) %all-to-all-start.2) | async-done | bytes 1048608 | tf_op jit(solution)/shard_map/all_to_all | solution.py:253
  150.6 5.0 %fusion.25 = f32[48,32,256]{2,1,0:T(8,128)S(1)} fusion(bf16[48,256,256]{2,1,0:T(8,128)(2,1)} %bitcast.195, bf16[48,32,256]{2,1,0:T(8,128)(2,1)} %gather_fusion.6, pred[48]{0:T(512)(128)(4,1)S(1)} %copy-done.14), kind=kOutput, calls=%fused_computation.47 | convolution fusion | flops 201719808 | bytes 8650800 | tf_op jit(solution)/shard_map/sab,sob->soa/dot_general | solution.py:326
  155.7 4.9 %fusion.19 = f32[64,32,256]{2,1,0:T(8,128)S(1)} fusion(bf16[64,256,256]{2,1,0:T(8,128)(2,1)} %bitcast.193, bf16[64,32,256]{2,1,0:T(8,128)(2,1)S(1)} %all-to-all-done.2, pred[64]{0:T(512)(128)(4,1)S(1)} %get-tuple-element.146), kind=kOutput, calls=%fused_computation.36 | convolution fusion | flops 268959744 | bytes 11534400 | tf_op jit(solution)/shard_map/eab,eoa->eob/dot_general | solution.py:328
  164.3 34.9 %shard_map.51 = (f32[256,256]{1,0:T(8,128)}, f32[1,128]{1,0:T(1,128)}) custom-call(f32[256,256]{1,0:T(8,128)} %bitcast.209, f32[1,128]{1,0:T(1,128)} %fusion.62.g_ref), custom_call_target="tpu_custom_call" | custom-call | tf_op jit(solution)/shard_map/pallas_call | solution.py:197
  202.0 13.5 %shard_map.52 = f32[1,128]{1,0:T(1,128)} custom-call(f32[1,128]{1,0:T(1,128)} %pad_bitcast_fusion.1.x_ref), custom_call_target="tpu_custom_call" | custom-call | tf_op jit(solution)/shard_map/pallas_call | solution.py:99
  220.0 8.5 %all-to-all-start.3 = ((bf16[64,32,256]{2,1,0:T(8,128)(2,1)}), bf16[64,32,256]{2,1,0:T(8,128)(2,1)S(1)}, u32[]{:S(2)}, u32[]{:S(2)}) async-start(bf16[64,32,256]{2,1,0:T(8,128)(2,1)} %select_select_fusion), calls=%async_computation.3 | async-start | bytes 2097152 | tf_op jit(solution)/shard_map/all_to_all | solution.py:253
  228.7 28.5 %all-to-all-done.3 = bf16[64,32,256]{2,1,0:T(8,128)(2,1)S(1)} async-done(((bf16[64,32,256]{2,1,0:T(8,128)(2,1)}), bf16[64,32,256]{2,1,0:T(8,128)(2,1)S(1)}, u32[]{:S(2)}, u32[]{:S(2)}) %all-to-all-start.3) | async-done | bytes 1048608 | tf_op jit(solution)/shard_map/all_to_all | solution.py:253
  258.9 5.0 %fusion.23 = f32[48,32,256]{2,1,0:T(8,128)S(1)} fusion(bf16[48,256,256]{2,1,0:T(8,128)(2,1)} %bitcast.196, bf16[48,32,256]{2,1,0:T(8,128)(2,1)} %gather_fusion.9, pred[48]{0:T(512)(128)(4,1)S(1)} %copy-done.14), kind=kOutput, calls=%fused_computation.45 | convolution fusion | flops 201719808 | bytes 8650800 | tf_op jit(solution)/shard_map/sab,sob->soa/dot_general | solution.py:326
  264.1 5.0 %fusion.17 = f32[64,32,256]{2,1,0:T(8,128)S(1)} fusion(bf16[64,256,256]{2,1,0:T(8,128)(2,1)} %bitcast.194, bf16[64,32,256]{2,1,0:T(8,128)(2,1)S(1)} %all-to-all-done.3, pred[64]{0:T(512)(128)(4,1)S(1)} %get-tuple-element.146), kind=kOutput, calls=%fused_computation.33 | convolution fusion | flops 268959744 | bytes 11534400 | tf_op jit(solution)/shard_map/eab,eoa->eob/dot_general | solution.py:328
  272.6 34.9 %shard_map.53 = (f32[256,256]{1,0:T(8,128)}, f32[1,128]{1,0:T(1,128)}) custom-call(f32[256,256]{1,0:T(8,128)} %bitcast.210, f32[1,128]{1,0:T(1,128)} %pad_bitcast_fusion.g_ref), custom_call_target="tpu_custom_call" | custom-call | tf_op jit(solution)/shard_map/pallas_call | solution.py:197
  (155 shorter events, 64.8 us)
Async XLA Ops:
  0.6 32.6 %copy-start.2 = (bf16[16,2048]{1,0:T(8,128)(2,1)S(1)}, bf16[16,2048]{1,0:T(8,128)(2,1)}, u32[]{:S(2)}) copy-start(bf16[16,2048]{1,0:T(8,128)(2,1)} %param.6) | copy-start | bytes 196612
  0.6 33.3 %copy-start.1 = (f32[32,2048]{1,0:T(8,128)S(1)}, f32[32,2048]{1,0:T(8,128)}, u32[]{:S(2)}) copy-start(f32[32,2048]{1,0:T(8,128)} %param.7) | copy-start | bytes 786436
  4.5 22.2 %all-to-all-start = ((s32[64,1,2]{2,1,0:T(1,128)}), s32[64,1,2]{2,1,0:T(1,128)S(1)}, u32[]{:S(2)}, u32[]{:S(2)}) async-start(s32[64,1,2]{2,1,0:T(1,128)} %copy.34), calls=%async_computation | async-start | bytes 65536 | tf_op jit(solution)/shard_map/all_to_all | solution.py:241
  17.5 16.4 %copy-start.5 = (pred[64]{0:T(512)(128)(4,1)}, pred[64]{0:T(512)(128)(4,1)S(1)}, u32[]{:S(2)}) copy-start(pred[64]{0:T(512)(128)(4,1)S(1)} %broadcast_compare_fusion) | copy-start | bytes 196
  17.5 16.4 %copy-start.7 = (pred[64]{0:T(512)(128)(4,1)}, pred[64]{0:T(512)(128)(4,1)S(1)}, u32[]{:S(2)}) copy-start(pred[64]{0:T(512)(128)(4,1)S(1)} %iota_compare_fusion.1) | copy-start | bytes 196
  26.8 7.2 %copy-start.9 = (pred[64]{0:T(512)(128)(4,1)}, pred[64]{0:T(512)(128)(4,1)S(1)}, u32[]{:S(2)}) copy-start(pred[64]{0:T(512)(128)(4,1)S(1)} %compare_bitcast_fusion) | copy-start | bytes 196
  26.8 9.9 %copy-start.3 = (s32[1024]{0:T(1024)}, s32[1024]{0:T(1024)S(1)}, u32[]{:S(2)}) copy-start(s32[1024]{0:T(1024)S(1)} %pad_clamp_fusion.1) | copy-start | bytes 12292
  28.5 22.1 %all-to-all-start.1 = ((bf16[64,16,256]{2,1,0:T(8,128)(2,1)}), bf16[64,16,256]{2,1,0:T(8,128)(2,1)S(1)}, u32[]{:S(2)}, u32[]{:S(2)}) async-start(bf16[64,16,256]{2,1,0:T(8,128)(2,1)} %select_select_fusion.2), calls=%async_computation.1 | async-start | bytes 1048576 | tf_op jit(solution)/shard_map/all_to_all | solution.py:253
  34.1 16.8 %copy-start.11 = (pred[64]{0:T(512)(128)(4,1)}, pred[64]{0:T(512)(128)(4,1)S(1)}, u32[]{:S(2)}) copy-start(pred[64]{0:T(512)(128)(4,1)S(1)} %get-tuple-element.147) | copy-start | bytes 196
  34.1 16.8 %copy-start.4 = (s32[1024]{0:T(1024)}, s32[1024]{0:T(1024)S(1)}, u32[]{:S(2)}) copy-start(s32[1024]{0:T(1024)S(1)} %pad_clamp_fusion) | copy-start | bytes 12292
  34.1 17.5 %copy-start.13 = (pred[48]{0:T(512)(128)(4,1)}, pred[48]{0:T(512)(128)(4,1)S(1)}, u32[]{:S(2)}) copy-start(pred[48]{0:T(512)(128)(4,1)S(1)} %broadcast_compare_fusion.1) | copy-start | bytes 148
  100.4 11.0 %copy-start.6 = (pred[64]{0:T(512)(128)(4,1)S(1)}, pred[64]{0:T(512)(128)(4,1)}, u32[]{:S(2)}) copy-start(pred[64]{0:T(512)(128)(4,1)} %copy-done.5) | copy-start | bytes 196
  100.4 11.0 %copy-start.8 = (pred[64]{0:T(512)(128)(4,1)S(1)}, pred[64]{0:T(512)(128)(4,1)}, u32[]{:S(2)}) copy-start(pred[64]{0:T(512)(128)(4,1)} %copy-done.7) | copy-start | bytes 196
  100.4 11.0 %copy-start.10 = (pred[64]{0:T(512)(128)(4,1)S(1)}, pred[64]{0:T(512)(128)(4,1)}, u32[]{:S(2)}) copy-start(pred[64]{0:T(512)(128)(4,1)} %copy-done.9) | copy-start | bytes 196
  112.7 36.1 %all-to-all-start.2 = ((bf16[64,32,256]{2,1,0:T(8,128)(2,1)}), bf16[64,32,256]{2,1,0:T(8,128)(2,1)S(1)}, u32[]{:S(2)}, u32[]{:S(2)}) async-start(bf16[64,32,256]{2,1,0:T(8,128)(2,1)} %select_select_fusion.1), calls=%async_computation.2 | async-start | bytes 2097152 | tf_op jit(solution)/shard_map/all_to_all | solution.py:253
  127.9 20.9 %copy-start.12 = (pred[64]{0:T(512)(128)(4,1)S(1)}, pred[64]{0:T(512)(128)(4,1)}, u32[]{:S(2)}) copy-start(pred[64]{0:T(512)(128)(4,1)} %copy-done.11) | copy-start | bytes 196
  127.9 22.7 %copy-start.14 = (pred[48]{0:T(512)(128)(4,1)S(1)}, pred[48]{0:T(512)(128)(4,1)}, u32[]{:S(2)}) copy-start(pred[48]{0:T(512)(128)(4,1)} %copy-done.13) | copy-start | bytes 148
  220.0 37.1 %all-to-all-start.3 = ((bf16[64,32,256]{2,1,0:T(8,128)(2,1)}), bf16[64,32,256]{2,1,0:T(8,128)(2,1)S(1)}, u32[]{:S(2)}, u32[]{:S(2)}) async-start(bf16[64,32,256]{2,1,0:T(8,128)(2,1)} %select_select_fusion), calls=%async_computation.3 | async-start | bytes 2097152 | tf_op jit(solution)/shard_map/all_to_all | solution.py:253
  264.1 43.5 %copy-start.15 = (f32[1,128]{1,0:T(1,128)S(1)}, f32[1,128]{1,0:T(1,128)}, u32[]{:S(2)}) copy-start(f32[1,128]{1,0:T(1,128)} %shard_map.52) | copy-start | bytes 1540
  264.1 44.1 %copy-start = (f32[256,256]{1,0:T(8,128)S(1)}, f32[256,256]{1,0:T(8,128)}, u32[]{:S(2)}) copy-start(f32[256,256]{1,0:T(8,128)} %get-tuple-element.101) | copy-start | bytes 786436

commit v8 on v7

--- a/solution.py
+++ b/solution.py
@@ -111,32 +111,31 @@
     return out.reshape(-1)[:size].reshape(shape)
 
 
-def fused_kernel(n_rows, n_cols, z_ref, g_ref, zo_ref, go_ref, recv_z, recv_g, sems):
+def fused_kernel(n_rows, n_cols, z_ref, g_ref, zo_ref, go_ref, recv_z, recv_g, recv_s, rows_sum, sems):
     row = lax.axis_index("rows")
     col = lax.axis_index("cols")
-    total = n_rows * n_cols
-    me = row * n_cols + col
     barrier = pltpu.get_barrier_semaphore()
 
-    def peer_of(k):
-        peer = lax.rem(me + k, total)
-        return peer, (peer // n_cols, lax.rem(peer, n_cols))
-
     def greet(k, carry):
-        _, device = peer_of(k)
-        pl.semaphore_signal(barrier, inc=1, device_id=device, device_id_type=MESH)
-        return carry
-
-    lax.fori_loop(1, total, greet, 0)
-    pl.semaphore_wait(barrier, total - 1)
-    z_send, z_recv, g_send, g_recv = sems
-
-    def z_copy(peer, slot):
+        pl.semaphore_signal(
+            barrier, inc=1, device_id={"rows": lax.rem(row + k, n_rows)}, device_id_type=MESH
+        )
+        return carry
+
+    lax.fori_loop(1, n_rows, greet, 0)
+    for k in range(1, n_cols):
+        pl.semaphore_signal(
+            barrier, inc=1, device_id={"cols": lax.rem(col + k, n_cols)}, device_id_type=MESH
+        )
+    pl.semaphore_wait(barrier, n_rows - 1 + n_cols - 1)
+    z_send, z_recv, g_send, g_recv, s_send, s_recv = sems
+
+    def col_copy(src, dst, send, recv, peer, slot):
         return pltpu.make_async_remote_copy(
-            src_ref=z_ref,
-            dst_ref=recv_z.at[slot],
-            send_sem=z_send.at[peer],
-            recv_sem=z_recv.at[slot],
+            src_ref=src,
+            dst_ref=dst.at[slot],
+            send_sem=send.at[peer],
+            recv_sem=recv.at[slot],
             device_id={"cols": peer},
             device_id_type=MESH,
         )
@@ -147,49 +146,57 @@
             dst_ref=recv_g.at[slot],
             send_sem=g_send.at[peer],
             recv_sem=g_recv.at[slot],
-            device_id=(peer // n_cols, lax.rem(peer, n_cols)),
+            device_id={"rows": peer},
             device_id_type=MESH,
         )
 
     for k in range(1, n_cols):
-        z_copy(lax.rem(col + k, n_cols), col).start()
+        col_copy(z_ref, recv_z, z_send, z_recv, lax.rem(col + k, n_cols), col).start()
 
     def start(k, carry):
-        peer, _ = peer_of(k)
-        g_copy(peer, me).start()
-        return carry
-
-    lax.fori_loop(1, total, start, 0)
+        g_copy(lax.rem(row + k, n_rows), row).start()
+        return carry
+
+    lax.fori_loop(1, n_rows, start, 0)
     recv_z[col] = z_ref[...]
-    recv_g[me] = g_ref[...]
+    recv_g[row] = g_ref[...]
+
+    def finish(k, carry):
+        peer = lax.rem(row + k, n_rows)
+        g_copy(peer, row).wait_send()
+        g_copy(peer, peer).wait_recv()
+        return carry
+
+    lax.fori_loop(1, n_rows, finish, 0)
+    rows_sum[...] = recv_g[0]
+
+    def add(s, carry):
+        rows_sum[...] += recv_g[s]
+        return carry
+
+    lax.fori_loop(1, n_rows, add, 0)
+    for k in range(1, n_cols):
+        col_copy(rows_sum, recv_s, s_send, s_recv, lax.rem(col + k, n_cols), col).start()
+    recv_s[col] = rows_sum[...]
     for k in range(1, n_cols):
         peer = lax.rem(col + k, n_cols)
-        z_copy(peer, col).wait_send()
-        z_copy(peer, peer).wait_recv()
+        col_copy(z_ref, recv_z, z_send, z_recv, peer, col).wait_send()
+        col_copy(z_ref, recv_z, z_send, z_recv, peer, peer).wait_recv()
     zo_ref[...] = recv_z[0]
     for k in range(1, n_cols):
         zo_ref[...] += recv_z[k]
-
-    def finish(k, carry):
-        peer, _ = peer_of(k)
-        g_copy(peer, me).wait_send()
-        g_copy(peer, peer).wait_recv()
-        return carry
-
-    lax.fori_loop(1, total, finish, 0)
-    go_ref[...] = recv_g[0]
-
-    def add(s, carry):
-        go_ref[...] += recv_g[s]
-        return carry
-
-    lax.fori_loop(1, total, add, 0)
+    for k in range(1, n_cols):
+        peer = lax.rem(col + k, n_cols)
+        col_copy(rows_sum, recv_s, s_send, s_recv, peer, col).wait_send()
+        col_copy(rows_sum, recv_s, s_send, s_recv, peer, peer).wait_recv()
+    go_ref[...] = recv_s[0]
+    for k in range(1, n_cols):
+        go_ref[...] += recv_s[k]
 
 
 def fused_sum(z, g, cid):
     n_rows = lax.axis_size("rows")
     n_cols = lax.axis_size("cols")
-    total = n_rows * n_cols
     z_tile = z.reshape(-1, z.shape[-1])
     size = g.shape[0]
     g_tile = jnp.pad(g, (0, 128 - size)).reshape(1, 128)
@@ -204,12 +211,16 @@
         out_specs=[vmem, vmem],
         scratch_shapes=[
             pltpu.VMEM((n_cols,) + z_tile.shape, jnp.float32),
-            pltpu.VMEM((total,) + g_tile.shape, jnp.float32),
+            pltpu.VMEM((n_rows,) + g_tile.shape, jnp.float32),
+            pltpu.VMEM((n_cols,) + g_tile.shape, jnp.float32),
+            pltpu.VMEM(g_tile.shape, jnp.float32),
             [
                 pltpu.SemaphoreType.DMA((n_cols,)),
                 pltpu.SemaphoreType.DMA((n_cols,)),
-                pltpu.SemaphoreType.DMA((total,)),
-                pltpu.SemaphoreType.DMA((total,)),
+                pltpu.SemaphoreType.DMA((n_rows,)),
+                pltpu.SemaphoreType.DMA((n_rows,)),
+                pltpu.SemaphoreType.DMA((n_cols,)),
+                pltpu.SemaphoreType.DMA((n_cols,)),
             ],
         ],
         compiler_params=pltpu.CompilerParams(collective_id=cid, has_side_effects=True),

time: 312 us -> 283 us (0.907)
  Pallas kernels: 89.8 us -> 61.5 us
    pallas_call x2, Pallas kernels: 69.9 us -> 41.4 us  [fused_sum(): pl.pallas_call(functools.partial(fused_kernel, n_rows, n_cols), out_shape...]
where the time goes in v8:
time: 283 us; the launch traced here: 282 us
  waiting for transfers between devices  64 us (23%)
  Pallas kernels  61.5 us (22%)
  matrix products  54.7 us (19%)
  local copies, waits for them, and re-layouts  47.9 us (17%)
  starting transfers between devices  33.4 us (12%)
  other arithmetic  17.5 us (6%)
  between operations  3.2 us (1%)
    all_to_all x3, waiting for transfers between devices, swap(): lax.all_to_all(parts, 'rows', split_axis=0, concat_axis=0, tiled=True)  56.4 us
    pallas_call x2, Pallas kernels, fused_sum(): pl.pallas_call(functools.partial(fused_kernel, n_rows, n_cols), out_shape...  41.4 us
    dot_general x7, matrix products, wendland(): jnp.einsum('nda,ndb->nab', left_f, right_f, precision=lax.Precision.HIGHEST)  30.2 us
    all_to_all x3, starting transfers between devices, swap(): lax.all_to_all(parts, 'rows', split_axis=0, concat_axis=0, tiled=True)  20.4 us
    pallas_call x2, Pallas kernels, allsum(): pl.pallas_call(functools.partial(allsum_kernel, axis, n), out_shape=jax.S...  20.1 us
    all_to_all x1, starting transfers between devices, local(): lax.all_to_all(request, 'rows', split_axis=0, concat_axis=0, tiled=True)  13 us
    dot_general x2, matrix products, apply_partial(): jnp.einsum('sab,sob->soa', own_k, far_w, preferred_element_type=jnp.float32)  9.96 us
    dot_general x2, matrix products, apply_partial(): jnp.einsum('eab,eoa->eob', in_k, their_w, preferred_element_type=jnp.floa...  9.92 us
  transfers between devices with their start and end apart: 4, of which 4 were waited for; matrix products, arithmetic and copies ran while one was open for 6% of the time, Pallas kernels for 0%

profile of v8, /device:TPU:1, one launch (start us, length us, event | category | flops | bytes accessed | tf_op | source)
XLA Modules:
  0.0 282.3 jit_solution(1065155577784515120)
XLA Ops:
  4.5 13.0 %all-to-all-start = ((s32[64,1,2]{2,1,0:T(1,128)}), s32[64,1,2]{2,1,0:T(1,128)S(1)}, u32[]{:S(2)}, u32[]{:S(2)}) async-start(s32[64,1,2]{2,1,0:T(1,128)} %copy.34), calls=%async_computation | async-start | bytes 65536 | tf_op jit(solution)/shard_map/all_to_all | solution.py:252
  19.0 7.7 %all-to-all-done = s32[64,1,2]{2,1,0:T(1,128)S(1)} async-done(((s32[64,1,2]{2,1,0:T(1,128)}), s32[64,1,2]{2,1,0:T(1,128)S(1)}, u32[]{:S(2)}, u32[]{:S(2)}) %all-to-all-start) | async-done | bytes 544 | tf_op jit(solution)/shard_map/all_to_all | solution.py:252
  28.5 4.7 %all-to-all-start.1 = ((bf16[64,16,256]{2,1,0:T(8,128)(2,1)}), bf16[64,16,256]{2,1,0:T(8,128)(2,1)S(1)}, u32[]{:S(2)}, u32[]{:S(2)}) async-start(bf16[64,16,256]{2,1,0:T(8,128)(2,1)} %select_select_fusion.2), calls=%async_computation.1 | async-start | bytes 1048576 | tf_op jit(solution)/shard_map/all_to_all | solution.py:264
  37.4 13.2 %all-to-all-done.1 = bf16[64,16,256]{2,1,0:T(8,128)(2,1)S(1)} async-done(((bf16[64,16,256]{2,1,0:T(8,128)(2,1)}), bf16[64,16,256]{2,1,0:T(8,128)(2,1)S(1)}, u32[]{:S(2)}, u32[]{:S(2)}) %all-to-all-start.1) | async-done | bytes 524320 | tf_op jit(solution)/shard_map/all_to_all | solution.py:264
  51.7 48.6 %while.16 = (s32[]{:T(128)}, bf16[7,16,256,256]{3,2,1,0:T(8,128)(2,1)}, f32[7,16,256]{2,1,0:T(8,128)}, f32[7,16,256]{2,1,0:T(8,128)}, pred[7,16]{1,0:T(8,128)(4,...) while((s32[]{:T(128)}, ...), condition=%wide.region_7.8_spmd, body=%wide.region_2.7_spmd.sunk | while | flops 50708480 | bytes 11177085 | solution.py:317
  52.5 4.4 %bitcast_dynamic-update-slice_fusion.6 = (bf16[7,16,256,256]{3,2,1,0:T(8,128)(2,1)}, f32[16,256,256]{2,1,0:T(8,128)S(1)}) fusion(bf16[7,16,256,256]{3,2,1,0:T(8,128)(2,1)} %get-tuple-element.212, s32[]{:T(128)} %get-tuple-element.211, bf16[7,16,16,256]{3,2,1,0:T(8,128)(2,1)S(1)} %get-tuple-element.225, ...), kind=kOutput, calls=%fused_computation.13.clone.1 | convolution fusion | flops 48234496 | bytes 6588416 | tf_op jit(solution)/shard_map/while/body/eval_jaxpr/nda,ndb->nab/dot_general | solution.py:24
  59.5 4.3 %bitcast_dynamic-update-slice_fusion.6 = (bf16[7,16,256,256]{3,2,1,0:T(8,128)(2,1)}, f32[16,256,256]{2,1,0:T(8,128)S(1)}) fusion(bf16[7,16,256,256]{3,2,1,0:T(8,128)(2,1)} %get-tuple-element.212, s32[]{:T(128)} %get-tuple-element.211, bf16[7,16,16,256]{3,2,1,0:T(8,128)(2,1)S(1)} %get-tuple-element.225, ...), kind=kOutput, calls=%fused_computation.13.clone.1 | convolution fusion | flops 48234496 | bytes 6588416 | tf_op jit(solution)/shard_map/while/body/eval_jaxpr/nda,ndb->nab/dot_general | solution.py:24
  66.4 4.3 %bitcast_dynamic-update-slice_fusion.6 = (bf16[7,16,256,256]{3,2,1,0:T(8,128)(2,1)}, f32[16,256,256]{2,1,0:T(8,128)S(1)}) fusion(bf16[7,16,256,256]{3,2,1,0:T(8,128)(2,1)} %get-tuple-element.212, s32[]{:T(128)} %get-tuple-element.211, bf16[7,16,16,256]{3,2,1,0:T(8,128)(2,1)S(1)} %get-tuple-element.225, ...), kind=kOutput, calls=%fused_computation.13.clone.1 | convolution fusion | flops 48234496 | bytes 6588416 | tf_op jit(solution)/shard_map/while/body/eval_jaxpr/nda,ndb->nab/dot_general | solution.py:24
  73.4 4.3 %bitcast_dynamic-update-slice_fusion.6 = (bf16[7,16,256,256]{3,2,1,0:T(8,128)(2,1)}, f32[16,256,256]{2,1,0:T(8,128)S(1)}) fusion(bf16[7,16,256,256]{3,2,1,0:T(8,128)(2,1)} %get-tuple-element.212, s32[]{:T(128)} %get-tuple-element.211, bf16[7,16,16,256]{3,2,1,0:T(8,128)(2,1)S(1)} %get-tuple-element.225, ...), kind=kOutput, calls=%fused_computation.13.clone.1 | convolution fusion | flops 48234496 | bytes 6588416 | tf_op jit(solution)/shard_map/while/body/eval_jaxpr/nda,ndb->nab/dot_general | solution.py:24
  87.3 4.3 %bitcast_dynamic-update-slice_fusion.6 = (bf16[7,16,256,256]{3,2,1,0:T(8,128)(2,1)}, f32[16,256,256]{2,1,0:T(8,128)S(1)}) fusion(bf16[7,16,256,256]{3,2,1,0:T(8,128)(2,1)} %get-tuple-element.212, s32[]{:T(128)} %get-tuple-element.211, bf16[7,16,16,256]{3,2,1,0:T(8,128)(2,1)S(1)} %get-tuple-element.225, ...), kind=kOutput, calls=%fused_computation.13.clone.1 | convolution fusion | flops 48234496 | bytes 6588416 | tf_op jit(solution)/shard_map/while/body/eval_jaxpr/nda,ndb->nab/dot_general | solution.py:24
  102.8 6.4 %shard_map.50 = f32[16,128]{1,0:T(8,128)} custom-call(f32[16,128]{1,0:T(8,128)} %reshape_reshape_broadcast_in_dim.3.x_ref), custom_call_target="tpu_custom_call" | custom-call | tf_op jit(solution)/shard_map/pallas_call | solution.py:99
  112.7 7.5 %all-to-all-start.2 = ((bf16[64,32,256]{2,1,0:T(8,128)(2,1)}), bf16[64,32,256]{2,1,0:T(8,128)(2,1)S(1)}, u32[]{:S(2)}, u32[]{:S(2)}) async-start(bf16[64,32,256]{2,1,0:T(8,128)(2,1)} %select_select_fusion.1), calls=%async_computation.2 | async-start | bytes 2097152 | tf_op jit(solution)/shard_map/all_to_all | solution.py:264
  120.3 7.7 %slice.56 = bf16[4,16,256,256]{3,2,1,0:T(8,128)(2,1)} slice(bf16[7,16,256,256]{3,2,1,0:T(8,128)(2,1)} %get-tuple-element.99), slice={[3:7], [0:16], [0:256], [0:256]} | slice | bytes 16777216 | tf_op jit(solution)/shard_map/slice | solution.py:329
  127.9 6.2 %slice.54 = bf16[3,16,256,256]{3,2,1,0:T(8,128)(2,1)} slice(bf16[7,16,256,256]{3,2,1,0:T(8,128)(2,1)} %get-tuple-element.99), slice={[0:3], [0:16], [0:256], [0:256]} | slice | bytes 12582912 | tf_op jit(solution)/shard_map/slice | solution.py:328
  134.1 14.7 %all-to-all-done.2 = bf16[64,32,256]{2,1,0:T(8,128)(2,1)S(1)} async-done(((bf16[64,32,256]{2,1,0:T(8,128)(2,1)}), bf16[64,32,256]{2,1,0:T(8,128)(2,1)S(1)}, u32[]{:S(2)}, u32[]{:S(2)}) %all-to-all-start.2) | async-done | bytes 1048608 | tf_op jit(solution)/shard_map/all_to_all | solution.py:264
  150.6 5.0 %fusion.25 = f32[48,32,256]{2,1,0:T(8,128)S(1)} fusion(bf16[48,256,256]{2,1,0:T(8,128)(2,1)} %bitcast.195, bf16[48,32,256]{2,1,0:T(8,128)(2,1)} %gather_fusion.6, pred[48]{0:T(512)(128)(4,1)S(1)} %copy-done.14), kind=kOutput, calls=%fused_computation.47 | convolution fusion | flops 201719808 | bytes 8650800 | tf_op jit(solution)/shard_map/sab,sob->soa/dot_general | solution.py:337
  155.7 4.9 %fusion.19 = f32[64,32,256]{2,1,0:T(8,128)S(1)} fusion(bf16[64,256,256]{2,1,0:T(8,128)(2,1)} %bitcast.193, bf16[64,32,256]{2,1,0:T(8,128)(2,1)S(1)} %all-to-all-done.2, pred[64]{0:T(512)(128)(4,1)S(1)} %get-tuple-element.146), kind=kOutput, calls=%fused_computation.36 | convolution fusion | flops 268959744 | bytes 11534400 | tf_op jit(solution)/shard_map/eab,eoa->eob/dot_general | solution.py:339
  164.3 21.2 %shard_map.51 = (f32[256,256]{1,0:T(8,128)}, f32[1,128]{1,0:T(1,128)}) custom-call(f32[256,256]{1,0:T(8,128)} %bitcast.209, f32[1,128]{1,0:T(1,128)} %fusion.62.g_ref), custom_call_target="tpu_custom_call" | custom-call | tf_op jit(solution)/shard_map/pallas_call | solution.py:204
  188.3 13.7 %shard_map.52 = f32[1,128]{1,0:T(1,128)} custom-call(f32[1,128]{1,0:T(1,128)} %pad_bitcast_fusion.1.x_ref), custom_call_target="tpu_custom_call" | custom-call | tf_op jit(solution)/shard_map/pallas_call | solution.py:99
  206.5 8.2 %all-to-all-start.3 = ((bf16[64,32,256]{2,1,0:T(8,128)(2,1)}), bf16[64,32,256]{2,1,0:T(8,128)(2,1)S(1)}, u32[]{:S(2)}, u32[]{:S(2)}) async-start(bf16[64,32,256]{2,1,0:T(8,128)(2,1)} %select_select_fusion), calls=%async_computation.3 | async-start | bytes 2097152 | tf_op jit(solution)/shard_map/all_to_all | solution.py:264
  214.7 28.5 %all-to-all-done.3 = bf16[64,32,256]{2,1,0:T(8,128)(2,1)S(1)} async-done(((bf16[64,32,256]{2,1,0:T(8,128)(2,1)}), bf16[64,32,256]{2,1,0:T(8,128)(2,1)S(1)}, u32[]{:S(2)}, u32[]{:S(2)}) %all-to-all-start.3) | async-done | bytes 1048608 | tf_op jit(solution)/shard_map/all_to_all | solution.py:264
  245.0 5.0 %fusion.23 = f32[48,32,256]{2,1,0:T(8,128)S(1)} fusion(bf16[48,256,256]{2,1,0:T(8,128)(2,1)} %bitcast.196, bf16[48,32,256]{2,1,0:T(8,128)(2,1)} %gather_fusion.9, pred[48]{0:T(512)(128)(4,1)S(1)} %copy-done.14), kind=kOutput, calls=%fused_computation.45 | convolution fusion | flops 201719808 | bytes 8650800 | tf_op jit(solution)/shard_map/sab,sob->soa/dot_general | solution.py:337
  250.1 5.0 %fusion.17 = f32[64,32,256]{2,1,0:T(8,128)S(1)} fusion(bf16[64,256,256]{2,1,0:T(8,128)(2,1)} %bitcast.194, bf16[64,32,256]{2,1,0:T(8,128)(2,1)S(1)} %all-to-all-done.3, pred[64]{0:T(512)(128)(4,1)S(1)} %get-tuple-element.146), kind=kOutput, calls=%fused_computation.33 | convolution fusion | flops 268959744 | bytes 11534400 | tf_op jit(solution)/shard_map/eab,eoa->eob/dot_general | solution.py:339
  258.7 20.2 %shard_map.53 = (f32[256,256]{1,0:T(8,128)}, f32[1,128]{1,0:T(1,128)}) custom-call(f32[256,256]{1,0:T(8,128)} %bitcast.210, f32[1,128]{1,0:T(1,128)} %pad_bitcast_fusion.g_ref), custom_call_target="tpu_custom_call" | custom-call | tf_op jit(solution)/shard_map/pallas_call | solution.py:204
  (155 shorter events, 64.8 us)
Async XLA Ops:
  0.6 32.6 %copy-start.2 = (bf16[16,2048]{1,0:T(8,128)(2,1)S(1)}, bf16[16,2048]{1,0:T(8,128)(2,1)}, u32[]{:S(2)}) copy-start(bf16[16,2048]{1,0:T(8,128)(2,1)} %param.6) | copy-start | bytes 196612
  0.6 33.3 %copy-start.1 = (f32[32,2048]{1,0:T(8,128)S(1)}, f32[32,2048]{1,0:T(8,128)}, u32[]{:S(2)}) copy-start(f32[32,2048]{1,0:T(8,128)} %param.7) | copy-start | bytes 786436
  4.5 22.2 %all-to-all-start = ((s32[64,1,2]{2,1,0:T(1,128)}), s32[64,1,2]{2,1,0:T(1,128)S(1)}, u32[]{:S(2)}, u32[]{:S(2)}) async-start(s32[64,1,2]{2,1,0:T(1,128)} %copy.34), calls=%async_computation | async-start | bytes 65536 | tf_op jit(solution)/shard_map/all_to_all | solution.py:252
  17.5 16.4 %copy-start.5 = (pred[64]{0:T(512)(128)(4,1)}, pred[64]{0:T(512)(128)(4,1)S(1)}, u32[]{:S(2)}) copy-start(pred[64]{0:T(512)(128)(4,1)S(1)} %broadcast_compare_fusion) | copy-start | bytes 196
  17.5 16.4 %copy-start.7 = (pred[64]{0:T(512)(128)(4,1)}, pred[64]{0:T(512)(128)(4,1)S(1)}, u32[]{:S(2)}) copy-start(pred[64]{0:T(512)(128)(4,1)S(1)} %iota_compare_fusion.1) | copy-start | bytes 196
  26.8 7.2 %copy-start.9 = (pred[64]{0:T(512)(128)(4,1)}, pred[64]{0:T(512)(128)(4,1)S(1)}, u32[]{:S(2)}) copy-start(pred[64]{0:T(512)(128)(4,1)S(1)} %compare_bitcast_fusion) | copy-start | bytes 196
  26.8 9.9 %copy-start.3 = (s32[1024]{0:T(1024)}, s32[1024]{0:T(1024)S(1)}, u32[]{:S(2)}) copy-start(s32[1024]{0:T(1024)S(1)} %pad_clamp_fusion.1) | copy-start | bytes 12292
  28.5 22.1 %all-to-all-start.1 = ((bf16[64,16,256]{2,1,0:T(8,128)(2,1)}), bf16[64,16,256]{2,1,0:T(8,128)(2,1)S(1)}, u32[]{:S(2)}, u32[]{:S(2)}) async-start(bf16[64,16,256]{2,1,0:T(8,128)(2,1)} %select_select_fusion.2), calls=%async_computation.1 | async-start | bytes 1048576 | tf_op jit(solution)/shard_map/all_to_all | solution.py:264
  34.1 16.8 %copy-start.11 = (pred[64]{0:T(512)(128)(4,1)}, pred[64]{0:T(512)(128)(4,1)S(1)}, u32[]{:S(2)}) copy-start(pred[64]{0:T(512)(128)(4,1)S(1)} %get-tuple-element.147) | copy-start | bytes 196
  34.1 16.8 %copy-start.4 = (s32[1024]{0:T(1024)}, s32[1024]{0:T(1024)S(1)}, u32[]{:S(2)}) copy-start(s32[1024]{0:T(1024)S(1)} %pad_clamp_fusion) | copy-start | bytes 12292
  34.1 17.5 %copy-start.13 = (pred[48]{0:T(512)(128)(4,1)}, pred[48]{0:T(512)(128)(4,1)S(1)}, u32[]{:S(2)}) copy-start(pred[48]{0:T(512)(128)(4,1)S(1)} %broadcast_compare_fusion.1) | copy-start | bytes 148
  100.4 11.0 %copy-start.6 = (pred[64]{0:T(512)(128)(4,1)S(1)}, pred[64]{0:T(512)(128)(4,1)}, u32[]{:S(2)}) copy-start(pred[64]{0:T(512)(128)(4,1)} %copy-done.5) | copy-start | bytes 196
  100.4 11.0 %copy-start.8 = (pred[64]{0:T(512)(128)(4,1)S(1)}, pred[64]{0:T(512)(128)(4,1)}, u32[]{:S(2)}) copy-start(pred[64]{0:T(512)(128)(4,1)} %copy-done.7) | copy-start | bytes 196
  100.4 11.0 %copy-start.10 = (pred[64]{0:T(512)(128)(4,1)S(1)}, pred[64]{0:T(512)(128)(4,1)}, u32[]{:S(2)}) copy-start(pred[64]{0:T(512)(128)(4,1)} %copy-done.9) | copy-start | bytes 196
  112.7 36.1 %all-to-all-start.2 = ((bf16[64,32,256]{2,1,0:T(8,128)(2,1)}), bf16[64,32,256]{2,1,0:T(8,128)(2,1)S(1)}, u32[]{:S(2)}, u32[]{:S(2)}) async-start(bf16[64,32,256]{2,1,0:T(8,128)(2,1)} %select_select_fusion.1), calls=%async_computation.2 | async-start | bytes 2097152 | tf_op jit(solution)/shard_map/all_to_all | solution.py:264
  127.9 20.9 %copy-start.12 = (pred[64]{0:T(512)(128)(4,1)S(1)}, pred[64]{0:T(512)(128)(4,1)}, u32[]{:S(2)}) copy-start(pred[64]{0:T(512)(128)(4,1)} %copy-done.11) | copy-start | bytes 196
  127.9 22.7 %copy-start.14 = (pred[48]{0:T(512)(128)(4,1)S(1)}, pred[48]{0:T(512)(128)(4,1)}, u32[]{:S(2)}) copy-start(pred[48]{0:T(512)(128)(4,1)} %copy-done.13) | copy-start | bytes 148
  206.5 36.8 %all-to-all-start.3 = ((bf16[64,32,256]{2,1,0:T(8,128)(2,1)}), bf16[64,32,256]{2,1,0:T(8,128)(2,1)S(1)}, u32[]{:S(2)}, u32[]{:S(2)}) async-start(bf16[64,32,256]{2,1,0:T(8,128)(2,1)} %select_select_fusion), calls=%async_computation.3 | async-start | bytes 2097152 | tf_op jit(solution)/shard_map/all_to_all | solution.py:264
  250.1 28.8 %copy-start.15 = (f32[1,128]{1,0:T(1,128)S(1)}, f32[1,128]{1,0:T(1,128)}, u32[]{:S(2)}) copy-start(f32[1,128]{1,0:T(1,128)} %shard_map.52) | copy-start | bytes 1540
  250.1 29.3 %copy-start = (f32[256,256]{1,0:T(8,128)S(1)}, f32[256,256]{1,0:T(8,128)}, u32[]{:S(2)}) copy-start(f32[256,256]{1,0:T(8,128)} %get-tuple-element.101) | copy-start | bytes 786436

commit v9 on v8

--- a/solution.py
+++ b/solution.py
@@ -228,6 +228,62 @@
     return z_out.reshape(z.shape), g_out.reshape(-1)[:size]
 
 
+def pair_kernel(chunk, live_ref, lsq_ref, rsq_ref, left_ref, right_ref, k_ref, row_ref, col_ref):
+    base = pl.program_id(0) * chunk
+
+    def body(p, carry):
+        inner = lax.dot_general(
+            left_ref[p].astype(jnp.float32),
+            right_ref[p].astype(jnp.float32),
+            (((0,), (0,)), ((), ())),
+            precision=lax.Precision.HIGHEST,
+            preferred_element_type=jnp.float32,
+        )
+        dist_sq = lsq_ref[p] + rsq_ref[p] - 2.0 * inner
+        scaled = jnp.sqrt(jnp.maximum(dist_sq, 0.0)) * (1.0 / RADIUS)
+        remain = jnp.maximum(1.0 - scaled, 0.0)
+        square = remain * remain
+        values = square * square * (4.0 * scaled + 1.0)
+        values = jnp.where(live_ref[base + p] != 0, values, 0.0)
+        k_ref[p] = values.astype(jnp.bfloat16)
+        row_ref[p] = jnp.sum(values, axis=1, keepdims=True)
+        col_ref[p] = jnp.sum(values, axis=0, keepdims=True)
+        return carry
+
+    lax.fori_loop(0, chunk, body, 0)
+
+
+def pair_blocks(left_x, right_x, live, chunk):
+    count, coord_dim, block_len = left_x.shape
+    left_f = left_x.astype(jnp.float32)
+    right_f = right_x.astype(jnp.float32)
+    left_sq = jnp.sum(left_f * left_f, axis=1)[:, :, None]
+    right_sq = jnp.sum(right_f * right_f, axis=1)[:, None, :]
+
+    def spec(*tail):
+        return pl.BlockSpec((chunk,) + tail, lambda i, live_ref: (i,) + (0,) * len(tail))
+
+    return pl.pallas_call(
+        functools.partial(pair_kernel, chunk),
+        out_shape=[
+            jax.ShapeDtypeStruct((count, block_len, block_len), jnp.bfloat16),
+            jax.ShapeDtypeStruct((count, block_len, 1), jnp.float32),
+            jax.ShapeDtypeStruct((count, 1, block_len), jnp.float32),
+        ],
+        grid_spec=pltpu.PrefetchScalarGridSpec(
+            num_scalar_prefetch=1,
+            grid=(count // chunk,),
+            in_specs=[
+                spec(block_len, 1),
+                spec(1, block_len),
+                spec(coord_dim, block_len),
+                spec(coord_dim, block_len),
+            ],
+            out_specs=[spec(block_len, block_len), spec(block_len, 1), spec(1, block_len)],
+        ),
+    )(live.astype(jnp.int32), left_sq, right_sq, left_x, right_x)
+
+
 def local(block_list, points, targets):
     row_count = lax.axis_size("rows")
     row_index = lax.axis_index("rows")
@@ -303,26 +359,12 @@
     right_x = jnp.concatenate([far_x, own_x[in_idx]], axis=0)
     pair_live = jnp.concatenate([is_live, in_off], axis=0)
     pair_count = slot_count + row_count
-    chunk = 16
+    chunk = 8
     pad = (-pair_count) % chunk
     left_x = jnp.pad(left_x, ((0, pad), (0, 0), (0, 0)))
     right_x = jnp.pad(right_x, ((0, pad), (0, 0), (0, 0)))
     pair_live = jnp.pad(pair_live, (0, pad))
-
-    def pair_step(pieces):
-        lx, rx, live = pieces
-        values = jnp.where(live[:, None, None], wendland(lx, rx), 0.0)
-        return (values.astype(jnp.bfloat16), jnp.sum(values, axis=2), jnp.sum(values, axis=1))
-
-    kernel_bf, row_sums, col_sums = lax.map(
-        pair_step,
-        (
-            left_x.reshape(-1, chunk, coord_dim, block_len),
-            right_x.reshape(-1, chunk, coord_dim, block_len),
-            pair_live.reshape(-1, chunk),
-        ),
-    )
-    kernel_bf = kernel_bf.reshape(-1, block_len, block_len)
+    kernel_bf, row_sums, col_sums = pair_blocks(left_x, right_x, pair_live, chunk)
     row_sums = row_sums.reshape(-1, block_len)
     col_sums = col_sums.reshape(-1, block_len)
     own_k = kernel_bf[:slot_count]

time: 283 us -> 321 us (1.13)
  Pallas kernels: 61.5 us -> 135 us
  matrix products: 54.7 us -> 24.5 us
  local copies, waits for them, and re-layouts: 47.9 us -> 31 us
  waiting for transfers between devices: 64 us -> 78 us
    pallas_call x0 -> x1, Pallas kernels: none -> 73.3 us  [pair_blocks(): pl.pallas_call(functools.partial(pair_kernel, chunk), out_shape=[jax.Shap...]
    dot_general x7 -> x0, matrix products: 30.2 us -> none  [wendland(): jnp.einsum('nda,ndb->nab', left_f, right_f, precision=lax.Precision.HIGHEST)]
    all_to_all x3, waiting for transfers between devices: 56.4 us -> 70.3 us  [swap(): lax.all_to_all(parts, 'rows', split_axis=0, concat_axis=0, tiled=True)]
    slice x2 -> x0, local copies, waits for them, and re-layouts: 13.8 us -> none  [the longest x1 7.65 us: local(): in_k = kernel_bf[slot_count:pair_count]]
    dynamic_update_slice x14 -> x0, local copies, waits for them, and re-layouts: 8.53 us -> none  [local(): lax.map(pair_step, (left_x.reshape(-1, chunk, coord_dim, block_len), righ...]
    reduce_sum x14 -> x2, other arithmetic: 5.32 us -> 0.8 us  [the longest x1 0.4 us: pair_blocks(): left_sq = jnp.sum(left_f * left_f, axis=1)[:, :, None]]
    broadcast_in_dim x7 -> x2, local copies, waits for them, and re-layouts: 4.47 us -> 8.29 us  [the longest x1 7.56 us: pair_blocks(): left_sq = jnp.sum(left_f * left_f, axis=1)[:, :, None]]
    slice x1, local copies, waits for them, and re-layouts: 0.81 us -> 4.51 us  [local(): row_sums[:slot_count].reshape(block_rows, slot_width, block_len)]
  transfers between devices with their start and end apart: 4 -> 4, of which waited for: 4 -> 4; matrix products, arithmetic and copies ran while one was open for 6% -> 1% of each run, Pallas kernels for 0% -> 0%
where the time goes in v9:
time: 321 us; the launch traced here: 320 us
  Pallas kernels  135 us (42%)
  waiting for transfers between devices  78 us (24%)
  starting transfers between devices  33.4 us (10%)
  local copies, waits for them, and re-layouts  31 us (10%)
  matrix products  24.5 us (8%)
  other arithmetic  15.4 us (5%)
    pallas_call x1, Pallas kernels, pair_blocks(): pl.pallas_call(functools.partial(pair_kernel, chunk), out_shape=[jax.Shap...  73.3 us
    all_to_all x3, waiting for transfers between devices, swap(): lax.all_to_all(parts, 'rows', split_axis=0, concat_axis=0, tiled=True)  70.3 us
    pallas_call x2, Pallas kernels, fused_sum(): pl.pallas_call(functools.partial(fused_kernel, n_rows, n_cols), out_shape...  41.3 us
    all_to_all x3, starting transfers between devices, swap(): lax.all_to_all(parts, 'rows', split_axis=0, concat_axis=0, tiled=True)  20.4 us
    pallas_call x2, Pallas kernels, allsum(): pl.pallas_call(functools.partial(allsum_kernel, axis, n), out_shape=jax.S...  20 us
    all_to_all x1, starting transfers between devices, local(): lax.all_to_all(request, 'rows', split_axis=0, concat_axis=0, tiled=True)  13 us
    dot_general x2, matrix products, apply_partial(): jnp.einsum('sab,sob->soa', own_k, far_w, preferred_element_type=jnp.float32)  9.97 us
    dot_general x2, matrix products, apply_partial(): jnp.einsum('eab,eoa->eob', in_k, their_w, preferred_element_type=jnp.floa...  9.88 us
  transfers between devices with their start and end apart: 4, of which 4 were waited for; matrix products, arithmetic and copies ran while one was open for 1% of the time, Pallas kernels for 0%

profile of v9, /device:TPU:1, one launch (start us, length us, event | category | flops | bytes accessed | tf_op | source)
XLA Modules:
  0.0 320.2 jit_solution(6562492646467168919)
XLA Ops:
  4.4 13.0 %all-to-all-start = ((s32[64,1,2]{2,1,0:T(1,128)}), s32[64,1,2]{2,1,0:T(1,128)S(1)}, u32[]{:S(2)}, u32[]{:S(2)}) async-start(s32[64,1,2]{2,1,0:T(1,128)} %copy.36), calls=%async_computation | async-start | bytes 65536 | tf_op jit(solution)/shard_map/all_to_all | solution.py:308
  18.9 7.7 %all-to-all-done = s32[64,1,2]{2,1,0:T(1,128)S(1)} async-done(((s32[64,1,2]{2,1,0:T(1,128)}), s32[64,1,2]{2,1,0:T(1,128)S(1)}, u32[]{:S(2)}, u32[]{:S(2)}) %all-to-all-start) | async-done | bytes 544 | tf_op jit(solution)/shard_map/all_to_all | solution.py:308
  28.4 4.7 %all-to-all-start.1 = ((bf16[64,16,256]{2,1,0:T(8,128)(2,1)}), bf16[64,16,256]{2,1,0:T(8,128)(2,1)S(1)}, u32[]{:S(2)}, u32[]{:S(2)}) async-start(bf16[64,16,256]{2,1,0:T(8,128)(2,1)} %select_select_fusion.2), calls=%async_computation.1 | async-start | bytes 1048576 | tf_op jit(solution)/shard_map/all_to_all | solution.py:320
  37.1 13.3 %all-to-all-done.1 = bf16[64,16,256]{2,1,0:T(8,128)(2,1)S(1)} async-done(((bf16[64,16,256]{2,1,0:T(8,128)(2,1)}), bf16[64,16,256]{2,1,0:T(8,128)(2,1)S(1)}, u32[]{:S(2)}, u32[]{:S(2)}) %all-to-all-start.1) | async-done | bytes 524320 | tf_op jit(solution)/shard_map/all_to_all | solution.py:320
  54.3 7.6 %copy.39.lsq_ref = f32[112,256,1]{2,1,0:T(8,128)} copy(f32[112,256,1]{1,0,2:T(8,128)S(1)} %bitcast.167) | data formatting | bytes 229376 | tf_op jit(solution)/shard_map/broadcast_in_dim | solution.py:260
  62.5 73.3 %shard_map.50 = (bf16[112,256,256]{2,1,0:T(8,128)(2,1)}, f32[112,256,1]{2,1,0:T(8,128)}, f32[112,1,256]{2,1,0:T(1,128)}) custom-call(s32[112]{0:T(128)} %add_convert_fusion.live_ref, f32[112,256,1]{2,1,0:T(8,128)} %copy.39.lsq_ref, f32[112,1,256]{2,1,0:T(1,128)} %broadcast_in_dim.223.rsq_ref, bf16[112,16,256]{2,1,0:T(8,128)(2,1)} %pad_maximum_fusion.left_ref, ...), custom_call_target="tpu_custom_call" | custom-call | tf_op jit(solution)/shard_map/pallas_call | solution.py:266
  135.9 4.5 %slice_reduce_fusion = f32[48,256]{1,0:T(8,128)S(1)} fusion(f32[112,256,1]{2,1,0:T(8,128)} %get-tuple-element.9), kind=kLoop, calls=%fused_computation.16 | loop fusion | bytes 98304 | tf_op jit(solution)/shard_map/slice | solution.py:372
  141.2 6.4 %shard_map.51 = f32[16,128]{1,0:T(8,128)} custom-call(f32[16,128]{1,0:T(8,128)} %reshape_reshape_broadcast_in_dim.3.x_ref), custom_call_target="tpu_custom_call" | custom-call | tf_op jit(solution)/shard_map/pallas_call | solution.py:99
  150.9 7.5 %all-to-all-start.2 = ((bf16[64,32,256]{2,1,0:T(8,128)(2,1)}), bf16[64,32,256]{2,1,0:T(8,128)(2,1)S(1)}, u32[]{:S(2)}, u32[]{:S(2)}) async-start(bf16[64,32,256]{2,1,0:T(8,128)(2,1)} %select_select_fusion.1), calls=%async_computation.2 | async-start | bytes 2097152 | tf_op jit(solution)/shard_map/all_to_all | solution.py:320
  158.5 28.5 %all-to-all-done.2 = bf16[64,32,256]{2,1,0:T(8,128)(2,1)S(1)} async-done(((bf16[64,32,256]{2,1,0:T(8,128)(2,1)}), bf16[64,32,256]{2,1,0:T(8,128)(2,1)S(1)}, u32[]{:S(2)}, u32[]{:S(2)}) %all-to-all-start.2) | async-done | bytes 1048608 | tf_op jit(solution)/shard_map/all_to_all | solution.py:320
  187.1 1.5 gather_fusion.6
  188.7 5.0 %fusion.6 = f32[48,32,256]{2,1,0:T(8,128)S(1)} fusion(bf16[112,256,256]{2,1,0:T(8,128)(2,1)} %get-tuple-element.11, bf16[48,32,256]{2,1,0:T(8,128)(2,1)} %gather_fusion.6, pred[48]{0:T(512)(128)(4,1)S(1)} %broadcast_compare_fusion.1), kind=kOutput, calls=%fused_computation.19 | convolution fusion | flops 201719808 | bytes 8650800 | tf_op jit(solution)/shard_map/sab,sob->soa/dot_general | solution.py:379
  193.8 4.9 %fusion.2 = f32[64,32,256]{2,1,0:T(8,128)S(1)} fusion(bf16[112,256,256]{2,1,0:T(8,128)(2,1)} %get-tuple-element.11, bf16[64,32,256]{2,1,0:T(8,128)(2,1)S(1)} %all-to-all-done.2, pred[64]{0:T(512)(128)(4,1)S(1)} %get-tuple-element.38), kind=kOutput, calls=%fused_computation.14 | convolution fusion | flops 268959744 | bytes 11534400 | tf_op jit(solution)/shard_map/eab,eoa->eob/dot_general | solution.py:381
  198.7 2.3 fusion.33
  202.4 21.2 %shard_map.52 = (f32[256,256]{1,0:T(8,128)}, f32[1,128]{1,0:T(1,128)}) custom-call(f32[256,256]{1,0:T(8,128)} %bitcast.163, f32[1,128]{1,0:T(1,128)} %fusion.63.g_ref), custom_call_target="tpu_custom_call" | custom-call | tf_op jit(solution)/shard_map/pallas_call | solution.py:204
  224.4 1.5 multiply_reduce_fusion.4
  226.3 13.6 %shard_map.53 = f32[1,128]{1,0:T(1,128)} custom-call(f32[1,128]{1,0:T(1,128)} %pad_bitcast_fusion.1.x_ref), custom_call_target="tpu_custom_call" | custom-call | tf_op jit(solution)/shard_map/pallas_call | solution.py:99
  244.3 8.2 %all-to-all-start.3 = ((bf16[64,32,256]{2,1,0:T(8,128)(2,1)}), bf16[64,32,256]{2,1,0:T(8,128)(2,1)S(1)}, u32[]{:S(2)}, u32[]{:S(2)}) async-start(bf16[64,32,256]{2,1,0:T(8,128)(2,1)} %select_select_fusion), calls=%async_computation.3 | async-start | bytes 2097152 | tf_op jit(solution)/shard_map/all_to_all | solution.py:320
  252.6 28.5 %all-to-all-done.3 = bf16[64,32,256]{2,1,0:T(8,128)(2,1)S(1)} async-done(((bf16[64,32,256]{2,1,0:T(8,128)(2,1)}), bf16[64,32,256]{2,1,0:T(8,128)(2,1)S(1)}, u32[]{:S(2)}, u32[]{:S(2)}) %all-to-all-start.3) | async-done | bytes 1048608 | tf_op jit(solution)/shard_map/all_to_all | solution.py:320
  281.2 1.5 gather_fusion.9
  282.8 5.0 %fusion.4 = f32[48,32,256]{2,1,0:T(8,128)S(1)} fusion(bf16[112,256,256]{2,1,0:T(8,128)(2,1)} %get-tuple-element.11, bf16[48,32,256]{2,1,0:T(8,128)(2,1)} %gather_fusion.9, pred[48]{0:T(512)(128)(4,1)S(1)} %broadcast_compare_fusion.1), kind=kOutput, calls=%fused_computation.17 | convolution fusion | flops 201719808 | bytes 8650800 | tf_op jit(solution)/shard_map/sab,sob->soa/dot_general | solution.py:379
  287.9 4.9 %fusion = f32[64,32,256]{2,1,0:T(8,128)S(1)} fusion(bf16[112,256,256]{2,1,0:T(8,128)(2,1)} %get-tuple-element.11, bf16[64,32,256]{2,1,0:T(8,128)(2,1)S(1)} %all-to-all-done.3, pred[64]{0:T(512)(128)(4,1)S(1)} %get-tuple-element.38), kind=kOutput, calls=%fused_computation.12 | convolution fusion | flops 268959744 | bytes 11534400 | tf_op jit(solution)/shard_map/eab,eoa->eob/dot_general | solution.py:381
  292.8 2.2 multiply_reduce_fusion.3
  296.4 20.2 %shard_map.54 = (f32[256,256]{1,0:T(8,128)}, f32[1,128]{1,0:T(1,128)}) custom-call(f32[256,256]{1,0:T(8,128)} %bitcast.164, f32[1,128]{1,0:T(1,128)} %pad_bitcast_fusion.g_ref), custom_call_target="tpu_custom_call" | custom-call | tf_op jit(solution)/shard_map/pallas_call | solution.py:204
  (89 shorter events, 30.0 us)
Async XLA Ops:
  4.4 22.2 %all-to-all-start = ((s32[64,1,2]{2,1,0:T(1,128)}), s32[64,1,2]{2,1,0:T(1,128)S(1)}, u32[]{:S(2)}, u32[]{:S(2)}) async-start(s32[64,1,2]{2,1,0:T(1,128)} %copy.36), calls=%async_computation | async-start | bytes 65536 | tf_op jit(solution)/shard_map/all_to_all | solution.py:308
  18.9 14.2 %copy-start.2 = (bf16[16,2048]{1,0:T(8,128)(2,1)S(1)}, bf16[16,2048]{1,0:T(8,128)(2,1)}, u32[]{:S(2)}) copy-start(bf16[16,2048]{1,0:T(8,128)(2,1)} %param.4) | copy-start | bytes 196612
  26.7 7.1 %copy-start.1 = (f32[32,2048]{1,0:T(8,128)S(1)}, f32[32,2048]{1,0:T(8,128)}, u32[]{:S(2)}) copy-start(f32[32,2048]{1,0:T(8,128)} %param.5) | copy-start | bytes 786436
  28.4 22.1 %all-to-all-start.1 = ((bf16[64,16,256]{2,1,0:T(8,128)(2,1)}), bf16[64,16,256]{2,1,0:T(8,128)(2,1)S(1)}, u32[]{:S(2)}, u32[]{:S(2)}) async-start(bf16[64,16,256]{2,1,0:T(8,128)(2,1)} %select_select_fusion.2), calls=%async_computation.1 | async-start | bytes 1048576 | tf_op jit(solution)/shard_map/all_to_all | solution.py:320
  135.9 4.5 %copy-start.3 = (f32[112,1,256]{2,1,0:T(1,128)S(1)}, f32[112,1,256]{2,1,0:T(1,128)}, u32[]{:S(2)}) copy-start(f32[112,1,256]{2,1,0:T(1,128)} %get-tuple-element.10) | copy-start | bytes 344068
  150.9 36.1 %all-to-all-start.2 = ((bf16[64,32,256]{2,1,0:T(8,128)(2,1)}), bf16[64,32,256]{2,1,0:T(8,128)(2,1)S(1)}, u32[]{:S(2)}, u32[]{:S(2)}) async-start(bf16[64,32,256]{2,1,0:T(8,128)(2,1)} %select_select_fusion.1), calls=%async_computation.2 | async-start | bytes 2097152 | tf_op jit(solution)/shard_map/all_to_all | solution.py:320
  244.3 36.8 %all-to-all-start.3 = ((bf16[64,32,256]{2,1,0:T(8,128)(2,1)}), bf16[64,32,256]{2,1,0:T(8,128)(2,1)S(1)}, u32[]{:S(2)}, u32[]{:S(2)}) async-start(bf16[64,32,256]{2,1,0:T(8,128)(2,1)} %select_select_fusion), calls=%async_computation.3 | async-start | bytes 2097152 | tf_op jit(solution)/shard_map/all_to_all | solution.py:320
  292.8 23.8 %copy-start.4 = (f32[1,128]{1,0:T(1,128)S(1)}, f32[1,128]{1,0:T(1,128)}, u32[]{:S(2)}) copy-start(f32[1,128]{1,0:T(1,128)} %shard_map.53) | copy-start | bytes 1540
  292.8 24.4 %copy-start = (f32[256,256]{1,0:T(8,128)S(1)}, f32[256,256]{1,0:T(8,128)}, u32[]{:S(2)}) copy-start(f32[256,256]{1,0:T(8,128)} %get-tuple-element.13) | copy-start | bytes 786436

commit v10 on v8

--- a/solution.py
+++ b/solution.py
@@ -303,7 +303,7 @@
     right_x = jnp.concatenate([far_x, own_x[in_idx]], axis=0)
     pair_live = jnp.concatenate([is_live, in_off], axis=0)
     pair_count = slot_count + row_count
-    chunk = 16
+    chunk = 112
     pad = (-pair_count) % chunk
     left_x = jnp.pad(left_x, ((0, pad), (0, 0), (0, 0)))
     right_x = jnp.pad(right_x, ((0, pad), (0, 0), (0, 0)))

time: 283 us -> 262 us (0.926)
  local copies, waits for them, and re-layouts: 47.9 us -> 20 us
  waiting for transfers between devices: 64 us -> 76.8 us
  other arithmetic: 17.5 us -> 13.6 us
    slice x3 -> x0, local copies, waits for them, and re-layouts: 14.7 us -> none  [the longest x1 7.65 us: local(): in_k = kernel_bf[slot_count:pair_count]]
    all_to_all x3, waiting for transfers between devices: 56.4 us -> 69.1 us  [swap(): lax.all_to_all(parts, 'rows', split_axis=0, concat_axis=0, tiled=True)]
    dynamic_update_slice x14 -> x0, local copies, waits for them, and re-layouts: 8.53 us -> none  [local(): lax.map(pair_step, (left_x.reshape(-1, chunk, coord_dim, block_len), righ...]
    broadcast_in_dim x7 -> x0, local copies, waits for them, and re-layouts: 4.47 us -> none  [pair_step(): values = jnp.where(live[:, None, None], wendland(lx, rx), 0.0)]
    reduce_sum x7 -> x1, other arithmetic: 4.55 us -> 0.4 us  [wendland(): left_sq = jnp.sum(left_f * left_f, axis=1)]
    dot_general x7 -> x1, matrix products: 30.2 us -> 28.5 us  [wendland(): jnp.einsum('nda,ndb->nab', left_f, right_f, precision=lax.Precision.HIGHEST)]
  transfers between devices with their start and end apart: 4 -> 4, of which waited for: 4 -> 4; matrix products, arithmetic and copies ran while one was open for 6% -> 2% of each run, Pallas kernels for 0% -> 0%
where the time goes in v10:
time: 262 us; the launch traced here: 261 us
  waiting for transfers between devices  76.8 us (29%)
  Pallas kernels  61.4 us (23%)
  matrix products  53 us (20%)
  starting transfers between devices  33.4 us (13%)
  local copies, waits for them, and re-layouts  20 us (8%)
  other arithmetic  13.6 us (5%)
  between operations  3.04 us (1%)
    all_to_all x3, waiting for transfers between devices, swap(): lax.all_to_all(parts, 'rows', split_axis=0, concat_axis=0, tiled=True)  69.1 us
    pallas_call x2, Pallas kernels, fused_sum(): pl.pallas_call(functools.partial(fused_kernel, n_rows, n_cols), out_shape...  41.3 us
    dot_general x1, matrix products, wendland(): jnp.einsum('nda,ndb->nab', left_f, right_f, precision=lax.Precision.HIGHEST)  28.5 us
    all_to_all x3, starting transfers between devices, swap(): lax.all_to_all(parts, 'rows', split_axis=0, concat_axis=0, tiled=True)  20.4 us
    pallas_call x2, Pallas kernels, allsum(): pl.pallas_call(functools.partial(allsum_kernel, axis, n), out_shape=jax.S...  20.1 us
    all_to_all x1, starting transfers between devices, local(): lax.all_to_all(request, 'rows', split_axis=0, concat_axis=0, tiled=True)  13 us
    dot_general x2, matrix products, apply_partial(): jnp.einsum('sab,sob->soa', own_k, far_w, preferred_element_type=jnp.float32)  9.96 us
    dot_general x2, matrix products, apply_partial(): jnp.einsum('eab,eoa->eob', in_k, their_w, preferred_element_type=jnp.floa...  9.92 us
  transfers between devices with their start and end apart: 4, of which 4 were waited for; matrix products, arithmetic and copies ran while one was open for 2% of the time, Pallas kernels for 0%

profile of v10, /device:TPU:1, one launch (start us, length us, event | category | flops | bytes accessed | tf_op | source)
XLA Modules:
  0.0 261.2 jit_solution(17568869867874595384)
XLA Ops:
  4.4 13.0 %all-to-all-start = ((s32[64,1,2]{2,1,0:T(1,128)}), s32[64,1,2]{2,1,0:T(1,128)S(1)}, u32[]{:S(2)}, u32[]{:S(2)}) async-start(s32[64,1,2]{2,1,0:T(1,128)} %copy.34), calls=%async_computation | async-start | bytes 65536 | tf_op jit(solution)/shard_map/all_to_all | solution.py:252
  18.9 7.7 %all-to-all-done = s32[64,1,2]{2,1,0:T(1,128)S(1)} async-done(((s32[64,1,2]{2,1,0:T(1,128)}), s32[64,1,2]{2,1,0:T(1,128)S(1)}, u32[]{:S(2)}, u32[]{:S(2)}) %all-to-all-start) | async-done | bytes 544 | tf_op jit(solution)/shard_map/all_to_all | solution.py:252
  28.4 4.7 %all-to-all-start.1 = ((bf16[64,16,256]{2,1,0:T(8,128)(2,1)}), bf16[64,16,256]{2,1,0:T(8,128)(2,1)S(1)}, u32[]{:S(2)}, u32[]{:S(2)}) async-start(bf16[64,16,256]{2,1,0:T(8,128)(2,1)} %select_select_fusion.2), calls=%async_computation.1 | async-start | bytes 1048576 | tf_op jit(solution)/shard_map/all_to_all | solution.py:264
  38.3 12.1 %all-to-all-done.1 = bf16[64,16,256]{2,1,0:T(8,128)(2,1)S(1)} async-done(((bf16[64,16,256]{2,1,0:T(8,128)(2,1)}), bf16[64,16,256]{2,1,0:T(8,128)(2,1)S(1)}, u32[]{:S(2)}, u32[]{:S(2)}) %all-to-all-start.1) | async-done | bytes 524320 | tf_op jit(solution)/shard_map/all_to_all | solution.py:264
  52.2 28.5 %fusion.73 = (f32[112,256]{1,0:T(8,128)S(1)}, f32[112,256]{1,0:T(8,128)S(1)}, bf16[112,256,256]{2,1,0:T(8,128)(2,1)}) fusion(bf16[64,16,256]{2,1,0:T(8,128)(2,1)S(1)} %gather_fusion.2, bf16[48,16,256]{2,1,0:T(8,128)(2,1)S(1)} %broadcast_select_fusion.4, bf16[64,16,256]{2,1,0:T(8,128)(2,1)S(1)} %get-tuple-element.44, ...), kind=kOutput, calls=%fused_computation.163 | convolution fusion | flops 353181696 | bytes 16973936 | tf_op jit(solution)/shard_map/while/body/eval_jaxpr/nda,ndb->nab/dot_general | solution.py:24
  81.5 6.4 %shard_map.50 = f32[16,128]{1,0:T(8,128)} custom-call(f32[16,128]{1,0:T(8,128)} %reshape_reshape_broadcast_in_dim.3.x_ref), custom_call_target="tpu_custom_call" | custom-call | tf_op jit(solution)/shard_map/pallas_call | solution.py:99
  90.0 1.3 select_select_fusion.1
  91.2 7.5 %all-to-all-start.2 = ((bf16[64,32,256]{2,1,0:T(8,128)(2,1)}), bf16[64,32,256]{2,1,0:T(8,128)(2,1)S(1)}, u32[]{:S(2)}, u32[]{:S(2)}) async-start(bf16[64,32,256]{2,1,0:T(8,128)(2,1)} %select_select_fusion.1), calls=%async_computation.2 | async-start | bytes 2097152 | tf_op jit(solution)/shard_map/all_to_all | solution.py:264
  98.8 28.5 %all-to-all-done.2 = bf16[64,32,256]{2,1,0:T(8,128)(2,1)S(1)} async-done(((bf16[64,32,256]{2,1,0:T(8,128)(2,1)}), bf16[64,32,256]{2,1,0:T(8,128)(2,1)S(1)}, u32[]{:S(2)}, u32[]{:S(2)}) %all-to-all-start.2) | async-done | bytes 1048608 | tf_op jit(solution)/shard_map/all_to_all | solution.py:264
  127.5 1.5 gather_fusion.6
  129.0 5.0 %fusion.6 = f32[48,32,256]{2,1,0:T(8,128)S(1)} fusion(bf16[112,256,256]{2,1,0:T(8,128)(2,1)} %get-tuple-element.41, bf16[48,32,256]{2,1,0:T(8,128)(2,1)} %gather_fusion.6, pred[48]{0:T(512)(128)(4,1)S(1)} %broadcast_compare_fusion.1), kind=kOutput, calls=%fused_computation.19 | convolution fusion | flops 201719808 | bytes 8650800 | tf_op jit(solution)/shard_map/sab,sob->soa/dot_general | solution.py:337
  134.1 4.9 %fusion.2 = f32[64,32,256]{2,1,0:T(8,128)S(1)} fusion(bf16[112,256,256]{2,1,0:T(8,128)(2,1)} %get-tuple-element.41, bf16[64,32,256]{2,1,0:T(8,128)(2,1)S(1)} %all-to-all-done.2, pred[64]{0:T(512)(128)(4,1)S(1)} %get-tuple-element.57), kind=kOutput, calls=%fused_computation.15 | convolution fusion | flops 268959744 | bytes 11534400 | tf_op jit(solution)/shard_map/eab,eoa->eob/dot_general | solution.py:339
  139.0 2.3 fusion.33
  142.7 21.2 %shard_map.51 = (f32[256,256]{1,0:T(8,128)}, f32[1,128]{1,0:T(1,128)}) custom-call(f32[256,256]{1,0:T(8,128)} %bitcast.159, f32[1,128]{1,0:T(1,128)} %fusion.62.g_ref), custom_call_target="tpu_custom_call" | custom-call | tf_op jit(solution)/shard_map/pallas_call | solution.py:204
  164.7 1.5 multiply_reduce_fusion.4
  166.6 13.6 %shard_map.52 = f32[1,128]{1,0:T(1,128)} custom-call(f32[1,128]{1,0:T(1,128)} %pad_bitcast_fusion.1.x_ref), custom_call_target="tpu_custom_call" | custom-call | tf_op jit(solution)/shard_map/pallas_call | solution.py:99
  184.7 8.2 %all-to-all-start.3 = ((bf16[64,32,256]{2,1,0:T(8,128)(2,1)}), bf16[64,32,256]{2,1,0:T(8,128)(2,1)S(1)}, u32[]{:S(2)}, u32[]{:S(2)}) async-start(bf16[64,32,256]{2,1,0:T(8,128)(2,1)} %select_select_fusion), calls=%async_computation.3 | async-start | bytes 2097152 | tf_op jit(solution)/shard_map/all_to_all | solution.py:264
  192.9 28.5 %all-to-all-done.3 = bf16[64,32,256]{2,1,0:T(8,128)(2,1)S(1)} async-done(((bf16[64,32,256]{2,1,0:T(8,128)(2,1)}), bf16[64,32,256]{2,1,0:T(8,128)(2,1)S(1)}, u32[]{:S(2)}, u32[]{:S(2)}) %all-to-all-start.3) | async-done | bytes 1048608 | tf_op jit(solution)/shard_map/all_to_all | solution.py:264
  221.6 1.5 gather_fusion.9
  223.1 5.0 %fusion.4 = f32[48,32,256]{2,1,0:T(8,128)S(1)} fusion(bf16[112,256,256]{2,1,0:T(8,128)(2,1)} %get-tuple-element.41, bf16[48,32,256]{2,1,0:T(8,128)(2,1)} %gather_fusion.9, pred[48]{0:T(512)(128)(4,1)S(1)} %broadcast_compare_fusion.1), kind=kOutput, calls=%fused_computation.17 | convolution fusion | flops 201719808 | bytes 8650800 | tf_op jit(solution)/shard_map/sab,sob->soa/dot_general | solution.py:337
  228.9 5.0 %fusion = f32[64,32,256]{2,1,0:T(8,128)S(1)} fusion(bf16[112,256,256]{2,1,0:T(8,128)(2,1)} %get-tuple-element.41, bf16[64,32,256]{2,1,0:T(8,128)(2,1)S(1)} %all-to-all-done.3, pred[64]{0:T(512)(128)(4,1)S(1)} %get-tuple-element.57), kind=kOutput, calls=%fused_computation.13 | convolution fusion | flops 268959744 | bytes 11534400 | tf_op jit(solution)/shard_map/eab,eoa->eob/dot_general | solution.py:339
  233.9 2.2 multiply_reduce_fusion.3
  237.5 20.2 %shard_map.53 = (f32[256,256]{1,0:T(8,128)}, f32[1,128]{1,0:T(1,128)}) custom-call(f32[256,256]{1,0:T(8,128)} %bitcast.160, f32[1,128]{1,0:T(1,128)} %pad_bitcast_fusion.g_ref), custom_call_target="tpu_custom_call" | custom-call | tf_op jit(solution)/shard_map/pallas_call | solution.py:204
  258.3 1.3 fusion.41
  (80 shorter events, 26.6 us)
Async XLA Ops:
  4.4 22.2 %all-to-all-start = ((s32[64,1,2]{2,1,0:T(1,128)}), s32[64,1,2]{2,1,0:T(1,128)S(1)}, u32[]{:S(2)}, u32[]{:S(2)}) async-start(s32[64,1,2]{2,1,0:T(1,128)} %copy.34), calls=%async_computation | async-start | bytes 65536 | tf_op jit(solution)/shard_map/all_to_all | solution.py:252
  28.4 22.1 %all-to-all-start.1 = ((bf16[64,16,256]{2,1,0:T(8,128)(2,1)}), bf16[64,16,256]{2,1,0:T(8,128)(2,1)S(1)}, u32[]{:S(2)}, u32[]{:S(2)}) async-start(bf16[64,16,256]{2,1,0:T(8,128)(2,1)} %select_select_fusion.2), calls=%async_computation.1 | async-start | bytes 1048576 | tf_op jit(solution)/shard_map/all_to_all | solution.py:264
  91.2 36.1 %all-to-all-start.2 = ((bf16[64,32,256]{2,1,0:T(8,128)(2,1)}), bf16[64,32,256]{2,1,0:T(8,128)(2,1)S(1)}, u32[]{:S(2)}, u32[]{:S(2)}) async-start(bf16[64,32,256]{2,1,0:T(8,128)(2,1)} %select_select_fusion.1), calls=%async_computation.2 | async-start | bytes 2097152 | tf_op jit(solution)/shard_map/all_to_all | solution.py:264
  184.7 36.8 %all-to-all-start.3 = ((bf16[64,32,256]{2,1,0:T(8,128)(2,1)}), bf16[64,32,256]{2,1,0:T(8,128)(2,1)S(1)}, u32[]{:S(2)}, u32[]{:S(2)}) async-start(bf16[64,32,256]{2,1,0:T(8,128)(2,1)} %select_select_fusion), calls=%async_computation.3 | async-start | bytes 2097152 | tf_op jit(solution)/shard_map/all_to_all | solution.py:264
  228.1 29.6 %copy-start.2 = (f32[1,128]{1,0:T(1,128)S(1)}, f32[1,128]{1,0:T(1,128)}, u32[]{:S(2)}) copy-start(f32[1,128]{1,0:T(1,128)} %shard_map.52) | copy-start | bytes 1540
  228.1 30.3 %copy-start = (f32[256,256]{1,0:T(8,128)S(1)}, f32[256,256]{1,0:T(8,128)}, u32[]{:S(2)}) copy-start(f32[256,256]{1,0:T(8,128)} %get-tuple-element.28) | copy-start | bytes 786436
  228.9 5.0 %copy-start.1 = (f32[8,32,256]{2,1,0:T(8,128)S(1)}, f32[8,32,256]{2,1,0:T(8,128)}, u32[]{:S(2)}) copy-start(f32[8,32,256]{2,1,0:T(8,128)} %reduce_sum.125) | copy-start | bytes 786436

commit v11 on v10

--- a/solution.py
+++ b/solution.py
@@ -19,10 +19,12 @@
 def wendland(left_x, right_x):
     left_f = left_x.astype(jnp.float32)
     right_f = right_x.astype(jnp.float32)
-    left_sq = jnp.sum(left_f * left_f, axis=1)
-    right_sq = jnp.sum(right_f * right_f, axis=1)
-    inner_prod = jnp.einsum("nda,ndb->nab", left_f, right_f, precision=lax.Precision.HIGHEST)
-    dist_sq = left_sq[:, :, None] + right_sq[:, None, :] - 2.0 * inner_prod
+    left_sq = jnp.sum(left_f * left_f, axis=1, keepdims=True)
+    right_sq = jnp.sum(right_f * right_f, axis=1, keepdims=True)
+    ones = jnp.ones_like(left_sq)
+    left_aug = jnp.concatenate([left_f, left_sq, ones], axis=1)
+    right_aug = jnp.concatenate([-2.0 * right_f, ones, right_sq], axis=1)
+    dist_sq = jnp.einsum("nda,ndb->nab", left_aug, right_aug, precision=lax.Precision.HIGHEST)
     scaled = jnp.sqrt(jnp.maximum(dist_sq, 0.0)) / RADIUS
     remain = jnp.maximum(1.0 - scaled, 0.0)
     square = remain * remain
@@ -334,8 +336,12 @@
 
     def apply_partial(weights):
         their_w, far_w = both_ways(weights)
-        direct = jnp.einsum("sab,sob->soa", own_k, far_w, preferred_element_type=jnp.float32)
-        direct = jnp.sum(direct.reshape(block_rows, slot_width, outputs, block_len), axis=1)
+        direct = jnp.einsum(
+            "rkab,rkob->roa",
+            own_k.reshape(block_rows, slot_width, block_len, block_len),
+            far_w.reshape(block_rows, slot_width, outputs, block_len),
+            preferred_element_type=jnp.float32,
+        )
         mirror = jnp.einsum("eab,eoa->eob", in_k, their_w, preferred_element_type=jnp.float32)
         return direct + collect(mirror)
 

time: 262 us -> 277 us (1.057)
  matrix products: 53 us -> 64.6 us
  local copies, waits for them, and re-layouts: 20 us -> 25.4 us
  waiting for transfers between devices: 76.8 us -> 72.7 us
    dot_general x3, matrix products: 38.5 us -> 50.4 us  [the longest x1 44.9 us: wendland(): jnp.einsum('nda,ndb->nab', left_aug, right_aug, precision=lax.Precision.H...]
    slice x0 -> x1, local copies, waits for them, and re-layouts: none -> 6.06 us  [local(): own_k = kernel_bf[:slot_count]]
    all_to_all x3, waiting for transfers between devices: 69.1 us -> 65 us  [swap(): lax.all_to_all(parts, 'rows', split_axis=0, concat_axis=0, tiled=True)]
    unnamed x13 -> x26, local copies, waits for them, and re-layouts: 3.5 us -> 0.08 us
    gather x3, local copies, waits for them, and re-layouts: 3.65 us -> 6.44 us  [per_slot(): chosen = got[pick_at]]
  transfers between devices with their start and end apart: 4 -> 4, of which waited for: 4 -> 4; matrix products, arithmetic and copies ran while one was open for 2% -> 3% of each run, Pallas kernels for 0% -> 0%
where the time goes in v11:
time: 277 us; the launch traced here: 276 us
  waiting for transfers between devices  72.7 us (26%)
  matrix products  64.6 us (23%)
  Pallas kernels  61.4 us (22%)
  starting transfers between devices  33.6 us (12%)
  local copies, waits for them, and re-layouts  25.4 us (9%)
  other arithmetic  14.9 us (5%)
  between operations  3.12 us (1%)
    all_to_all x3, waiting for transfers between devices, swap(): lax.all_to_all(parts, 'rows', split_axis=0, concat_axis=0, tiled=True)  65 us
    dot_general x1, matrix products, wendland(): jnp.einsum('nda,ndb->nab', left_aug, right_aug, precision=lax.Precision.H...  44.9 us
    pallas_call x2, Pallas kernels, fused_sum(): pl.pallas_call(functools.partial(fused_kernel, n_rows, n_cols), out_shape...  41.3 us
    all_to_all x3, starting transfers between devices, swap(): lax.all_to_all(parts, 'rows', split_axis=0, concat_axis=0, tiled=True)  20.7 us
    pallas_call x2, Pallas kernels, allsum(): pl.pallas_call(functools.partial(allsum_kernel, axis, n), out_shape=jax.S...  20.1 us
    all_to_all x1, starting transfers between devices, local(): lax.all_to_all(request, 'rows', split_axis=0, concat_axis=0, tiled=True)  13 us
    dot_general x2, matrix products, apply_partial(): jnp.einsum('eab,eoa->eob', in_k, their_w, preferred_element_type=jnp.floa...  10.2 us
    all_to_all x1, waiting for transfers between devices, local(): lax.all_to_all(request, 'rows', split_axis=0, concat_axis=0, tiled=True)  7.7 us
  transfers between devices with their start and end apart: 4, of which 4 were waited for; matrix products, arithmetic and copies ran while one was open for 3% of the time, Pallas kernels for 0%

profile of v11, /device:TPU:1, one launch (start us, length us, event | category | flops | bytes accessed | tf_op | source)
XLA Modules:
  0.0 275.8 jit_solution(2503742535913305794)
XLA Ops:
  4.5 13.0 %all-to-all-start = ((s32[64,1,2]{2,1,0:T(1,128)}), s32[64,1,2]{2,1,0:T(1,128)S(1)}, u32[]{:S(2)}, u32[]{:S(2)}) async-start(s32[64,1,2]{2,1,0:T(1,128)} %copy.23), calls=%async_computation | async-start | bytes 65536 | tf_op jit(solution)/shard_map/all_to_all | solution.py:254
  19.0 7.7 %all-to-all-done = s32[64,1,2]{2,1,0:T(1,128)S(1)} async-done(((s32[64,1,2]{2,1,0:T(1,128)}), s32[64,1,2]{2,1,0:T(1,128)S(1)}, u32[]{:S(2)}, u32[]{:S(2)}) %all-to-all-start) | async-done | bytes 544 | tf_op jit(solution)/shard_map/all_to_all | solution.py:254
  28.4 4.7 %all-to-all-start.1 = ((bf16[64,16,256]{2,1,0:T(8,128)(2,1)}), bf16[64,16,256]{2,1,0:T(8,128)(2,1)S(1)}, u32[]{:S(2)}, u32[]{:S(2)}) async-start(bf16[64,16,256]{2,1,0:T(8,128)(2,1)} %select_select_fusion.2), calls=%async_computation.1 | async-start | bytes 1048576 | tf_op jit(solution)/shard_map/all_to_all | solution.py:266
  36.5 14.0 %all-to-all-done.1 = bf16[64,16,256]{2,1,0:T(8,128)(2,1)S(1)} async-done(((bf16[64,16,256]{2,1,0:T(8,128)(2,1)}), bf16[64,16,256]{2,1,0:T(8,128)(2,1)S(1)}, u32[]{:S(2)}, u32[]{:S(2)}) %all-to-all-start.1) | async-done | bytes 524320 | tf_op jit(solution)/shard_map/all_to_all | solution.py:266
  52.8 44.9 %fusion.81 = (f32[112,256]{1,0:T(8,128)S(1)}, f32[112,256]{1,0:T(8,128)S(1)}, bf16[112,256,256]{2,1,0:T(8,128)(2,1)}) fusion(f32[112,1,256]{2,1,0:T(1,128)S(1)} %broadcast_in_dim.250, f32[112,1,256]{2,1,0:T(1,128)S(1)} %broadcast.332, f32[112,16,256]{2,1,0:T(8,128)S(1)} %get-tuple-element.42, f32[112,1,256]{2,1,0:T(1,128)S(1)} %broadcast_in_dim.244, ...), kind=kOutput, calls=%fused_computation.170 | convolution fusion | flops 1682874368 | bytes 18923632 | tf_op jit(solution)/shard_map/while/body/eval_jaxpr/nda,ndb->nab/dot_general | solution.py:27
  98.5 6.4 %shard_map.50 = f32[16,128]{1,0:T(8,128)} custom-call(f32[16,128]{1,0:T(8,128)} %reshape_reshape_broadcast_in_dim.3.x_ref), custom_call_target="tpu_custom_call" | custom-call | tf_op jit(solution)/shard_map/pallas_call | solution.py:101
  106.9 1.3 select_select_fusion.1
  108.2 7.7 %all-to-all-start.2 = ((bf16[64,32,256]{2,1,0:T(8,128)(2,1)}), bf16[64,32,256]{2,1,0:T(8,128)(2,1)S(1)}, u32[]{:S(2)}, u32[]{:S(2)}) async-start(bf16[64,32,256]{2,1,0:T(8,128)(2,1)} %select_select_fusion.1), calls=%async_computation.2 | async-start | bytes 2097152 | tf_op jit(solution)/shard_map/all_to_all | solution.py:266
  115.9 6.1 %slice.74 = bf16[48,256,256]{2,1,0:T(8,128)(2,1)} slice(bf16[112,256,256]{2,1,0:T(8,128)(2,1)} %get-tuple-element.41), slice={[0:48], [0:256], [0:256]} | slice | bytes 12582912 | tf_op jit(solution)/shard_map/slice | solution.py:330
  122.0 22.5 %all-to-all-done.2 = bf16[64,32,256]{2,1,0:T(8,128)(2,1)S(1)} async-done(((bf16[64,32,256]{2,1,0:T(8,128)(2,1)}), bf16[64,32,256]{2,1,0:T(8,128)(2,1)S(1)}, u32[]{:S(2)}, u32[]{:S(2)}) %all-to-all-start.2) | async-done | bytes 1048608 | tf_op jit(solution)/shard_map/all_to_all | solution.py:266
  145.6 2.9 %gather_fusion.6 = bf16[48,32,256]{2,1,0:T(8,128)(2,1)} fusion(bf16[64,32,256]{2,1,0:T(8,128)(2,1)} %broadcast_select_fusion.1, s32[1024]{0:T(1024)S(1)} %pad_clamp_fusion), kind=kCustom, calls=%fused_computation.6 | custom fusion | bytes 1573056 | tf_op jit(solution)/shard_map/gather | solution.py:286
  148.5 5.1 %fusion.2 = f32[64,32,256]{2,1,0:T(8,128)S(1)} fusion(bf16[112,256,256]{2,1,0:T(8,128)(2,1)} %get-tuple-element.41, bf16[64,32,256]{2,1,0:T(8,128)(2,1)S(1)} %all-to-all-done.2, pred[64]{0:T(512)(128)(4,1)S(1)} %get-tuple-element.59), kind=kOutput, calls=%fused_computation.15 | convolution fusion | flops 268959744 | bytes 11534400 | tf_op jit(solution)/shard_map/eab,eoa->eob/dot_general | solution.py:345
  153.6 2.0 fusion.17
  155.6 2.8 fusion.43
  159.0 21.1 %shard_map.51 = (f32[256,256]{1,0:T(8,128)}, f32[1,128]{1,0:T(1,128)}) custom-call(f32[256,256]{1,0:T(8,128)} %bitcast.211, f32[1,128]{1,0:T(1,128)} %fusion.70.g_ref), custom_call_target="tpu_custom_call" | custom-call | tf_op jit(solution)/shard_map/pallas_call | solution.py:206
  182.6 13.6 %shard_map.52 = f32[1,128]{1,0:T(1,128)} custom-call(f32[1,128]{1,0:T(1,128)} %pad_bitcast_fusion.1.x_ref), custom_call_target="tpu_custom_call" | custom-call | tf_op jit(solution)/shard_map/pallas_call | solution.py:101
  196.8 1.8 multiply_convert_fusion
  201.1 8.2 %all-to-all-start.3 = ((bf16[64,32,256]{2,1,0:T(8,128)(2,1)}), bf16[64,32,256]{2,1,0:T(8,128)(2,1)S(1)}, u32[]{:S(2)}, u32[]{:S(2)}) async-start(bf16[64,32,256]{2,1,0:T(8,128)(2,1)} %select_select_fusion), calls=%async_computation.3 | async-start | bytes 2097152 | tf_op jit(solution)/shard_map/all_to_all | solution.py:266
  209.3 28.5 %all-to-all-done.3 = bf16[64,32,256]{2,1,0:T(8,128)(2,1)S(1)} async-done(((bf16[64,32,256]{2,1,0:T(8,128)(2,1)}), bf16[64,32,256]{2,1,0:T(8,128)(2,1)S(1)}, u32[]{:S(2)}, u32[]{:S(2)}) %all-to-all-start.3) | async-done | bytes 1048608 | tf_op jit(solution)/shard_map/all_to_all | solution.py:266
  239.0 2.9 %gather_fusion.9 = bf16[48,32,256]{2,1,0:T(8,128)(2,1)} fusion(bf16[64,32,256]{2,1,0:T(8,128)(2,1)} %broadcast_select_fusion, s32[1024]{0:T(1024)S(1)} %pad_clamp_fusion), kind=kCustom, calls=%fused_computation.9 | custom fusion | bytes 1573056 | tf_op jit(solution)/shard_map/gather | solution.py:286
  241.9 5.1 %fusion = f32[64,32,256]{2,1,0:T(8,128)S(1)} fusion(bf16[112,256,256]{2,1,0:T(8,128)(2,1)} %get-tuple-element.41, bf16[64,32,256]{2,1,0:T(8,128)(2,1)S(1)} %all-to-all-done.3, pred[64]{0:T(512)(128)(4,1)S(1)} %get-tuple-element.59), kind=kOutput, calls=%fused_computation.13 | convolution fusion | flops 268959744 | bytes 11534400 | tf_op jit(solution)/shard_map/eab,eoa->eob/dot_general | solution.py:345
  247.0 2.0 fusion.14
  249.1 2.8 %multiply_reduce_fusion.2 = (f32[32]{0:T(128)S(1)}, f32[32]{0:T(128)S(1)}, f32[8,32,256]{2,1,0:T(8,128)}) fusion(f32[8,32,256]{2,1,0:T(8,128)S(1)} %copy-done.3, f32[8,256]{1,0:T(8,128)S(1)} %sqrt.11, f32[8,32,256]{2,0,1:T(8,128)S(1)} %fusion.14, bf16[8,6,256,256]{3,2,1,0:T(8,128)(2,1)S(1)} %bitcast.197, bf16[8,6,32,256]{3,2,1,0:T(8,128)(2,1)S(1)} %bitcast.208, ...), kind=kOutput, calls=%fused_computation.82 | convolution fusion | flops 202112960 | bytes 7872816 | tf_op jit(solution)/shard_map/rkab,rkob->roa/dot_general | solution.py:339
  252.4 20.2 %shard_map.53 = (f32[256,256]{1,0:T(8,128)}, f32[1,128]{1,0:T(1,128)}) custom-call(f32[256,256]{1,0:T(8,128)} %bitcast.212, f32[1,128]{1,0:T(1,128)} %pad_bitcast_fusion.g_ref), custom_call_target="tpu_custom_call" | custom-call | tf_op jit(solution)/shard_map/pallas_call | solution.py:206
  (97 shorter events, 25.5 us)
Async XLA Ops:
  0.6 32.5 %copy-start.5 = (bf16[16,2048]{1,0:T(8,128)(2,1)S(1)}, bf16[16,2048]{1,0:T(8,128)(2,1)}, u32[]{:S(2)}) copy-start(bf16[16,2048]{1,0:T(8,128)(2,1)} %param.4) | copy-start | bytes 196612
  4.5 22.2 %all-to-all-start = ((s32[64,1,2]{2,1,0:T(1,128)}), s32[64,1,2]{2,1,0:T(1,128)S(1)}, u32[]{:S(2)}, u32[]{:S(2)}) async-start(s32[64,1,2]{2,1,0:T(1,128)} %copy.23), calls=%async_computation | async-start | bytes 65536 | tf_op jit(solution)/shard_map/all_to_all | solution.py:254
  28.4 22.1 %all-to-all-start.1 = ((bf16[64,16,256]{2,1,0:T(8,128)(2,1)}), bf16[64,16,256]{2,1,0:T(8,128)(2,1)S(1)}, u32[]{:S(2)}, u32[]{:S(2)}) async-start(bf16[64,16,256]{2,1,0:T(8,128)(2,1)} %select_select_fusion.2), calls=%async_computation.1 | async-start | bytes 1048576 | tf_op jit(solution)/shard_map/all_to_all | solution.py:266
  52.8 52.8 %copy-start = (f32[32,2048]{1,0:T(8,128)S(1)}, f32[32,2048]{1,0:T(8,128)}, u32[]{:S(2)}) copy-start(f32[32,2048]{1,0:T(8,128)} %param.5) | copy-start | bytes 786436
  106.9 9.0 %copy-start.6 = (s32[8,6]{1,0:T(8,128)S(1)}, s32[8,6]{1,0:T(8,128)}, u32[]{:S(2)}) copy-start(s32[8,6]{1,0:T(8,128)} %param.3) | copy-start | bytes 580
  108.2 36.3 %all-to-all-start.2 = ((bf16[64,32,256]{2,1,0:T(8,128)(2,1)}), bf16[64,32,256]{2,1,0:T(8,128)(2,1)S(1)}, u32[]{:S(2)}, u32[]{:S(2)}) async-start(bf16[64,32,256]{2,1,0:T(8,128)(2,1)} %select_select_fusion.1), calls=%async_computation.2 | async-start | bytes 2097152 | tf_op jit(solution)/shard_map/all_to_all | solution.py:266
  145.6 10.0 %slice-start = ((s8[6291456]{0:T(1024)(128)(4,1)}), s8[2097152]{0:T(1024)(128)(4,1)S(1)}, s32[]{:S(2)}) async-start(s8[6291456]{0:T(1024)(128)(4,1)} %bitcast.192), calls=%async_computation.4 | async-start | bytes 4194304
  148.5 7.1 %slice-start.1 = ((s8[6291456]{0:T(1024)(128)(4,1)}), s8[4194304]{0:T(1024)(128)(4,1)S(1)}, s32[]{:S(2)}) async-start(s8[6291456]{0:T(1024)(128)(4,1)} %bitcast.192), calls=%async_computation.5 | async-start | bytes 8388608
  153.6 2.0 copy-start.2
  201.1 36.8 %all-to-all-start.3 = ((bf16[64,32,256]{2,1,0:T(8,128)(2,1)}), bf16[64,32,256]{2,1,0:T(8,128)(2,1)S(1)}, u32[]{:S(2)}, u32[]{:S(2)}) async-start(bf16[64,32,256]{2,1,0:T(8,128)(2,1)} %select_select_fusion), calls=%async_computation.3 | async-start | bytes 2097152 | tf_op jit(solution)/shard_map/all_to_all | solution.py:266
  239.0 10.0 %slice-start.2 = ((s8[6291456]{0:T(1024)(128)(4,1)}), s8[2097152]{0:T(1024)(128)(4,1)S(1)}, s32[]{:S(2)}) async-start(s8[6291456]{0:T(1024)(128)(4,1)} %bitcast.195), calls=%async_computation.6 | async-start | bytes 4194304
  241.9 7.1 %slice-start.3 = ((s8[6291456]{0:T(1024)(128)(4,1)}), s8[4194304]{0:T(1024)(128)(4,1)S(1)}, s32[]{:S(2)}) async-start(s8[6291456]{0:T(1024)(128)(4,1)} %bitcast.195), calls=%async_computation.7 | async-start | bytes 8388608
  241.9 7.1 %copy-start.3 = (f32[8,32,256]{2,1,0:T(8,128)S(1)}, f32[8,32,256]{2,1,0:T(8,128)}, u32[]{:S(2)}) copy-start(f32[8,32,256]{2,1,0:T(8,128)} %get-tuple-element.38) | copy-start | bytes 786436
  247.0 2.0 copy-start.1
  249.0 23.6 %copy-start.7 = (f32[1,128]{1,0:T(1,128)S(1)}, f32[1,128]{1,0:T(1,128)}, u32[]{:S(2)}) copy-start(f32[1,128]{1,0:T(1,128)} %shard_map.52) | copy-start | bytes 1540
  249.0 24.2 %copy-start.4 = (f32[8,32,256]{2,1,0:T(8,128)S(1)}, f32[8,32,256]{2,1,0:T(8,128)}, u32[]{:S(2)}) copy-start(f32[8,32,256]{2,1,0:T(8,128)} %get-tuple-element.38) | copy-start | bytes 786436

commit v12 on v10

--- a/solution.py
+++ b/solution.py
@@ -334,8 +334,12 @@
 
     def apply_partial(weights):
         their_w, far_w = both_ways(weights)
-        direct = jnp.einsum("sab,sob->soa", own_k, far_w, preferred_element_type=jnp.float32)
-        direct = jnp.sum(direct.reshape(block_rows, slot_width, outputs, block_len), axis=1)
+        direct = jnp.einsum(
+            "rkab,rkob->roa",
+            own_k.reshape(block_rows, slot_width, block_len, block_len),
+            far_w.reshape(block_rows, slot_width, outputs, block_len),
+            preferred_element_type=jnp.float32,
+        )
         mirror = jnp.einsum("eab,eoa->eob", in_k, their_w, preferred_element_type=jnp.float32)
         return direct + collect(mirror)
 

time: 262 us -> 259 us (0.989)
  local copies, waits for them, and re-layouts: 20 us -> 25.7 us
  waiting for transfers between devices: 76.8 us -> 71.9 us
  matrix products: 53 us -> 48.3 us
    slice x0 -> x1, local copies, waits for them, and re-layouts: none -> 6.06 us  [local(): own_k = kernel_bf[:slot_count]]
    all_to_all x3, waiting for transfers between devices: 69.1 us -> 64.2 us  [swap(): lax.all_to_all(parts, 'rows', split_axis=0, concat_axis=0, tiled=True)]
    dot_general x2, matrix products: 9.96 us -> 5.55 us  [apply_partial(): jnp.einsum('rkab,rkob->roa', own_k.reshape(block_rows, slot_width, block_...]
  transfers between devices with their start and end apart: 4 -> 4, of which waited for: 4 -> 4; matrix products, arithmetic and copies ran while one was open for 2% -> 4% of each run, Pallas kernels for 0% -> 0%
where the time goes in v12:
time: 259 us; the launch traced here: 258 us
  waiting for transfers between devices  71.9 us (28%)
  Pallas kernels  61.4 us (24%)
  matrix products  48.3 us (19%)
  starting transfers between devices  33.4 us (13%)
  local copies, waits for them, and re-layouts  25.7 us (10%)
  other arithmetic  14.5 us (6%)
  between operations  3.07 us (1%)
    all_to_all x3, waiting for transfers between devices, swap(): lax.all_to_all(parts, 'rows', split_axis=0, concat_axis=0, tiled=True)  64.2 us
    pallas_call x2, Pallas kernels, fused_sum(): pl.pallas_call(functools.partial(fused_kernel, n_rows, n_cols), out_shape...  41.3 us
    dot_general x1, matrix products, wendland(): jnp.einsum('nda,ndb->nab', left_f, right_f, precision=lax.Precision.HIGHEST)  28.5 us
    all_to_all x3, starting transfers between devices, swap(): lax.all_to_all(parts, 'rows', split_axis=0, concat_axis=0, tiled=True)  20.4 us
    pallas_call x2, Pallas kernels, allsum(): pl.pallas_call(functools.partial(allsum_kernel, axis, n), out_shape=jax.S...  20 us
    all_to_all x1, starting transfers between devices, local(): lax.all_to_all(request, 'rows', split_axis=0, concat_axis=0, tiled=True)  13 us
    dot_general x2, matrix products, apply_partial(): jnp.einsum('eab,eoa->eob', in_k, their_w, preferred_element_type=jnp.floa...  10.2 us
    all_to_all x1, waiting for transfers between devices, local(): lax.all_to_all(request, 'rows', split_axis=0, concat_axis=0, tiled=True)  7.7 us
  transfers between devices with their start and end apart: 4, of which 4 were waited for; matrix products, arithmetic and copies ran while one was open for 4% of the time, Pallas kernels for 0%

profile of v12, /device:TPU:1, one launch (start us, length us, event | category | flops | bytes accessed | tf_op | source)
XLA Modules:
  0.0 258.3 jit_solution(5302467714197117433)
XLA Ops:
  4.4 13.0 %all-to-all-start = ((s32[64,1,2]{2,1,0:T(1,128)}), s32[64,1,2]{2,1,0:T(1,128)S(1)}, u32[]{:S(2)}, u32[]{:S(2)}) async-start(s32[64,1,2]{2,1,0:T(1,128)} %copy.23), calls=%async_computation | async-start | bytes 65536 | tf_op jit(solution)/shard_map/all_to_all | solution.py:252
  18.9 7.7 %all-to-all-done = s32[64,1,2]{2,1,0:T(1,128)S(1)} async-done(((s32[64,1,2]{2,1,0:T(1,128)}), s32[64,1,2]{2,1,0:T(1,128)S(1)}, u32[]{:S(2)}, u32[]{:S(2)}) %all-to-all-start) | async-done | bytes 544 | tf_op jit(solution)/shard_map/all_to_all | solution.py:252
  28.4 4.7 %all-to-all-start.1 = ((bf16[64,16,256]{2,1,0:T(8,128)(2,1)}), bf16[64,16,256]{2,1,0:T(8,128)(2,1)S(1)}, u32[]{:S(2)}, u32[]{:S(2)}) async-start(bf16[64,16,256]{2,1,0:T(8,128)(2,1)} %select_select_fusion.2), calls=%async_computation.1 | async-start | bytes 1048576 | tf_op jit(solution)/shard_map/all_to_all | solution.py:264
  37.3 13.2 %all-to-all-done.1 = bf16[64,16,256]{2,1,0:T(8,128)(2,1)S(1)} async-done(((bf16[64,16,256]{2,1,0:T(8,128)(2,1)}), bf16[64,16,256]{2,1,0:T(8,128)(2,1)S(1)}, u32[]{:S(2)}, u32[]{:S(2)}) %all-to-all-start.1) | async-done | bytes 524320 | tf_op jit(solution)/shard_map/all_to_all | solution.py:264
  52.2 28.5 %fusion.70 = (f32[112,256]{1,0:T(8,128)S(1)}, f32[112,256]{1,0:T(8,128)S(1)}, bf16[112,256,256]{2,1,0:T(8,128)(2,1)}) fusion(bf16[64,16,256]{2,1,0:T(8,128)(2,1)S(1)} %gather_fusion.2, bf16[48,16,256]{2,1,0:T(8,128)(2,1)S(1)} %broadcast_select_fusion.4, bf16[64,16,256]{2,1,0:T(8,128)(2,1)S(1)} %get-tuple-element.44, ...), kind=kOutput, calls=%fused_computation.158 | convolution fusion | flops 353181696 | bytes 16973936 | tf_op jit(solution)/shard_map/while/body/eval_jaxpr/nda,ndb->nab/dot_general | solution.py:24
  81.6 6.4 %shard_map.50 = f32[16,128]{1,0:T(8,128)} custom-call(f32[16,128]{1,0:T(8,128)} %reshape_reshape_broadcast_in_dim.3.x_ref), custom_call_target="tpu_custom_call" | custom-call | tf_op jit(solution)/shard_map/pallas_call | solution.py:99
  90.0 1.3 select_select_fusion.1
  91.3 7.5 %all-to-all-start.2 = ((bf16[64,32,256]{2,1,0:T(8,128)(2,1)}), bf16[64,32,256]{2,1,0:T(8,128)(2,1)S(1)}, u32[]{:S(2)}, u32[]{:S(2)}) async-start(bf16[64,32,256]{2,1,0:T(8,128)(2,1)} %select_select_fusion.1), calls=%async_computation.2 | async-start | bytes 2097152 | tf_op jit(solution)/shard_map/all_to_all | solution.py:264
  98.8 6.1 %slice.74 = bf16[48,256,256]{2,1,0:T(8,128)(2,1)} slice(bf16[112,256,256]{2,1,0:T(8,128)(2,1)} %get-tuple-element.41), slice={[0:48], [0:256], [0:256]} | slice | bytes 12582912 | tf_op jit(solution)/shard_map/slice | solution.py:328
  104.9 22.5 %all-to-all-done.2 = bf16[64,32,256]{2,1,0:T(8,128)(2,1)S(1)} async-done(((bf16[64,32,256]{2,1,0:T(8,128)(2,1)}), bf16[64,32,256]{2,1,0:T(8,128)(2,1)S(1)}, u32[]{:S(2)}, u32[]{:S(2)}) %all-to-all-start.2) | async-done | bytes 1048608 | tf_op jit(solution)/shard_map/all_to_all | solution.py:264
  128.4 2.8 %gather_fusion.6 = bf16[48,32,256]{2,1,0:T(8,128)(2,1)} fusion(bf16[64,32,256]{2,1,0:T(8,128)(2,1)} %broadcast_select_fusion.1, s32[1024]{0:T(1024)S(1)} %pad_clamp_fusion), kind=kCustom, calls=%fused_computation.6 | custom fusion | bytes 1573056 | tf_op jit(solution)/shard_map/gather | solution.py:284
  131.2 5.1 %fusion.2 = f32[64,32,256]{2,1,0:T(8,128)S(1)} fusion(bf16[112,256,256]{2,1,0:T(8,128)(2,1)} %get-tuple-element.41, bf16[64,32,256]{2,1,0:T(8,128)(2,1)S(1)} %all-to-all-done.2, pred[64]{0:T(512)(128)(4,1)S(1)} %get-tuple-element.57), kind=kOutput, calls=%fused_computation.15 | convolution fusion | flops 268959744 | bytes 11534400 | tf_op jit(solution)/shard_map/eab,eoa->eob/dot_general | solution.py:343
  136.3 2.0 fusion.7
  138.3 2.8 %fusion.32 = (f32[32]{0:T(128)S(1)}, f32[32]{0:T(128)S(1)}, f32[8,32,256]{2,1,0:T(8,128)}) fusion(f32[4,8,8,256]{3,2,1,0:T(8,128)S(1)} %bitcast.204, f32[8,256]{1,0:T(8,128)S(1)} %sqrt.11, f32[8,32,256]{2,0,1:T(8,128)S(1)} %fusion.7, bf16[8,6,256,256]{3,2,1,0:T(8,128)(2,1)S(1)} %bitcast.194, bf16[8,6,32,256]{3,2,1,0:T(8,128)(2,1)S(1)} %bitcast.209, ...), kind=kOutput, calls=%fused_computation.61 | convolution fusion | flops 202112960 | bytes 7872816 | tf_op jit(solution)/shard_map/rkab,rkob->roa/dot_general | solution.py:337
  141.7 21.2 %shard_map.51 = (f32[256,256]{1,0:T(8,128)}, f32[1,128]{1,0:T(1,128)}) custom-call(f32[256,256]{1,0:T(8,128)} %bitcast.211, f32[1,128]{1,0:T(1,128)} %fusion.59.g_ref), custom_call_target="tpu_custom_call" | custom-call | tf_op jit(solution)/shard_map/pallas_call | solution.py:204
  165.3 13.6 %shard_map.52 = f32[1,128]{1,0:T(1,128)} custom-call(f32[1,128]{1,0:T(1,128)} %pad_bitcast_fusion.1.x_ref), custom_call_target="tpu_custom_call" | custom-call | tf_op jit(solution)/shard_map/pallas_call | solution.py:99
  179.5 1.8 multiply_convert_fusion
  183.8 8.2 %all-to-all-start.3 = ((bf16[64,32,256]{2,1,0:T(8,128)(2,1)}), bf16[64,32,256]{2,1,0:T(8,128)(2,1)S(1)}, u32[]{:S(2)}, u32[]{:S(2)}) async-start(bf16[64,32,256]{2,1,0:T(8,128)(2,1)} %select_select_fusion), calls=%async_computation.3 | async-start | bytes 2097152 | tf_op jit(solution)/shard_map/all_to_all | solution.py:264
  192.0 28.5 %all-to-all-done.3 = bf16[64,32,256]{2,1,0:T(8,128)(2,1)S(1)} async-done(((bf16[64,32,256]{2,1,0:T(8,128)(2,1)}), bf16[64,32,256]{2,1,0:T(8,128)(2,1)S(1)}, u32[]{:S(2)}, u32[]{:S(2)}) %all-to-all-start.3) | async-done | bytes 1048608 | tf_op jit(solution)/shard_map/all_to_all | solution.py:264
  221.7 2.8 %gather_fusion.9 = bf16[48,32,256]{2,1,0:T(8,128)(2,1)} fusion(bf16[64,32,256]{2,1,0:T(8,128)(2,1)} %broadcast_select_fusion, s32[1024]{0:T(1024)S(1)} %pad_clamp_fusion), kind=kCustom, calls=%fused_computation.9 | custom fusion | bytes 1573056 | tf_op jit(solution)/shard_map/gather | solution.py:284
  224.5 5.1 %fusion = f32[64,32,256]{2,1,0:T(8,128)S(1)} fusion(bf16[112,256,256]{2,1,0:T(8,128)(2,1)} %get-tuple-element.41, bf16[64,32,256]{2,1,0:T(8,128)(2,1)S(1)} %all-to-all-done.3, pred[64]{0:T(512)(128)(4,1)S(1)} %get-tuple-element.57), kind=kOutput, calls=%fused_computation.13 | convolution fusion | flops 268959744 | bytes 11534400 | tf_op jit(solution)/shard_map/eab,eoa->eob/dot_general | solution.py:343
  229.6 2.0 fusion.4
  231.6 2.8 %multiply_reduce_fusion.3 = (f32[32]{0:T(128)S(1)}, f32[32]{0:T(128)S(1)}, f32[8,32,256]{2,1,0:T(8,128)}) fusion(f32[8,32,256]{2,1,0:T(8,128)S(1)} %copy-done.3, f32[8,256]{1,0:T(8,128)S(1)} %sqrt.11, f32[8,32,256]{2,0,1:T(8,128)S(1)} %fusion.4, bf16[8,6,256,256]{3,2,1,0:T(8,128)(2,1)S(1)} %bitcast.197, bf16[8,6,32,256]{3,2,1,0:T(8,128)(2,1)S(1)} %bitcast.208, ...), kind=kOutput, calls=%fused_computation.70 | convolution fusion | flops 202112960 | bytes 7872816 | tf_op jit(solution)/shard_map/rkab,rkob->roa/dot_general | solution.py:337
  234.9 20.2 %shard_map.53 = (f32[256,256]{1,0:T(8,128)}, f32[1,128]{1,0:T(1,128)}) custom-call(f32[256,256]{1,0:T(8,128)} %bitcast.212, f32[1,128]{1,0:T(1,128)} %pad_bitcast_fusion.g_ref), custom_call_target="tpu_custom_call" | custom-call | tf_op jit(solution)/shard_map/pallas_call | solution.py:204
  (93 shorter events, 25.7 us)
Async XLA Ops:
  4.4 22.2 %all-to-all-start = ((s32[64,1,2]{2,1,0:T(1,128)}), s32[64,1,2]{2,1,0:T(1,128)S(1)}, u32[]{:S(2)}, u32[]{:S(2)}) async-start(s32[64,1,2]{2,1,0:T(1,128)} %copy.23), calls=%async_computation | async-start | bytes 65536 | tf_op jit(solution)/shard_map/all_to_all | solution.py:252
  28.4 22.1 %all-to-all-start.1 = ((bf16[64,16,256]{2,1,0:T(8,128)(2,1)}), bf16[64,16,256]{2,1,0:T(8,128)(2,1)S(1)}, u32[]{:S(2)}, u32[]{:S(2)}) async-start(bf16[64,16,256]{2,1,0:T(8,128)(2,1)} %select_select_fusion.2), calls=%async_computation.1 | async-start | bytes 1048576 | tf_op jit(solution)/shard_map/all_to_all | solution.py:264
  52.2 36.5 %copy-start = (f32[32,2048]{1,0:T(8,128)S(1)}, f32[32,2048]{1,0:T(8,128)}, u32[]{:S(2)}) copy-start(f32[32,2048]{1,0:T(8,128)} %param.5) | copy-start | bytes 786436
  80.8 18.0 %copy-start.6 = (s32[8,6]{1,0:T(8,128)S(1)}, s32[8,6]{1,0:T(8,128)}, u32[]{:S(2)}) copy-start(s32[8,6]{1,0:T(8,128)} %param.3) | copy-start | bytes 580
  91.3 36.1 %all-to-all-start.2 = ((bf16[64,32,256]{2,1,0:T(8,128)(2,1)}), bf16[64,32,256]{2,1,0:T(8,128)(2,1)S(1)}, u32[]{:S(2)}, u32[]{:S(2)}) async-start(bf16[64,32,256]{2,1,0:T(8,128)(2,1)} %select_select_fusion.1), calls=%async_computation.2 | async-start | bytes 2097152 | tf_op jit(solution)/shard_map/all_to_all | solution.py:264
  104.9 33.4 %slice-start = ((s8[6291456]{0:T(1024)(128)(4,1)}), s8[2097152]{0:T(1024)(128)(4,1)S(1)}, s32[]{:S(2)}) async-start(s8[6291456]{0:T(1024)(128)(4,1)} %bitcast.192), calls=%async_computation.4 | async-start | bytes 4194304
  131.2 7.1 %slice-start.1 = ((s8[6291456]{0:T(1024)(128)(4,1)}), s8[4194304]{0:T(1024)(128)(4,1)S(1)}, s32[]{:S(2)}) async-start(s8[6291456]{0:T(1024)(128)(4,1)} %bitcast.192), calls=%async_computation.5 | async-start | bytes 8388608
  131.2 7.1 %copy-start.2 = (bf16[48,32,256]{2,1,0:T(8,128)(2,1)S(1)}, bf16[48,32,256]{2,1,0:T(8,128)(2,1)}, u32[]{:S(2)}) copy-start(bf16[48,32,256]{2,1,0:T(8,128)(2,1)} %gather_fusion.6) | copy-start | bytes 2359300
  183.8 36.8 %all-to-all-start.3 = ((bf16[64,32,256]{2,1,0:T(8,128)(2,1)}), bf16[64,32,256]{2,1,0:T(8,128)(2,1)S(1)}, u32[]{:S(2)}, u32[]{:S(2)}) async-start(bf16[64,32,256]{2,1,0:T(8,128)(2,1)} %select_select_fusion), calls=%async_computation.3 | async-start | bytes 2097152 | tf_op jit(solution)/shard_map/all_to_all | solution.py:264
  192.0 39.5 %slice-start.2 = ((s8[6291456]{0:T(1024)(128)(4,1)}), s8[2097152]{0:T(1024)(128)(4,1)S(1)}, s32[]{:S(2)}) async-start(s8[6291456]{0:T(1024)(128)(4,1)} %bitcast.195), calls=%async_computation.6 | async-start | bytes 4194304
  224.4 7.1 %slice-start.3 = ((s8[6291456]{0:T(1024)(128)(4,1)}), s8[4194304]{0:T(1024)(128)(4,1)S(1)}, s32[]{:S(2)}) async-start(s8[6291456]{0:T(1024)(128)(4,1)} %bitcast.195), calls=%async_computation.7 | async-start | bytes 8388608
  224.4 7.1 %copy-start.1 = (bf16[48,32,256]{2,1,0:T(8,128)(2,1)S(1)}, bf16[48,32,256]{2,1,0:T(8,128)(2,1)}, u32[]{:S(2)}) copy-start(bf16[48,32,256]{2,1,0:T(8,128)(2,1)} %gather_fusion.9) | copy-start | bytes 2359300
  224.5 7.1 %copy-start.3 = (f32[8,32,256]{2,1,0:T(8,128)S(1)}, f32[8,32,256]{2,1,0:T(8,128)}, u32[]{:S(2)}) copy-start(f32[8,32,256]{2,1,0:T(8,128)} %get-tuple-element.38) | copy-start | bytes 786436
  224.5 30.6 %copy-start.7 = (f32[1,128]{1,0:T(1,128)S(1)}, f32[1,128]{1,0:T(1,128)}, u32[]{:S(2)}) copy-start(f32[1,128]{1,0:T(1,128)} %shard_map.52) | copy-start | bytes 1540
  229.5 26.2 %copy-start.4 = (f32[8,32,256]{2,1,0:T(8,128)S(1)}, f32[8,32,256]{2,1,0:T(8,128)}, u32[]{:S(2)}) copy-start(f32[8,32,256]{2,1,0:T(8,128)} %get-tuple-element.38) | copy-start | bytes 786436
  229.6 26.2 %copy-start.5 = (f32[256,256]{1,0:T(8,128)S(1)}, f32[256,256]{1,0:T(8,128)}, u32[]{:S(2)}) copy-start(f32[256,256]{1,0:T(8,128)} %get-tuple-element.28) | copy-start | bytes 786436

commit v13 on v12

--- a/solution.py
+++ b/solution.py
@@ -248,10 +248,16 @@
     asking_row = jnp.full((row_count,), -1, jnp.int32).at[place_at].set(slot_row, mode="drop")
     ask_live = asking_row >= 0
     ask_row = jnp.maximum(asking_row, 0)
-    request = jnp.stack([wanted, asking_row], axis=1).reshape(row_count, 1, 2)
-    incoming = lax.all_to_all(request, "rows", split_axis=0, concat_axis=0, tiled=True).reshape(
-        row_count, 2
+    own_x = points.reshape(coord_dim, block_rows, block_len).transpose(1, 0, 2)
+    asked_x = jnp.where(ask_live[:, None, None], own_x[ask_row], jnp.zeros((), own_x.dtype))
+    request = jnp.zeros((row_count, coord_dim, 128), own_x.dtype)
+    request = request.at[:, 0, 0].set(wanted.astype(own_x.dtype))
+    request = request.at[:, 0, 1].set(asking_row.astype(own_x.dtype))
+    first_swap = lax.all_to_all(
+        jnp.concatenate([asked_x, request], axis=2), "rows", split_axis=0, concat_axis=0, tiled=True
     )
+    their_x = first_swap[:, :, :block_len]
+    incoming = first_swap[:, 0, block_len:block_len + 2].astype(jnp.int32)
     in_live = incoming[:, 0] >= 0
     in_idx = jnp.maximum(incoming[:, 0], 0)
     their_row = jnp.arange(row_count, dtype=jnp.int32) * block_rows + jnp.maximum(incoming[:, 1], 0)
@@ -297,38 +303,16 @@
     def global_sum(values):
         return allsum(values, "rows", 0)
 
-    own_x = points.reshape(coord_dim, block_rows, block_len).transpose(1, 0, 2)
-    their_x, far_x = both_ways(own_x)
-    left_x = jnp.concatenate([own_x[slot_row], their_x], axis=0)
-    right_x = jnp.concatenate([far_x, own_x[in_idx]], axis=0)
-    pair_live = jnp.concatenate([is_live, in_off], axis=0)
-    pair_count = slot_count + row_count
-    chunk = 112
-    pad = (-pair_count) % chunk
-    left_x = jnp.pad(left_x, ((0, pad), (0, 0), (0, 0)))
-    right_x = jnp.pad(right_x, ((0, pad), (0, 0), (0, 0)))
-    pair_live = jnp.pad(pair_live, (0, pad))
-
-    def pair_step(pieces):
-        lx, rx, live = pieces
+    far_x = per_slot(swap(served_part(own_x)))
+
+    def pair_pass(lx, rx, live):
         values = jnp.where(live[:, None, None], wendland(lx, rx), 0.0)
         return (values.astype(jnp.bfloat16), jnp.sum(values, axis=2), jnp.sum(values, axis=1))
 
-    kernel_bf, row_sums, col_sums = lax.map(
-        pair_step,
-        (
-            left_x.reshape(-1, chunk, coord_dim, block_len),
-            right_x.reshape(-1, chunk, coord_dim, block_len),
-            pair_live.reshape(-1, chunk),
-        ),
-    )
-    kernel_bf = kernel_bf.reshape(-1, block_len, block_len)
-    row_sums = row_sums.reshape(-1, block_len)
-    col_sums = col_sums.reshape(-1, block_len)
-    own_k = kernel_bf[:slot_count]
-    in_k = kernel_bf[slot_count:pair_count]
-    degree_direct = jnp.sum(row_sums[:slot_count].reshape(block_rows, slot_width, block_len), axis=1)
-    degree_mirror = collect(col_sums[slot_count:pair_count])
+    in_k, _, in_col_sums = pair_pass(their_x, own_x[in_idx], in_off)
+    own_k, own_row_sums, _ = pair_pass(own_x[slot_row], far_x, is_live)
+    degree_direct = jnp.sum(own_row_sums.reshape(block_rows, slot_width, block_len), axis=1)
+    degree_mirror = collect(in_col_sums)
     degree_part = (degree_direct + degree_mirror)[:, None, :]
     inv_root = 1.0 / jnp.sqrt(1.0 + column_total(degree_part))
 

time: 259 us -> 265 us (1.023)
  waiting for transfers between devices: 71.9 us -> 78.6 us
  local copies, waits for them, and re-layouts: 25.7 us -> 20.7 us
  starting transfers between devices: 33.4 us -> 36.9 us
  matrix products: 48.3 us -> 51 us
    all_to_all x1, waiting for transfers between devices: 7.7 us -> 22.2 us  [local(): lax.all_to_all(jnp.concatenate([asked_x, request], axis=2), 'rows', split...]
    all_to_all x3, waiting for transfers between devices: 64.2 us -> 56.4 us  [swap(): lax.all_to_all(parts, 'rows', split_axis=0, concat_axis=0, tiled=True)]
    scatter x0 -> x2, local copies, waits for them, and re-layouts: none -> 6.18 us  [the longest x1 6.12 us: local(): request = request.at[:, 0, 1].set(asking_row.astype(own_x.dtype))]
    slice x2 -> x1, local copies, waits for them, and re-layouts: 6.07 us -> 0.02 us  [local(): incoming = first_swap[:, 0, block_len:block_len + 2].astype(jnp.int32)]
    gather x3, local copies, waits for them, and re-layouts: 6.15 us -> 1.82 us  [per_slot(): chosen = got[pick_at]]
    dot_general x2, matrix products: 5.55 us -> 9.64 us  [apply_partial(): jnp.einsum('rkab,rkob->roa', own_k.reshape(block_rows, slot_width, block_...]
    all_to_all x3, starting transfers between devices: 20.4 us -> 23.9 us  [swap(): lax.all_to_all(parts, 'rows', split_axis=0, concat_axis=0, tiled=True)]
    dot_general x1 -> x2, matrix products: 28.5 us -> 27.4 us  [wendland(): jnp.einsum('nda,ndb->nab', left_f, right_f, precision=lax.Precision.HIGHEST)]
  transfers between devices with their start and end apart: 4 -> 4, of which waited for: 4 -> 4; matrix products, arithmetic and copies ran while one was open for 4% -> 6% of each run, Pallas kernels for 0% -> 0%
where the time goes in v13:
time: 265 us; the launch traced here: 264 us
  waiting for transfers between devices  78.6 us (30%)
  Pallas kernels  61.4 us (23%)
  matrix products  51 us (19%)
  starting transfers between devices  36.9 us (14%)
  local copies, waits for them, and re-layouts  20.7 us (8%)
  other arithmetic  12.8 us (5%)
  between operations  3.03 us (1%)
    all_to_all x3, waiting for transfers between devices, swap(): lax.all_to_all(parts, 'rows', split_axis=0, concat_axis=0, tiled=True)  56.4 us
    pallas_call x2, Pallas kernels, fused_sum(): pl.pallas_call(functools.partial(fused_kernel, n_rows, n_cols), out_shape...  41.3 us
    dot_general x2, matrix products, wendland(): jnp.einsum('nda,ndb->nab', left_f, right_f, precision=lax.Precision.HIGHEST)  27.4 us
    all_to_all x3, starting transfers between devices, swap(): lax.all_to_all(parts, 'rows', split_axis=0, concat_axis=0, tiled=True)  23.9 us
    all_to_all x1, waiting for transfers between devices, local(): lax.all_to_all(jnp.concatenate([asked_x, request], axis=2), 'rows', split...  22.2 us
    pallas_call x2, Pallas kernels, allsum(): pl.pallas_call(functools.partial(allsum_kernel, axis, n), out_shape=jax.S...  20 us
    all_to_all x1, starting transfers between devices, local(): lax.all_to_all(jnp.concatenate([asked_x, request], axis=2), 'rows', split...  13 us
    dot_general x2, matrix products, apply_partial(): jnp.einsum('eab,eoa->eob', in_k, their_w, preferred_element_type=jnp.floa...  9.94 us
  transfers between devices with their start and end apart: 4, of which 4 were waited for; matrix products, arithmetic and copies ran while one was open for 6% of the time, Pallas kernels for 0%

profile of v13, /device:TPU:1, one launch (start us, length us, event | category | flops | bytes accessed | tf_op | source)
XLA Modules:
  0.0 264.4 jit_solution(2704724004543589398)
XLA Ops:
  6.2 6.1 %scatter.27 = bf16[64,16,128]{2,1,0:T(8,128)(2,1)S(1)} dynamic-update-slice(bf16[64,16,128]{2,1,0:T(8,128)(2,1)S(1)} %scatter.26, bf16[64,1,1]{2,1,0:T(2,128)(2,1)S(1)} %copy.68, s32[]{:T(128)} %constant.110.clone.1, s32[]{:T(128)} %bitcast.6, s32[]{:T(128)} %bitcast.7) | dynamic-update-slice | bytes 260 | tf_op jit(solution)/shard_map/scatter | solution.py:255
  13.3 13.0 %all-to-all-start = ((bf16[64,16,384]{2,1,0:T(8,128)(2,1)}), bf16[64,16,384]{2,1,0:T(8,128)(2,1)S(1)}, u32[]{:S(2)}, u32[]{:S(2)}) async-start(bf16[64,16,384]{2,1,0:T(8,128)(2,1)} %pad_maximum_fusion), calls=%async_computation | async-start | bytes 1572864 | tf_op jit(solution)/shard_map/all_to_all | solution.py:256
  27.1 22.2 %all-to-all-done = bf16[64,16,384]{2,1,0:T(8,128)(2,1)S(1)} async-done(((bf16[64,16,384]{2,1,0:T(8,128)(2,1)}), bf16[64,16,384]{2,1,0:T(8,128)(2,1)S(1)}, u32[]{:S(2)}, u32[]{:S(2)}) %all-to-all-start) | async-done | bytes 786464 | tf_op jit(solution)/shard_map/all_to_all | solution.py:256
  51.2 6.2 %all-to-all-start.1 = ((bf16[64,16,256]{2,1,0:T(8,128)(2,1)}), bf16[64,16,256]{2,1,0:T(8,128)(2,1)S(1)}, u32[]{:S(2)}, u32[]{:S(2)}) async-start(bf16[64,16,256]{2,1,0:T(8,128)(2,1)} %broadcast_select_fusion.2), calls=%async_computation.1 | async-start | bytes 1048576 | tf_op jit(solution)/shard_map/all_to_all | solution.py:270
  57.7 15.1 %fusion.73 = (f32[64,256]{1,0:T(8,128)S(1)}, bf16[64,256,256]{2,1,0:T(8,128)(2,1)}) fusion(bf16[64,16,256]{2,1,0:T(8,128)(2,1)S(1)} %gather_fusion.2, bf16[64,16,384]{2,1,0:T(8,128)(2,1)S(1)} %all-to-all-done, f32[64,256]{1,0:T(8,128)S(1)} %multiply_reduce_fusion, f32[64,256]{1,0:T(8,128)S(1)} %multiply_reduce_fusion.1, pred[64]{0:T(512)(128)(4,1)S(1)} %compare_and_fusion), kind=kOutput, calls=%fused_computation.160 | convolution fusion | flops 197115904 | bytes 9634304 | tf_op jit(solution)/shard_map/nda,ndb->nab/dot_general | solution.py:24
  72.8 2.0 all-to-all-done.1
  75.6 12.3 %fusion.71 = (bf16[48,256,256]{1,2,0:T(8,128)(2,1)}, f32[48,256]{1,0:T(8,128)S(1)}) fusion(bf16[48,16,256]{2,1,0:T(8,128)(2,1)S(1)} %gather_fusion, bf16[48,16,256]{2,1,0:T(8,128)(2,1)S(1)} %gather_fusion.3, pred[48]{0:T(512)(128)(4,1)S(1)} %broadcast_compare_fusion.2, f32[48,256]{1,0:T(8,128)S(1)} %multiply_reduce_fusion.2, ...), kind=kOutput, calls=%fused_computation.158 | convolution fusion | flops 148033536 | bytes 7225392 | tf_op jit(solution)/shard_map/nda,ndb->nab/dot_general | solution.py:24
  88.7 6.4 %shard_map.50 = f32[16,128]{1,0:T(8,128)} custom-call(f32[16,128]{1,0:T(8,128)} %reshape_reshape_broadcast_in_dim.3.x_ref), custom_call_target="tpu_custom_call" | custom-call | tf_op jit(solution)/shard_map/pallas_call | solution.py:99
  97.1 1.3 select_select_fusion.1
  98.3 9.5 %all-to-all-start.2 = ((bf16[64,32,256]{2,1,0:T(8,128)(2,1)}), bf16[64,32,256]{2,1,0:T(8,128)(2,1)S(1)}, u32[]{:S(2)}, u32[]{:S(2)}) async-start(bf16[64,32,256]{2,1,0:T(8,128)(2,1)} %select_select_fusion.1), calls=%async_computation.2 | async-start | bytes 2097152 | tf_op jit(solution)/shard_map/all_to_all | solution.py:270
  110.5 25.9 %all-to-all-done.2 = bf16[64,32,256]{2,1,0:T(8,128)(2,1)S(1)} async-done(((bf16[64,32,256]{2,1,0:T(8,128)(2,1)}), bf16[64,32,256]{2,1,0:T(8,128)(2,1)S(1)}, u32[]{:S(2)}, u32[]{:S(2)}) %all-to-all-start.2) | async-done | bytes 1048608 | tf_op jit(solution)/shard_map/all_to_all | solution.py:270
  136.4 5.0 %fusion.2 = f32[64,32,256]{2,1,0:T(8,128)S(1)} fusion(bf16[64,256,256]{2,1,0:T(8,128)(2,1)} %get-tuple-element.56, bf16[64,32,256]{2,1,0:T(8,128)(2,1)S(1)} %all-to-all-done.2, pred[64]{0:T(512)(128)(4,1)S(1)} %iota_compare_fusion.1), kind=kOutput, calls=%fused_computation.16 | convolution fusion | flops 268959744 | bytes 11534400 | tf_op jit(solution)/shard_map/eab,eoa->eob/dot_general | solution.py:327
  141.4 2.0 fusion.7
  144.1 4.8 %fusion.33 = (f32[32]{0:T(128)S(1)}, f32[32]{0:T(128)S(1)}, f32[8,32,256]{2,1,0:T(8,128)}) fusion(f32[4,8,8,256]{3,2,1,0:T(8,128)S(1)} %bitcast.202, f32[8,256]{1,0:T(8,128)S(1)} %sqrt.14, f32[8,32,256]{2,0,1:T(8,128)S(1)} %fusion.7, bf16[8,6,256,256]{2,3,1,0:T(8,128)(2,1)} %bitcast.197, bf16[8,6,32,256]{3,2,1,0:T(8,128)(2,1)S(1)} %bitcast.207, ...), kind=kOutput, calls=%fused_computation.63 | convolution fusion | flops 202112960 | bytes 7872816 | tf_op jit(solution)/shard_map/rkab,rkob->roa/dot_general | solution.py:321
  149.5 21.2 %shard_map.51 = (f32[256,256]{1,0:T(8,128)}, f32[1,128]{1,0:T(1,128)}) custom-call(f32[256,256]{1,0:T(8,128)} %bitcast.209, f32[1,128]{1,0:T(1,128)} %fusion.59.g_ref), custom_call_target="tpu_custom_call" | custom-call | tf_op jit(solution)/shard_map/pallas_call | solution.py:204
  171.5 1.2 multiply_reduce_fusion.6
  173.2 13.6 %shard_map.52 = f32[1,128]{1,0:T(1,128)} custom-call(f32[1,128]{1,0:T(1,128)} %pad_bitcast_fusion.1.x_ref), custom_call_target="tpu_custom_call" | custom-call | tf_op jit(solution)/shard_map/pallas_call | solution.py:99
  189.9 1.3 select_select_fusion
  191.1 8.2 %all-to-all-start.3 = ((bf16[64,32,256]{2,1,0:T(8,128)(2,1)}), bf16[64,32,256]{2,1,0:T(8,128)(2,1)S(1)}, u32[]{:S(2)}, u32[]{:S(2)}) async-start(bf16[64,32,256]{2,1,0:T(8,128)(2,1)} %select_select_fusion), calls=%async_computation.3 | async-start | bytes 2097152 | tf_op jit(solution)/shard_map/all_to_all | solution.py:270
  199.4 28.5 %all-to-all-done.3 = bf16[64,32,256]{2,1,0:T(8,128)(2,1)S(1)} async-done(((bf16[64,32,256]{2,1,0:T(8,128)(2,1)}), bf16[64,32,256]{2,1,0:T(8,128)(2,1)S(1)}, u32[]{:S(2)}, u32[]{:S(2)}) %all-to-all-start.3) | async-done | bytes 1048608 | tf_op jit(solution)/shard_map/all_to_all | solution.py:270
  227.9 5.0 %fusion = f32[64,32,256]{2,1,0:T(8,128)S(1)} fusion(bf16[64,256,256]{2,1,0:T(8,128)(2,1)} %get-tuple-element.56, bf16[64,32,256]{2,1,0:T(8,128)(2,1)S(1)} %all-to-all-done.3, pred[64]{0:T(512)(128)(4,1)S(1)} %iota_compare_fusion.1), kind=kOutput, calls=%fused_computation.14 | convolution fusion | flops 268959744 | bytes 11534400 | tf_op jit(solution)/shard_map/eab,eoa->eob/dot_general | solution.py:327
  232.9 2.0 fusion.4
  235.6 4.8 %multiply_reduce_fusion.5 = (f32[32]{0:T(128)S(1)}, f32[32]{0:T(128)S(1)}, f32[8,32,256]{2,1,0:T(8,128)}) fusion(f32[8,32,256]{2,1,0:T(8,128)S(1)} %get-tuple-element.39, f32[8,256]{1,0:T(8,128)S(1)} %sqrt.14, f32[8,32,256]{2,0,1:T(8,128)S(1)} %fusion.4, bf16[8,6,256,256]{2,3,1,0:T(8,128)(2,1)} %bitcast.198, bf16[8,6,32,256]{3,2,1,0:T(8,128)(2,1)S(1)} %bitcast.206, ...), kind=kOutput, calls=%fused_computation.72 | convolution fusion | flops 202112960 | bytes 7872816 | tf_op jit(solution)/shard_map/rkab,rkob->roa/dot_general | solution.py:321
  241.0 20.2 %shard_map.53 = (f32[256,256]{1,0:T(8,128)}, f32[1,128]{1,0:T(1,128)}) custom-call(f32[256,256]{1,0:T(8,128)} %bitcast.210, f32[1,128]{1,0:T(1,128)} %pad_bitcast_fusion.g_ref), custom_call_target="tpu_custom_call" | custom-call | tf_op jit(solution)/shard_map/pallas_call | solution.py:204
  (80 shorter events, 23.8 us)
Async XLA Ops:
  13.3 36.0 %all-to-all-start = ((bf16[64,16,384]{2,1,0:T(8,128)(2,1)}), bf16[64,16,384]{2,1,0:T(8,128)(2,1)S(1)}, u32[]{:S(2)}, u32[]{:S(2)}) async-start(bf16[64,16,384]{2,1,0:T(8,128)(2,1)} %pad_maximum_fusion), calls=%async_computation | async-start | bytes 1572864 | tf_op jit(solution)/shard_map/all_to_all | solution.py:256
  51.2 23.5 %all-to-all-start.1 = ((bf16[64,16,256]{2,1,0:T(8,128)(2,1)}), bf16[64,16,256]{2,1,0:T(8,128)(2,1)S(1)}, u32[]{:S(2)}, u32[]{:S(2)}) async-start(bf16[64,16,256]{2,1,0:T(8,128)(2,1)} %broadcast_select_fusion.2), calls=%async_computation.1 | async-start | bytes 1048576 | tf_op jit(solution)/shard_map/all_to_all | solution.py:270
  75.6 20.2 %copy-start = (f32[32,2048]{1,0:T(8,128)S(1)}, f32[32,2048]{1,0:T(8,128)}, u32[]{:S(2)}) copy-start(f32[32,2048]{1,0:T(8,128)} %param.9) | copy-start | bytes 786436
  87.9 20.0 %copy-start.2 = (s32[8,6]{1,0:T(8,128)S(1)}, s32[8,6]{1,0:T(8,128)}, u32[]{:S(2)}) copy-start(s32[8,6]{1,0:T(8,128)} %param.7) | copy-start | bytes 580
  98.3 38.1 %all-to-all-start.2 = ((bf16[64,32,256]{2,1,0:T(8,128)(2,1)}), bf16[64,32,256]{2,1,0:T(8,128)(2,1)S(1)}, u32[]{:S(2)}, u32[]{:S(2)}) async-start(bf16[64,32,256]{2,1,0:T(8,128)(2,1)} %select_select_fusion.1), calls=%async_computation.2 | async-start | bytes 2097152 | tf_op jit(solution)/shard_map/all_to_all | solution.py:270
  191.1 36.8 %all-to-all-start.3 = ((bf16[64,32,256]{2,1,0:T(8,128)(2,1)}), bf16[64,32,256]{2,1,0:T(8,128)(2,1)S(1)}, u32[]{:S(2)}, u32[]{:S(2)}) async-start(bf16[64,32,256]{2,1,0:T(8,128)(2,1)} %select_select_fusion), calls=%async_computation.3 | async-start | bytes 2097152 | tf_op jit(solution)/shard_map/all_to_all | solution.py:270
  232.9 28.3 %copy-start.3 = (f32[1,128]{1,0:T(1,128)S(1)}, f32[1,128]{1,0:T(1,128)}, u32[]{:S(2)}) copy-start(f32[1,128]{1,0:T(1,128)} %shard_map.52) | copy-start | bytes 1540
  232.9 29.0 %copy-start.1 = (f32[256,256]{1,0:T(8,128)S(1)}, f32[256,256]{1,0:T(8,128)}, u32[]{:S(2)}) copy-start(f32[256,256]{1,0:T(8,128)} %get-tuple-element.31) | copy-start | bytes 786436

commit v14 on v13

--- a/solution.py
+++ b/solution.py
@@ -250,9 +250,10 @@
     ask_row = jnp.maximum(asking_row, 0)
     own_x = points.reshape(coord_dim, block_rows, block_len).transpose(1, 0, 2)
     asked_x = jnp.where(ask_live[:, None, None], own_x[ask_row], jnp.zeros((), own_x.dtype))
-    request = jnp.zeros((row_count, coord_dim, 128), own_x.dtype)
-    request = request.at[:, 0, 0].set(wanted.astype(own_x.dtype))
-    request = request.at[:, 0, 1].set(asking_row.astype(own_x.dtype))
+    lane = lax.broadcasted_iota(jnp.int32, (row_count, coord_dim, 128), 2)
+    sublane = lax.broadcasted_iota(jnp.int32, (row_count, coord_dim, 128), 1)
+    request = jnp.where(lane == 0, wanted[:, None, None], asking_row[:, None, None])
+    request = jnp.where((sublane == 0) & (lane < 2), request, 0).astype(own_x.dtype)
     first_swap = lax.all_to_all(
         jnp.concatenate([asked_x, request], axis=2), "rows", split_axis=0, concat_axis=0, tiled=True
     )

time: 265 us -> 259 us (0.977)
  local copies, waits for them, and re-layouts: 20.7 us -> 13.7 us
    scatter x2 -> x0, local copies, waits for them, and re-layouts: 6.18 us -> none  [the longest x1 6.12 us: local(): request = request.at[:, 0, 1].set(asking_row.astype(own_x.dtype))]
where the time goes in v14:
time: 259 us; the launch traced here: 258 us
  waiting for transfers between devices  78.6 us (30%)
  Pallas kernels  61.4 us (24%)
  matrix products  51 us (20%)
  starting transfers between devices  36.9 us (14%)
  local copies, waits for them, and re-layouts  13.7 us (5%)
  other arithmetic  13 us (5%)
  between operations  3.03 us (1%)
    all_to_all x3, waiting for transfers between devices, swap(): lax.all_to_all(parts, 'rows', split_axis=0, concat_axis=0, tiled=True)  56.4 us
    pallas_call x2, Pallas kernels, fused_sum(): pl.pallas_call(functools.partial(fused_kernel, n_rows, n_cols), out_shape...  41.3 us
    dot_general x2, matrix products, wendland(): jnp.einsum('nda,ndb->nab', left_f, right_f, precision=lax.Precision.HIGHEST)  27.4 us
    all_to_all x3, starting transfers between devices, swap(): lax.all_to_all(parts, 'rows', split_axis=0, concat_axis=0, tiled=True)  23.9 us
    all_to_all x1, waiting for transfers between devices, local(): lax.all_to_all(jnp.concatenate([asked_x, request], axis=2), 'rows', split...  22.2 us
    pallas_call x2, Pallas kernels, allsum(): pl.pallas_call(functools.partial(allsum_kernel, axis, n), out_shape=jax.S...  20.1 us
    all_to_all x1, starting transfers between devices, local(): lax.all_to_all(jnp.concatenate([asked_x, request], axis=2), 'rows', split...  13 us
    dot_general x2, matrix products, apply_partial(): jnp.einsum('eab,eoa->eob', in_k, their_w, preferred_element_type=jnp.floa...  9.94 us
  transfers between devices with their start and end apart: 4, of which 4 were waited for; matrix products, arithmetic and copies ran while one was open for 6% of the time, Pallas kernels for 0%

profile of v14, /device:TPU:1, one launch (start us, length us, event | category | flops | bytes accessed | tf_op | source)
XLA Modules:
  0.0 257.6 jit_solution(13916792596892019895)
XLA Ops:
  6.5 13.0 %all-to-all-start = ((bf16[64,16,384]{2,1,0:T(8,128)(2,1)}), bf16[64,16,384]{2,1,0:T(8,128)(2,1)S(1)}, u32[]{:S(2)}, u32[]{:S(2)}) async-start(bf16[64,16,384]{2,1,0:T(8,128)(2,1)} %pad_maximum_fusion), calls=%async_computation | async-start | bytes 1572864 | tf_op jit(solution)/shard_map/all_to_all | solution.py:257
  20.3 22.2 %all-to-all-done = bf16[64,16,384]{2,1,0:T(8,128)(2,1)S(1)} async-done(((bf16[64,16,384]{2,1,0:T(8,128)(2,1)}), bf16[64,16,384]{2,1,0:T(8,128)(2,1)S(1)}, u32[]{:S(2)}, u32[]{:S(2)}) %all-to-all-start) | async-done | bytes 786464 | tf_op jit(solution)/shard_map/all_to_all | solution.py:257
  44.5 6.2 %all-to-all-start.1 = ((bf16[64,16,256]{2,1,0:T(8,128)(2,1)}), bf16[64,16,256]{2,1,0:T(8,128)(2,1)S(1)}, u32[]{:S(2)}, u32[]{:S(2)}) async-start(bf16[64,16,256]{2,1,0:T(8,128)(2,1)} %broadcast_select_fusion.2), calls=%async_computation.1 | async-start | bytes 1048576 | tf_op jit(solution)/shard_map/all_to_all | solution.py:271
  50.9 15.1 %fusion.72 = (f32[64,256]{1,0:T(8,128)S(1)}, bf16[64,256,256]{2,1,0:T(8,128)(2,1)}) fusion(bf16[64,16,256]{2,1,0:T(8,128)(2,1)S(1)} %gather_fusion.2, bf16[64,16,384]{2,1,0:T(8,128)(2,1)S(1)} %all-to-all-done, f32[64,256]{1,0:T(8,128)S(1)} %multiply_reduce_fusion, f32[64,256]{1,0:T(8,128)S(1)} %multiply_reduce_fusion.1, pred[64]{0:T(512)(128)(4,1)S(1)} %compare_and_fusion), kind=kOutput, calls=%fused_computation.161 | convolution fusion | flops 197115904 | bytes 9634304 | tf_op jit(solution)/shard_map/nda,ndb->nab/dot_general | solution.py:24
  66.0 2.0 all-to-all-done.1
  68.8 12.3 %fusion.71 = (bf16[48,256,256]{1,2,0:T(8,128)(2,1)}, f32[48,256]{1,0:T(8,128)S(1)}) fusion(bf16[48,16,256]{2,1,0:T(8,128)(2,1)S(1)} %gather_fusion, bf16[48,16,256]{2,1,0:T(8,128)(2,1)S(1)} %gather_fusion.3, pred[48]{0:T(512)(128)(4,1)S(1)} %broadcast_compare_fusion.2, f32[48,256]{1,0:T(8,128)S(1)} %multiply_reduce_fusion.2, ...), kind=kOutput, calls=%fused_computation.160 | convolution fusion | flops 148033536 | bytes 7225392 | tf_op jit(solution)/shard_map/nda,ndb->nab/dot_general | solution.py:24
  81.9 6.4 %shard_map.50 = f32[16,128]{1,0:T(8,128)} custom-call(f32[16,128]{1,0:T(8,128)} %reshape_reshape_broadcast_in_dim.3.x_ref), custom_call_target="tpu_custom_call" | custom-call | tf_op jit(solution)/shard_map/pallas_call | solution.py:99
  90.3 1.3 select_select_fusion.1
  91.6 9.5 %all-to-all-start.2 = ((bf16[64,32,256]{2,1,0:T(8,128)(2,1)}), bf16[64,32,256]{2,1,0:T(8,128)(2,1)S(1)}, u32[]{:S(2)}, u32[]{:S(2)}) async-start(bf16[64,32,256]{2,1,0:T(8,128)(2,1)} %select_select_fusion.1), calls=%async_computation.2 | async-start | bytes 2097152 | tf_op jit(solution)/shard_map/all_to_all | solution.py:271
  103.7 25.9 %all-to-all-done.2 = bf16[64,32,256]{2,1,0:T(8,128)(2,1)S(1)} async-done(((bf16[64,32,256]{2,1,0:T(8,128)(2,1)}), bf16[64,32,256]{2,1,0:T(8,128)(2,1)S(1)}, u32[]{:S(2)}, u32[]{:S(2)}) %all-to-all-start.2) | async-done | bytes 1048608 | tf_op jit(solution)/shard_map/all_to_all | solution.py:271
  129.6 5.0 %fusion.2 = f32[64,32,256]{2,1,0:T(8,128)S(1)} fusion(bf16[64,256,256]{2,1,0:T(8,128)(2,1)} %get-tuple-element.28, bf16[64,32,256]{2,1,0:T(8,128)(2,1)S(1)} %all-to-all-done.2, pred[64]{0:T(512)(128)(4,1)S(1)} %iota_compare_fusion.1), kind=kOutput, calls=%fused_computation.16 | convolution fusion | flops 268959744 | bytes 11534400 | tf_op jit(solution)/shard_map/eab,eoa->eob/dot_general | solution.py:328
  134.6 2.0 fusion.7
  137.3 4.8 %fusion.33 = (f32[32]{0:T(128)S(1)}, f32[32]{0:T(128)S(1)}, f32[8,32,256]{2,1,0:T(8,128)}) fusion(f32[4,8,8,256]{3,2,1,0:T(8,128)S(1)} %bitcast.196, f32[8,256]{1,0:T(8,128)S(1)} %sqrt.14, f32[8,32,256]{2,0,1:T(8,128)S(1)} %fusion.7, bf16[8,6,256,256]{2,3,1,0:T(8,128)(2,1)} %bitcast.191, bf16[8,6,32,256]{3,2,1,0:T(8,128)(2,1)S(1)} %bitcast.201, ...), kind=kOutput, calls=%fused_computation.64 | convolution fusion | flops 202112960 | bytes 7872816 | tf_op jit(solution)/shard_map/rkab,rkob->roa/dot_general | solution.py:322
  142.8 21.2 %shard_map.51 = (f32[256,256]{1,0:T(8,128)}, f32[1,128]{1,0:T(1,128)}) custom-call(f32[256,256]{1,0:T(8,128)} %bitcast.203, f32[1,128]{1,0:T(1,128)} %fusion.59.g_ref), custom_call_target="tpu_custom_call" | custom-call | tf_op jit(solution)/shard_map/pallas_call | solution.py:204
  164.7 1.2 multiply_reduce_fusion.6
  166.4 13.6 %shard_map.52 = f32[1,128]{1,0:T(1,128)} custom-call(f32[1,128]{1,0:T(1,128)} %pad_bitcast_fusion.1.x_ref), custom_call_target="tpu_custom_call" | custom-call | tf_op jit(solution)/shard_map/pallas_call | solution.py:99
  183.1 1.3 select_select_fusion
  184.4 8.2 %all-to-all-start.3 = ((bf16[64,32,256]{2,1,0:T(8,128)(2,1)}), bf16[64,32,256]{2,1,0:T(8,128)(2,1)S(1)}, u32[]{:S(2)}, u32[]{:S(2)}) async-start(bf16[64,32,256]{2,1,0:T(8,128)(2,1)} %select_select_fusion), calls=%async_computation.3 | async-start | bytes 2097152 | tf_op jit(solution)/shard_map/all_to_all | solution.py:271
  192.6 28.5 %all-to-all-done.3 = bf16[64,32,256]{2,1,0:T(8,128)(2,1)S(1)} async-done(((bf16[64,32,256]{2,1,0:T(8,128)(2,1)}), bf16[64,32,256]{2,1,0:T(8,128)(2,1)S(1)}, u32[]{:S(2)}, u32[]{:S(2)}) %all-to-all-start.3) | async-done | bytes 1048608 | tf_op jit(solution)/shard_map/all_to_all | solution.py:271
  221.1 5.0 %fusion = f32[64,32,256]{2,1,0:T(8,128)S(1)} fusion(bf16[64,256,256]{2,1,0:T(8,128)(2,1)} %get-tuple-element.28, bf16[64,32,256]{2,1,0:T(8,128)(2,1)S(1)} %all-to-all-done.3, pred[64]{0:T(512)(128)(4,1)S(1)} %iota_compare_fusion.1), kind=kOutput, calls=%fused_computation.14 | convolution fusion | flops 268959744 | bytes 11534400 | tf_op jit(solution)/shard_map/eab,eoa->eob/dot_general | solution.py:328
  226.1 2.0 fusion.4
  228.8 4.8 %multiply_reduce_fusion.5 = (f32[32]{0:T(128)S(1)}, f32[32]{0:T(128)S(1)}, f32[8,32,256]{2,1,0:T(8,128)}) fusion(f32[8,32,256]{2,1,0:T(8,128)S(1)} %get-tuple-element.15, f32[8,256]{1,0:T(8,128)S(1)} %sqrt.14, f32[8,32,256]{2,0,1:T(8,128)S(1)} %fusion.4, bf16[8,6,256,256]{2,3,1,0:T(8,128)(2,1)} %bitcast.192, bf16[8,6,32,256]{3,2,1,0:T(8,128)(2,1)S(1)} %bitcast.200, ...), kind=kOutput, calls=%fused_computation.73 | convolution fusion | flops 202112960 | bytes 7872816 | tf_op jit(solution)/shard_map/rkab,rkob->roa/dot_general | solution.py:322
  234.2 20.2 %shard_map.53 = (f32[256,256]{1,0:T(8,128)}, f32[1,128]{1,0:T(1,128)}) custom-call(f32[256,256]{1,0:T(8,128)} %bitcast.204, f32[1,128]{1,0:T(1,128)} %pad_bitcast_fusion.g_ref), custom_call_target="tpu_custom_call" | custom-call | tf_op jit(solution)/shard_map/pallas_call | solution.py:204
  255.1 1.1 subtract_bitcast_fusion
  (76 shorter events, 22.0 us)
Async XLA Ops:
  6.5 36.0 %all-to-all-start = ((bf16[64,16,384]{2,1,0:T(8,128)(2,1)}), bf16[64,16,384]{2,1,0:T(8,128)(2,1)S(1)}, u32[]{:S(2)}, u32[]{:S(2)}) async-start(bf16[64,16,384]{2,1,0:T(8,128)(2,1)} %pad_maximum_fusion), calls=%async_computation | async-start | bytes 1572864 | tf_op jit(solution)/shard_map/all_to_all | solution.py:257
  44.5 23.5 %all-to-all-start.1 = ((bf16[64,16,256]{2,1,0:T(8,128)(2,1)}), bf16[64,16,256]{2,1,0:T(8,128)(2,1)S(1)}, u32[]{:S(2)}, u32[]{:S(2)}) async-start(bf16[64,16,256]{2,1,0:T(8,128)(2,1)} %broadcast_select_fusion.2), calls=%async_computation.1 | async-start | bytes 1048576 | tf_op jit(solution)/shard_map/all_to_all | solution.py:271
  68.8 20.2 %copy-start = (f32[32,2048]{1,0:T(8,128)S(1)}, f32[32,2048]{1,0:T(8,128)}, u32[]{:S(2)}) copy-start(f32[32,2048]{1,0:T(8,128)} %param.5) | copy-start | bytes 786436
  81.1 20.0 %copy-start.2 = (s32[8,6]{1,0:T(8,128)S(1)}, s32[8,6]{1,0:T(8,128)}, u32[]{:S(2)}) copy-start(s32[8,6]{1,0:T(8,128)} %param.3) | copy-start | bytes 580
  91.6 38.1 %all-to-all-start.2 = ((bf16[64,32,256]{2,1,0:T(8,128)(2,1)}), bf16[64,32,256]{2,1,0:T(8,128)(2,1)S(1)}, u32[]{:S(2)}, u32[]{:S(2)}) async-start(bf16[64,32,256]{2,1,0:T(8,128)(2,1)} %select_select_fusion.1), calls=%async_computation.2 | async-start | bytes 2097152 | tf_op jit(solution)/shard_map/all_to_all | solution.py:271
  184.4 36.8 %all-to-all-start.3 = ((bf16[64,32,256]{2,1,0:T(8,128)(2,1)}), bf16[64,32,256]{2,1,0:T(8,128)(2,1)S(1)}, u32[]{:S(2)}, u32[]{:S(2)}) async-start(bf16[64,32,256]{2,1,0:T(8,128)(2,1)} %select_select_fusion), calls=%async_computation.3 | async-start | bytes 2097152 | tf_op jit(solution)/shard_map/all_to_all | solution.py:271
  226.1 28.3 %copy-start.3 = (f32[1,128]{1,0:T(1,128)S(1)}, f32[1,128]{1,0:T(1,128)}, u32[]{:S(2)}) copy-start(f32[1,128]{1,0:T(1,128)} %shard_map.52) | copy-start | bytes 1540
  226.1 29.0 %copy-start.1 = (f32[256,256]{1,0:T(8,128)S(1)}, f32[256,256]{1,0:T(8,128)}, u32[]{:S(2)}) copy-start(f32[256,256]{1,0:T(8,128)} %get-tuple-element.7) | copy-start | bytes 786436

commit v15 on v14

--- a/solution.py
+++ b/solution.py
@@ -325,8 +325,9 @@
             far_w.reshape(block_rows, slot_width, outputs, block_len),
             preferred_element_type=jnp.float32,
         )
-        mirror = jnp.einsum("eab,eoa->eob", in_k, their_w, preferred_element_type=jnp.float32)
-        return direct + collect(mirror)
+        picked = collect_map.astype(their_w.dtype)[:, None, :, None] * jnp.swapaxes(their_w, 0, 1)[None]
+        mirror = jnp.einsum("joea,eab->job", picked, in_k, preferred_element_type=jnp.float32)
+        return direct + mirror
 
     resid = targets.reshape(outputs, block_rows, block_len).transpose(1, 0, 2)
     direction = resid

time: 259 us -> 256 us (0.988)
  matrix products: 51 us -> 46.3 us
    dot_general x3 -> x1, matrix products: 4.06 us -> 0.14 us  [collect(): jnp.dot(collect_map, flat, precision=lax.Precision.HIGHEST, preferred_ele...]
    dot_general x2, matrix products: 9.64 us -> 6.83 us  [apply_partial(): jnp.einsum('rkab,rkob->roa', own_k.reshape(block_rows, slot_width, block_...]
  transfers between devices with their start and end apart: 4 -> 4, of which waited for: 4 -> 4; matrix products, arithmetic and copies ran while one was open for 6% -> 7% of each run, Pallas kernels for 0% -> 0%
where the time goes in v15:
time: 256 us; the launch traced here: 255 us
  waiting for transfers between devices  78.6 us (31%)
  Pallas kernels  61.4 us (24%)
  matrix products  46.3 us (18%)
  starting transfers between devices  36.9 us (14%)
  local copies, waits for them, and re-layouts  14.7 us (6%)
  other arithmetic  14.1 us (6%)
  between operations  3.06 us (1%)
    all_to_all x3, waiting for transfers between devices, swap(): lax.all_to_all(parts, 'rows', split_axis=0, concat_axis=0, tiled=True)  56.5 us
    pallas_call x2, Pallas kernels, fused_sum(): pl.pallas_call(functools.partial(fused_kernel, n_rows, n_cols), out_shape...  41.3 us
    dot_general x2, matrix products, wendland(): jnp.einsum('nda,ndb->nab', left_f, right_f, precision=lax.Precision.HIGHEST)  27.4 us
    all_to_all x3, starting transfers between devices, swap(): lax.all_to_all(parts, 'rows', split_axis=0, concat_axis=0, tiled=True)  23.9 us
    all_to_all x1, waiting for transfers between devices, local(): lax.all_to_all(jnp.concatenate([asked_x, request], axis=2), 'rows', split...  22.2 us
    pallas_call x2, Pallas kernels, allsum(): pl.pallas_call(functools.partial(allsum_kernel, axis, n), out_shape=jax.S...  20.1 us
    all_to_all x1, starting transfers between devices, local(): lax.all_to_all(jnp.concatenate([asked_x, request], axis=2), 'rows', split...  13 us
    dot_general x2, matrix products, apply_partial(): jnp.einsum('joea,eab->job', picked, in_k, preferred_element_type=jnp.floa...  12 us
  transfers between devices with their start and end apart: 4, of which 4 were waited for; matrix products, arithmetic and copies ran while one was open for 7% of the time, Pallas kernels for 0%

profile of v15, /device:TPU:1, one launch (start us, length us, event | category | flops | bytes accessed | tf_op | source)
XLA Modules:
  0.0 255.0 jit_solution(4184026096798061737)
XLA Ops:
  6.5 13.0 %all-to-all-start = ((bf16[64,16,384]{2,1,0:T(8,128)(2,1)}), bf16[64,16,384]{2,1,0:T(8,128)(2,1)S(1)}, u32[]{:S(2)}, u32[]{:S(2)}) async-start(bf16[64,16,384]{2,1,0:T(8,128)(2,1)} %pad_maximum_fusion), calls=%async_computation | async-start | bytes 1572864 | tf_op jit(solution)/shard_map/all_to_all | solution.py:257
  20.3 22.2 %all-to-all-done = bf16[64,16,384]{2,1,0:T(8,128)(2,1)S(1)} async-done(((bf16[64,16,384]{2,1,0:T(8,128)(2,1)}), bf16[64,16,384]{2,1,0:T(8,128)(2,1)S(1)}, u32[]{:S(2)}, u32[]{:S(2)}) %all-to-all-start) | async-done | bytes 786464 | tf_op jit(solution)/shard_map/all_to_all | solution.py:257
  44.5 6.2 %all-to-all-start.1 = ((bf16[64,16,256]{2,1,0:T(8,128)(2,1)}), bf16[64,16,256]{2,1,0:T(8,128)(2,1)S(1)}, u32[]{:S(2)}, u32[]{:S(2)}) async-start(bf16[64,16,256]{2,1,0:T(8,128)(2,1)} %broadcast_select_fusion.2), calls=%async_computation.1 | async-start | bytes 1048576 | tf_op jit(solution)/shard_map/all_to_all | solution.py:271
  50.9 15.1 %fusion.69 = (f32[64,256]{1,0:T(8,128)S(1)}, bf16[64,256,256]{2,1,0:T(8,128)(2,1)}) fusion(bf16[64,16,256]{2,1,0:T(8,128)(2,1)S(1)} %gather_fusion.2, bf16[64,16,384]{2,1,0:T(8,128)(2,1)S(1)} %all-to-all-done, f32[64,256]{1,0:T(8,128)S(1)} %multiply_reduce_fusion, f32[64,256]{1,0:T(8,128)S(1)} %multiply_reduce_fusion.1, pred[64]{0:T(512)(128)(4,1)S(1)} %compare_and_fusion), kind=kOutput, calls=%fused_computation.155 | convolution fusion | flops 197115904 | bytes 9634304 | tf_op jit(solution)/shard_map/nda,ndb->nab/dot_general | solution.py:24
  66.0 2.0 all-to-all-done.1
  68.9 12.2 %fusion.68 = (bf16[48,256,256]{1,2,0:T(8,128)(2,1)}, f32[48,256]{1,0:T(8,128)S(1)}) fusion(bf16[48,16,256]{2,1,0:T(8,128)(2,1)S(1)} %gather_fusion, bf16[48,16,256]{2,1,0:T(8,128)(2,1)S(1)} %gather_fusion.3, pred[48]{0:T(512)(128)(4,1)S(1)} %broadcast_compare_fusion.2, f32[48,256]{1,0:T(8,128)S(1)} %multiply_reduce_fusion.2, ...), kind=kOutput, calls=%fused_computation.154 | convolution fusion | flops 148033536 | bytes 7225392 | tf_op jit(solution)/shard_map/nda,ndb->nab/dot_general | solution.py:24
  81.9 6.4 %shard_map.50 = f32[16,128]{1,0:T(8,128)} custom-call(f32[16,128]{1,0:T(8,128)} %reshape_reshape_broadcast_in_dim.3.x_ref), custom_call_target="tpu_custom_call" | custom-call | tf_op jit(solution)/shard_map/pallas_call | solution.py:99
  90.3 1.3 select_select_fusion.1
  91.6 9.5 %all-to-all-start.2 = ((bf16[64,32,256]{2,1,0:T(8,128)(2,1)}), bf16[64,32,256]{2,1,0:T(8,128)(2,1)S(1)}, u32[]{:S(2)}, u32[]{:S(2)}) async-start(bf16[64,32,256]{2,1,0:T(8,128)(2,1)} %select_select_fusion.1), calls=%async_computation.2 | async-start | bytes 2097152 | tf_op jit(solution)/shard_map/all_to_all | solution.py:271
  103.7 25.9 %all-to-all-done.2 = bf16[64,32,256]{2,1,0:T(8,128)(2,1)S(1)} async-done(((bf16[64,32,256]{2,1,0:T(8,128)(2,1)}), bf16[64,32,256]{2,1,0:T(8,128)(2,1)S(1)}, u32[]{:S(2)}, u32[]{:S(2)}) %all-to-all-start.2) | async-done | bytes 1048608 | tf_op jit(solution)/shard_map/all_to_all | solution.py:271
  129.6 1.2 broadcast_select_fusion.1
  130.8 1.6 gather_fusion.6
  132.4 6.2 %fusion.14 = f32[8,32,256]{2,1,0:T(8,128)S(1)} fusion(bf16[64,256,256]{2,1,0:T(8,128)(2,1)} %get-tuple-element.32, bf16[32,64,256]{2,0,1:T(8,128)(2,1)} %get-tuple-element.23, bf16[8,64]{1,0:T(8,128)(2,1)S(1)} %convert_convert_fusion), kind=kOutput, calls=%fused_computation.30 | convolution fusion | flops 2151677952 | bytes 9700352 | tf_op jit(solution)/shard_map/joea,eab->job/dot_general | solution.py:329
  138.6 2.0 fusion.39
  141.3 21.2 %shard_map.51 = (f32[256,256]{1,0:T(8,128)}, f32[1,128]{1,0:T(1,128)}) custom-call(f32[256,256]{1,0:T(8,128)} %bitcast.196, f32[1,128]{1,0:T(1,128)} %fusion.58.g_ref), custom_call_target="tpu_custom_call" | custom-call | tf_op jit(solution)/shard_map/pallas_call | solution.py:204
  163.2 1.2 multiply_reduce_fusion.6
  164.9 13.6 %shard_map.52 = f32[1,128]{1,0:T(1,128)} custom-call(f32[1,128]{1,0:T(1,128)} %pad_bitcast_fusion.1.x_ref), custom_call_target="tpu_custom_call" | custom-call | tf_op jit(solution)/shard_map/pallas_call | solution.py:99
  181.6 1.3 select_select_fusion
  182.8 8.2 %all-to-all-start.3 = ((bf16[64,32,256]{2,1,0:T(8,128)(2,1)}), bf16[64,32,256]{2,1,0:T(8,128)(2,1)S(1)}, u32[]{:S(2)}, u32[]{:S(2)}) async-start(bf16[64,32,256]{2,1,0:T(8,128)(2,1)} %select_select_fusion), calls=%async_computation.3 | async-start | bytes 2097152 | tf_op jit(solution)/shard_map/all_to_all | solution.py:271
  191.1 28.5 %all-to-all-done.3 = bf16[64,32,256]{2,1,0:T(8,128)(2,1)S(1)} async-done(((bf16[64,32,256]{2,1,0:T(8,128)(2,1)}), bf16[64,32,256]{2,1,0:T(8,128)(2,1)S(1)}, u32[]{:S(2)}, u32[]{:S(2)}) %all-to-all-start.3) | async-done | bytes 1048608 | tf_op jit(solution)/shard_map/all_to_all | solution.py:271
  219.8 5.8 %fusion.19 = f32[8,32,256]{2,1,0:T(8,128)S(1)} fusion(bf16[64,256,256]{2,1,0:T(8,128)(2,1)} %get-tuple-element.32, bf16[32,64,256]{2,0,1:T(8,128)(2,1)S(1)} %get-tuple-element.21, bf16[8,64]{1,0:T(8,128)(2,1)S(1)} %convert_convert_fusion), kind=kOutput, calls=%fused_computation.31 | convolution fusion | flops 2151677952 | bytes 9700352 | tf_op jit(solution)/shard_map/joea,eab->job/dot_general | solution.py:329
  226.2 4.8 %multiply_reduce_fusion.5 = (f32[32]{0:T(128)S(1)}, f32[32]{0:T(128)S(1)}, f32[8,32,256]{2,1,0:T(8,128)}) fusion(f32[8,32,256]{2,1,0:T(8,128)S(1)} %get-tuple-element.15, f32[8,256]{1,0:T(8,128)S(1)} %sqrt.14, f32[8,32,256]{2,1,0:T(8,128)S(1)} %fusion.19, bf16[8,6,256,256]{2,3,1,0:T(8,128)(2,1)} %bitcast.184, bf16[8,6,32,256]{3,2,1,0:T(8,128)(2,1)S(1)} %bitcast.194, ...), kind=kOutput, calls=%fused_computation.73 | convolution fusion | flops 202112960 | bytes 7872816 | tf_op jit(solution)/shard_map/rkab,rkob->roa/dot_general | solution.py:322
  231.6 20.2 %shard_map.53 = (f32[256,256]{1,0:T(8,128)}, f32[1,128]{1,0:T(1,128)}) custom-call(f32[256,256]{1,0:T(8,128)} %bitcast.197, f32[1,128]{1,0:T(1,128)} %pad_bitcast_fusion.g_ref), custom_call_target="tpu_custom_call" | custom-call | tf_op jit(solution)/shard_map/pallas_call | solution.py:204
  252.4 1.1 subtract_bitcast_fusion
  (81 shorter events, 21.3 us)
Async XLA Ops:
  6.5 36.0 %all-to-all-start = ((bf16[64,16,384]{2,1,0:T(8,128)(2,1)}), bf16[64,16,384]{2,1,0:T(8,128)(2,1)S(1)}, u32[]{:S(2)}, u32[]{:S(2)}) async-start(bf16[64,16,384]{2,1,0:T(8,128)(2,1)} %pad_maximum_fusion), calls=%async_computation | async-start | bytes 1572864 | tf_op jit(solution)/shard_map/all_to_all | solution.py:257
  44.5 23.5 %all-to-all-start.1 = ((bf16[64,16,256]{2,1,0:T(8,128)(2,1)}), bf16[64,16,256]{2,1,0:T(8,128)(2,1)S(1)}, u32[]{:S(2)}, u32[]{:S(2)}) async-start(bf16[64,16,256]{2,1,0:T(8,128)(2,1)} %broadcast_select_fusion.2), calls=%async_computation.1 | async-start | bytes 1048576 | tf_op jit(solution)/shard_map/all_to_all | solution.py:271
  68.9 20.2 %copy-start = (f32[32,2048]{1,0:T(8,128)S(1)}, f32[32,2048]{1,0:T(8,128)}, u32[]{:S(2)}) copy-start(f32[32,2048]{1,0:T(8,128)} %param.5) | copy-start | bytes 786436
  81.1 20.0 %copy-start.3 = (s32[8,6]{1,0:T(8,128)S(1)}, s32[8,6]{1,0:T(8,128)}, u32[]{:S(2)}) copy-start(s32[8,6]{1,0:T(8,128)} %param.3) | copy-start | bytes 580
  91.6 38.1 %all-to-all-start.2 = ((bf16[64,32,256]{2,1,0:T(8,128)(2,1)}), bf16[64,32,256]{2,1,0:T(8,128)(2,1)S(1)}, u32[]{:S(2)}, u32[]{:S(2)}) async-start(bf16[64,32,256]{2,1,0:T(8,128)(2,1)} %select_select_fusion.1), calls=%async_computation.2 | async-start | bytes 2097152 | tf_op jit(solution)/shard_map/all_to_all | solution.py:271
  130.8 7.8 %slice-start = ((s8[6291456]{0:T(1024)(128)(4,1)}), s8[2097152]{0:T(1024)(128)(4,1)S(1)}, s32[]{:S(2)}) async-start(s8[6291456]{0:T(1024)(128)(4,1)} %bitcast.185), calls=%async_computation.4 | async-start | bytes 4194304
  132.4 6.2 %slice-start.1 = ((s8[6291456]{0:T(1024)(128)(4,1)}), s8[4194304]{0:T(1024)(128)(4,1)S(1)}, s32[]{:S(2)}) async-start(s8[6291456]{0:T(1024)(128)(4,1)} %bitcast.185), calls=%async_computation.5 | async-start | bytes 8388608
  132.4 6.2 %copy-start.1 = (bf16[48,32,256]{2,1,0:T(8,128)(2,1)S(1)}, bf16[48,32,256]{2,1,0:T(8,128)(2,1)}, u32[]{:S(2)}) copy-start(bf16[48,32,256]{2,1,0:T(8,128)(2,1)} %gather_fusion.6) | copy-start | bytes 2359300
  182.8 36.8 %all-to-all-start.3 = ((bf16[64,32,256]{2,1,0:T(8,128)(2,1)}), bf16[64,32,256]{2,1,0:T(8,128)(2,1)S(1)}, u32[]{:S(2)}, u32[]{:S(2)}) async-start(bf16[64,32,256]{2,1,0:T(8,128)(2,1)} %select_select_fusion), calls=%async_computation.3 | async-start | bytes 2097152 | tf_op jit(solution)/shard_map/all_to_all | solution.py:271
  225.6 26.2 %copy-start.4 = (f32[1,128]{1,0:T(1,128)S(1)}, f32[1,128]{1,0:T(1,128)}, u32[]{:S(2)}) copy-start(f32[1,128]{1,0:T(1,128)} %shard_map.52) | copy-start | bytes 1540
  225.6 26.9 %copy-start.2 = (f32[256,256]{1,0:T(8,128)S(1)}, f32[256,256]{1,0:T(8,128)}, u32[]{:S(2)}) copy-start(f32[256,256]{1,0:T(8,128)} %get-tuple-element.7) | copy-start | bytes 786436

commit v16 on v15

--- a/solution.py
+++ b/solution.py
@@ -111,7 +111,9 @@
     return out.reshape(-1)[:size].reshape(shape)
 
 
-def fused_kernel(n_rows, n_cols, z_ref, g_ref, zo_ref, go_ref, recv_z, recv_g, recv_s, rows_sum, sems):
+def fused_kernel(
+    n_rows, n_cols, z_ref, g_ref, zo_ref, go_ref, recv_z, gathered, recv_g, recv_s, rows_sum, sems
+):
     row = lax.axis_index("rows")
     col = lax.axis_index("cols")
     barrier = pltpu.get_barrier_semaphore()
@@ -128,7 +130,7 @@
             barrier, inc=1, device_id={"cols": lax.rem(col + k, n_cols)}, device_id_type=MESH
         )
     pl.semaphore_wait(barrier, n_rows - 1 + n_cols - 1)
-    z_send, z_recv, g_send, g_recv, s_send, s_recv = sems
+    z_send, z_recv, g_send, g_recv, s_send, s_recv, a_send, a_recv = sems
 
     def col_copy(src, dst, send, recv, peer, slot):
         return pltpu.make_async_remote_copy(
@@ -151,15 +153,25 @@
         )
 
     for k in range(1, n_cols):
-        col_copy(z_ref, recv_z, z_send, z_recv, lax.rem(col + k, n_cols), col).start()
+        peer = lax.rem(col + k, n_cols)
+        col_copy(z_ref.at[peer], recv_z, z_send, z_recv, peer, col).start()
 
     def start(k, carry):
         g_copy(lax.rem(row + k, n_rows), row).start()
         return carry
 
     lax.fori_loop(1, n_rows, start, 0)
-    recv_z[col] = z_ref[...]
+    recv_z[col] = z_ref[col]
     recv_g[row] = g_ref[...]
+    for k in range(1, n_cols):
+        peer = lax.rem(col + k, n_cols)
+        col_copy(z_ref.at[peer], recv_z, z_send, z_recv, peer, col).wait_send()
+        col_copy(z_ref.at[peer], recv_z, z_send, z_recv, peer, peer).wait_recv()
+    gathered[col] = recv_z[0]
+    for k in range(1, n_cols):
+        gathered[col] += recv_z[k]
+    for k in range(1, n_cols):
+        col_copy(gathered.at[col], gathered, a_send, a_recv, lax.rem(col + k, n_cols), col).start()
 
     def finish(k, carry):
         peer = lax.rem(row + k, n_rows)
@@ -180,11 +192,9 @@
     recv_s[col] = rows_sum[...]
     for k in range(1, n_cols):
         peer = lax.rem(col + k, n_cols)
-        col_copy(z_ref, recv_z, z_send, z_recv, peer, col).wait_send()
-        col_copy(z_ref, recv_z, z_send, z_recv, peer, peer).wait_recv()
-    zo_ref[...] = recv_z[0]
-    for k in range(1, n_cols):
-        zo_ref[...] += recv_z[k]
+        col_copy(gathered.at[col], gathered, a_send, a_recv, peer, col).wait_send()
+        col_copy(gathered.at[peer], gathered, a_send, a_recv, peer, peer).wait_recv()
+    zo_ref[...] = gathered[...]
     for k in range(1, n_cols):
         peer = lax.rem(col + k, n_cols)
         col_copy(rows_sum, recv_s, s_send, s_recv, peer, col).wait_send()
@@ -197,7 +207,7 @@
 def fused_sum(z, g, cid):
     n_rows = lax.axis_size("rows")
     n_cols = lax.axis_size("cols")
-    z_tile = z.reshape(-1, z.shape[-1])
+    z_tile = z.reshape(n_cols, -1, z.shape[-1])
     size = g.shape[0]
     g_tile = jnp.pad(g, (0, 128 - size)).reshape(1, 128)
     vmem = pl.BlockSpec(memory_space=pltpu.VMEM)
@@ -210,7 +220,8 @@
         in_specs=[vmem, vmem],
         out_specs=[vmem, vmem],
         scratch_shapes=[
-            pltpu.VMEM((n_cols,) + z_tile.shape, jnp.float32),
+            pltpu.VMEM(z_tile.shape, jnp.float32),
+            pltpu.VMEM(z_tile.shape, jnp.float32),
             pltpu.VMEM((n_rows,) + g_tile.shape, jnp.float32),
             pltpu.VMEM((n_cols,) + g_tile.shape, jnp.float32),
             pltpu.VMEM(g_tile.shape, jnp.float32),
@@ -219,6 +230,8 @@
                 pltpu.SemaphoreType.DMA((n_cols,)),
                 pltpu.SemaphoreType.DMA((n_rows,)),
                 pltpu.SemaphoreType.DMA((n_rows,)),
+                pltpu.SemaphoreType.DMA((n_cols,)),
+                pltpu.SemaphoreType.DMA((n_cols,)),
                 pltpu.SemaphoreType.DMA((n_cols,)),
                 pltpu.SemaphoreType.DMA((n_cols,)),
             ],

time: 256 us -> 250 us (0.977)
  Pallas kernels: 61.4 us -> 56.2 us
    pallas_call x2, Pallas kernels: 41.3 us -> 35.6 us  [fused_sum(): pl.pallas_call(functools.partial(fused_kernel, n_rows, n_cols), out_shape...]
where the time goes in v16:
time: 250 us; the launch traced here: 249 us
  waiting for transfers between devices  78.6 us (31%)
  Pallas kernels  56.2 us (22%)
  matrix products  46.3 us (19%)
  starting transfers between devices  35.9 us (14%)
  local copies, waits for them, and re-layouts  14.7 us (6%)
  other arithmetic  14.1 us (6%)
  between operations  3.06 us (1%)
    all_to_all x3, waiting for transfers between devices, swap(): lax.all_to_all(parts, 'rows', split_axis=0, concat_axis=0, tiled=True)  56.5 us
    pallas_call x2, Pallas kernels, fused_sum(): pl.pallas_call(functools.partial(fused_kernel, n_rows, n_cols), out_shape...  35.6 us
    dot_general x2, matrix products, wendland(): jnp.einsum('nda,ndb->nab', left_f, right_f, precision=lax.Precision.HIGHEST)  27.4 us
    all_to_all x3, starting transfers between devices, swap(): lax.all_to_all(parts, 'rows', split_axis=0, concat_axis=0, tiled=True)  22.9 us
    all_to_all x1, waiting for transfers between devices, local(): lax.all_to_all(jnp.concatenate([asked_x, request], axis=2), 'rows', split...  22.2 us
    pallas_call x2, Pallas kernels, allsum(): pl.pallas_call(functools.partial(allsum_kernel, axis, n), out_shape=jax.S...  20.6 us
    all_to_all x1, starting transfers between devices, local(): lax.all_to_all(jnp.concatenate([asked_x, request], axis=2), 'rows', split...  13 us
    dot_general x2, matrix products, apply_partial(): jnp.einsum('joea,eab->job', picked, in_k, preferred_element_type=jnp.floa...  12 us
  transfers between devices with their start and end apart: 4, of which 4 were waited for; matrix products, arithmetic and copies ran while one was open for 7% of the time, Pallas kernels for 0%

profile of v16, /device:TPU:1, one launch (start us, length us, event | category | flops | bytes accessed | tf_op | source)
XLA Modules:
  0.0 248.9 jit_solution(4294176361534012874)
XLA Ops:
  6.5 13.0 %all-to-all-start = ((bf16[64,16,384]{2,1,0:T(8,128)(2,1)}), bf16[64,16,384]{2,1,0:T(8,128)(2,1)S(1)}, u32[]{:S(2)}, u32[]{:S(2)}) async-start(bf16[64,16,384]{2,1,0:T(8,128)(2,1)} %pad_maximum_fusion), calls=%async_computation | async-start | bytes 1572864 | tf_op jit(solution)/shard_map/all_to_all | solution.py:270
  20.3 22.2 %all-to-all-done = bf16[64,16,384]{2,1,0:T(8,128)(2,1)S(1)} async-done(((bf16[64,16,384]{2,1,0:T(8,128)(2,1)}), bf16[64,16,384]{2,1,0:T(8,128)(2,1)S(1)}, u32[]{:S(2)}, u32[]{:S(2)}) %all-to-all-start) | async-done | bytes 786464 | tf_op jit(solution)/shard_map/all_to_all | solution.py:270
  44.5 6.2 %all-to-all-start.1 = ((bf16[64,16,256]{2,1,0:T(8,128)(2,1)}), bf16[64,16,256]{2,1,0:T(8,128)(2,1)S(1)}, u32[]{:S(2)}, u32[]{:S(2)}) async-start(bf16[64,16,256]{2,1,0:T(8,128)(2,1)} %broadcast_select_fusion.2), calls=%async_computation.1 | async-start | bytes 1048576 | tf_op jit(solution)/shard_map/all_to_all | solution.py:284
  50.9 15.1 %fusion.69 = (f32[64,256]{1,0:T(8,128)S(1)}, bf16[64,256,256]{2,1,0:T(8,128)(2,1)}) fusion(bf16[64,16,256]{2,1,0:T(8,128)(2,1)S(1)} %gather_fusion.2, bf16[64,16,384]{2,1,0:T(8,128)(2,1)S(1)} %all-to-all-done, f32[64,256]{1,0:T(8,128)S(1)} %multiply_reduce_fusion, f32[64,256]{1,0:T(8,128)S(1)} %multiply_reduce_fusion.1, pred[64]{0:T(512)(128)(4,1)S(1)} %compare_and_fusion), kind=kOutput, calls=%fused_computation.155 | convolution fusion | flops 197115904 | bytes 9634304 | tf_op jit(solution)/shard_map/nda,ndb->nab/dot_general | solution.py:24
  66.0 2.0 all-to-all-done.1
  68.9 12.2 %fusion.68 = (bf16[48,256,256]{1,2,0:T(8,128)(2,1)}, f32[48,256]{1,0:T(8,128)S(1)}) fusion(bf16[48,16,256]{2,1,0:T(8,128)(2,1)S(1)} %gather_fusion, bf16[48,16,256]{2,1,0:T(8,128)(2,1)S(1)} %gather_fusion.3, pred[48]{0:T(512)(128)(4,1)S(1)} %broadcast_compare_fusion.2, f32[48,256]{1,0:T(8,128)S(1)} %multiply_reduce_fusion.2, ...), kind=kOutput, calls=%fused_computation.154 | convolution fusion | flops 148033536 | bytes 7225392 | tf_op jit(solution)/shard_map/nda,ndb->nab/dot_general | solution.py:24
  81.9 6.4 %shard_map.50 = f32[16,128]{1,0:T(8,128)} custom-call(f32[16,128]{1,0:T(8,128)} %reshape_reshape_broadcast_in_dim.3.x_ref), custom_call_target="tpu_custom_call" | custom-call | tf_op jit(solution)/shard_map/pallas_call | solution.py:99
  90.3 1.3 select_select_fusion.1
  91.6 9.5 %all-to-all-start.2 = ((bf16[64,32,256]{2,1,0:T(8,128)(2,1)}), bf16[64,32,256]{2,1,0:T(8,128)(2,1)S(1)}, u32[]{:S(2)}, u32[]{:S(2)}) async-start(bf16[64,32,256]{2,1,0:T(8,128)(2,1)} %select_select_fusion.1), calls=%async_computation.2 | async-start | bytes 2097152 | tf_op jit(solution)/shard_map/all_to_all | solution.py:284
  103.7 25.9 %all-to-all-done.2 = bf16[64,32,256]{2,1,0:T(8,128)(2,1)S(1)} async-done(((bf16[64,32,256]{2,1,0:T(8,128)(2,1)}), bf16[64,32,256]{2,1,0:T(8,128)(2,1)S(1)}, u32[]{:S(2)}, u32[]{:S(2)}) %all-to-all-start.2) | async-done | bytes 1048608 | tf_op jit(solution)/shard_map/all_to_all | solution.py:284
  129.6 1.2 broadcast_select_fusion.1
  130.8 1.6 gather_fusion.6
  132.4 6.2 %fusion.14 = f32[8,32,256]{2,1,0:T(8,128)S(1)} fusion(bf16[64,256,256]{2,1,0:T(8,128)(2,1)} %get-tuple-element.32, bf16[32,64,256]{2,0,1:T(8,128)(2,1)} %get-tuple-element.23, bf16[8,64]{1,0:T(8,128)(2,1)S(1)} %convert_convert_fusion), kind=kOutput, calls=%fused_computation.30 | convolution fusion | flops 2151677952 | bytes 9700352 | tf_op jit(solution)/shard_map/joea,eab->job/dot_general | solution.py:342
  138.6 2.0 fusion.39
  141.3 17.8 %shard_map.51 = (f32[4,64,256]{2,1,0:T(8,128)}, f32[1,128]{1,0:T(1,128)}) custom-call(f32[4,64,256]{2,1,0:T(8,128)} %bitcast.195, f32[1,128]{1,0:T(1,128)} %fusion.58.g_ref), custom_call_target="tpu_custom_call" | custom-call | tf_op jit(solution)/shard_map/pallas_call | solution.py:214
  159.9 1.2 multiply_reduce_fusion.6
  161.6 14.2 %shard_map.52 = f32[1,128]{1,0:T(1,128)} custom-call(f32[1,128]{1,0:T(1,128)} %pad_bitcast_fusion.1.x_ref), custom_call_target="tpu_custom_call" | custom-call | tf_op jit(solution)/shard_map/pallas_call | solution.py:99
  178.8 1.3 select_select_fusion
  180.0 7.2 %all-to-all-start.3 = ((bf16[64,32,256]{2,1,0:T(8,128)(2,1)}), bf16[64,32,256]{2,1,0:T(8,128)(2,1)S(1)}, u32[]{:S(2)}, u32[]{:S(2)}) async-start(bf16[64,32,256]{2,1,0:T(8,128)(2,1)} %select_select_fusion), calls=%async_computation.3 | async-start | bytes 2097152 | tf_op jit(solution)/shard_map/all_to_all | solution.py:284
  187.3 28.5 %all-to-all-done.3 = bf16[64,32,256]{2,1,0:T(8,128)(2,1)S(1)} async-done(((bf16[64,32,256]{2,1,0:T(8,128)(2,1)}), bf16[64,32,256]{2,1,0:T(8,128)(2,1)S(1)}, u32[]{:S(2)}, u32[]{:S(2)}) %all-to-all-start.3) | async-done | bytes 1048608 | tf_op jit(solution)/shard_map/all_to_all | solution.py:284
  216.0 5.8 %fusion.19 = f32[8,32,256]{2,1,0:T(8,128)S(1)} fusion(bf16[64,256,256]{2,1,0:T(8,128)(2,1)} %get-tuple-element.32, bf16[32,64,256]{2,0,1:T(8,128)(2,1)S(1)} %get-tuple-element.21, bf16[8,64]{1,0:T(8,128)(2,1)S(1)} %convert_convert_fusion), kind=kOutput, calls=%fused_computation.31 | convolution fusion | flops 2151677952 | bytes 9700352 | tf_op jit(solution)/shard_map/joea,eab->job/dot_general | solution.py:342
  222.5 4.8 %multiply_reduce_fusion.5 = (f32[32]{0:T(128)S(1)}, f32[32]{0:T(128)S(1)}, f32[8,32,256]{2,1,0:T(8,128)}) fusion(f32[8,32,256]{2,1,0:T(8,128)S(1)} %get-tuple-element.15, f32[8,256]{1,0:T(8,128)S(1)} %sqrt.14, f32[8,32,256]{2,1,0:T(8,128)S(1)} %fusion.19, bf16[8,6,256,256]{2,3,1,0:T(8,128)(2,1)} %bitcast.181, bf16[8,6,32,256]{3,2,1,0:T(8,128)(2,1)S(1)} %bitcast.191, ...), kind=kOutput, calls=%fused_computation.73 | convolution fusion | flops 202112960 | bytes 7872816 | tf_op jit(solution)/shard_map/rkab,rkob->roa/dot_general | solution.py:335
  227.8 17.8 %shard_map.53 = (f32[4,64,256]{2,1,0:T(8,128)}, f32[1,128]{1,0:T(1,128)}) custom-call(f32[4,64,256]{2,1,0:T(8,128)} %bitcast.196, f32[1,128]{1,0:T(1,128)} %pad_bitcast_fusion.g_ref), custom_call_target="tpu_custom_call" | custom-call | tf_op jit(solution)/shard_map/pallas_call | solution.py:214
  246.3 1.1 subtract_bitcast_fusion
  (81 shorter events, 21.3 us)
Async XLA Ops:
  6.5 36.0 %all-to-all-start = ((bf16[64,16,384]{2,1,0:T(8,128)(2,1)}), bf16[64,16,384]{2,1,0:T(8,128)(2,1)S(1)}, u32[]{:S(2)}, u32[]{:S(2)}) async-start(bf16[64,16,384]{2,1,0:T(8,128)(2,1)} %pad_maximum_fusion), calls=%async_computation | async-start | bytes 1572864 | tf_op jit(solution)/shard_map/all_to_all | solution.py:270
  44.5 23.5 %all-to-all-start.1 = ((bf16[64,16,256]{2,1,0:T(8,128)(2,1)}), bf16[64,16,256]{2,1,0:T(8,128)(2,1)S(1)}, u32[]{:S(2)}, u32[]{:S(2)}) async-start(bf16[64,16,256]{2,1,0:T(8,128)(2,1)} %broadcast_select_fusion.2), calls=%async_computation.1 | async-start | bytes 1048576 | tf_op jit(solution)/shard_map/all_to_all | solution.py:284
  68.9 20.2 %copy-start = (f32[32,2048]{1,0:T(8,128)S(1)}, f32[32,2048]{1,0:T(8,128)}, u32[]{:S(2)}) copy-start(f32[32,2048]{1,0:T(8,128)} %param.5) | copy-start | bytes 786436
  81.1 20.0 %copy-start.3 = (s32[8,6]{1,0:T(8,128)S(1)}, s32[8,6]{1,0:T(8,128)}, u32[]{:S(2)}) copy-start(s32[8,6]{1,0:T(8,128)} %param.3) | copy-start | bytes 580
  91.6 38.1 %all-to-all-start.2 = ((bf16[64,32,256]{2,1,0:T(8,128)(2,1)}), bf16[64,32,256]{2,1,0:T(8,128)(2,1)S(1)}, u32[]{:S(2)}, u32[]{:S(2)}) async-start(bf16[64,32,256]{2,1,0:T(8,128)(2,1)} %select_select_fusion.1), calls=%async_computation.2 | async-start | bytes 2097152 | tf_op jit(solution)/shard_map/all_to_all | solution.py:284
  130.8 7.8 %slice-start = ((s8[6291456]{0:T(1024)(128)(4,1)}), s8[2097152]{0:T(1024)(128)(4,1)S(1)}, s32[]{:S(2)}) async-start(s8[6291456]{0:T(1024)(128)(4,1)} %bitcast.182), calls=%async_computation.4 | async-start | bytes 4194304
  132.4 6.2 %slice-start.1 = ((s8[6291456]{0:T(1024)(128)(4,1)}), s8[4194304]{0:T(1024)(128)(4,1)S(1)}, s32[]{:S(2)}) async-start(s8[6291456]{0:T(1024)(128)(4,1)} %bitcast.182), calls=%async_computation.5 | async-start | bytes 8388608
  132.4 6.2 %copy-start.1 = (bf16[48,32,256]{2,1,0:T(8,128)(2,1)S(1)}, bf16[48,32,256]{2,1,0:T(8,128)(2,1)}, u32[]{:S(2)}) copy-start(bf16[48,32,256]{2,1,0:T(8,128)(2,1)} %gather_fusion.6) | copy-start | bytes 2359300
  180.0 35.8 %all-to-all-start.3 = ((bf16[64,32,256]{2,1,0:T(8,128)(2,1)}), bf16[64,32,256]{2,1,0:T(8,128)(2,1)S(1)}, u32[]{:S(2)}, u32[]{:S(2)}) async-start(bf16[64,32,256]{2,1,0:T(8,128)(2,1)} %select_select_fusion), calls=%async_computation.3 | async-start | bytes 2097152 | tf_op jit(solution)/shard_map/all_to_all | solution.py:284
  221.8 23.8 %copy-start.4 = (f32[1,128]{1,0:T(1,128)S(1)}, f32[1,128]{1,0:T(1,128)}, u32[]{:S(2)}) copy-start(f32[1,128]{1,0:T(1,128)} %shard_map.52) | copy-start | bytes 1540
  221.8 24.5 %copy-start.2 = (f32[4,64,256]{2,1,0:T(8,128)S(1)}, f32[4,64,256]{2,1,0:T(8,128)}, u32[]{:S(2)}) copy-start(f32[4,64,256]{2,1,0:T(8,128)} %get-tuple-element.7) | copy-start | bytes 786436

commit v17 on v16

--- a/solution.py
+++ b/solution.py
@@ -239,6 +239,84 @@
         compiler_params=pltpu.CompilerParams(collective_id=cid, has_side_effects=True),
     )(z_tile, g_tile)
     return z_out.reshape(z.shape), g_out.reshape(-1)[:size]
+
+
+def rows_sum_kernel(n, group, x_ref, o_ref, recv1, recv2, sems):
+    me = lax.axis_index("rows")
+    pos = lax.rem(me, group)
+    base = me - pos
+    grp = me // group
+    groups = n // group
+    barrier = pltpu.get_barrier_semaphore()
+
+    def near(k):
+        return base + lax.rem(pos + k, group)
+
+    def far(k):
+        return lax.rem(grp + k, groups) * group + pos
+
+    for k in range(1, group):
+        pl.semaphore_signal(barrier, inc=1, device_id={"rows": near(k)}, device_id_type=MESH)
+    for k in range(1, groups):
+        pl.semaphore_signal(barrier, inc=1, device_id={"rows": far(k)}, device_id_type=MESH)
+    pl.semaphore_wait(barrier, group - 1 + groups - 1)
+    send1, got1, send2, got2 = sems
+
+    def copy(src, dst, send, got, device, slot, peer_slot):
+        return pltpu.make_async_remote_copy(
+            src_ref=src,
+            dst_ref=dst.at[slot],
+            send_sem=send.at[peer_slot],
+            recv_sem=got.at[slot],
+            device_id={"rows": device},
+            device_id_type=MESH,
+        )
+
+    for k in range(1, group):
+        copy(x_ref, recv1, send1, got1, near(k), pos, lax.rem(pos + k, group)).start()
+    recv1[pos] = x_ref[...]
+    for k in range(1, group):
+        other = lax.rem(pos + k, group)
+        copy(x_ref, recv1, send1, got1, near(k), pos, other).wait_send()
+        copy(x_ref, recv1, send1, got1, near(k), other, other).wait_recv()
+    recv2[grp] = recv1[0]
+    for k in range(1, group):
+        recv2[grp] += recv1[k]
+    for k in range(1, groups):
+        copy(recv2.at[grp], recv2, send2, got2, far(k), grp, lax.rem(grp + k, groups)).start()
+    for k in range(1, groups):
+        other = lax.rem(grp + k, groups)
+        copy(recv2.at[grp], recv2, send2, got2, far(k), grp, other).wait_send()
+        copy(recv2.at[grp], recv2, send2, got2, far(k), other, other).wait_recv()
+    o_ref[...] = recv2[0]
+    for k in range(1, groups):
+        o_ref[...] += recv2[k]
+
+
+def rows_sum(x, cid):
+    n = lax.axis_size("rows")
+    group = 16 if n % 16 == 0 and n > 16 else (4 if n % 4 == 0 else n)
+    groups = n // group
+    size = x.shape[0]
+    tile = jnp.pad(x, (0, 128 - size)).reshape(1, 128)
+    out = pl.pallas_call(
+        functools.partial(rows_sum_kernel, n, group),
+        out_shape=jax.ShapeDtypeStruct(tile.shape, jnp.float32),
+        in_specs=[pl.BlockSpec(memory_space=pltpu.VMEM)],
+        out_specs=pl.BlockSpec(memory_space=pltpu.VMEM),
+        scratch_shapes=[
+            pltpu.VMEM((group,) + tile.shape, jnp.float32),
+            pltpu.VMEM((groups,) + tile.shape, jnp.float32),
+            [
+                pltpu.SemaphoreType.DMA((group,)),
+                pltpu.SemaphoreType.DMA((group,)),
+                pltpu.SemaphoreType.DMA((groups,)),
+                pltpu.SemaphoreType.DMA((groups,)),
+            ],
+        ],
+        compiler_params=pltpu.CompilerParams(collective_id=cid, has_side_effects=True),
+    )(tile)
+    return out.reshape(-1)[:size]
 
 
 def local(block_list, points, targets):
@@ -315,7 +393,7 @@
         return allsum(partial_value, "cols", 1 if partial_value.shape[1] == 1 else 2)
 
     def global_sum(values):
-        return allsum(values, "rows", 0)
+        return rows_sum(values, 8)
 
     far_x = per_slot(swap(served_part(own_x)))
 

time: 250 us -> 249 us (level)
    pallas_call x2 -> x1, Pallas kernels: 20.6 us -> 6.42 us  [allsum(): pl.pallas_call(functools.partial(allsum_kernel, axis, n), out_shape=jax.S...]
    pallas_call x0 -> x1, Pallas kernels: none -> 12.5 us  [rows_sum(): pl.pallas_call(functools.partial(rows_sum_kernel, n, group), out_shape=ja...]
where the time goes in v17:
time: 249 us; the launch traced here: 248 us
  waiting for transfers between devices  78.6 us (32%)
  Pallas kernels  54.5 us (22%)
  matrix products  46.3 us (19%)
  starting transfers between devices  36.6 us (15%)
  local copies, waits for them, and re-layouts  14.7 us (6%)
  other arithmetic  14.1 us (6%)
  between operations  3.06 us (1%)
    all_to_all x3, waiting for transfers between devices, swap(): lax.all_to_all(parts, 'rows', split_axis=0, concat_axis=0, tiled=True)  56.5 us
    pallas_call x2, Pallas kernels, fused_sum(): pl.pallas_call(functools.partial(fused_kernel, n_rows, n_cols), out_shape...  35.6 us
    dot_general x2, matrix products, wendland(): jnp.einsum('nda,ndb->nab', left_f, right_f, precision=lax.Precision.HIGHEST)  27.4 us
    all_to_all x3, starting transfers between devices, swap(): lax.all_to_all(parts, 'rows', split_axis=0, concat_axis=0, tiled=True)  23.6 us
    all_to_all x1, waiting for transfers between devices, local(): lax.all_to_all(jnp.concatenate([asked_x, request], axis=2), 'rows', split...  22.2 us
    all_to_all x1, starting transfers between devices, local(): lax.all_to_all(jnp.concatenate([asked_x, request], axis=2), 'rows', split...  13 us
    pallas_call x1, Pallas kernels, rows_sum(): pl.pallas_call(functools.partial(rows_sum_kernel, n, group), out_shape=ja...  12.5 us
    dot_general x2, matrix products, apply_partial(): jnp.einsum('joea,eab->job', picked, in_k, preferred_element_type=jnp.floa...  12 us
  transfers between devices with their start and end apart: 4, of which 4 were waited for; matrix products, arithmetic and copies ran while one was open for 7% of the time, Pallas kernels for 0%

profile of v17, /device:TPU:1, one launch (start us, length us, event | category | flops | bytes accessed | tf_op | source)
XLA Modules:
  0.0 247.9 jit_solution(16256795609140431127)
XLA Ops:
  6.5 13.0 %all-to-all-start = ((bf16[64,16,384]{2,1,0:T(8,128)(2,1)}), bf16[64,16,384]{2,1,0:T(8,128)(2,1)S(1)}, u32[]{:S(2)}, u32[]{:S(2)}) async-start(bf16[64,16,384]{2,1,0:T(8,128)(2,1)} %pad_maximum_fusion), calls=%async_computation | async-start | bytes 1572864 | tf_op jit(solution)/shard_map/all_to_all | solution.py:348
  20.3 22.2 %all-to-all-done = bf16[64,16,384]{2,1,0:T(8,128)(2,1)S(1)} async-done(((bf16[64,16,384]{2,1,0:T(8,128)(2,1)}), bf16[64,16,384]{2,1,0:T(8,128)(2,1)S(1)}, u32[]{:S(2)}, u32[]{:S(2)}) %all-to-all-start) | async-done | bytes 786464 | tf_op jit(solution)/shard_map/all_to_all | solution.py:348
  44.5 6.2 %all-to-all-start.1 = ((bf16[64,16,256]{2,1,0:T(8,128)(2,1)}), bf16[64,16,256]{2,1,0:T(8,128)(2,1)S(1)}, u32[]{:S(2)}, u32[]{:S(2)}) async-start(bf16[64,16,256]{2,1,0:T(8,128)(2,1)} %broadcast_select_fusion.2), calls=%async_computation.1 | async-start | bytes 1048576 | tf_op jit(solution)/shard_map/all_to_all | solution.py:362
  50.9 15.1 %fusion.69 = (f32[64,256]{1,0:T(8,128)S(1)}, bf16[64,256,256]{2,1,0:T(8,128)(2,1)}) fusion(bf16[64,16,256]{2,1,0:T(8,128)(2,1)S(1)} %gather_fusion.2, bf16[64,16,384]{2,1,0:T(8,128)(2,1)S(1)} %all-to-all-done, f32[64,256]{1,0:T(8,128)S(1)} %multiply_reduce_fusion, f32[64,256]{1,0:T(8,128)S(1)} %multiply_reduce_fusion.1, pred[64]{0:T(512)(128)(4,1)S(1)} %compare_and_fusion), kind=kOutput, calls=%fused_computation.155 | convolution fusion | flops 197115904 | bytes 9634304 | tf_op jit(solution)/shard_map/nda,ndb->nab/dot_general | solution.py:24
  66.0 2.0 all-to-all-done.1
  68.9 12.2 %fusion.68 = (bf16[48,256,256]{1,2,0:T(8,128)(2,1)}, f32[48,256]{1,0:T(8,128)S(1)}) fusion(bf16[48,16,256]{2,1,0:T(8,128)(2,1)S(1)} %gather_fusion, bf16[48,16,256]{2,1,0:T(8,128)(2,1)S(1)} %gather_fusion.3, pred[48]{0:T(512)(128)(4,1)S(1)} %broadcast_compare_fusion.2, f32[48,256]{1,0:T(8,128)S(1)} %multiply_reduce_fusion.2, ...), kind=kOutput, calls=%fused_computation.154 | convolution fusion | flops 148033536 | bytes 7225392 | tf_op jit(solution)/shard_map/nda,ndb->nab/dot_general | solution.py:24
  81.9 6.4 %shard_map.50 = f32[16,128]{1,0:T(8,128)} custom-call(f32[16,128]{1,0:T(8,128)} %reshape_reshape_broadcast_in_dim.3.x_ref), custom_call_target="tpu_custom_call" | custom-call | tf_op jit(solution)/shard_map/pallas_call | solution.py:99
  90.3 1.3 select_select_fusion.1
  91.6 9.5 %all-to-all-start.2 = ((bf16[64,32,256]{2,1,0:T(8,128)(2,1)}), bf16[64,32,256]{2,1,0:T(8,128)(2,1)S(1)}, u32[]{:S(2)}, u32[]{:S(2)}) async-start(bf16[64,32,256]{2,1,0:T(8,128)(2,1)} %select_select_fusion.1), calls=%async_computation.2 | async-start | bytes 2097152 | tf_op jit(solution)/shard_map/all_to_all | solution.py:362
  103.7 25.9 %all-to-all-done.2 = bf16[64,32,256]{2,1,0:T(8,128)(2,1)S(1)} async-done(((bf16[64,32,256]{2,1,0:T(8,128)(2,1)}), bf16[64,32,256]{2,1,0:T(8,128)(2,1)S(1)}, u32[]{:S(2)}, u32[]{:S(2)}) %all-to-all-start.2) | async-done | bytes 1048608 | tf_op jit(solution)/shard_map/all_to_all | solution.py:362
  129.6 1.2 broadcast_select_fusion.1
  130.8 1.6 gather_fusion.6
  132.4 6.2 %fusion.14 = f32[8,32,256]{2,1,0:T(8,128)S(1)} fusion(bf16[64,256,256]{2,1,0:T(8,128)(2,1)} %get-tuple-element.32, bf16[32,64,256]{2,0,1:T(8,128)(2,1)} %get-tuple-element.23, bf16[8,64]{1,0:T(8,128)(2,1)S(1)} %convert_convert_fusion), kind=kOutput, calls=%fused_computation.30 | convolution fusion | flops 2151677952 | bytes 9700352 | tf_op jit(solution)/shard_map/joea,eab->job/dot_general | solution.py:420
  138.6 2.0 fusion.39
  141.3 17.8 %shard_map.51 = (f32[4,64,256]{2,1,0:T(8,128)}, f32[1,128]{1,0:T(1,128)}) custom-call(f32[4,64,256]{2,1,0:T(8,128)} %bitcast.195, f32[1,128]{1,0:T(1,128)} %fusion.58.g_ref), custom_call_target="tpu_custom_call" | custom-call | tf_op jit(solution)/shard_map/pallas_call | solution.py:214
  159.9 1.2 multiply_reduce_fusion.6
  161.6 12.5 %shard_map.52 = f32[1,128]{1,0:T(1,128)} custom-call(f32[1,128]{1,0:T(1,128)} %pad_bitcast_fusion.1.x_ref), custom_call_target="tpu_custom_call" | custom-call | tf_op jit(solution)/shard_map/pallas_call | solution.py:302
  177.1 1.3 select_select_fusion
  178.4 7.9 %all-to-all-start.3 = ((bf16[64,32,256]{2,1,0:T(8,128)(2,1)}), bf16[64,32,256]{2,1,0:T(8,128)(2,1)S(1)}, u32[]{:S(2)}, u32[]{:S(2)}) async-start(bf16[64,32,256]{2,1,0:T(8,128)(2,1)} %select_select_fusion), calls=%async_computation.3 | async-start | bytes 2097152 | tf_op jit(solution)/shard_map/all_to_all | solution.py:362
  186.3 28.5 %all-to-all-done.3 = bf16[64,32,256]{2,1,0:T(8,128)(2,1)S(1)} async-done(((bf16[64,32,256]{2,1,0:T(8,128)(2,1)}), bf16[64,32,256]{2,1,0:T(8,128)(2,1)S(1)}, u32[]{:S(2)}, u32[]{:S(2)}) %all-to-all-start.3) | async-done | bytes 1048608 | tf_op jit(solution)/shard_map/all_to_all | solution.py:362
  215.1 5.8 %fusion.19 = f32[8,32,256]{2,1,0:T(8,128)S(1)} fusion(bf16[64,256,256]{2,1,0:T(8,128)(2,1)} %get-tuple-element.32, bf16[32,64,256]{2,0,1:T(8,128)(2,1)S(1)} %get-tuple-element.21, bf16[8,64]{1,0:T(8,128)(2,1)S(1)} %convert_convert_fusion), kind=kOutput, calls=%fused_computation.31 | convolution fusion | flops 2151677952 | bytes 9700352 | tf_op jit(solution)/shard_map/joea,eab->job/dot_general | solution.py:420
  221.5 4.8 %multiply_reduce_fusion.5 = (f32[32]{0:T(128)S(1)}, f32[32]{0:T(128)S(1)}, f32[8,32,256]{2,1,0:T(8,128)}) fusion(f32[8,32,256]{2,1,0:T(8,128)S(1)} %get-tuple-element.15, f32[8,256]{1,0:T(8,128)S(1)} %sqrt.14, f32[8,32,256]{2,1,0:T(8,128)S(1)} %fusion.19, bf16[8,6,256,256]{2,3,1,0:T(8,128)(2,1)} %bitcast.181, bf16[8,6,32,256]{3,2,1,0:T(8,128)(2,1)S(1)} %bitcast.191, ...), kind=kOutput, calls=%fused_computation.73 | convolution fusion | flops 202112960 | bytes 7872816 | tf_op jit(solution)/shard_map/rkab,rkob->roa/dot_general | solution.py:413
  226.8 17.8 %shard_map.53 = (f32[4,64,256]{2,1,0:T(8,128)}, f32[1,128]{1,0:T(1,128)}) custom-call(f32[4,64,256]{2,1,0:T(8,128)} %bitcast.196, f32[1,128]{1,0:T(1,128)} %pad_bitcast_fusion.g_ref), custom_call_target="tpu_custom_call" | custom-call | tf_op jit(solution)/shard_map/pallas_call | solution.py:214
  245.3 1.1 subtract_bitcast_fusion
  (81 shorter events, 21.3 us)
Async XLA Ops:
  6.5 36.0 %all-to-all-start = ((bf16[64,16,384]{2,1,0:T(8,128)(2,1)}), bf16[64,16,384]{2,1,0:T(8,128)(2,1)S(1)}, u32[]{:S(2)}, u32[]{:S(2)}) async-start(bf16[64,16,384]{2,1,0:T(8,128)(2,1)} %pad_maximum_fusion), calls=%async_computation | async-start | bytes 1572864 | tf_op jit(solution)/shard_map/all_to_all | solution.py:348
  44.5 23.5 %all-to-all-start.1 = ((bf16[64,16,256]{2,1,0:T(8,128)(2,1)}), bf16[64,16,256]{2,1,0:T(8,128)(2,1)S(1)}, u32[]{:S(2)}, u32[]{:S(2)}) async-start(bf16[64,16,256]{2,1,0:T(8,128)(2,1)} %broadcast_select_fusion.2), calls=%async_computation.1 | async-start | bytes 1048576 | tf_op jit(solution)/shard_map/all_to_all | solution.py:362
  68.9 20.2 %copy-start = (f32[32,2048]{1,0:T(8,128)S(1)}, f32[32,2048]{1,0:T(8,128)}, u32[]{:S(2)}) copy-start(f32[32,2048]{1,0:T(8,128)} %param.5) | copy-start | bytes 786436
  81.1 20.0 %copy-start.3 = (s32[8,6]{1,0:T(8,128)S(1)}, s32[8,6]{1,0:T(8,128)}, u32[]{:S(2)}) copy-start(s32[8,6]{1,0:T(8,128)} %param.3) | copy-start | bytes 580
  91.6 38.1 %all-to-all-start.2 = ((bf16[64,32,256]{2,1,0:T(8,128)(2,1)}), bf16[64,32,256]{2,1,0:T(8,128)(2,1)S(1)}, u32[]{:S(2)}, u32[]{:S(2)}) async-start(bf16[64,32,256]{2,1,0:T(8,128)(2,1)} %select_select_fusion.1), calls=%async_computation.2 | async-start | bytes 2097152 | tf_op jit(solution)/shard_map/all_to_all | solution.py:362
  130.8 7.8 %slice-start = ((s8[6291456]{0:T(1024)(128)(4,1)}), s8[2097152]{0:T(1024)(128)(4,1)S(1)}, s32[]{:S(2)}) async-start(s8[6291456]{0:T(1024)(128)(4,1)} %bitcast.182), calls=%async_computation.4 | async-start | bytes 4194304
  132.4 6.2 %slice-start.1 = ((s8[6291456]{0:T(1024)(128)(4,1)}), s8[4194304]{0:T(1024)(128)(4,1)S(1)}, s32[]{:S(2)}) async-start(s8[6291456]{0:T(1024)(128)(4,1)} %bitcast.182), calls=%async_computation.5 | async-start | bytes 8388608
  132.4 6.2 %copy-start.1 = (bf16[48,32,256]{2,1,0:T(8,128)(2,1)S(1)}, bf16[48,32,256]{2,1,0:T(8,128)(2,1)}, u32[]{:S(2)}) copy-start(bf16[48,32,256]{2,1,0:T(8,128)(2,1)} %gather_fusion.6) | copy-start | bytes 2359300
  178.4 36.5 %all-to-all-start.3 = ((bf16[64,32,256]{2,1,0:T(8,128)(2,1)}), bf16[64,32,256]{2,1,0:T(8,128)(2,1)S(1)}, u32[]{:S(2)}, u32[]{:S(2)}) async-start(bf16[64,32,256]{2,1,0:T(8,128)(2,1)} %select_select_fusion), calls=%async_computation.3 | async-start | bytes 2097152 | tf_op jit(solution)/shard_map/all_to_all | solution.py:362
  220.8 23.8 %copy-start.4 = (f32[1,128]{1,0:T(1,128)S(1)}, f32[1,128]{1,0:T(1,128)}, u32[]{:S(2)}) copy-start(f32[1,128]{1,0:T(1,128)} %shard_map.52) | copy-start | bytes 1540
  220.8 24.5 %copy-start.2 = (f32[4,64,256]{2,1,0:T(8,128)S(1)}, f32[4,64,256]{2,1,0:T(8,128)}, u32[]{:S(2)}) copy-start(f32[4,64,256]{2,1,0:T(8,128)} %get-tuple-element.7) | copy-start | bytes 786436

commit v18 on v17

--- a/solution.py
+++ b/solution.py
@@ -112,25 +112,33 @@
 
 
 def fused_kernel(
-    n_rows, n_cols, z_ref, g_ref, zo_ref, go_ref, recv_z, gathered, recv_g, recv_s, rows_sum, sems
+    n_rows, n_cols, group, z_ref, g_ref, zo_ref, go_ref, recv_z, gathered, recv_g, recv_b, recv_s, rows_sum,
+    sems,
 ):
     row = lax.axis_index("rows")
     col = lax.axis_index("cols")
     barrier = pltpu.get_barrier_semaphore()
 
-    def greet(k, carry):
-        pl.semaphore_signal(
-            barrier, inc=1, device_id={"rows": lax.rem(row + k, n_rows)}, device_id_type=MESH
-        )
-        return carry
-
-    lax.fori_loop(1, n_rows, greet, 0)
+    pos = lax.rem(row, group)
+    grp = row // group
+    groups = n_rows // group
+
+    def near(k):
+        return row - pos + lax.rem(pos + k, group)
+
+    def far(k):
+        return lax.rem(grp + k, groups) * group + pos
+
+    for k in range(1, group):
+        pl.semaphore_signal(barrier, inc=1, device_id={"rows": near(k)}, device_id_type=MESH)
+    for k in range(1, groups):
+        pl.semaphore_signal(barrier, inc=1, device_id={"rows": far(k)}, device_id_type=MESH)
     for k in range(1, n_cols):
         pl.semaphore_signal(
             barrier, inc=1, device_id={"cols": lax.rem(col + k, n_cols)}, device_id_type=MESH
         )
-    pl.semaphore_wait(barrier, n_rows - 1 + n_cols - 1)
-    z_send, z_recv, g_send, g_recv, s_send, s_recv, a_send, a_recv = sems
+    pl.semaphore_wait(barrier, group - 1 + groups - 1 + n_cols - 1)
+    z_send, z_recv, g_send, g_recv, s_send, s_recv, a_send, a_recv, b_send, b_recv = sems
 
     def col_copy(src, dst, send, recv, peer, slot):
         return pltpu.make_async_remote_copy(
@@ -142,13 +150,13 @@
             device_id_type=MESH,
         )
 
-    def g_copy(peer, slot):
+    def row_copy(src, dst, send, recv, device, slot, peer_slot):
         return pltpu.make_async_remote_copy(
-            src_ref=g_ref,
-            dst_ref=recv_g.at[slot],
-            send_sem=g_send.at[peer],
-            recv_sem=g_recv.at[slot],
-            device_id={"rows": peer},
+            src_ref=src,
+            dst_ref=dst.at[slot],
+            send_sem=send.at[peer_slot],
+            recv_sem=recv.at[slot],
+            device_id={"rows": device},
             device_id_type=MESH,
         )
 
@@ -156,13 +164,10 @@
         peer = lax.rem(col + k, n_cols)
         col_copy(z_ref.at[peer], recv_z, z_send, z_recv, peer, col).start()
 
-    def start(k, carry):
-        g_copy(lax.rem(row + k, n_rows), row).start()
-        return carry
-
-    lax.fori_loop(1, n_rows, start, 0)
+    for k in range(1, group):
+        row_copy(g_ref, recv_g, g_send, g_recv, near(k), pos, lax.rem(pos + k, group)).start()
     recv_z[col] = z_ref[col]
-    recv_g[row] = g_ref[...]
+    recv_g[pos] = g_ref[...]
     for k in range(1, n_cols):
         peer = lax.rem(col + k, n_cols)
         col_copy(z_ref.at[peer], recv_z, z_send, z_recv, peer, col).wait_send()
@@ -173,20 +178,22 @@
     for k in range(1, n_cols):
         col_copy(gathered.at[col], gathered, a_send, a_recv, lax.rem(col + k, n_cols), col).start()
 
-    def finish(k, carry):
-        peer = lax.rem(row + k, n_rows)
-        g_copy(peer, row).wait_send()
-        g_copy(peer, peer).wait_recv()
-        return carry
-
-    lax.fori_loop(1, n_rows, finish, 0)
-    rows_sum[...] = recv_g[0]
-
-    def add(s, carry):
-        rows_sum[...] += recv_g[s]
-        return carry
-
-    lax.fori_loop(1, n_rows, add, 0)
+    for k in range(1, group):
+        other = lax.rem(pos + k, group)
+        row_copy(g_ref, recv_g, g_send, g_recv, near(k), pos, other).wait_send()
+        row_copy(g_ref, recv_g, g_send, g_recv, near(k), other, other).wait_recv()
+    recv_b[grp] = recv_g[0]
+    for k in range(1, group):
+        recv_b[grp] += recv_g[k]
+    for k in range(1, groups):
+        row_copy(recv_b.at[grp], recv_b, b_send, b_recv, far(k), grp, lax.rem(grp + k, groups)).start()
+    for k in range(1, groups):
+        other = lax.rem(grp + k, groups)
+        row_copy(recv_b.at[grp], recv_b, b_send, b_recv, far(k), grp, other).wait_send()
+        row_copy(recv_b.at[grp], recv_b, b_send, b_recv, far(k), other, other).wait_recv()
+    rows_sum[...] = recv_b[0]
+    for k in range(1, groups):
+        rows_sum[...] += recv_b[k]
     for k in range(1, n_cols):
         col_copy(rows_sum, recv_s, s_send, s_recv, lax.rem(col + k, n_cols), col).start()
     recv_s[col] = rows_sum[...]
@@ -211,8 +218,10 @@
     size = g.shape[0]
     g_tile = jnp.pad(g, (0, 128 - size)).reshape(1, 128)
     vmem = pl.BlockSpec(memory_space=pltpu.VMEM)
+    group = 16 if n_rows % 16 == 0 and n_rows > 16 else (4 if n_rows % 4 == 0 else n_rows)
+    groups = n_rows // group
     z_out, g_out = pl.pallas_call(
-        functools.partial(fused_kernel, n_rows, n_cols),
+        functools.partial(fused_kernel, n_rows, n_cols, group),
         out_shape=[
             jax.ShapeDtypeStruct(z_tile.shape, jnp.float32),
             jax.ShapeDtypeStruct(g_tile.shape, jnp.float32),
@@ -222,18 +231,21 @@
         scratch_shapes=[
             pltpu.VMEM(z_tile.shape, jnp.float32),
             pltpu.VMEM(z_tile.shape, jnp.float32),
-            pltpu.VMEM((n_rows,) + g_tile.shape, jnp.float32),
+            pltpu.VMEM((group,) + g_tile.shape, jnp.float32),
+            pltpu.VMEM((groups,) + g_tile.shape, jnp.float32),
             pltpu.VMEM((n_cols,) + g_tile.shape, jnp.float32),
             pltpu.VMEM(g_tile.shape, jnp.float32),
             [
                 pltpu.SemaphoreType.DMA((n_cols,)),
                 pltpu.SemaphoreType.DMA((n_cols,)),
-                pltpu.SemaphoreType.DMA((n_rows,)),
-                pltpu.SemaphoreType.DMA((n_rows,)),
-                pltpu.SemaphoreType.DMA((n_cols,)),
-                pltpu.SemaphoreType.DMA((n_cols,)),
-                pltpu.SemaphoreType.DMA((n_cols,)),
-                pltpu.SemaphoreType.DMA((n_cols,)),
+                pltpu.SemaphoreType.DMA((group,)),
+                pltpu.SemaphoreType.DMA((group,)),
+                pltpu.SemaphoreType.DMA((n_cols,)),
+                pltpu.SemaphoreType.DMA((n_cols,)),
+                pltpu.SemaphoreType.DMA((n_cols,)),
+                pltpu.SemaphoreType.DMA((n_cols,)),
+                pltpu.SemaphoreType.DMA((groups,)),
+                pltpu.SemaphoreType.DMA((groups,)),
             ],
         ],
         compiler_params=pltpu.CompilerParams(collective_id=cid, has_side_effects=True),

time: 249 us -> 246 us (0.988)
  Pallas kernels: 54.5 us -> 51.5 us
    pallas_call x2, Pallas kernels: 35.6 us -> 32.4 us  [fused_sum(): pl.pallas_call(functools.partial(fused_kernel, n_rows, n_cols, group), ou...]
where the time goes in v18:
time: 246 us
  waiting for transfers between devices  78.6 us (32%)
  Pallas kernels  51.5 us (21%)
  matrix products  46.3 us (19%)
  starting transfers between devices  37.3 us (15%)
  local copies, waits for them, and re-layouts  14.7 us (6%)
  other arithmetic  14.1 us (6%)
  between operations  3.06 us (1%)
    all_to_all x3, waiting for transfers between devices, swap(): lax.all_to_all(parts, 'rows', split_axis=0, concat_axis=0, tiled=True)  56.5 us
    pallas_call x2, Pallas kernels, fused_sum(): pl.pallas_call(functools.partial(fused_kernel, n_rows, n_cols, group), ou...  32.4 us
    dot_general x2, matrix products, wendland(): jnp.einsum('nda,ndb->nab', left_f, right_f, precision=lax.Precision.HIGHEST)  27.4 us
    all_to_all x3, starting transfers between devices, swap(): lax.all_to_all(parts, 'rows', split_axis=0, concat_axis=0, tiled=True)  24.3 us
    all_to_all x1, waiting for transfers between devices, local(): lax.all_to_all(jnp.concatenate([asked_x, request], axis=2), 'rows', split...  22.2 us
    all_to_all x1, starting transfers between devices, local(): lax.all_to_all(jnp.concatenate([asked_x, request], axis=2), 'rows', split...  13 us
    pallas_call x1, Pallas kernels, rows_sum(): pl.pallas_call(functools.partial(rows_sum_kernel, n, group), out_shape=ja...  12.7 us
    dot_general x2, matrix products, apply_partial(): jnp.einsum('joea,eab->job', picked, in_k, preferred_element_type=jnp.floa...  12 us
  transfers between devices with their start and end apart: 4, of which 4 were waited for; matrix products, arithmetic and copies ran while one was open for 7% of the time, Pallas kernels for 0%

profile of v18, /device:TPU:1, one launch (start us, length us, event | category | flops | bytes accessed | tf_op | source)
XLA Modules:
  0.0 245.6 jit_solution(9983039240230637323)
XLA Ops:
  6.5 13.0 %all-to-all-start = ((bf16[64,16,384]{2,1,0:T(8,128)(2,1)}), bf16[64,16,384]{2,1,0:T(8,128)(2,1)S(1)}, u32[]{:S(2)}, u32[]{:S(2)}) async-start(bf16[64,16,384]{2,1,0:T(8,128)(2,1)} %pad_maximum_fusion), calls=%async_computation | async-start | bytes 1572864 | tf_op jit(solution)/shard_map/all_to_all | solution.py:360
  20.3 22.2 %all-to-all-done = bf16[64,16,384]{2,1,0:T(8,128)(2,1)S(1)} async-done(((bf16[64,16,384]{2,1,0:T(8,128)(2,1)}), bf16[64,16,384]{2,1,0:T(8,128)(2,1)S(1)}, u32[]{:S(2)}, u32[]{:S(2)}) %all-to-all-start) | async-done | bytes 786464 | tf_op jit(solution)/shard_map/all_to_all | solution.py:360
  44.5 6.2 %all-to-all-start.1 = ((bf16[64,16,256]{2,1,0:T(8,128)(2,1)}), bf16[64,16,256]{2,1,0:T(8,128)(2,1)S(1)}, u32[]{:S(2)}, u32[]{:S(2)}) async-start(bf16[64,16,256]{2,1,0:T(8,128)(2,1)} %broadcast_select_fusion.2), calls=%async_computation.1 | async-start | bytes 1048576 | tf_op jit(solution)/shard_map/all_to_all | solution.py:374
  50.9 15.1 %fusion.69 = (f32[64,256]{1,0:T(8,128)S(1)}, bf16[64,256,256]{2,1,0:T(8,128)(2,1)}) fusion(bf16[64,16,256]{2,1,0:T(8,128)(2,1)S(1)} %gather_fusion.2, bf16[64,16,384]{2,1,0:T(8,128)(2,1)S(1)} %all-to-all-done, f32[64,256]{1,0:T(8,128)S(1)} %multiply_reduce_fusion, f32[64,256]{1,0:T(8,128)S(1)} %multiply_reduce_fusion.1, pred[64]{0:T(512)(128)(4,1)S(1)} %compare_and_fusion), kind=kOutput, calls=%fused_computation.155 | convolution fusion | flops 197115904 | bytes 9634304 | tf_op jit(solution)/shard_map/nda,ndb->nab/dot_general | solution.py:24
  66.0 2.0 all-to-all-done.1
  68.9 12.2 %fusion.68 = (bf16[48,256,256]{1,2,0:T(8,128)(2,1)}, f32[48,256]{1,0:T(8,128)S(1)}) fusion(bf16[48,16,256]{2,1,0:T(8,128)(2,1)S(1)} %gather_fusion, bf16[48,16,256]{2,1,0:T(8,128)(2,1)S(1)} %gather_fusion.3, pred[48]{0:T(512)(128)(4,1)S(1)} %broadcast_compare_fusion.2, f32[48,256]{1,0:T(8,128)S(1)} %multiply_reduce_fusion.2, ...), kind=kOutput, calls=%fused_computation.154 | convolution fusion | flops 148033536 | bytes 7225392 | tf_op jit(solution)/shard_map/nda,ndb->nab/dot_general | solution.py:24
  81.9 6.4 %shard_map.50 = f32[16,128]{1,0:T(8,128)} custom-call(f32[16,128]{1,0:T(8,128)} %reshape_reshape_broadcast_in_dim.3.x_ref), custom_call_target="tpu_custom_call" | custom-call | tf_op jit(solution)/shard_map/pallas_call | solution.py:99
  90.3 1.3 select_select_fusion.1
  91.6 9.5 %all-to-all-start.2 = ((bf16[64,32,256]{2,1,0:T(8,128)(2,1)}), bf16[64,32,256]{2,1,0:T(8,128)(2,1)S(1)}, u32[]{:S(2)}, u32[]{:S(2)}) async-start(bf16[64,32,256]{2,1,0:T(8,128)(2,1)} %select_select_fusion.1), calls=%async_computation.2 | async-start | bytes 2097152 | tf_op jit(solution)/shard_map/all_to_all | solution.py:374
  103.7 25.9 %all-to-all-done.2 = bf16[64,32,256]{2,1,0:T(8,128)(2,1)S(1)} async-done(((bf16[64,32,256]{2,1,0:T(8,128)(2,1)}), bf16[64,32,256]{2,1,0:T(8,128)(2,1)S(1)}, u32[]{:S(2)}, u32[]{:S(2)}) %all-to-all-start.2) | async-done | bytes 1048608 | tf_op jit(solution)/shard_map/all_to_all | solution.py:374
  129.6 1.2 broadcast_select_fusion.1
  130.8 1.6 gather_fusion.6
  132.4 6.2 %fusion.14 = f32[8,32,256]{2,1,0:T(8,128)S(1)} fusion(bf16[64,256,256]{2,1,0:T(8,128)(2,1)} %get-tuple-element.32, bf16[32,64,256]{2,0,1:T(8,128)(2,1)} %get-tuple-element.23, bf16[8,64]{1,0:T(8,128)(2,1)S(1)} %convert_convert_fusion), kind=kOutput, calls=%fused_computation.30 | convolution fusion | flops 2151677952 | bytes 9700352 | tf_op jit(solution)/shard_map/joea,eab->job/dot_general | solution.py:432
  138.6 2.0 fusion.39
  141.3 16.2 %shard_map.51 = (f32[4,64,256]{2,1,0:T(8,128)}, f32[1,128]{1,0:T(1,128)}) custom-call(f32[4,64,256]{2,1,0:T(8,128)} %bitcast.195, f32[1,128]{1,0:T(1,128)} %fusion.58.g_ref), custom_call_target="tpu_custom_call" | custom-call | tf_op jit(solution)/shard_map/pallas_call | solution.py:223
  158.3 1.2 multiply_reduce_fusion.6
  160.0 12.7 %shard_map.52 = f32[1,128]{1,0:T(1,128)} custom-call(f32[1,128]{1,0:T(1,128)} %pad_bitcast_fusion.1.x_ref), custom_call_target="tpu_custom_call" | custom-call | tf_op jit(solution)/shard_map/pallas_call | solution.py:314
  175.7 1.3 select_select_fusion
  177.0 8.6 %all-to-all-start.3 = ((bf16[64,32,256]{2,1,0:T(8,128)(2,1)}), bf16[64,32,256]{2,1,0:T(8,128)(2,1)S(1)}, u32[]{:S(2)}, u32[]{:S(2)}) async-start(bf16[64,32,256]{2,1,0:T(8,128)(2,1)} %select_select_fusion), calls=%async_computation.3 | async-start | bytes 2097152 | tf_op jit(solution)/shard_map/all_to_all | solution.py:374
  185.6 28.5 %all-to-all-done.3 = bf16[64,32,256]{2,1,0:T(8,128)(2,1)S(1)} async-done(((bf16[64,32,256]{2,1,0:T(8,128)(2,1)}), bf16[64,32,256]{2,1,0:T(8,128)(2,1)S(1)}, u32[]{:S(2)}, u32[]{:S(2)}) %all-to-all-start.3) | async-done | bytes 1048608 | tf_op jit(solution)/shard_map/all_to_all | solution.py:374
  214.3 5.8 %fusion.19 = f32[8,32,256]{2,1,0:T(8,128)S(1)} fusion(bf16[64,256,256]{2,1,0:T(8,128)(2,1)} %get-tuple-element.32, bf16[32,64,256]{2,0,1:T(8,128)(2,1)S(1)} %get-tuple-element.21, bf16[8,64]{1,0:T(8,128)(2,1)S(1)} %convert_convert_fusion), kind=kOutput, calls=%fused_computation.31 | convolution fusion | flops 2151677952 | bytes 9700352 | tf_op jit(solution)/shard_map/joea,eab->job/dot_general | solution.py:432
  220.8 4.8 %multiply_reduce_fusion.5 = (f32[32]{0:T(128)S(1)}, f32[32]{0:T(128)S(1)}, f32[8,32,256]{2,1,0:T(8,128)}) fusion(f32[8,32,256]{2,1,0:T(8,128)S(1)} %get-tuple-element.15, f32[8,256]{1,0:T(8,128)S(1)} %sqrt.14, f32[8,32,256]{2,1,0:T(8,128)S(1)} %fusion.19, bf16[8,6,256,256]{2,3,1,0:T(8,128)(2,1)} %bitcast.181, bf16[8,6,32,256]{3,2,1,0:T(8,128)(2,1)S(1)} %bitcast.191, ...), kind=kOutput, calls=%fused_computation.73 | convolution fusion | flops 202112960 | bytes 7872816 | tf_op jit(solution)/shard_map/rkab,rkob->roa/dot_general | solution.py:425
  226.1 16.2 %shard_map.53 = (f32[4,64,256]{2,1,0:T(8,128)}, f32[1,128]{1,0:T(1,128)}) custom-call(f32[4,64,256]{2,1,0:T(8,128)} %bitcast.196, f32[1,128]{1,0:T(1,128)} %pad_bitcast_fusion.g_ref), custom_call_target="tpu_custom_call" | custom-call | tf_op jit(solution)/shard_map/pallas_call | solution.py:223
  243.0 1.1 subtract_bitcast_fusion
  (81 shorter events, 21.3 us)
Async XLA Ops:
  6.5 36.0 %all-to-all-start = ((bf16[64,16,384]{2,1,0:T(8,128)(2,1)}), bf16[64,16,384]{2,1,0:T(8,128)(2,1)S(1)}, u32[]{:S(2)}, u32[]{:S(2)}) async-start(bf16[64,16,384]{2,1,0:T(8,128)(2,1)} %pad_maximum_fusion), calls=%async_computation | async-start | bytes 1572864 | tf_op jit(solution)/shard_map/all_to_all | solution.py:360
  44.5 23.5 %all-to-all-start.1 = ((bf16[64,16,256]{2,1,0:T(8,128)(2,1)}), bf16[64,16,256]{2,1,0:T(8,128)(2,1)S(1)}, u32[]{:S(2)}, u32[]{:S(2)}) async-start(bf16[64,16,256]{2,1,0:T(8,128)(2,1)} %broadcast_select_fusion.2), calls=%async_computation.1 | async-start | bytes 1048576 | tf_op jit(solution)/shard_map/all_to_all | solution.py:374
  68.9 20.2 %copy-start = (f32[32,2048]{1,0:T(8,128)S(1)}, f32[32,2048]{1,0:T(8,128)}, u32[]{:S(2)}) copy-start(f32[32,2048]{1,0:T(8,128)} %param.5) | copy-start | bytes 786436
  81.1 20.0 %copy-start.3 = (s32[8,6]{1,0:T(8,128)S(1)}, s32[8,6]{1,0:T(8,128)}, u32[]{:S(2)}) copy-start(s32[8,6]{1,0:T(8,128)} %param.3) | copy-start | bytes 580
  91.6 38.1 %all-to-all-start.2 = ((bf16[64,32,256]{2,1,0:T(8,128)(2,1)}), bf16[64,32,256]{2,1,0:T(8,128)(2,1)S(1)}, u32[]{:S(2)}, u32[]{:S(2)}) async-start(bf16[64,32,256]{2,1,0:T(8,128)(2,1)} %select_select_fusion.1), calls=%async_computation.2 | async-start | bytes 2097152 | tf_op jit(solution)/shard_map/all_to_all | solution.py:374
  130.8 7.8 %slice-start = ((s8[6291456]{0:T(1024)(128)(4,1)}), s8[2097152]{0:T(1024)(128)(4,1)S(1)}, s32[]{:S(2)}) async-start(s8[6291456]{0:T(1024)(128)(4,1)} %bitcast.182), calls=%async_computation.4 | async-start | bytes 4194304
  132.4 6.2 %slice-start.1 = ((s8[6291456]{0:T(1024)(128)(4,1)}), s8[4194304]{0:T(1024)(128)(4,1)S(1)}, s32[]{:S(2)}) async-start(s8[6291456]{0:T(1024)(128)(4,1)} %bitcast.182), calls=%async_computation.5 | async-start | bytes 8388608
  132.4 6.2 %copy-start.1 = (bf16[48,32,256]{2,1,0:T(8,128)(2,1)S(1)}, bf16[48,32,256]{2,1,0:T(8,128)(2,1)}, u32[]{:S(2)}) copy-start(bf16[48,32,256]{2,1,0:T(8,128)(2,1)} %gather_fusion.6) | copy-start | bytes 2359300
  177.0 37.1 %all-to-all-start.3 = ((bf16[64,32,256]{2,1,0:T(8,128)(2,1)}), bf16[64,32,256]{2,1,0:T(8,128)(2,1)S(1)}, u32[]{:S(2)}, u32[]{:S(2)}) async-start(bf16[64,32,256]{2,1,0:T(8,128)(2,1)} %select_select_fusion), calls=%async_computation.3 | async-start | bytes 2097152 | tf_op jit(solution)/shard_map/all_to_all | solution.py:374
  220.1 22.2 %copy-start.4 = (f32[1,128]{1,0:T(1,128)S(1)}, f32[1,128]{1,0:T(1,128)}, u32[]{:S(2)}) copy-start(f32[1,128]{1,0:T(1,128)} %shard_map.52) | copy-start | bytes 1540
  220.1 22.8 %copy-start.2 = (f32[4,64,256]{2,1,0:T(8,128)S(1)}, f32[4,64,256]{2,1,0:T(8,128)}, u32[]{:S(2)}) copy-start(f32[4,64,256]{2,1,0:T(8,128)} %get-tuple-element.7) | copy-start | bytes 786436

commit v19 on v18

--- a/solution.py
+++ b/solution.py
@@ -218,7 +218,7 @@
     size = g.shape[0]
     g_tile = jnp.pad(g, (0, 128 - size)).reshape(1, 128)
     vmem = pl.BlockSpec(memory_space=pltpu.VMEM)
-    group = 16 if n_rows % 16 == 0 and n_rows > 16 else (4 if n_rows % 4 == 0 else n_rows)
+    group = 8 if n_rows % 8 == 0 and n_rows > 8 else (4 if n_rows % 4 == 0 else n_rows)
     groups = n_rows // group
     z_out, g_out = pl.pallas_call(
         functools.partial(fused_kernel, n_rows, n_cols, group),
@@ -307,7 +307,7 @@
 
 def rows_sum(x, cid):
     n = lax.axis_size("rows")
-    group = 16 if n % 16 == 0 and n > 16 else (4 if n % 4 == 0 else n)
+    group = 8 if n % 8 == 0 and n > 8 else (4 if n % 4 == 0 else n)
     groups = n // group
     size = x.shape[0]
     tile = jnp.pad(x, (0, 128 - size)).reshape(1, 128)

time: 246 us -> 254 us (1.033)
  Pallas kernels: 51.5 us -> 60.6 us
    pallas_call x2, Pallas kernels: 32.4 us -> 38.5 us  [fused_sum(): pl.pallas_call(functools.partial(fused_kernel, n_rows, n_cols, group), ou...]
    pallas_call x1, Pallas kernels: 12.7 us -> 15.7 us  [rows_sum(): pl.pallas_call(functools.partial(rows_sum_kernel, n, group), out_shape=ja...]
where the time goes in v19:
time: 254 us; the launch traced here: 253 us
  waiting for transfers between devices  78.6 us (31%)
  Pallas kernels  60.6 us (24%)
  matrix products  46.3 us (18%)
  starting transfers between devices  35.8 us (14%)
  local copies, waits for them, and re-layouts  14.7 us (6%)
  other arithmetic  14.1 us (6%)
  between operations  3.06 us (1%)
    all_to_all x3, waiting for transfers between devices, swap(): lax.all_to_all(parts, 'rows', split_axis=0, concat_axis=0, tiled=True)  56.5 us
    pallas_call x2, Pallas kernels, fused_sum(): pl.pallas_call(functools.partial(fused_kernel, n_rows, n_cols, group), ou...  38.5 us
    dot_general x2, matrix products, wendland(): jnp.einsum('nda,ndb->nab', left_f, right_f, precision=lax.Precision.HIGHEST)  27.4 us
    all_to_all x3, starting transfers between devices, swap(): lax.all_to_all(parts, 'rows', split_axis=0, concat_axis=0, tiled=True)  22.9 us
    all_to_all x1, waiting for transfers between devices, local(): lax.all_to_all(jnp.concatenate([asked_x, request], axis=2), 'rows', split...  22.2 us
    pallas_call x1, Pallas kernels, rows_sum(): pl.pallas_call(functools.partial(rows_sum_kernel, n, group), out_shape=ja...  15.7 us
    all_to_all x1, starting transfers between devices, local(): lax.all_to_all(jnp.concatenate([asked_x, request], axis=2), 'rows', split...  13 us
    dot_general x2, matrix products, apply_partial(): jnp.einsum('joea,eab->job', picked, in_k, preferred_element_type=jnp.floa...  12 us
  transfers between devices with their start and end apart: 4, of which 4 were waited for; matrix products, arithmetic and copies ran while one was open for 7% of the time, Pallas kernels for 0%

profile of v19, /device:TPU:1, one launch (start us, length us, event | category | flops | bytes accessed | tf_op | source)
XLA Modules:
  0.0 253.2 jit_solution(8261755058865644157)
XLA Ops:
  6.5 13.0 %all-to-all-start = ((bf16[64,16,384]{2,1,0:T(8,128)(2,1)}), bf16[64,16,384]{2,1,0:T(8,128)(2,1)S(1)}, u32[]{:S(2)}, u32[]{:S(2)}) async-start(bf16[64,16,384]{2,1,0:T(8,128)(2,1)} %pad_maximum_fusion), calls=%async_computation | async-start | bytes 1572864 | tf_op jit(solution)/shard_map/all_to_all | solution.py:360
  20.3 22.2 %all-to-all-done = bf16[64,16,384]{2,1,0:T(8,128)(2,1)S(1)} async-done(((bf16[64,16,384]{2,1,0:T(8,128)(2,1)}), bf16[64,16,384]{2,1,0:T(8,128)(2,1)S(1)}, u32[]{:S(2)}, u32[]{:S(2)}) %all-to-all-start) | async-done | bytes 786464 | tf_op jit(solution)/shard_map/all_to_all | solution.py:360
  44.5 6.2 %all-to-all-start.1 = ((bf16[64,16,256]{2,1,0:T(8,128)(2,1)}), bf16[64,16,256]{2,1,0:T(8,128)(2,1)S(1)}, u32[]{:S(2)}, u32[]{:S(2)}) async-start(bf16[64,16,256]{2,1,0:T(8,128)(2,1)} %broadcast_select_fusion.2), calls=%async_computation.1 | async-start | bytes 1048576 | tf_op jit(solution)/shard_map/all_to_all | solution.py:374
  50.9 15.1 %fusion.69 = (f32[64,256]{1,0:T(8,128)S(1)}, bf16[64,256,256]{2,1,0:T(8,128)(2,1)}) fusion(bf16[64,16,256]{2,1,0:T(8,128)(2,1)S(1)} %gather_fusion.2, bf16[64,16,384]{2,1,0:T(8,128)(2,1)S(1)} %all-to-all-done, f32[64,256]{1,0:T(8,128)S(1)} %multiply_reduce_fusion, f32[64,256]{1,0:T(8,128)S(1)} %multiply_reduce_fusion.1, pred[64]{0:T(512)(128)(4,1)S(1)} %compare_and_fusion), kind=kOutput, calls=%fused_computation.155 | convolution fusion | flops 197115904 | bytes 9634304 | tf_op jit(solution)/shard_map/nda,ndb->nab/dot_general | solution.py:24
  66.0 2.0 all-to-all-done.1
  68.9 12.2 %fusion.68 = (bf16[48,256,256]{1,2,0:T(8,128)(2,1)}, f32[48,256]{1,0:T(8,128)S(1)}) fusion(bf16[48,16,256]{2,1,0:T(8,128)(2,1)S(1)} %gather_fusion, bf16[48,16,256]{2,1,0:T(8,128)(2,1)S(1)} %gather_fusion.3, pred[48]{0:T(512)(128)(4,1)S(1)} %broadcast_compare_fusion.2, f32[48,256]{1,0:T(8,128)S(1)} %multiply_reduce_fusion.2, ...), kind=kOutput, calls=%fused_computation.154 | convolution fusion | flops 148033536 | bytes 7225392 | tf_op jit(solution)/shard_map/nda,ndb->nab/dot_general | solution.py:24
  81.9 6.4 %shard_map.50 = f32[16,128]{1,0:T(8,128)} custom-call(f32[16,128]{1,0:T(8,128)} %reshape_reshape_broadcast_in_dim.3.x_ref), custom_call_target="tpu_custom_call" | custom-call | tf_op jit(solution)/shard_map/pallas_call | solution.py:99
  90.3 1.3 select_select_fusion.1
  91.6 9.5 %all-to-all-start.2 = ((bf16[64,32,256]{2,1,0:T(8,128)(2,1)}), bf16[64,32,256]{2,1,0:T(8,128)(2,1)S(1)}, u32[]{:S(2)}, u32[]{:S(2)}) async-start(bf16[64,32,256]{2,1,0:T(8,128)(2,1)} %select_select_fusion.1), calls=%async_computation.2 | async-start | bytes 2097152 | tf_op jit(solution)/shard_map/all_to_all | solution.py:374
  103.7 25.9 %all-to-all-done.2 = bf16[64,32,256]{2,1,0:T(8,128)(2,1)S(1)} async-done(((bf16[64,32,256]{2,1,0:T(8,128)(2,1)}), bf16[64,32,256]{2,1,0:T(8,128)(2,1)S(1)}, u32[]{:S(2)}, u32[]{:S(2)}) %all-to-all-start.2) | async-done | bytes 1048608 | tf_op jit(solution)/shard_map/all_to_all | solution.py:374
  129.6 1.2 broadcast_select_fusion.1
  130.8 1.6 gather_fusion.6
  132.4 6.2 %fusion.14 = f32[8,32,256]{2,1,0:T(8,128)S(1)} fusion(bf16[64,256,256]{2,1,0:T(8,128)(2,1)} %get-tuple-element.32, bf16[32,64,256]{2,0,1:T(8,128)(2,1)} %get-tuple-element.23, bf16[8,64]{1,0:T(8,128)(2,1)S(1)} %convert_convert_fusion), kind=kOutput, calls=%fused_computation.30 | convolution fusion | flops 2151677952 | bytes 9700352 | tf_op jit(solution)/shard_map/joea,eab->job/dot_general | solution.py:432
  138.6 2.0 fusion.39
  141.3 19.2 %shard_map.51 = (f32[4,64,256]{2,1,0:T(8,128)}, f32[1,128]{1,0:T(1,128)}) custom-call(f32[4,64,256]{2,1,0:T(8,128)} %bitcast.195, f32[1,128]{1,0:T(1,128)} %fusion.58.g_ref), custom_call_target="tpu_custom_call" | custom-call | tf_op jit(solution)/shard_map/pallas_call | solution.py:223
  161.3 1.2 multiply_reduce_fusion.6
  163.0 15.7 %shard_map.52 = f32[1,128]{1,0:T(1,128)} custom-call(f32[1,128]{1,0:T(1,128)} %pad_bitcast_fusion.1.x_ref), custom_call_target="tpu_custom_call" | custom-call | tf_op jit(solution)/shard_map/pallas_call | solution.py:314
  181.7 1.3 select_select_fusion
  183.0 7.2 %all-to-all-start.3 = ((bf16[64,32,256]{2,1,0:T(8,128)(2,1)}), bf16[64,32,256]{2,1,0:T(8,128)(2,1)S(1)}, u32[]{:S(2)}, u32[]{:S(2)}) async-start(bf16[64,32,256]{2,1,0:T(8,128)(2,1)} %select_select_fusion), calls=%async_computation.3 | async-start | bytes 2097152 | tf_op jit(solution)/shard_map/all_to_all | solution.py:374
  190.2 28.5 %all-to-all-done.3 = bf16[64,32,256]{2,1,0:T(8,128)(2,1)S(1)} async-done(((bf16[64,32,256]{2,1,0:T(8,128)(2,1)}), bf16[64,32,256]{2,1,0:T(8,128)(2,1)S(1)}, u32[]{:S(2)}, u32[]{:S(2)}) %all-to-all-start.3) | async-done | bytes 1048608 | tf_op jit(solution)/shard_map/all_to_all | solution.py:374
  218.9 5.8 %fusion.19 = f32[8,32,256]{2,1,0:T(8,128)S(1)} fusion(bf16[64,256,256]{2,1,0:T(8,128)(2,1)} %get-tuple-element.32, bf16[32,64,256]{2,0,1:T(8,128)(2,1)S(1)} %get-tuple-element.21, bf16[8,64]{1,0:T(8,128)(2,1)S(1)} %convert_convert_fusion), kind=kOutput, calls=%fused_computation.31 | convolution fusion | flops 2151677952 | bytes 9700352 | tf_op jit(solution)/shard_map/joea,eab->job/dot_general | solution.py:432
  225.3 4.8 %multiply_reduce_fusion.5 = (f32[32]{0:T(128)S(1)}, f32[32]{0:T(128)S(1)}, f32[8,32,256]{2,1,0:T(8,128)}) fusion(f32[8,32,256]{2,1,0:T(8,128)S(1)} %get-tuple-element.15, f32[8,256]{1,0:T(8,128)S(1)} %sqrt.14, f32[8,32,256]{2,1,0:T(8,128)S(1)} %fusion.19, bf16[8,6,256,256]{2,3,1,0:T(8,128)(2,1)} %bitcast.181, bf16[8,6,32,256]{3,2,1,0:T(8,128)(2,1)S(1)} %bitcast.191, ...), kind=kOutput, calls=%fused_computation.73 | convolution fusion | flops 202112960 | bytes 7872816 | tf_op jit(solution)/shard_map/rkab,rkob->roa/dot_general | solution.py:425
  230.7 19.2 %shard_map.53 = (f32[4,64,256]{2,1,0:T(8,128)}, f32[1,128]{1,0:T(1,128)}) custom-call(f32[4,64,256]{2,1,0:T(8,128)} %bitcast.196, f32[1,128]{1,0:T(1,128)} %pad_bitcast_fusion.g_ref), custom_call_target="tpu_custom_call" | custom-call | tf_op jit(solution)/shard_map/pallas_call | solution.py:223
  250.6 1.1 subtract_bitcast_fusion
  (81 shorter events, 21.3 us)
Async XLA Ops:
  6.5 36.0 %all-to-all-start = ((bf16[64,16,384]{2,1,0:T(8,128)(2,1)}), bf16[64,16,384]{2,1,0:T(8,128)(2,1)S(1)}, u32[]{:S(2)}, u32[]{:S(2)}) async-start(bf16[64,16,384]{2,1,0:T(8,128)(2,1)} %pad_maximum_fusion), calls=%async_computation | async-start | bytes 1572864 | tf_op jit(solution)/shard_map/all_to_all | solution.py:360
  44.5 23.5 %all-to-all-start.1 = ((bf16[64,16,256]{2,1,0:T(8,128)(2,1)}), bf16[64,16,256]{2,1,0:T(8,128)(2,1)S(1)}, u32[]{:S(2)}, u32[]{:S(2)}) async-start(bf16[64,16,256]{2,1,0:T(8,128)(2,1)} %broadcast_select_fusion.2), calls=%async_computation.1 | async-start | bytes 1048576 | tf_op jit(solution)/shard_map/all_to_all | solution.py:374
  68.9 20.2 %copy-start = (f32[32,2048]{1,0:T(8,128)S(1)}, f32[32,2048]{1,0:T(8,128)}, u32[]{:S(2)}) copy-start(f32[32,2048]{1,0:T(8,128)} %param.5) | copy-start | bytes 786436
  81.1 20.0 %copy-start.3 = (s32[8,6]{1,0:T(8,128)S(1)}, s32[8,6]{1,0:T(8,128)}, u32[]{:S(2)}) copy-start(s32[8,6]{1,0:T(8,128)} %param.3) | copy-start | bytes 580
  91.6 38.1 %all-to-all-start.2 = ((bf16[64,32,256]{2,1,0:T(8,128)(2,1)}), bf16[64,32,256]{2,1,0:T(8,128)(2,1)S(1)}, u32[]{:S(2)}, u32[]{:S(2)}) async-start(bf16[64,32,256]{2,1,0:T(8,128)(2,1)} %select_select_fusion.1), calls=%async_computation.2 | async-start | bytes 2097152 | tf_op jit(solution)/shard_map/all_to_all | solution.py:374
  130.8 7.8 %slice-start = ((s8[6291456]{0:T(1024)(128)(4,1)}), s8[2097152]{0:T(1024)(128)(4,1)S(1)}, s32[]{:S(2)}) async-start(s8[6291456]{0:T(1024)(128)(4,1)} %bitcast.182), calls=%async_computation.4 | async-start | bytes 4194304
  132.4 6.2 %slice-start.1 = ((s8[6291456]{0:T(1024)(128)(4,1)}), s8[4194304]{0:T(1024)(128)(4,1)S(1)}, s32[]{:S(2)}) async-start(s8[6291456]{0:T(1024)(128)(4,1)} %bitcast.182), calls=%async_computation.5 | async-start | bytes 8388608
  132.4 6.2 %copy-start.1 = (bf16[48,32,256]{2,1,0:T(8,128)(2,1)S(1)}, bf16[48,32,256]{2,1,0:T(8,128)(2,1)}, u32[]{:S(2)}) copy-start(bf16[48,32,256]{2,1,0:T(8,128)(2,1)} %gather_fusion.6) | copy-start | bytes 2359300
  183.0 35.7 %all-to-all-start.3 = ((bf16[64,32,256]{2,1,0:T(8,128)(2,1)}), bf16[64,32,256]{2,1,0:T(8,128)(2,1)S(1)}, u32[]{:S(2)}, u32[]{:S(2)}) async-start(bf16[64,32,256]{2,1,0:T(8,128)(2,1)} %select_select_fusion), calls=%async_computation.3 | async-start | bytes 2097152 | tf_op jit(solution)/shard_map/all_to_all | solution.py:374
  224.7 25.2 %copy-start.4 = (f32[1,128]{1,0:T(1,128)S(1)}, f32[1,128]{1,0:T(1,128)}, u32[]{:S(2)}) copy-start(f32[1,128]{1,0:T(1,128)} %shard_map.52) | copy-start | bytes 1540
  224.7 25.9 %copy-start.2 = (f32[4,64,256]{2,1,0:T(8,128)S(1)}, f32[4,64,256]{2,1,0:T(8,128)}, u32[]{:S(2)}) copy-start(f32[4,64,256]{2,1,0:T(8,128)} %get-tuple-element.7) | copy-start | bytes 786436

commit v20 on v19

--- a/solution.py
+++ b/solution.py
@@ -218,7 +218,7 @@
     size = g.shape[0]
     g_tile = jnp.pad(g, (0, 128 - size)).reshape(1, 128)
     vmem = pl.BlockSpec(memory_space=pltpu.VMEM)
-    group = 8 if n_rows % 8 == 0 and n_rows > 8 else (4 if n_rows % 4 == 0 else n_rows)
+    group = 32 if n_rows % 32 == 0 and n_rows > 32 else (4 if n_rows % 4 == 0 else n_rows)
     groups = n_rows // group
     z_out, g_out = pl.pallas_call(
         functools.partial(fused_kernel, n_rows, n_cols, group),
@@ -307,7 +307,7 @@
 
 def rows_sum(x, cid):
     n = lax.axis_size("rows")
-    group = 8 if n % 8 == 0 and n > 8 else (4 if n % 4 == 0 else n)
+    group = 32 if n % 32 == 0 and n > 32 else (4 if n % 4 == 0 else n)
     groups = n // group
     size = x.shape[0]
     tile = jnp.pad(x, (0, 128 - size)).reshape(1, 128)

time: 254 us -> 250 us (0.984)
  Pallas kernels: 60.6 us -> 55.2 us
    pallas_call x2, Pallas kernels: 38.5 us -> 34.7 us  [fused_sum(): pl.pallas_call(functools.partial(fused_kernel, n_rows, n_cols, group), ou...]
where the time goes in v20:
time: 250 us; the launch traced here: 249 us
  waiting for transfers between devices  78.6 us (31%)
  Pallas kernels  55.2 us (22%)
  matrix products  46.3 us (19%)
  starting transfers between devices  37.4 us (15%)
  local copies, waits for them, and re-layouts  14.7 us (6%)
  other arithmetic  14.1 us (6%)
  between operations  3.06 us (1%)
    all_to_all x3, waiting for transfers between devices, swap(): lax.all_to_all(parts, 'rows', split_axis=0, concat_axis=0, tiled=True)  56.5 us
    pallas_call x2, Pallas kernels, fused_sum(): pl.pallas_call(functools.partial(fused_kernel, n_rows, n_cols, group), ou...  34.7 us
    dot_general x2, matrix products, wendland(): jnp.einsum('nda,ndb->nab', left_f, right_f, precision=lax.Precision.HIGHEST)  27.4 us
    all_to_all x3, starting transfers between devices, swap(): lax.all_to_all(parts, 'rows', split_axis=0, concat_axis=0, tiled=True)  24.4 us
    all_to_all x1, waiting for transfers between devices, local(): lax.all_to_all(jnp.concatenate([asked_x, request], axis=2), 'rows', split...  22.2 us
    pallas_call x1, Pallas kernels, rows_sum(): pl.pallas_call(functools.partial(rows_sum_kernel, n, group), out_shape=ja...  14 us
    all_to_all x1, starting transfers between devices, local(): lax.all_to_all(jnp.concatenate([asked_x, request], axis=2), 'rows', split...  13 us
    dot_general x2, matrix products, apply_partial(): jnp.einsum('joea,eab->job', picked, in_k, preferred_element_type=jnp.floa...  12 us
  transfers between devices with their start and end apart: 4, of which 4 were waited for; matrix products, arithmetic and copies ran while one was open for 7% of the time, Pallas kernels for 0%

profile of v20, /device:TPU:1, one launch (start us, length us, event | category | flops | bytes accessed | tf_op | source)
XLA Modules:
  0.0 249.3 jit_solution(17112497263810694276)
XLA Ops:
  6.5 13.0 %all-to-all-start = ((bf16[64,16,384]{2,1,0:T(8,128)(2,1)}), bf16[64,16,384]{2,1,0:T(8,128)(2,1)S(1)}, u32[]{:S(2)}, u32[]{:S(2)}) async-start(bf16[64,16,384]{2,1,0:T(8,128)(2,1)} %pad_maximum_fusion), calls=%async_computation | async-start | bytes 1572864 | tf_op jit(solution)/shard_map/all_to_all | solution.py:360
  20.3 22.2 %all-to-all-done = bf16[64,16,384]{2,1,0:T(8,128)(2,1)S(1)} async-done(((bf16[64,16,384]{2,1,0:T(8,128)(2,1)}), bf16[64,16,384]{2,1,0:T(8,128)(2,1)S(1)}, u32[]{:S(2)}, u32[]{:S(2)}) %all-to-all-start) | async-done | bytes 786464 | tf_op jit(solution)/shard_map/all_to_all | solution.py:360
  44.5 6.2 %all-to-all-start.1 = ((bf16[64,16,256]{2,1,0:T(8,128)(2,1)}), bf16[64,16,256]{2,1,0:T(8,128)(2,1)S(1)}, u32[]{:S(2)}, u32[]{:S(2)}) async-start(bf16[64,16,256]{2,1,0:T(8,128)(2,1)} %broadcast_select_fusion.2), calls=%async_computation.1 | async-start | bytes 1048576 | tf_op jit(solution)/shard_map/all_to_all | solution.py:374
  50.9 15.1 %fusion.69 = (f32[64,256]{1,0:T(8,128)S(1)}, bf16[64,256,256]{2,1,0:T(8,128)(2,1)}) fusion(bf16[64,16,256]{2,1,0:T(8,128)(2,1)S(1)} %gather_fusion.2, bf16[64,16,384]{2,1,0:T(8,128)(2,1)S(1)} %all-to-all-done, f32[64,256]{1,0:T(8,128)S(1)} %multiply_reduce_fusion, f32[64,256]{1,0:T(8,128)S(1)} %multiply_reduce_fusion.1, pred[64]{0:T(512)(128)(4,1)S(1)} %compare_and_fusion), kind=kOutput, calls=%fused_computation.155 | convolution fusion | flops 197115904 | bytes 9634304 | tf_op jit(solution)/shard_map/nda,ndb->nab/dot_general | solution.py:24
  66.0 2.0 all-to-all-done.1
  68.9 12.2 %fusion.68 = (bf16[48,256,256]{1,2,0:T(8,128)(2,1)}, f32[48,256]{1,0:T(8,128)S(1)}) fusion(bf16[48,16,256]{2,1,0:T(8,128)(2,1)S(1)} %gather_fusion, bf16[48,16,256]{2,1,0:T(8,128)(2,1)S(1)} %gather_fusion.3, pred[48]{0:T(512)(128)(4,1)S(1)} %broadcast_compare_fusion.2, f32[48,256]{1,0:T(8,128)S(1)} %multiply_reduce_fusion.2, ...), kind=kOutput, calls=%fused_computation.154 | convolution fusion | flops 148033536 | bytes 7225392 | tf_op jit(solution)/shard_map/nda,ndb->nab/dot_general | solution.py:24
  81.9 6.4 %shard_map.50 = f32[16,128]{1,0:T(8,128)} custom-call(f32[16,128]{1,0:T(8,128)} %reshape_reshape_broadcast_in_dim.3.x_ref), custom_call_target="tpu_custom_call" | custom-call | tf_op jit(solution)/shard_map/pallas_call | solution.py:99
  90.3 1.3 select_select_fusion.1
  91.6 9.5 %all-to-all-start.2 = ((bf16[64,32,256]{2,1,0:T(8,128)(2,1)}), bf16[64,32,256]{2,1,0:T(8,128)(2,1)S(1)}, u32[]{:S(2)}, u32[]{:S(2)}) async-start(bf16[64,32,256]{2,1,0:T(8,128)(2,1)} %select_select_fusion.1), calls=%async_computation.2 | async-start | bytes 2097152 | tf_op jit(solution)/shard_map/all_to_all | solution.py:374
  103.7 25.9 %all-to-all-done.2 = bf16[64,32,256]{2,1,0:T(8,128)(2,1)S(1)} async-done(((bf16[64,32,256]{2,1,0:T(8,128)(2,1)}), bf16[64,32,256]{2,1,0:T(8,128)(2,1)S(1)}, u32[]{:S(2)}, u32[]{:S(2)}) %all-to-all-start.2) | async-done | bytes 1048608 | tf_op jit(solution)/shard_map/all_to_all | solution.py:374
  129.6 1.2 broadcast_select_fusion.1
  130.8 1.6 gather_fusion.6
  132.4 6.2 %fusion.14 = f32[8,32,256]{2,1,0:T(8,128)S(1)} fusion(bf16[64,256,256]{2,1,0:T(8,128)(2,1)} %get-tuple-element.32, bf16[32,64,256]{2,0,1:T(8,128)(2,1)} %get-tuple-element.23, bf16[8,64]{1,0:T(8,128)(2,1)S(1)} %convert_convert_fusion), kind=kOutput, calls=%fused_computation.30 | convolution fusion | flops 2151677952 | bytes 9700352 | tf_op jit(solution)/shard_map/joea,eab->job/dot_general | solution.py:432
  138.6 2.0 fusion.39
  141.3 17.4 %shard_map.51 = (f32[4,64,256]{2,1,0:T(8,128)}, f32[1,128]{1,0:T(1,128)}) custom-call(f32[4,64,256]{2,1,0:T(8,128)} %bitcast.195, f32[1,128]{1,0:T(1,128)} %fusion.58.g_ref), custom_call_target="tpu_custom_call" | custom-call | tf_op jit(solution)/shard_map/pallas_call | solution.py:223
  159.4 1.2 multiply_reduce_fusion.6
  161.1 14.0 %shard_map.52 = f32[1,128]{1,0:T(1,128)} custom-call(f32[1,128]{1,0:T(1,128)} %pad_bitcast_fusion.1.x_ref), custom_call_target="tpu_custom_call" | custom-call | tf_op jit(solution)/shard_map/pallas_call | solution.py:314
  178.2 1.3 select_select_fusion
  179.4 8.7 %all-to-all-start.3 = ((bf16[64,32,256]{2,1,0:T(8,128)(2,1)}), bf16[64,32,256]{2,1,0:T(8,128)(2,1)S(1)}, u32[]{:S(2)}, u32[]{:S(2)}) async-start(bf16[64,32,256]{2,1,0:T(8,128)(2,1)} %select_select_fusion), calls=%async_computation.3 | async-start | bytes 2097152 | tf_op jit(solution)/shard_map/all_to_all | solution.py:374
  188.2 28.5 %all-to-all-done.3 = bf16[64,32,256]{2,1,0:T(8,128)(2,1)S(1)} async-done(((bf16[64,32,256]{2,1,0:T(8,128)(2,1)}), bf16[64,32,256]{2,1,0:T(8,128)(2,1)S(1)}, u32[]{:S(2)}, u32[]{:S(2)}) %all-to-all-start.3) | async-done | bytes 1048608 | tf_op jit(solution)/shard_map/all_to_all | solution.py:374
  216.9 5.8 %fusion.19 = f32[8,32,256]{2,1,0:T(8,128)S(1)} fusion(bf16[64,256,256]{2,1,0:T(8,128)(2,1)} %get-tuple-element.32, bf16[32,64,256]{2,0,1:T(8,128)(2,1)S(1)} %get-tuple-element.21, bf16[8,64]{1,0:T(8,128)(2,1)S(1)} %convert_convert_fusion), kind=kOutput, calls=%fused_computation.31 | convolution fusion | flops 2151677952 | bytes 9700352 | tf_op jit(solution)/shard_map/joea,eab->job/dot_general | solution.py:432
  223.3 4.8 %multiply_reduce_fusion.5 = (f32[32]{0:T(128)S(1)}, f32[32]{0:T(128)S(1)}, f32[8,32,256]{2,1,0:T(8,128)}) fusion(f32[8,32,256]{2,1,0:T(8,128)S(1)} %get-tuple-element.15, f32[8,256]{1,0:T(8,128)S(1)} %sqrt.14, f32[8,32,256]{2,1,0:T(8,128)S(1)} %fusion.19, bf16[8,6,256,256]{2,3,1,0:T(8,128)(2,1)} %bitcast.181, bf16[8,6,32,256]{3,2,1,0:T(8,128)(2,1)S(1)} %bitcast.191, ...), kind=kOutput, calls=%fused_computation.73 | convolution fusion | flops 202112960 | bytes 7872816 | tf_op jit(solution)/shard_map/rkab,rkob->roa/dot_general | solution.py:425
  228.7 17.4 %shard_map.53 = (f32[4,64,256]{2,1,0:T(8,128)}, f32[1,128]{1,0:T(1,128)}) custom-call(f32[4,64,256]{2,1,0:T(8,128)} %bitcast.196, f32[1,128]{1,0:T(1,128)} %pad_bitcast_fusion.g_ref), custom_call_target="tpu_custom_call" | custom-call | tf_op jit(solution)/shard_map/pallas_call | solution.py:223
  246.7 1.1 subtract_bitcast_fusion
  (81 shorter events, 21.3 us)
Async XLA Ops:
  6.5 36.0 %all-to-all-start = ((bf16[64,16,384]{2,1,0:T(8,128)(2,1)}), bf16[64,16,384]{2,1,0:T(8,128)(2,1)S(1)}, u32[]{:S(2)}, u32[]{:S(2)}) async-start(bf16[64,16,384]{2,1,0:T(8,128)(2,1)} %pad_maximum_fusion), calls=%async_computation | async-start | bytes 1572864 | tf_op jit(solution)/shard_map/all_to_all | solution.py:360
  44.5 23.5 %all-to-all-start.1 = ((bf16[64,16,256]{2,1,0:T(8,128)(2,1)}), bf16[64,16,256]{2,1,0:T(8,128)(2,1)S(1)}, u32[]{:S(2)}, u32[]{:S(2)}) async-start(bf16[64,16,256]{2,1,0:T(8,128)(2,1)} %broadcast_select_fusion.2), calls=%async_computation.1 | async-start | bytes 1048576 | tf_op jit(solution)/shard_map/all_to_all | solution.py:374
  68.9 20.2 %copy-start = (f32[32,2048]{1,0:T(8,128)S(1)}, f32[32,2048]{1,0:T(8,128)}, u32[]{:S(2)}) copy-start(f32[32,2048]{1,0:T(8,128)} %param.5) | copy-start | bytes 786436
  81.1 20.0 %copy-start.3 = (s32[8,6]{1,0:T(8,128)S(1)}, s32[8,6]{1,0:T(8,128)}, u32[]{:S(2)}) copy-start(s32[8,6]{1,0:T(8,128)} %param.3) | copy-start | bytes 580
  91.6 38.1 %all-to-all-start.2 = ((bf16[64,32,256]{2,1,0:T(8,128)(2,1)}), bf16[64,32,256]{2,1,0:T(8,128)(2,1)S(1)}, u32[]{:S(2)}, u32[]{:S(2)}) async-start(bf16[64,32,256]{2,1,0:T(8,128)(2,1)} %select_select_fusion.1), calls=%async_computation.2 | async-start | bytes 2097152 | tf_op jit(solution)/shard_map/all_to_all | solution.py:374
  130.8 7.8 %slice-start = ((s8[6291456]{0:T(1024)(128)(4,1)}), s8[2097152]{0:T(1024)(128)(4,1)S(1)}, s32[]{:S(2)}) async-start(s8[6291456]{0:T(1024)(128)(4,1)} %bitcast.182), calls=%async_computation.4 | async-start | bytes 4194304
  132.4 6.2 %slice-start.1 = ((s8[6291456]{0:T(1024)(128)(4,1)}), s8[4194304]{0:T(1024)(128)(4,1)S(1)}, s32[]{:S(2)}) async-start(s8[6291456]{0:T(1024)(128)(4,1)} %bitcast.182), calls=%async_computation.5 | async-start | bytes 8388608
  132.4 6.2 %copy-start.1 = (bf16[48,32,256]{2,1,0:T(8,128)(2,1)S(1)}, bf16[48,32,256]{2,1,0:T(8,128)(2,1)}, u32[]{:S(2)}) copy-start(bf16[48,32,256]{2,1,0:T(8,128)(2,1)} %gather_fusion.6) | copy-start | bytes 2359300
  179.4 37.3 %all-to-all-start.3 = ((bf16[64,32,256]{2,1,0:T(8,128)(2,1)}), bf16[64,32,256]{2,1,0:T(8,128)(2,1)S(1)}, u32[]{:S(2)}, u32[]{:S(2)}) async-start(bf16[64,32,256]{2,1,0:T(8,128)(2,1)} %select_select_fusion), calls=%async_computation.3 | async-start | bytes 2097152 | tf_op jit(solution)/shard_map/all_to_all | solution.py:374
  222.7 23.4 %copy-start.4 = (f32[1,128]{1,0:T(1,128)S(1)}, f32[1,128]{1,0:T(1,128)}, u32[]{:S(2)}) copy-start(f32[1,128]{1,0:T(1,128)} %shard_map.52) | copy-start | bytes 1540
  222.7 24.0 %copy-start.2 = (f32[4,64,256]{2,1,0:T(8,128)S(1)}, f32[4,64,256]{2,1,0:T(8,128)}, u32[]{:S(2)}) copy-start(f32[4,64,256]{2,1,0:T(8,128)} %get-tuple-element.7) | copy-start | bytes 786436
